TPU v7x, 256 devices: a whole 4x4x8 slice. The times are simulated.
256 devices in a mesh: seq: 64 (over x_lo, z, y), head: 4 (over x_hi, core).
Axes of the slice: x: 4 (x_hi: 2, x_lo: 2; x = x_hi * 2 + x_lo), y: 4, z: 8, core: 2. Of those that a mesh axis runs over, the one named last changes fastest.
Arguments:
- tokens: bfloat16 [32768, 2048], P(('seq', 'head'))
- ln_gain: float32 [2048], replicated, may hold values from 0.1 to 1.9
- w_qkv: bfloat16 [2048, 3, 2048], P(None, None, 'head')
- slopes: float32 [16], P('head')
- w_out: bfloat16 [2048, 2048], P('head'), may hold values from -0.125 to 0.125
- seg_ids: int32 [32768], P('seq'), may hold values from 0 to 31, never falling along the last dimension, each value on 1 to 2048 neighbouring positions
Outputs:
- hidden: bfloat16 [32768, 2048], P(('seq', 'head'))
- key_cache: bfloat16 [32768, 2048], P('seq', 'head')
- value_cache: bfloat16 [32768, 2048], P('seq', 'head')
Inputs may be any that keep to these rules, and one draw needn't show every extreme that they name: `seg_ids`: Non-decreasing along the stream; each prompt number names 1 to 2048 consecutive tokens, one prompt exactly 2048.
All inputs are finite; a program needn't handle non-finite values.
Results may differ from a plain program's by a relative error of at most 0.0075.
Values may be sent and summed in bfloat16 or wider, within the bound.
A program may use at most 128 MiB of HBM per device.

v0:
```python
import jax
import jax.numpy as jnp
from jax import lax
from jax.sharding import PartitionSpec as P

HD = 128
SPAN = 4


EPSILON = 1e-05
NEG_FILL = -1e30


def shifted(value, axis, steps):
    count = lax.axis_size(axis)
    leading, last = (max(0, -steps), min(count, count - steps))
    return lax.ppermute(value, axis, [(source, source + steps) for source in range(leading, last)])


def layer_norm(inputs, ln_gain):
    row_mean = jnp.mean(inputs, axis=-1, keepdims=True)
    centred = inputs - row_mean
    variance = jnp.mean(centred * centred, axis=-1, keepdims=True)
    return (centred * lax.rsqrt(variance + EPSILON) * ln_gain).astype(jnp.bfloat16)


def attend_one(
    run_state, queries, q_pos, seg_query, slopes_dev, key_rows, value_rows, seg_key, k_pos
):
    prev_max, prev_sum, prev_acc = run_state
    scores = jnp.einsum(
        "qhe,khe->qhk", queries, key_rows, preferred_element_type=jnp.float32
    ) * HD ** (-0.5)
    distance = (q_pos[:, None] - k_pos[None, :]).astype(jnp.float32)
    scores = scores - slopes_dev[None, :, None] * distance[:, None, :]
    valid_mask = (
        (seg_query[:, None] == seg_key[None, :])
        & (k_pos[None, :] <= q_pos[:, None])
        & (k_pos[None, :] >= 0)
    )[:, None, :]
    scores = jnp.where(valid_mask, scores, NEG_FILL)
    row_max = jnp.maximum(prev_max, jnp.max(scores, axis=-1))
    expo = jnp.where(valid_mask, jnp.exp(scores - row_max[..., None]), 0.0)
    rescale = jnp.exp(prev_max - row_max)
    new_sum = prev_sum * rescale + jnp.sum(expo, axis=-1)
    new_acc = prev_acc * rescale[..., None] + jnp.einsum(
        "qhk,khe->qhe", expo.astype(jnp.bfloat16), value_rows, preferred_element_type=jnp.float32
    )
    return (row_max, new_sum, new_acc)


def on_device(tokens, ln_gain, w_qkv, slopes, w_out, seg_ids):
    inputs = tokens.astype(jnp.float32)
    normed = layer_norm(inputs, ln_gain)
    width_local = w_qkv.shape[2]
    heads_dev = slopes.shape[0]
    joined = w_qkv.reshape(w_qkv.shape[0], 3 * width_local)
    qkv_rows = jnp.dot(
        lax.all_gather(normed, "head", axis=0, tiled=True),
        joined,
        preferred_element_type=jnp.float32,
    ).astype(jnp.bfloat16)
    block_len = qkv_rows.shape[0]
    queries = qkv_rows[:, :width_local].reshape(block_len, heads_dev, HD)
    key_cache = qkv_rows[:, width_local : 2 * width_local]
    value_cache = qkv_rows[:, 2 * width_local :]
    seq_index = lax.axis_index("seq")
    offsets = jnp.arange(block_len, dtype=jnp.int32)
    q_pos = seq_index * block_len + offsets
    own_kv = jnp.stack([key_cache, value_cache])

    def visit_block(run_state, kv_pair, seg_key, steps_back):
        k_pos = (seq_index - steps_back) * block_len + offsets

        def compute(current):
            return attend_one(
                current,
                queries,
                q_pos,
                seg_ids,
                slopes,
                kv_pair[0].reshape(block_len, heads_dev, HD),
                kv_pair[1].reshape(block_len, heads_dev, HD),
                seg_key,
                k_pos,
            )

        if steps_back == 0:
            return compute(run_state)
        return compute(run_state)

    initial = (
        jnp.full((block_len, heads_dev), NEG_FILL, jnp.float32),
        jnp.zeros((block_len, heads_dev), jnp.float32),
        jnp.zeros((block_len, heads_dev, HD), jnp.float32),
    )
    run_state = visit_block(initial, own_kv, seg_ids, 0)
    carried = (own_kv, seg_ids)
    for steps_back in range(1, SPAN + 1):
        carried = shifted((carried[0], carried[1]), "seq", 1)
        run_state = visit_block(run_state, carried[0], carried[1], steps_back)
    context = (
        (run_state[2] / run_state[1][..., None])
        .astype(jnp.bfloat16)
        .reshape(block_len, width_local)
    )
    summed = lax.psum_scatter(
        jnp.dot(context, w_out, preferred_element_type=jnp.float32).astype(jnp.bfloat16),
        "head",
        scatter_dimension=0,
        tiled=True,
    ).astype(jnp.float32)
    hidden = (inputs + summed).astype(jnp.bfloat16)
    return (hidden, key_cache, value_cache)


def solution(mesh):
    in_specs = (
        P(("seq", "head"), None),
        P(),
        P(None, None, "head"),
        P("head"),
        P("head", None),
        P("seq"),
    )
    out_specs = (P(("seq", "head"), None), P("seq", "head"), P("seq", "head"))
    return jax.shard_map(
        on_device, mesh=mesh, in_specs=in_specs, out_specs=out_specs, check_vma=False
    )
```

profile of v0, /device:TPU:6, one launch (start us, length us, event | category | flops | bytes accessed | tf_op | source)
XLA Modules:
  0.0 269.6 jit_solution(12639082960373073595)
XLA Ops:
  7.2 0.0 copy-start
  7.2 0.0 all-gather.2.cloned.1.call-start
  7.2 1.3 convert_reduce_fusion
  8.6 1.3 fusion.74
  9.9 2.2 fusion.76
  12.1 0.0 all-gather.2.cloned.1.call-update
  12.1 0.0 reduce-scatter.2.cloned.1.call-start
  12.2 8.9 %copy.29 = bf16[2048,3,512]{0,2,1:T(8,128)(2,1)} copy(bf16[2048,3,512]{2,0,1:T(8,128)(2,1)} %param.8) | data formatting | bytes 12582912 | tf_op args[2]
  21.1 21.8 %all-gather.2.cloned.1.call-done = bf16[512,2048]{1,0:T(8,128)(2,1)} async-done(((bf16[128,2048]{1,0:T(8,128)(2,1)}), bf16[512,2048]{1,0:T(8,128)(2,1)}) %all-gather.2.cloned.1.call-update) | async-done | bytes 2097168 | tf_op jit(solution)/shard_map/all_gather | solution.py:59
  42.8 6.9 %convolution_convert_fusion.1 = bf16[512,1536]{1,0:T(8,128)(2,1)S(1)} fusion(bf16[512,2048]{1,0:T(8,128)(2,1)} %all-gather.2.cloned.1.call-done, bf16[2048,1536]{0,1:T(8,128)(2,1)} %bitcast.159), kind=kOutput, calls=%fused_computation.26 | convolution fusion | flops 3222011904 | bytes 9961472 | tf_op jit(solution)/shard_map/dot_general | solution.py:58
  49.7 0.0 copy-start.20
  49.7 0.1 slice_bitcast_fusion
  49.9 0.0 copy-start.9
  49.9 0.0 copy-start.4
  49.9 0.8 copy-done.9
  50.7 0.1 pad_maximum_fusion
  50.8 0.0 copy-start.21
  50.8 3.4 %collective-permute-start.1 = (bf16[2,512,512]{2,1,0:T(8,128)(2,1)S(1)}, bf16[2,512,512]{2,1,0:T(8,128)(2,1)}, u32[]{:S(2)}, u32[]{:S(2)}) collective-permute-start(bf16[2,512,512]{2,1,0:T(8,128)(2,1)S(1)} %pad_maximum_fusion), channel_id=1, source_target_pairs={{0,4},{4,8},{8,12},{12,16},{16,20},{20,24},{24,28},{28,32},{32,36}... | collective-permute-start | bytes 3145736 | tf_op jit(solution)/shard_map/ppermute | solution.py:17
  54.2 28.1 %collective-permute-done.1 = bf16[2,512,512]{2,1,0:T(8,128)(2,1)} collective-permute-done((bf16[2,512,512]{2,1,0:T(8,128)(2,1)S(1)}, bf16[2,512,512]{2,1,0:T(8,128)(2,1)}, u32[]{:S(2)}, u32[]{:S(2)}) %collective-permute-start.1) | collective-permute-done | bytes 1048608 | tf_op jit(solution)/shard_map/ppermute | solution.py:17
  82.3 1.9 collective-permute-start.3
  84.2 1.9 collective-permute-start
  86.2 2.6 subtract_convert_fusion
  88.8 24.4 %collective-permute-done = s32[512]{0:T(512)S(1)} collective-permute-done((s32[512]{0:T(512)S(1)}, s32[512]{0:T(512)S(1)}, u32[]{:S(2)}, u32[]{:S(2)}) %collective-permute-start) | collective-permute-done | bytes 2080 | tf_op jit(solution)/shard_map/ppermute | solution.py:17
  113.2 1.9 collective-permute-start.2
  115.2 7.8 %collective-permute-done.2 = s32[512]{0:T(512)S(1)} collective-permute-done((s32[512]{0:T(512)S(1)}, s32[512]{0:T(512)S(1)}, u32[]{:S(2)}, u32[]{:S(2)}) %collective-permute-start.2) | collective-permute-done | bytes 2080 | tf_op jit(solution)/shard_map/ppermute | solution.py:17
  122.9 1.9 collective-permute-start.4
  124.9 7.8 %collective-permute-done.4 = s32[512]{0:T(512)S(1)} collective-permute-done((s32[512]{0:T(512)S(1)}, s32[512]{0:T(512)S(1)}, u32[]{:S(2)}, u32[]{:S(2)}) %collective-permute-start.4) | collective-permute-done | bytes 2080 | tf_op jit(solution)/shard_map/ppermute | solution.py:17
  132.6 1.9 collective-permute-start.6
  134.6 1.9 collective-permute-start.5
  136.5 5.9 %collective-permute-done.6 = s32[512]{0:T(512)S(1)} collective-permute-done((s32[512]{0:T(512)S(1)}, s32[512]{0:T(512)S(1)}, u32[]{:S(2)}, u32[]{:S(2)}) %collective-permute-start.6) | collective-permute-done | bytes 2080 | tf_op jit(solution)/shard_map/ppermute | solution.py:17
  142.4 2.6 and_and_fusion
  145.0 1.0 copy.55
  146.0 4.4 %fusion.15 = (f32[512,4]{0,1:T(4,128)S(1)}, f32[4,512,512]{2,1,0:T(8,128)}) fusion(f32[512,512]{0,1:T(8,128)} %get-tuple-element.42, f32[4]{0:T(128)S(1)} %copy-done.21, pred[512,512]{0,1:T(8,128)(4,1)} %get-tuple-element.37, bf16[64,4,8,128]{3,2,1,0:T(8,128)(2,1)S(1)} %get-tuple-element.21, bf16[512,512]{1,0:T(8,128)(2,1)} %copy-done.9), kind=kOutput, calls=%fused_computation.27 | convolution fusion | flops 273676288 | bytes 6561808 | tf_op jit(solution)/shard_map/qhe,khe->qhk/dot_general | solution.py:31
  150.4 2.1 fusion.122
  152.5 2.1 copy.56
  154.5 0.9 reshape_squeeze.24
  155.5 6.8 %collective-permute-done.5 = bf16[2,512,512]{2,1,0:T(8,128)(2,1)} collective-permute-done((bf16[2,512,512]{2,1,0:T(8,128)(2,1)}, bf16[2,512,512]{2,1,0:T(8,128)(2,1)}, u32[]{:S(2)}, u32[]{:S(2)}) %collective-permute-start.5) | collective-permute-done | bytes 1048608 | tf_op jit(solution)/shard_map/ppermute | solution.py:17
  162.3 1.9 collective-permute-start.7
  164.2 2.1 fusion.121
  166.3 1.0 copy.57
  167.3 1.2 reshape_squeeze.26
  168.4 2.7 fusion.84
  171.1 2.1 fusion.120
  173.2 1.0 copy.58
  174.2 1.2 reshape_squeeze.28
  175.4 2.7 fusion.82
  178.1 11.0 %collective-permute-done.7 = bf16[2,512,512]{2,1,0:T(8,128)(2,1)} collective-permute-done((bf16[2,512,512]{2,1,0:T(8,128)(2,1)}, bf16[2,512,512]{2,1,0:T(8,128)(2,1)}, u32[]{:S(2)}, u32[]{:S(2)}) %collective-permute-start.7) | collective-permute-done | bytes 1048608 | tf_op jit(solution)/shard_map/ppermute | solution.py:17
  189.1 2.1 fusion.119
  191.1 1.0 copy.59
  192.2 1.2 reshape_squeeze.30
  193.4 0.7 fusion.80
  194.1 1.5 copy-done.1
  195.6 0.3 copy-done.5
  195.9 9.3 %fusion.5 = (f32[512,4]{0,1:T(4,128)S(1)}, f32[512,4]{0,1:T(4,128)S(1)}, f32[512,4]{0,1:T(4,128)S(1)}, f32[512,4]{0,1:T(4,128)S(1)}, f32[512,4]{0,1:T(4,128)S(1)}, /*index=5*/f32[4,512,512]{2,1,0:T(8,128)S(1)}) fusion(f32[4,512,512]{2,1,0:T(8,128)} %get-tuple-element.44, f32[512,4]{0,1:T(4,128)S(1)} %broadcast_maximum_fusion, ...), kind=kOutput, calls=%fused_computation.15 | convolution fusion | flops 296736768 | bytes 28622864 | tf_op jit(solution)/shard_map/qhe,khe->qhk/dot_general | solution.py:31
  205.2 7.0 %fusion.7 = (f32[512,4]{0,1:T(4,128)S(1)}, f32[512,4]{0,1:T(4,128)S(1)}, f32[512,4]{0,1:T(4,128)S(1)}, f32[512,4]{0,1:T(4,128)S(1)}) fusion(f32[4,512,512]{2,1,0:T(8,128)S(1)} %get-tuple-element.45, f32[512,4]{0,1:T(4,128)S(1)} %get-tuple-element.20, f32[512,512]{0,1:T(8,128)} %get-tuple-element.39, f32[4]{0:T(128)S(1)} %copy-done.21, ...), kind=kLoop, calls=%fused_computation.17 | loop fusion | flops 29351936 | bytes 22085648 | tf_op jit(solution)/shard_map/reduce_sum | solution.py:45
  212.3 1.8 fusion.69
  214.2 1.9 fusion.63
  216.2 1.9 fusion.57
  218.1 1.9 fusion.51
  220.0 1.8 divide_convert_fusion
  221.8 2.6 convolution_convert_fusion
  224.4 0.0 reduce-scatter.2.cloned.1.call-update
  224.5 36.4 %reduce-scatter.2.cloned.1.call-done = bf16[128,2048]{1,0:T(8,128)(2,1)} async-done(((bf16[512,2048]{1,0:T(8,128)(2,1)}), bf16[128,2048]{1,0:T(8,128)(2,1)}) %reduce-scatter.2.cloned.1.call-update) | async-done | bytes 524304 | tf_op jit(solution)/shard_map/reduce_scatter | solution.py:107
  260.8 2.0 fusion.77
  (50 shorter events, 0.2 us)
Async XLA Ops:
  7.2 214.7 %copy-start = (bf16[512,2048]{1,0:T(8,128)(2,1)S(1)}, bf16[512,2048]{1,0:T(8,128)(2,1)}, u32[]{:S(2)}) copy-start(bf16[512,2048]{1,0:T(8,128)(2,1)} %param.10) | copy-start | bytes 6291460
  7.2 35.7 %all-gather.2.cloned.1.call-start = ((), (), s32[]{:S(2)}) async-start(), calls=%async_computation.1 | async-start | bytes 2621440 | tf_op jit(solution)/shard_map/all_gather | solution.py:59
  12.1 248.7 %reduce-scatter.2.cloned.1.call-start = ((), (), s32[]{:S(2)}) async-start(), calls=%async_computation.2 | async-start | bytes 2621440 | tf_op jit(solution)/shard_map/reduce_scatter | solution.py:107
  49.7 34.5 %copy-start.20 = (s32[512]{0:T(512)S(1)}, s32[512]{0:T(512)}, u32[]{:S(2)}) copy-start(s32[512]{0:T(512)} %param.11) | copy-start | bytes 6148
  49.9 0.8 copy-start.9
  49.9 95.1 %copy-start.4 = (bf16[512,512]{1,0:T(8,128)(2,1)}, bf16[512,512]{1,0:T(8,128)(2,1)S(1)}, u32[]{:S(2)}) copy-start(bf16[512,512]{1,0:T(8,128)(2,1)S(1)} %get-tuple-element.22) | copy-start | bytes 1572868
  50.8 95.2 %copy-start.21 = (f32[4]{0:T(128)S(1)}, f32[4]{0:T(128)}, u32[]{:S(2)}) copy-start(f32[4]{0:T(128)} %param.9) | copy-start | bytes 52
  50.8 31.5 %collective-permute-start.1 = (bf16[2,512,512]{2,1,0:T(8,128)(2,1)S(1)}, bf16[2,512,512]{2,1,0:T(8,128)(2,1)}, u32[]{:S(2)}, u32[]{:S(2)}) collective-permute-start(bf16[2,512,512]{2,1,0:T(8,128)(2,1)S(1)} %pad_maximum_fusion), channel_id=1, source_target_pairs={{0,4},{4,8},{8,12},{12,16},{16,20},{20,24},{24,28},{28,32},{32,36}... | collective-permute-start | bytes 3145736 | tf_op jit(solution)/shard_map/ppermute | solution.py:17
  82.3 52.2 %collective-permute-start.3 = (bf16[2,512,512]{2,1,0:T(8,128)(2,1)}, bf16[2,512,512]{2,1,0:T(8,128)(2,1)}, u32[]{:S(2)}, u32[]{:S(2)}) collective-permute-start(bf16[2,512,512]{2,1,0:T(8,128)(2,1)} %collective-permute-done.1), channel_id=1, source_target_pairs={{0,4},{4,8},{8,12},{12,16},{16,20},{20,24},{24,28},{28,32},{32,36}... | collective-permute-start | bytes 3145736 | tf_op jit(solution)/shard_map/ppermute | solution.py:17
  84.2 29.0 %collective-permute-start = (s32[512]{0:T(512)S(1)}, s32[512]{0:T(512)S(1)}, u32[]{:S(2)}, u32[]{:S(2)}) collective-permute-start(s32[512]{0:T(512)S(1)} %copy-done.20), channel_id=1, source_target_pairs={{0,4},{4,8},{8,12},{12,16},{16,20},{20,24},{24,28},{28,32},{32,36}... | collective-permute-start | bytes 6152 | tf_op jit(solution)/shard_map/ppermute | solution.py:17
  113.2 9.7 %collective-permute-start.2 = (s32[512]{0:T(512)S(1)}, s32[512]{0:T(512)S(1)}, u32[]{:S(2)}, u32[]{:S(2)}) collective-permute-start(s32[512]{0:T(512)S(1)} %collective-permute-done), channel_id=1, source_target_pairs={{0,4},{4,8},{8,12},{12,16},{16,20},{20,24},{24,28},{28,32},{32,36}... | collective-permute-start | bytes 6152 | tf_op jit(solution)/shard_map/ppermute | solution.py:17
  122.9 9.7 %collective-permute-start.4 = (s32[512]{0:T(512)S(1)}, s32[512]{0:T(512)S(1)}, u32[]{:S(2)}, u32[]{:S(2)}) collective-permute-start(s32[512]{0:T(512)S(1)} %collective-permute-done.2), channel_id=1, source_target_pairs={{0,4},{4,8},{8,12},{12,16},{16,20},{20,24},{24,28},{28,32},{32,36}... | collective-permute-start | bytes 6152 | tf_op jit(solution)/shard_map/ppermute | solution.py:17
  132.6 9.8 %collective-permute-start.6 = (s32[512]{0:T(512)S(1)}, s32[512]{0:T(512)S(1)}, u32[]{:S(2)}, u32[]{:S(2)}) collective-permute-start(s32[512]{0:T(512)S(1)} %collective-permute-done.4), channel_id=1, source_target_pairs={{0,4},{4,8},{8,12},{12,16},{16,20},{20,24},{24,28},{28,32},{32,36}... | collective-permute-start | bytes 6152 | tf_op jit(solution)/shard_map/ppermute | solution.py:17
  134.6 27.7 %collective-permute-start.5 = (bf16[2,512,512]{2,1,0:T(8,128)(2,1)}, bf16[2,512,512]{2,1,0:T(8,128)(2,1)}, u32[]{:S(2)}, u32[]{:S(2)}) collective-permute-start(bf16[2,512,512]{2,1,0:T(8,128)(2,1)} %collective-permute-done.3), channel_id=1, source_target_pairs={{0,4},{4,8},{8,12},{12,16},{16,20},{20,24},{24,28},{28,32},{32,36}... | collective-permute-start | bytes 3145736 | tf_op jit(solution)/shard_map/ppermute | solution.py:17
  162.3 26.8 %collective-permute-start.7 = (bf16[2,512,512]{2,1,0:T(8,128)(2,1)}, bf16[2,512,512]{2,1,0:T(8,128)(2,1)}, u32[]{:S(2)}, u32[]{:S(2)}) collective-permute-start(bf16[2,512,512]{2,1,0:T(8,128)(2,1)} %collective-permute-done.5), channel_id=1, source_target_pairs={{0,4},{4,8},{8,12},{12,16},{16,20},{20,24},{24,28},{28,32},{32,36}... | collective-permute-start | bytes 3145736 | tf_op jit(solution)/shard_map/ppermute | solution.py:17
  193.4 2.2 copy-start.1
  193.4 2.5 copy-start.5
  195.9 9.3 %copy-start.2 = (f32[4,512,512]{2,1,0:T(8,128)S(1)}, f32[4,512,512]{2,1,0:T(8,128)}, u32[]{:S(2)}) copy-start(f32[4,512,512]{2,1,0:T(8,128)} %fusion.82) | copy-start | bytes 12582916
  205.2 7.1 %copy-start.13 = (f32[512,512]{0,1:T(8,128)S(1)}, f32[512,512]{0,1:T(8,128)}, u32[]{:S(2)}) copy-start(f32[512,512]{0,1:T(8,128)} %get-tuple-element.42) | copy-start | bytes 3145732
  205.2 7.1 %copy-start.14 = (bf16[512,512]{0,1:T(8,128)(2,1)S(1)}, bf16[512,512]{0,1:T(8,128)(2,1)}, u32[]{:S(2)}) copy-start(bf16[512,512]{0,1:T(8,128)(2,1)} %copy.55) | copy-start | bytes 1572868
  205.2 7.1 %copy-start.19 = (pred[512,512]{0,1:T(8,128)(4,1)S(1)}, pred[512,512]{0,1:T(8,128)(4,1)}, u32[]{:S(2)}) copy-start(pred[512,512]{0,1:T(8,128)(4,1)} %get-tuple-element.37) | copy-start | bytes 786436
  205.2 7.1 %copy-start.22 = (f32[4,512,512]{2,1,0:T(8,128)S(1)}, f32[4,512,512]{2,1,0:T(8,128)}, u32[]{:S(2)}) copy-start(f32[4,512,512]{2,1,0:T(8,128)} %get-tuple-element.44) | copy-start | bytes 12582916
  212.3 1.9 copy-start.8
  212.3 1.9 copy-start.12
  212.3 1.9 copy-start.15
  214.2 1.9 copy-start.7
  214.2 1.9 copy-start.11
  214.2 1.9 copy-start.16
  216.1 1.9 copy-start.6
  216.1 1.9 copy-start.10
  216.2 1.9 copy-start.17
  218.1 1.9 copy-start.18
  221.8 39.0 %copy-start.3 = (bf16[128,2048]{1,0:T(8,128)(2,1)S(1)}, bf16[128,2048]{1,0:T(8,128)(2,1)}, u32[]{:S(2)}) copy-start(bf16[128,2048]{1,0:T(8,128)(2,1)} %param.6) | copy-start | bytes 1572868
Sparse Core Ops, SparseCore 0:
  12.3 30.5 all-gather.1
  224.6 36.1 reduce-scatter.1
where the time goes:
time: 273 us; the launch traced here: 270 us
  waiting for transfers between devices  150 us (55%)
  matrix products  38.5 us (14%)
  local copies, waits for them, and re-layouts  30.5 us (11%)
  other arithmetic  19.2 us (7%)
  starting transfers between devices  16.9 us (6%)
  between operations  14.6 us (5%)
    ppermute x8, waiting for transfers between devices, shifted(): lax.ppermute(value, axis, [(source, source + steps) for source in range(l...  91.8 us
    reduce_scatter x1, waiting for transfers between devices, on_device(): lax.psum_scatter(jnp.dot(context, w_out, preferred_element_type=jnp.float...  36.4 us
    all_gather x1, waiting for transfers between devices, on_device(): lax.all_gather(normed, 'head', axis=0, tiled=True)  21.8 us
    dot_general x5, matrix products, attend_one(): jnp.einsum('qhe,khe->qhk', queries, key_rows, preferred_element_type=jnp....  19.8 us
    ppermute x8, starting transfers between devices, shifted(): lax.ppermute(value, axis, [(source, source + steps) for source in range(l...  16.8 us
    unnamed x48, local copies, waits for them, and re-layouts  11.7 us
    dot_general x5, matrix products, attend_one(): jnp.einsum('qhk,khe->qhe', expo.astype(jnp.bfloat16), value_rows, preferr...  9.28 us
    slice x4, local copies, waits for them, and re-layouts, compute(): kv_pair[1].reshape(block_len, heads_dev, HD)  8.28 us
  transfers between devices with their start and end apart: 10, of which 9 were waited for; matrix products, arithmetic and copies ran while one was open for 14% of the time, Pallas kernels for 0%

commit v1 on v0

v1 whole, which is shorter than its diff:
```python
import jax
import jax.numpy as jnp
from jax import lax
from jax.sharding import PartitionSpec as P

HD = 128
SPAN = 4


EPSILON = 1e-05
NEG_FILL = -1e30


def shifted(value, axis, steps):
    count = lax.axis_size(axis)
    leading, last = (max(0, -steps), min(count, count - steps))
    return lax.ppermute(value, axis, [(source, source + steps) for source in range(leading, last)])


def swapped(value, axis, mask):
    count = lax.axis_size(axis)
    return lax.ppermute(value, axis, [(source, source ^ mask) for source in range(count)])


def layer_norm(inputs, ln_gain):
    row_mean = jnp.mean(inputs, axis=-1, keepdims=True)
    centred = inputs - row_mean
    variance = jnp.mean(centred * centred, axis=-1, keepdims=True)
    return (centred * lax.rsqrt(variance + EPSILON) * ln_gain).astype(jnp.bfloat16)


def attend_one(run_state, queries, q_pos, seg_query, slopes_dev, keys, values, seg_key, k_pos):
    prev_max, prev_sum, prev_acc = run_state
    scores = jnp.einsum(
        "hqe,hke->hqk", queries, keys, preferred_element_type=jnp.float32
    ) * HD ** (-0.5)
    distance = (q_pos[:, None] - k_pos[None, :]).astype(jnp.float32)
    scores = scores - slopes_dev[:, None, None] * distance[None, :, :]
    valid_mask = (
        (seg_query[:, None] == seg_key[None, :])
        & (k_pos[None, :] <= q_pos[:, None])
        & (k_pos[None, :] >= 0)
    )[None, :, :]
    scores = jnp.where(valid_mask, scores, NEG_FILL)
    row_max = jnp.maximum(prev_max, jnp.max(scores, axis=-1))
    expo = jnp.where(valid_mask, jnp.exp(scores - row_max[..., None]), 0.0)
    rescale = jnp.exp(prev_max - row_max)
    new_sum = prev_sum * rescale + jnp.sum(expo, axis=-1)
    new_acc = prev_acc * rescale[..., None] + jnp.einsum(
        "hqk,hke->hqe", expo.astype(jnp.bfloat16), values, preferred_element_type=jnp.float32
    )
    return (row_max, new_sum, new_acc)


def on_device(tokens, ln_gain, w_qkv, slopes, w_out, seg_ids):
    inputs = tokens.astype(jnp.float32)
    normed = layer_norm(inputs, ln_gain)
    rows_dev = normed.shape[0]
    head = lax.axis_index("head")
    n_head = lax.axis_size("head")

    cross = swapped(normed, "head", 2)
    partner = swapped(jnp.stack([normed, cross]), "head", 1)
    pieces = jnp.stack([normed, partner[0], cross, partner[1]])
    order = jnp.arange(n_head, dtype=jnp.int32) ^ head
    block_rows = jnp.take(pieces, order, axis=0).reshape(n_head * rows_dev, normed.shape[1])

    width_local = w_qkv.shape[2]
    heads_dev = slopes.shape[0]
    joined = w_qkv.reshape(w_qkv.shape[0], 3 * width_local)
    qkv_rows = jnp.dot(block_rows, joined, preferred_element_type=jnp.float32).astype(jnp.bfloat16)
    block_len = qkv_rows.shape[0]
    key_cache = qkv_rows[:, width_local : 2 * width_local]
    value_cache = qkv_rows[:, 2 * width_local :]

    def head_major(cols):
        return cols.reshape(block_len, heads_dev, HD).transpose(1, 0, 2)

    queries = head_major(qkv_rows[:, :width_local])
    keys_hm = head_major(key_cache)
    values_hm = head_major(value_cache)

    seg_rows = seg_ids.astype(jnp.bfloat16).reshape(block_len // HD, HD)
    pad_rows = (-seg_rows.shape[0]) % 8
    seg_rows = jnp.concatenate([seg_rows, jnp.zeros((pad_rows, HD), jnp.bfloat16)], axis=0)
    kv_len = heads_dev * block_len
    payload = jnp.concatenate(
        [keys_hm.reshape(kv_len, HD), values_hm.reshape(kv_len, HD), seg_rows], axis=0
    )
    arrived = [shifted(payload, "seq", steps) for steps in range(1, SPAN + 1)]

    seq_index = lax.axis_index("seq")
    offsets = jnp.arange(block_len, dtype=jnp.int32)
    q_pos = seq_index * block_len + offsets

    initial = (
        jnp.full((heads_dev, block_len), NEG_FILL, jnp.float32),
        jnp.zeros((heads_dev, block_len), jnp.float32),
        jnp.zeros((heads_dev, block_len, HD), jnp.float32),
    )
    run_state = attend_one(
        initial, queries, q_pos, seg_ids, slopes, keys_hm, values_hm, seg_ids, q_pos
    )
    for steps_back in range(1, SPAN + 1):
        got = arrived[steps_back - 1]
        k_pos = (seq_index - steps_back) * block_len + offsets
        keys_in = got[:kv_len].reshape(heads_dev, block_len, HD)
        values_in = got[kv_len : 2 * kv_len].reshape(heads_dev, block_len, HD)
        seg_in = got[2 * kv_len : 2 * kv_len + block_len // HD].reshape(block_len).astype(jnp.int32)
        run_state = attend_one(
            run_state, queries, q_pos, seg_ids, slopes, keys_in, values_in, seg_in, k_pos
        )
    context = (run_state[2] / run_state[1][..., None]).astype(jnp.bfloat16)
    partial = jnp.einsum(
        "hqe,hed->qd",
        context,
        w_out.reshape(heads_dev, HD, w_out.shape[1]),
        preferred_element_type=jnp.float32,
    ).astype(jnp.bfloat16)

    partial4 = partial.reshape(n_head, rows_dev, partial.shape[1])
    sent = jnp.take(partial4, jnp.stack([head ^ 1, head ^ 3]), axis=0)
    kept = jnp.take(partial4, jnp.stack([head, head ^ 2]), axis=0)
    chip_sum = kept.astype(jnp.float32) + swapped(sent, "head", 1).astype(jnp.float32)
    other_chip = swapped(chip_sum[1].astype(jnp.bfloat16), "head", 2).astype(jnp.float32)
    hidden = (inputs + chip_sum[0] + other_chip).astype(jnp.bfloat16)
    return (hidden, key_cache, value_cache)


def solution(mesh):
    in_specs = (
        P(("seq", "head"), None),
        P(),
        P(None, None, "head"),
        P("head"),
        P("head", None),
        P("seq"),
    )
    out_specs = (P(("seq", "head"), None), P("seq", "head"), P("seq", "head"))
    return jax.shard_map(
        on_device, mesh=mesh, in_specs=in_specs, out_specs=out_specs, check_vma=False
    )
```

time: 273 us -> 235 us (0.86); the launches traced: 270 us -> 235 us
  waiting for transfers between devices: 150 us -> 110 us
  between operations: 14.6 us -> 1.01 us
  other arithmetic: 19.2 us -> 25.7 us
  matrix products: 38.5 us -> 44.4 us
  local copies, waits for them, and re-layouts: 30.5 us -> 34.5 us
    reduce_scatter x1 -> x0, waiting for transfers between devices: 36.4 us -> none  [on_device(): lax.psum_scatter(jnp.dot(context, w_out, preferred_element_type=jnp.float...]
    ppermute x0 -> x4, waiting for transfers between devices: none -> 27 us  [swapped(): lax.ppermute(value, axis, [(source, source ^ mask) for source in range(co...]
    all_gather x1 -> x0, waiting for transfers between devices: 21.8 us -> none  [on_device(): lax.all_gather(normed, 'head', axis=0, tiled=True)]
    another operation x9 -> x0, local copies, waits for them, and re-layouts: 10.5 us -> none  [the longest x5 6.12 us: compute(): kv_pair[1].reshape(block_len, heads_dev, HD)]
    gather x0 -> x3, local copies, waits for them, and re-layouts: none -> 9.05 us  [the longest x1 3.64 us: on_device(): jnp.take(pieces, order, axis=0).reshape(n_head * rows_dev, normed.shape[1])]
    ppermute x8 -> x4, waiting for transfers between devices: 91.8 us -> 83.4 us  [shifted(): lax.ppermute(value, axis, [(source, source + steps) for source in range(l...]
    concatenate x0 -> x1, local copies, waits for them, and re-layouts: none -> 6.9 us  [on_device(): jnp.concatenate([keys_hm.reshape(kv_len, HD), values_hm.reshape(kv_len, H...]
    dot_general x12 -> x11, matrix products: 38.5 us -> 44.4 us  [the longest x4 17 us: attend_one(): jnp.einsum('hqk,hke->hqe', expo.astype(jnp.bfloat16), values, preferred_e...]
  transfers between devices with their start and end apart: 10 -> 8, of which waited for: 9 -> 6; matrix products, arithmetic and copies ran while one was open for 14% -> 7% of each run, Pallas kernels for 0% -> 0%
where the time goes in v1:
time: 235 us
  waiting for transfers between devices  110 us (47%)
  matrix products  44.4 us (19%)
  local copies, waits for them, and re-layouts  34.5 us (15%)
  other arithmetic  25.7 us (11%)
  starting transfers between devices  18.4 us (8%)
    ppermute x4, waiting for transfers between devices, shifted(): lax.ppermute(value, axis, [(source, source + steps) for source in range(l...  83.4 us
    ppermute x4, waiting for transfers between devices, swapped(): lax.ppermute(value, axis, [(source, source ^ mask) for source in range(co...  27 us
    dot_general x4, matrix products, attend_one(): jnp.einsum('hqk,hke->hqe', expo.astype(jnp.bfloat16), values, preferred_e...  17 us
    ppermute x4, starting transfers between devices, shifted(): lax.ppermute(value, axis, [(source, source + steps) for source in range(l...  15.7 us
    dot_general x5, matrix products, attend_one(): jnp.einsum('hqe,hke->hqk', queries, keys, preferred_element_type=jnp.floa...  13.8 us
    unnamed x44, local copies, waits for them, and re-layouts  9.12 us
    dot_general x1, matrix products, on_device(): jnp.einsum('hqe,hed->qd', context, w_out.reshape(heads_dev, HD, w_out.sha...  7.24 us
    concatenate x1, local copies, waits for them, and re-layouts, on_device(): jnp.concatenate([keys_hm.reshape(kv_len, HD), values_hm.reshape(kv_len, H...  6.9 us
  transfers between devices with their start and end apart: 8, of which 6 were waited for; matrix products, arithmetic and copies ran while one was open for 7% of the time, Pallas kernels for 0%

profile of v1, /device:TPU:6, one launch (start us, length us, event | category | flops | bytes accessed | tf_op | source)
XLA Modules:
  0.0 234.5 jit_solution(6764167502303989794)
XLA Ops:
  0.6 0.0 copy-start
  0.6 1.3 convert_reduce_fusion
  2.0 1.3 fusion.54
  3.3 1.4 fusion.56
  4.8 1.5 collective-permute-start
  6.2 1.4 fusion.122
  7.7 12.3 %collective-permute-done = bf16[128,2048]{1,0:T(8,128)(2,1)S(1)} collective-permute-done((bf16[128,2048]{1,0:T(8,128)(2,1)S(1)}, bf16[128,2048]{1,0:T(8,128)(2,1)S(1)}, u32[]{:S(2)}, u32[]{:S(2)}) %collective-permute-start) | collective-permute-done | bytes 524320 | tf_op jit(solution)/shard_map/ppermute | solution.py:22
  20.0 1.1 pad_maximum_fusion.1
  21.1 0.0 collective-permute-start.1
  21.1 8.9 %copy.11 = bf16[2048,3,512]{0,2,1:T(8,128)(2,1)} copy(bf16[2048,3,512]{2,0,1:T(8,128)(2,1)} %param.10) | data formatting | bytes 12582912 | tf_op args[2]
  30.0 0.0 collective-permute-done.1
  30.0 1.3 fusion.110
  31.3 1.6 pad_maximum_fusion
  32.9 3.6 %gather_fusion = bf16[4,128,2048]{2,1,0:T(8,128)(2,1)} fusion(bf16[4,128,2048]{2,1,0:T(8,128)(2,1)} %pad_maximum_fusion, s32[1024]{0:T(1024)S(1)} %pad_clamp_fusion.2), kind=kCustom, calls=%fused_computation.2 | custom fusion | bytes 4194320 | tf_op jit(solution)/shard_map/jit(_take)/gather | solution.py:66
  36.5 1.9 broadcast_select_fusion
  38.4 6.3 %convolution_convert_fusion = bf16[512,1536]{1,0:T(8,128)(2,1)S(1)} fusion(bf16[512,2048]{1,0:T(8,128)(2,1)S(1)} %bitcast.126, bf16[2048,1536]{0,1:T(8,128)(2,1)} %bitcast.123), kind=kOutput, calls=%fused_computation.24 | convolution fusion | flops 3222011904 | bytes 9961472 | tf_op jit(solution)/shard_map/dot_general | solution.py:71
  44.7 0.1 slice_bitcast_fusion.1
  44.9 0.0 copy-start.7
  44.9 0.0 copy-start.9
  44.9 1.1 copy_bitcast_fusion.1
  46.0 0.9 copy_bitcast_fusion
  46.9 6.9 %concatenate.3 = bf16[4104,128]{1,0:T(8,128)(2,1)} concatenate(bf16[2048,128]{1,0:T(8,128)(2,1)} %bitcast.130, bf16[2048,128]{1,0:T(8,128)(2,1)} %bitcast.131, bf16[4,128]{1,0:T(4,128)(2,1)S(1)} %convert_bitcast_fusion, bf16[4,128]{1,0:T(4,128)(2,1)S(1)} %broadcast_in_dim.158), dimensions={0} | concatenate | bytes 2101248 | tf_op jit(solution)/shard_map/concatenate | solution.py:87
  53.8 3.8 %collective-permute-start.5 = (bf16[4104,128]{1,0:T(8,128)(2,1)}, bf16[4104,128]{1,0:T(8,128)(2,1)}, u32[]{:S(2)}, u32[]{:S(2)}) collective-permute-start(bf16[4104,128]{1,0:T(8,128)(2,1)} %concatenate.3), channel_id=1, source_target_pairs={{0,16},{4,20},{8,24},{12,28},{16,32},{20,36},{24,40},{28,44},{32,4... | collective-permute-start | bytes 3151880 | tf_op jit(solution)/shard_map/ppermute | solution.py:17
  57.7 4.9 %collective-permute-start.4 = (bf16[4104,128]{1,0:T(8,128)(2,1)}, bf16[4104,128]{1,0:T(8,128)(2,1)}, u32[]{:S(2)}, u32[]{:S(2)}) collective-permute-start(bf16[4104,128]{1,0:T(8,128)(2,1)} %concatenate.3), channel_id=1, source_target_pairs={{0,12},{4,16},{8,20},{12,24},{16,28},{20,32},{24,36},{28,40},{32,4... | collective-permute-start | bytes 3151880 | tf_op jit(solution)/shard_map/ppermute | solution.py:17
  62.6 3.9 %collective-permute-start.3 = (bf16[4104,128]{1,0:T(8,128)(2,1)}, bf16[4104,128]{1,0:T(8,128)(2,1)S(1)}, u32[]{:S(2)}, u32[]{:S(2)}) collective-permute-start(bf16[4104,128]{1,0:T(8,128)(2,1)} %concatenate.3), channel_id=1, source_target_pairs={{0,8},{4,12},{8,16},{12,20},{16,24},{20,28},{24,32},{28,36},{32,40... | collective-permute-start | bytes 3151880 | tf_op jit(solution)/shard_map/ppermute | solution.py:17
  66.5 0.1 compare_and_fusion
  66.6 3.1 %collective-permute-start.2 = (bf16[4104,128]{1,0:T(8,128)(2,1)}, bf16[4104,128]{1,0:T(8,128)(2,1)S(1)}, u32[]{:S(2)}, u32[]{:S(2)}) collective-permute-start(bf16[4104,128]{1,0:T(8,128)(2,1)} %concatenate.3), channel_id=1, source_target_pairs={{0,4},{4,8},{8,12},{12,16},{16,20},{20,24},{24,28},{28,32},{32,36}... | collective-permute-start | bytes 3151880 | tf_op jit(solution)/shard_map/ppermute | solution.py:17
  69.7 1.6 subtract_convert_fusion
  71.3 14.7 %collective-permute-done.5 = bf16[4104,128]{1,0:T(8,128)(2,1)} collective-permute-done((bf16[4104,128]{1,0:T(8,128)(2,1)}, bf16[4104,128]{1,0:T(8,128)(2,1)}, u32[]{:S(2)}, u32[]{:S(2)}) %collective-permute-start.5) | collective-permute-done | bytes 1050656 | tf_op jit(solution)/shard_map/ppermute | solution.py:17
  86.0 0.7 fusion.80
  86.7 23.0 %collective-permute-done.4 = bf16[4104,128]{1,0:T(8,128)(2,1)} collective-permute-done((bf16[4104,128]{1,0:T(8,128)(2,1)}, bf16[4104,128]{1,0:T(8,128)(2,1)}, u32[]{:S(2)}, u32[]{:S(2)}) %collective-permute-start.4) | collective-permute-done | bytes 1050656 | tf_op jit(solution)/shard_map/ppermute | solution.py:17
  109.7 0.7 fusion.81
  110.3 23.4 %collective-permute-done.3 = bf16[4104,128]{1,0:T(8,128)(2,1)S(1)} collective-permute-done((bf16[4104,128]{1,0:T(8,128)(2,1)}, bf16[4104,128]{1,0:T(8,128)(2,1)S(1)}, u32[]{:S(2)}, u32[]{:S(2)}) %collective-permute-start.3) | collective-permute-done | bytes 1050656 | tf_op jit(solution)/shard_map/ppermute | solution.py:17
  133.8 22.3 %collective-permute-done.2 = bf16[4104,128]{1,0:T(8,128)(2,1)S(1)} collective-permute-done((bf16[4104,128]{1,0:T(8,128)(2,1)}, bf16[4104,128]{1,0:T(8,128)(2,1)S(1)}, u32[]{:S(2)}, u32[]{:S(2)}) %collective-permute-start.2) | collective-permute-done | bytes 1050656 | tf_op jit(solution)/shard_map/ppermute | solution.py:17
  156.1 2.6 %and_and_fusion = (pred[512,512]{0,1:T(8,128)(4,1)}, pred[512,512]{0,1:T(8,128)(4,1)}, pred[512,512]{0,1:T(8,128)(4,1)}, pred[512,512]{0,1:T(8,128)(4,1)S(1)}, pred[512,512]{0,1:T(8,128)(4,1)S(1)}) fusion(s32[512]{0:T(512)S(1)} %iota_add_fusion.4, s32[512]{0:T(512)S(1)} %copy-done.19, s32[512]{0:T(512)S(1)} %get-tuple-element.53, s32[512]{0:T(512)S(1)} %fusion.80, ...), kind=kLoop, calls=%fused_computation.67 | loop fusion | flops 5242880 | bytes 1333760 | tf_op jit(solution)/shard_map/and | solution.py:40
  158.7 0.0 copy-done.20
  158.7 3.1 %fusion.10 = (f32[4,512]{1,0:T(4,128)S(1)}, f32[4,512,512]{1,2,0:T(8,128)}) fusion(f32[512,512]{0,1:T(8,128)S(1)} %get-tuple-element.49, f32[4]{0:T(128)S(1)} %copy-done.20, pred[512,512]{0,1:T(8,128)(4,1)S(1)} %get-tuple-element.44, bf16[64,4,8,128]{3,2,1,0:T(8,128)(2,1)S(1)} %get-tuple-element.26, bf16[512,512]{1,0:T(8,128)(2,1)S(1)} %get-tuple-element.28), kind=kOutput, calls=%fused_computation.25 | convolution fusion | flops 273676288 | bytes 6561808 | tf_op jit(solution)/shard_map/hqe,hke->hqk/dot_general | solution.py:34
  161.8 0.0 copy-done.13
  161.8 2.1 fusion.108
  163.9 0.7 fusion.65
  164.6 0.9 fusion.107
  165.5 0.7 fusion.66
  166.2 2.1 fusion.109
  168.2 0.7 fusion.64
  169.0 1.1 fusion.106
  170.1 8.6 %fusion = (f32[4,512]{1,0:T(4,128)S(1)}, f32[4,512]{1,0:T(4,128)S(1)}, f32[4,512]{1,0:T(4,128)S(1)}, f32[4,512]{1,0:T(4,128)S(1)}, f32[4,512]{1,0:T(4,128)S(1)}, /*index=5*/f32[4,512,512]{1,2,0:T(8,128)S(1)}) fusion(f32[4,512,512]{1,2,0:T(8,128)} %get-tuple-element.51, f32[4,512]{1,0:T(4,128)S(1)} %broadcast_maximum_fusion, f32[512,512]{0,1:T(8,128)} %copy-done.13, ...), kind=kOutput, calls=%fused_computation.14 | convolution fusion | flops 296736768 | bytes 28622864 | tf_op jit(solution)/shard_map/hqe,hke->hqk/dot_general | solution.py:34
  178.7 5.7 %fusion.19 = f32[4,512,128]{2,1,0:T(8,128)} fusion(bf16[4,512,128]{2,1,0:T(8,128)(2,1)} %bitcast.136, f32[4,512,512]{1,2,0:T(8,128)S(1)} %fusion.66, f32[4,512]{1,0:T(4,128)S(1)} %get-tuple-element.24, f32[512,512]{0,1:T(8,128)} %get-tuple-element.47, f32[4]{0:T(128)S(1)} %copy-done.20, pred[512,512]{0,1:T(8,128)(4,1)S(1)} %copy-done.11), kind=kOutput, calls=%fused_computation.35 | convolution fusion | flops 275775488 | bytes 7086096 | tf_op jit(solution)/shard_map/hqk,hke->hqe/dot_general | solution.py:49
  184.4 0.0 copy-start.16
  184.4 2.9 %fusion.17 = f32[4,512,128]{2,1,0:T(8,128)} fusion(bf16[4,512,128]{2,1,0:T(8,128)(2,1)S(1)} %bitcast.135, f32[4,512,512]{1,2,0:T(8,128)S(1)} %fusion.65, f32[4,512]{1,0:T(4,128)S(1)} %get-tuple-element.23, f32[512,512]{0,1:T(8,128)S(1)} %copy-done.6, f32[4]{0:T(128)S(1)} %copy-done.20, pred[512,512]{0,1:T(8,128)(4,1)S(1)} %copy-done.12), kind=kOutput, calls=%fused_computation.34 | convolution fusion | flops 275775488 | bytes 7086096 | tf_op jit(solution)/shard_map/hqk,hke->hqe/dot_general | solution.py:49
  187.4 3.0 %fusion.15 = f32[4,512,128]{2,1,0:T(8,128)} fusion(bf16[4,512,128]{2,1,0:T(8,128)(2,1)S(1)} %bitcast.137, f32[4,512,512]{1,2,0:T(8,128)S(1)} %fusion.64, f32[4,512]{1,0:T(4,128)S(1)} %get-tuple-element.22, f32[512,512]{0,1:T(8,128)S(1)} %get-tuple-element.45, f32[4]{0:T(128)S(1)} %copy-done.20, pred[512,512]{0,1:T(8,128)(4,1)S(1)} %copy-done.10), kind=kOutput, calls=%fused_computation.33 | convolution fusion | flops 275775488 | bytes 7086096 | tf_op jit(solution)/shard_map/hqk,hke->hqe/dot_general | solution.py:49
  190.4 5.7 %fusion.2 = (f32[4,512]{1,0:T(4,128)S(1)}, f32[4,512]{1,0:T(4,128)S(1)}, f32[4,512]{1,0:T(4,128)S(1)}, f32[4,512]{1,0:T(4,128)S(1)}) fusion(f32[4,512,512]{1,2,0:T(8,128)S(1)} %get-tuple-element.52, f32[4,512]{1,0:T(4,128)S(1)} %get-tuple-element.25, f32[512,512]{0,1:T(8,128)S(1)} %get-tuple-element.46, f32[4]{0:T(128)S(1)} %copy-done.20, ...), kind=kLoop, calls=%fused_computation.16 | loop fusion | flops 29351936 | bytes 22085648 | tf_op jit(solution)/shard_map/reduce_sum | solution.py:48
  196.2 5.4 %fusion.28 = f32[4,512,128]{2,1,0:T(8,128)} fusion(f32[4,512,512]{1,2,0:T(8,128)} %get-tuple-element.51, f32[4,512]{1,0:T(4,128)S(1)} %broadcast_maximum_fusion, f32[512,512]{0,1:T(8,128)S(1)} %copy-done.14, f32[4]{0:T(128)S(1)} %copy-done.20, pred[512,512]{0,1:T(8,128)(4,1)S(1)} %copy-done.18, f32[4,512]{1,0:T(4,128)S(1)} %get-tuple-element.21, ...), kind=kOutput, calls=%fused_computation.42 | convolution fusion | flops 276299776 | bytes 7102480 | tf_op jit(solution)/shard_map/hqk,hke->hqe/dot_general | solution.py:49
  201.6 7.2 %bitcast_convert_fusion = bf16[512,2048]{1,0:T(8,128)(2,1)} fusion(bf16[4,128,2048]{2,1,0:T(8,128)(2,1)S(1)} %bitcast.122, f32[4,512,128]{2,1,0:T(8,128)} %fusion.15, f32[4,512,128]{2,1,0:T(8,128)} %fusion.17, f32[4,512,128]{2,1,0:T(8,128)} %fusion.19, f32[4,512,128]{2,1,0:T(8,128)} %fusion.28, bf16[4,512,128]{2,1,0:T(8,128)(2,1)} %bitcast.134, ...), kind=kOutput, calls=%fused_computation.3 | convolution fusion | flops 1352925184 | bytes 14458896 | tf_op jit(solution)/shard_map/hqe,hed->qd/dot_general | solution.py:114
  208.9 2.2 gather_fusion.2
  211.1 1.1 broadcast_select_fusion.1
  212.2 0.0 collective-permute-start.6
  212.2 0.1 compare_and_fusion.1
  212.3 3.2 %gather_fusion.1 = bf16[2,128,2048]{2,1,0:T(8,128)(2,1)} fusion(bf16[4,128,2048]{2,1,0:T(8,128)(2,1)} %bitcast.125, s32[1024]{0:T(1024)S(1)} %pad_clamp_fusion.1), kind=kCustom, calls=%fused_computation.clone | custom fusion | bytes 2097160 | tf_op jit(solution)/shard_map/jit(_take)/gather | solution.py:123
  215.5 0.0 collective-permute-done.6
  215.5 2.0 convert_add_fusion
  217.6 0.1 fusion.63
  217.6 1.2 collective-permute-start.7
  218.8 14.7 %collective-permute-done.7 = bf16[128,2048]{1,0:T(8,128)(2,1)S(1)} collective-permute-done((bf16[128,2048]{1,0:T(8,128)(2,1)S(1)}, bf16[128,2048]{1,0:T(8,128)(2,1)S(1)}, u32[]{:S(2)}, u32[]{:S(2)}) %collective-permute-start.7) | collective-permute-done | bytes 524320 | tf_op jit(solution)/shard_map/ppermute | solution.py:22
  233.5 1.0 fusion.58
  (56 shorter events, 0.2 us)
Async XLA Ops:
  0.6 201.0 %copy-start = (bf16[512,2048]{1,0:T(8,128)(2,1)S(1)}, bf16[512,2048]{1,0:T(8,128)(2,1)}, u32[]{:S(2)}) copy-start(bf16[512,2048]{1,0:T(8,128)(2,1)} %param.12) | copy-start | bytes 6291460
  4.8 15.3 %collective-permute-start = (bf16[128,2048]{1,0:T(8,128)(2,1)S(1)}, bf16[128,2048]{1,0:T(8,128)(2,1)S(1)}, u32[]{:S(2)}, u32[]{:S(2)}) collective-permute-start(bf16[128,2048]{1,0:T(8,128)(2,1)S(1)} %fusion.56), channel_id=1, source_target_pairs={{0,2},{1,3},{2,0},{3,1},{4,6},{5,7},{6,4},{7,5},{8,10},{9,11},{10,... | collective-permute-start | bytes 1572872 | tf_op jit(solution)/shard_map/ppermute | solution.py:22
  21.1 8.9 %collective-permute-start.1 = (bf16[2,128,2048]{2,1,0:T(8,128)(2,1)}, bf16[2,128,2048]{2,1,0:T(8,128)(2,1)}, u32[]{:S(2)}, u32[]{:S(2)}) collective-permute-start(bf16[2,128,2048]{2,1,0:T(8,128)(2,1)} %pad_maximum_fusion.1), channel_id=1, source_target_pairs={{0,1},{1,0},{2,3},{3,2},{4,5},{5,4},{6,7},{7,6},{8,9},{9,8},{10,11... | collective-permute-start | bytes 3145736 | tf_op jit(solution)/shard_map/ppermute | solution.py:22
  21.1 8.9 %copy-start.19 = (s32[512]{0:T(512)S(1)}, s32[512]{0:T(512)}, u32[]{:S(2)}) copy-start(s32[512]{0:T(512)} %param.13) | copy-start | bytes 6148
  44.9 1.1 copy-start.7
  44.9 113.8 %copy-start.9 = (bf16[512,512]{1,0:T(8,128)(2,1)}, bf16[512,512]{1,0:T(8,128)(2,1)S(1)}, u32[]{:S(2)}) copy-start(bf16[512,512]{1,0:T(8,128)(2,1)S(1)} %get-tuple-element.28) | copy-start | bytes 1572868
  46.9 111.8 %copy-start.20 = (f32[4]{0:T(128)S(1)}, f32[4]{0:T(128)}, u32[]{:S(2)}) copy-start(f32[4]{0:T(128)} %param.11) | copy-start | bytes 52
  53.8 32.2 %collective-permute-start.5 = (bf16[4104,128]{1,0:T(8,128)(2,1)}, bf16[4104,128]{1,0:T(8,128)(2,1)}, u32[]{:S(2)}, u32[]{:S(2)}) collective-permute-start(bf16[4104,128]{1,0:T(8,128)(2,1)} %concatenate.3), channel_id=1, source_target_pairs={{0,16},{4,20},{8,24},{12,28},{16,32},{20,36},{24,40},{28,44},{32,4... | collective-permute-start | bytes 3151880 | tf_op jit(solution)/shard_map/ppermute | solution.py:17
  57.7 52.0 %collective-permute-start.4 = (bf16[4104,128]{1,0:T(8,128)(2,1)}, bf16[4104,128]{1,0:T(8,128)(2,1)}, u32[]{:S(2)}, u32[]{:S(2)}) collective-permute-start(bf16[4104,128]{1,0:T(8,128)(2,1)} %concatenate.3), channel_id=1, source_target_pairs={{0,12},{4,16},{8,20},{12,24},{16,28},{20,32},{24,36},{28,40},{32,4... | collective-permute-start | bytes 3151880 | tf_op jit(solution)/shard_map/ppermute | solution.py:17
  62.6 71.1 %collective-permute-start.3 = (bf16[4104,128]{1,0:T(8,128)(2,1)}, bf16[4104,128]{1,0:T(8,128)(2,1)S(1)}, u32[]{:S(2)}, u32[]{:S(2)}) collective-permute-start(bf16[4104,128]{1,0:T(8,128)(2,1)} %concatenate.3), channel_id=1, source_target_pairs={{0,8},{4,12},{8,16},{12,20},{16,24},{20,28},{24,32},{28,36},{32,40... | collective-permute-start | bytes 3151880 | tf_op jit(solution)/shard_map/ppermute | solution.py:17
  66.6 89.5 %collective-permute-start.2 = (bf16[4104,128]{1,0:T(8,128)(2,1)}, bf16[4104,128]{1,0:T(8,128)(2,1)S(1)}, u32[]{:S(2)}, u32[]{:S(2)}) collective-permute-start(bf16[4104,128]{1,0:T(8,128)(2,1)} %concatenate.3), channel_id=1, source_target_pairs={{0,4},{4,8},{8,12},{12,16},{16,20},{20,24},{24,28},{28,32},{32,36}... | collective-permute-start | bytes 3151880 | tf_op jit(solution)/shard_map/ppermute | solution.py:17
  71.3 90.5 %copy-start.13 = (f32[512,512]{0,1:T(8,128)}, f32[512,512]{0,1:T(8,128)S(1)}, u32[]{:S(2)}) copy-start(f32[512,512]{0,1:T(8,128)S(1)} %get-tuple-element.49) | copy-start | bytes 3145732
  71.3 119.1 %copy-start.3 = (f32[512,512]{0,1:T(8,128)}, f32[512,512]{0,1:T(8,128)S(1)}, u32[]{:S(2)}) copy-start(f32[512,512]{0,1:T(8,128)S(1)} %get-tuple-element.46) | copy-start | bytes 3145732
  158.7 5.2 %copy-start.17 = (pred[512,512]{0,1:T(8,128)(4,1)}, pred[512,512]{0,1:T(8,128)(4,1)S(1)}, u32[]{:S(2)}) copy-start(pred[512,512]{0,1:T(8,128)(4,1)S(1)} %get-tuple-element.44) | copy-start | bytes 786436
  168.2 1.8 copy-start.10
  168.2 1.8 copy-start.11
  178.6 11.7 %copy-start.2 = (f32[4,512,512]{1,2,0:T(8,128)}, f32[4,512,512]{1,2,0:T(8,128)S(1)}, u32[]{:S(2)}) copy-start(f32[4,512,512]{1,2,0:T(8,128)S(1)} %get-tuple-element.52) | copy-start | bytes 12582916
  178.7 5.8 %copy-start.6 = (f32[512,512]{0,1:T(8,128)S(1)}, f32[512,512]{0,1:T(8,128)}, u32[]{:S(2)}) copy-start(f32[512,512]{0,1:T(8,128)} %get-tuple-element.48) | copy-start | bytes 3145732
  178.7 5.7 %copy-start.12 = (pred[512,512]{0,1:T(8,128)(4,1)S(1)}, pred[512,512]{0,1:T(8,128)(4,1)}, u32[]{:S(2)}) copy-start(pred[512,512]{0,1:T(8,128)(4,1)} %get-tuple-element.42) | copy-start | bytes 786436
  178.7 5.7 %copy-start.15 = (bf16[2048,128]{1,0:T(8,128)(2,1)S(1)}, bf16[2048,128]{1,0:T(8,128)(2,1)}, u32[]{:S(2)}) copy-start(bf16[2048,128]{1,0:T(8,128)(2,1)} %get-tuple-element.33) | copy-start | bytes 1572868
  184.4 3.0 %copy-start.16 = (bf16[2048,128]{1,0:T(8,128)(2,1)S(1)}, bf16[2048,128]{1,0:T(8,128)(2,1)}, u32[]{:S(2)}) copy-start(bf16[2048,128]{1,0:T(8,128)(2,1)} %get-tuple-element.36) | copy-start | bytes 1572868
  187.4 3.0 %copy-start.5 = (f32[512,512]{0,1:T(8,128)S(1)}, f32[512,512]{0,1:T(8,128)}, u32[]{:S(2)}) copy-start(f32[512,512]{0,1:T(8,128)} %get-tuple-element.47) | copy-start | bytes 3145732
  190.4 5.8 %copy-start.8 = (bf16[512,512]{1,0:T(8,128)(2,1)S(1)}, bf16[512,512]{1,0:T(8,128)(2,1)}, u32[]{:S(2)}) copy-start(bf16[512,512]{1,0:T(8,128)(2,1)} %copy-done.7) | copy-start | bytes 1572868
  190.4 5.8 %copy-start.14 = (f32[512,512]{0,1:T(8,128)S(1)}, f32[512,512]{0,1:T(8,128)}, u32[]{:S(2)}) copy-start(f32[512,512]{0,1:T(8,128)} %copy-done.13) | copy-start | bytes 3145732
  190.4 5.8 %copy-start.18 = (pred[512,512]{0,1:T(8,128)(4,1)S(1)}, pred[512,512]{0,1:T(8,128)(4,1)}, u32[]{:S(2)}) copy-start(pred[512,512]{0,1:T(8,128)(4,1)} %copy-done.17) | copy-start | bytes 786436
  196.2 5.4 %copy-start.4 = (f32[512,512]{0,1:T(8,128)S(1)}, f32[512,512]{0,1:T(8,128)}, u32[]{:S(2)}) copy-start(f32[512,512]{0,1:T(8,128)} %copy-done.3) | copy-start | bytes 3145732
  212.2 21.3 %copy-start.1 = (bf16[128,2048]{1,0:T(8,128)(2,1)S(1)}, bf16[128,2048]{1,0:T(8,128)(2,1)}, u32[]{:S(2)}) copy-start(bf16[128,2048]{1,0:T(8,128)(2,1)} %param.8) | copy-start | bytes 1572868
  212.2 3.3 %collective-permute-start.6 = (bf16[2,128,2048]{2,1,0:T(8,128)(2,1)}, bf16[2,128,2048]{2,1,0:T(8,128)(2,1)}, u32[]{:S(2)}, u32[]{:S(2)}) collective-permute-start(bf16[2,128,2048]{2,1,0:T(8,128)(2,1)} %broadcast_select_fusion.1), channel_id=1, source_target_pairs={{0,1},{1,0},{2,3},{3,2},{4,5},{5,4},{6,7},{7,6},{8,9},{9,8},{10,11... | collective-permute-start | bytes 3145736 | tf_op jit(solution)/shard_map/ppermute | solution.py:22
  217.6 15.9 %collective-permute-start.7 = (bf16[128,2048]{1,0:T(8,128)(2,1)S(1)}, bf16[128,2048]{1,0:T(8,128)(2,1)S(1)}, u32[]{:S(2)}, u32[]{:S(2)}) collective-permute-start(bf16[128,2048]{1,0:T(8,128)(2,1)S(1)} %fusion.63), channel_id=1, source_target_pairs={{0,2},{1,3},{2,0},{3,1},{4,6},{5,7},{6,4},{7,5},{8,10},{9,11},{10,... | collective-permute-start | bytes 1572872 | tf_op jit(solution)/shard_map/ppermute | solution.py:22

commit v2 on v1

v2 whole, which is shorter than its diff:
```python
import jax
import jax.numpy as jnp
from jax import lax
from jax.sharding import PartitionSpec as P
from jax.experimental import pallas as pl
from jax.experimental.pallas import tpu as pltpu

HD = 128
SPAN = 4


EPSILON = 1e-05
NEG_FILL = -1e30


def shifted(value, axis, steps):
    count = lax.axis_size(axis)
    leading, last = (max(0, -steps), min(count, count - steps))
    return lax.ppermute(value, axis, [(source, source + steps) for source in range(leading, last)])


def swapped(value, axis, mask):
    count = lax.axis_size(axis)
    return lax.ppermute(value, axis, [(source, source ^ mask) for source in range(count)])


def layer_norm(inputs, ln_gain):
    row_mean = jnp.mean(inputs, axis=-1, keepdims=True)
    centred = inputs - row_mean
    variance = jnp.mean(centred * centred, axis=-1, keepdims=True)
    return (centred * lax.rsqrt(variance + EPSILON) * ln_gain).astype(jnp.bfloat16)


TQ = 256
TK = 256


def attention_kernel(flags_ref, q_ref, *refs):
    span = len(refs) - 8
    kvs = refs[: span + 1]
    segq_ref, segk_ref, bias_ref, o_ref, m_sc, l_sc, acc_sc = refs[span + 1 :]
    heads = m_sc.shape[0]
    block_len = q_ref.shape[0]
    n_q = block_len // TQ
    n_t = block_len // TK
    width = heads * HD
    scale = HD ** (-0.5)
    for qt in range(n_q):
        m_sc[...] = jnp.full(m_sc.shape, NEG_FILL, jnp.float32)
        l_sc[...] = jnp.zeros(l_sc.shape, jnp.float32)
        acc_sc[...] = jnp.zeros(acc_sc.shape, jnp.float32)
        segq = segq_ref[pl.ds(qt * TQ, TQ), :]
        steps = [(0, qt)] + [(0, t) for t in range(n_t) if t * TK < qt * TQ]
        steps += [(blk, t) for blk in range(1, span + 1) for t in range(n_t)]
        for blk, t in steps:
            diag = blk == 0 and t == qt

            def body(blk=blk, t=t, diag=diag):
                segk = segk_ref[pl.ds(blk, 1), pl.ds(t * TK, TK)]
                valid = segq == segk
                if diag:
                    rows = lax.broadcasted_iota(jnp.int32, (TQ, TK), 0)
                    cols = lax.broadcasted_iota(jnp.int32, (TQ, TK), 1)
                    valid = valid & (cols <= rows)
                def one_head(h, carry):
                    lanes = pl.multiple_of(h * HD, HD)
                    q = q_ref[pl.ds(qt * TQ, TQ), pl.ds(lanes, HD)]
                    k = kvs[blk][pl.ds(t * TK, TK), pl.ds(lanes, HD)]
                    v = kvs[blk][pl.ds(t * TK, TK), pl.ds(width + lanes, HD)]
                    s = lax.dot_general(
                        q, k, (((1,), (1,)), ((), ())), preferred_element_type=jnp.float32
                    )
                    s = s * scale + bias_ref[pl.ds(h, 1), pl.ds(blk * block_len + t * TK, TK)]
                    s = jnp.where(valid, s, NEG_FILL)
                    m_prev = m_sc[h]
                    m_new = jnp.maximum(m_prev, jnp.max(s, axis=1, keepdims=True))
                    p = jnp.exp(s - m_new)
                    rescale = jnp.exp(m_prev - m_new)
                    l_sc[h] = l_sc[h] * rescale + jnp.sum(p, axis=1, keepdims=True)
                    acc_sc[h] = acc_sc[h] * rescale + jnp.dot(
                        p.astype(jnp.bfloat16), v, preferred_element_type=jnp.float32
                    )
                    m_sc[h] = m_new
                    return carry

                lax.fori_loop(0, heads, one_head, 0)

            if diag:
                body()
            else:
                pl.when(flags_ref[qt * (span + 1) * n_t + blk * n_t + t] != 0)(body)
        for h in range(heads):
            o_ref[pl.ds(qt * TQ, TQ), pl.ds(h * HD, HD)] = (acc_sc[h] / l_sc[h]).astype(o_ref.dtype)


def attention(queries, kv_blocks, seg_q, seg_k, slopes):
    block_len, width = queries.shape
    heads = width // HD
    span = len(kv_blocks) - 1
    n_q, n_t = block_len // TQ, block_len // TK
    offsets = jnp.arange(block_len, dtype=jnp.int32)
    rel = (jnp.arange(span + 1, dtype=jnp.int32)[:, None] * -block_len + offsets[None, :]).reshape(-1)
    bias = slopes[:, None] * rel.astype(jnp.float32)[None, :]
    seg_first = seg_q.reshape(n_q, TQ)[:, 0]
    seg_last = seg_k.reshape(span + 1, n_t, TK)[:, :, -1]
    flags = (seg_last[None, :, :] >= seg_first[:, None, None]).astype(jnp.int32).reshape(-1)
    seg_rows = jnp.concatenate(
        [seg_k, jnp.full(((-seg_k.shape[0]) % 8, block_len), -1, jnp.int32)], axis=0
    )
    vmem = pl.BlockSpec(memory_space=pltpu.VMEM)
    work = heads * block_len * (span + 1) * block_len
    return pl.pallas_call(
        attention_kernel,
        out_shape=jax.ShapeDtypeStruct((block_len, width), jnp.bfloat16),
        in_specs=[pl.BlockSpec(memory_space=pltpu.SMEM)] + [vmem] * (span + 5),
        out_specs=vmem,
        scratch_shapes=[
            pltpu.VMEM((heads, TQ, 1), jnp.float32),
            pltpu.VMEM((heads, TQ, 1), jnp.float32),
            pltpu.VMEM((heads, TQ, HD), jnp.float32),
        ],
        cost_estimate=pl.CostEstimate(
            flops=4 * work * HD, transcendentals=work, bytes_accessed=(span + 2) * block_len * width * 4
        ),
    )(flags, queries, *kv_blocks, seg_q.reshape(block_len, 1), seg_rows, bias)


def on_device(tokens, ln_gain, w_qkv, slopes, w_out, seg_ids):
    seg_all = lax.all_gather(seg_ids, "seq", axis=0, tiled=True)
    inputs = tokens.astype(jnp.float32)
    normed = layer_norm(inputs, ln_gain)
    rows_dev = normed.shape[0]
    head = lax.axis_index("head")
    n_head = lax.axis_size("head")

    cross = swapped(normed, "head", 2)
    partner = swapped(jnp.stack([normed, cross]), "head", 1)
    pieces = jnp.stack([normed, partner[0], cross, partner[1]])
    order = jnp.arange(n_head, dtype=jnp.int32) ^ head
    block_rows = jnp.take(pieces, order, axis=0).reshape(n_head * rows_dev, normed.shape[1])

    width_local = w_qkv.shape[2]
    heads_dev = slopes.shape[0]
    joined = w_qkv.reshape(w_qkv.shape[0], 3 * width_local)
    qkv_rows = jnp.dot(block_rows, joined, preferred_element_type=jnp.float32).astype(jnp.bfloat16)
    block_len = qkv_rows.shape[0]
    key_cache = qkv_rows[:, width_local : 2 * width_local]
    value_cache = qkv_rows[:, 2 * width_local :]

    kv_own = qkv_rows[:, width_local:]
    arrived = [shifted(kv_own, "seq", steps) for steps in range(1, SPAN + 1)]

    seq_index = lax.axis_index("seq")
    reach = SPAN * block_len
    seg_padded = jnp.concatenate([jnp.full((reach,), -1, jnp.int32), seg_all])
    window = lax.dynamic_slice_in_dim(seg_padded, seq_index * block_len, reach + block_len)
    seg_k = window.reshape(SPAN + 1, block_len)[::-1]
    context = attention(qkv_rows[:, :width_local], [kv_own] + arrived, seg_ids, seg_k, slopes)
    partial = jnp.dot(context, w_out, preferred_element_type=jnp.float32).astype(jnp.bfloat16)

    partial4 = partial.reshape(n_head, rows_dev, partial.shape[1])
    sent = jnp.take(partial4, jnp.stack([head ^ 1, head ^ 3]), axis=0)
    kept = jnp.take(partial4, jnp.stack([head, head ^ 2]), axis=0)
    chip_sum = kept.astype(jnp.float32) + swapped(sent, "head", 1).astype(jnp.float32)
    other_chip = swapped(chip_sum[1].astype(jnp.bfloat16), "head", 2).astype(jnp.float32)
    hidden = (inputs + chip_sum[0] + other_chip).astype(jnp.bfloat16)
    return (hidden, key_cache, value_cache)


def solution(mesh):
    in_specs = (
        P(("seq", "head"), None),
        P(),
        P(None, None, "head"),
        P("head"),
        P("head", None),
        P("seq"),
    )
    out_specs = (P(("seq", "head"), None), P("seq", "head"), P("seq", "head"))
    return jax.shard_map(
        on_device, mesh=mesh, in_specs=in_specs, out_specs=out_specs, check_vma=False
    )
```

time: 235 us -> 401 us (1.71)
  the two profiles are of different devices: /device:TPU:6 before, /device:TPU:26 now
where the time goes in v2:
time: 401 us; the launch traced here: 400 us
  blocking collectives  150 us (37%)
  waiting for transfers between devices  149 us (37%)
  Pallas kernels  33.7 us (8%)
  local copies, waits for them, and re-layouts  25.1 us (6%)
  other arithmetic  18.3 us (5%)
  starting transfers between devices  13.2 us (3%)
  matrix products  9.96 us (2%)
    all_gather x1, blocking collectives, on_device(): seg_all = lax.all_gather(seg_ids, 'seq', axis=0, tiled=True)  150 us
    ppermute x4, waiting for transfers between devices, shifted(): lax.ppermute(value, axis, [(source, source + steps) for source in range(l...  133 us
    pallas_call x1, Pallas kernels, attention(): pl.pallas_call(attention_kernel, out_shape=jax.ShapeDtypeStruct((block_le...  33.7 us
    ppermute x4, waiting for transfers between devices, swapped(): lax.ppermute(value, axis, [(source, source ^ mask) for source in range(co...  15.8 us
    ppermute x4, starting transfers between devices, shifted(): lax.ppermute(value, axis, [(source, source + steps) for source in range(l...  11 us
    unnamed x22, local copies, waits for them, and re-layouts  9.91 us
  transfers between devices with their start and end apart: 8, of which 5 were waited for; matrix products, arithmetic and copies ran while one was open for 4% of the time, Pallas kernels for 0%

profile of v2, /device:TPU:26, one launch (start us, length us, event | category | flops | bytes accessed | tf_op | source)
XLA Modules:
  0.0 399.9 jit_solution(1635610446882476160)
XLA Ops:
  0.6 0.0 copy-start
  0.6 0.0 copy-start.1
  0.7 0.0 copy-start.3
  0.7 0.0 copy-start.4
  0.7 1.3 convert_reduce_fusion
  2.0 1.3 fusion.2
  3.4 2.2 fusion.4
  5.6 2.1 collective-permute-start
  7.7 0.0 copy-done.4
  7.7 149.7 %all-gather = s32[64,1,512]{2,1,0:T(1,128)S(1)} all-gather(s32[1,1,512]{2,1,0:T(1,128)S(1)} %bitcast.31), channel_id=1, replica_groups=mesh['seq'=64,'head'=4] {'seq'}, dimensions={0}, use_global_device_ids=true | all-gather | bytes 133120 | tf_op jit(solution)/shard_map/all_gather | solution.py:129
  157.5 0.1 pad_dynamic-slice_fusion
  157.5 0.0 copy-done.1
  157.5 0.0 copy-done.3
  157.6 0.4 fusion.15
  157.9 0.0 collective-permute-done
  157.9 2.1 pad_maximum_fusion.1
  160.1 0.0 collective-permute-start.1
  160.1 0.1 slice_reduce_fusion
  160.2 8.8 %copy.21 = bf16[2048,3,512]{0,2,1:T(8,128)(2,1)} copy(bf16[2048,3,512]{2,0,1:T(8,128)(2,1)} %param.10) | data formatting | bytes 12582912 | tf_op args[2]
  169.0 0.1 rev.3
  169.1 0.1 slice.47
  169.2 0.1 copy.23
  169.3 0.1 copy.20
  169.4 0.1 compare_convert_fusion
  169.5 0.6 reshape.132.flags_ref
  170.0 0.6 concatenate.7.refs_6_
  170.6 0.9 copy.22.refs_5_
  171.5 0.1 add_convert_fusion
  171.6 0.1 compare_and_fusion
  171.7 0.0 collective-permute-done.1
  171.7 1.3 fusion.10
  173.0 2.6 pad_maximum_fusion
  175.6 3.6 gather_fusion
  179.3 1.9 broadcast_select_fusion
  181.1 6.3 %convolution_convert_fusion.1 = bf16[512,1536]{1,0:T(8,128)(2,1)S(1)} fusion(bf16[512,2048]{1,0:T(8,128)(2,1)S(1)} %bitcast.29, bf16[2048,1536]{0,1:T(8,128)(2,1)} %bitcast.26), kind=kOutput, calls=%fused_computation.4 | convolution fusion | flops 3222011904 | bytes 9961472 | tf_op jit(solution)/shard_map/dot_general | solution.py:145
  187.5 0.0 copy-start.5
  187.5 0.1 slice.52.refs_0_
  187.6 0.0 copy-start.2
  187.6 5.2 %collective-permute-start.2 = (bf16[512,1024]{1,0:T(8,128)(2,1)S(1)}, bf16[512,1024]{1,0:T(8,128)(2,1)S(1)}, u32[]{:S(2)}, u32[]{:S(2)}) collective-permute-start(bf16[512,1024]{1,0:T(8,128)(2,1)S(1)} %slice.52.refs_0_), channel_id=1, source_target_pairs={{0,4},{4,8},{8,12},{12,16},{16,20},{20,24},{24,28},{28,32},{32,36}... | collective-permute-start | bytes 3145736 | tf_op jit(solution)/shard_map/ppermute | solution.py:19
  192.8 1.9 collective-permute-start.3
  194.8 1.9 collective-permute-start.4
  196.7 1.9 collective-permute-start.5
  198.6 0.0 copy-done.5
  198.6 0.7 broadcast_multiply_fusion.refs_7_
  199.3 1.2 fusion.9
  200.5 37.1 %collective-permute-done.2.refs_1_ = bf16[512,1024]{1,0:T(8,128)(2,1)S(1)} collective-permute-done((bf16[512,1024]{1,0:T(8,128)(2,1)S(1)}, bf16[512,1024]{1,0:T(8,128)(2,1)S(1)}, u32[]{:S(2)}, u32[]{:S(2)}) %collective-permute-start.2) | collective-permute-done | bytes 1048608 | tf_op jit(solution)/shard_map/ppermute | solution.py:19
  237.6 39.3 %collective-permute-done.3.refs_2_ = bf16[512,1024]{1,0:T(8,128)(2,1)S(1)} collective-permute-done((bf16[512,1024]{1,0:T(8,128)(2,1)S(1)}, bf16[512,1024]{1,0:T(8,128)(2,1)S(1)}, u32[]{:S(2)}, u32[]{:S(2)}) %collective-permute-start.3) | collective-permute-done | bytes 1048608 | tf_op jit(solution)/shard_map/ppermute | solution.py:19
  276.9 22.6 %collective-permute-done.4.refs_3_ = bf16[512,1024]{1,0:T(8,128)(2,1)S(1)} collective-permute-done((bf16[512,1024]{1,0:T(8,128)(2,1)S(1)}, bf16[512,1024]{1,0:T(8,128)(2,1)S(1)}, u32[]{:S(2)}, u32[]{:S(2)}) %collective-permute-start.4) | collective-permute-done | bytes 1048608 | tf_op jit(solution)/shard_map/ppermute | solution.py:19
  299.5 34.3 %collective-permute-done.5.refs_4_ = bf16[512,1024]{1,0:T(8,128)(2,1)S(1)} collective-permute-done((bf16[512,1024]{1,0:T(8,128)(2,1)S(1)}, bf16[512,1024]{1,0:T(8,128)(2,1)S(1)}, u32[]{:S(2)}, u32[]{:S(2)}) %collective-permute-start.5) | collective-permute-done | bytes 1048608 | tf_op jit(solution)/shard_map/ppermute | solution.py:19
  333.8 0.0 copy-done.6
  333.8 1.0 copy-done.9
  334.8 33.7 %shard_map.85 = bf16[512,512]{1,0:T(8,128)(2,1)} custom-call(s32[20]{0:T(128)} %reshape.132.flags_ref, bf16[512,512]{1,0:T(8,128)(2,1)} %get-tuple-element.10.q_ref, bf16[512,1024]{1,0:T(8,128)(2,1)} %copy-done.2, bf16[512,1024]{1,0:T(8,128)(2,1)} %copy-done.6, bf16[512,1024]{1,0:T(8,128)(2,1)} %copy-done.7, bf16[512,1024]{1,0:T(8,128)(2,1)} %copy-done.8, ...), custom_call_target="tpu_custom_call" | custom-call | flops 2684354560 | bytes 6291456 | tf_op jit(solution)/shard_map/pallas_call | solution.py:112
  368.5 3.6 convolution_convert_fusion
  372.1 3.2 gather_fusion.2
  375.3 2.3 broadcast_select_fusion.1
  377.6 0.0 collective-permute-start.6
  377.6 0.1 compare_and_fusion.1
  377.7 3.2 gather_fusion.1
  380.9 0.0 collective-permute-done.6
  380.9 2.0 convert_add_fusion
  382.9 0.1 fusion.7
  383.0 0.1 collective-permute-start.7
  383.1 15.8 %collective-permute-done.7 = bf16[128,2048]{1,0:T(8,128)(2,1)S(1)} collective-permute-done((bf16[128,2048]{1,0:T(8,128)(2,1)S(1)}, bf16[128,2048]{1,0:T(8,128)(2,1)S(1)}, u32[]{:S(2)}, u32[]{:S(2)}) %collective-permute-start.7) | collective-permute-done | bytes 524320 | tf_op jit(solution)/shard_map/ppermute | solution.py:24
  398.9 1.0 fusion.6
  (20 shorter events, 0.1 us)
Async XLA Ops:
  0.6 367.8 %copy-start = (bf16[512,2048]{1,0:T(8,128)(2,1)S(1)}, bf16[512,2048]{1,0:T(8,128)(2,1)}, u32[]{:S(2)}) copy-start(bf16[512,2048]{1,0:T(8,128)(2,1)} %param.12) | copy-start | bytes 6291460
  0.6 156.9 %copy-start.1 = (bf16[128,2048]{1,0:T(8,128)(2,1)S(1)}, bf16[128,2048]{1,0:T(8,128)(2,1)}, u32[]{:S(2)}) copy-start(bf16[128,2048]{1,0:T(8,128)(2,1)} %param.8) | copy-start | bytes 1572868
  0.7 156.9 %copy-start.3 = (f32[2048]{0:T(1024)S(1)}, f32[2048]{0:T(1024)}, u32[]{:S(2)}) copy-start(f32[2048]{0:T(1024)} %param.9) | copy-start | bytes 24580
  0.7 7.0 %copy-start.4 = (s32[512]{0:T(512)S(1)}, s32[512]{0:T(512)}, u32[]{:S(2)}) copy-start(s32[512]{0:T(512)} %param.13) | copy-start | bytes 6148
  5.6 152.3 %collective-permute-start = (bf16[128,2048]{1,0:T(8,128)(2,1)}, bf16[128,2048]{1,0:T(8,128)(2,1)}, u32[]{:S(2)}, u32[]{:S(2)}) collective-permute-start(bf16[128,2048]{1,0:T(8,128)(2,1)} %fusion.4), channel_id=1, source_target_pairs={{0,2},{1,3},{2,0},{3,1},{4,6},{5,7},{6,4},{7,5},{8,10},{9,11},{10,... | collective-permute-start | bytes 1572872 | tf_op jit(solution)/shard_map/ppermute | solution.py:24
  160.1 11.6 %collective-permute-start.1 = (bf16[2,128,2048]{2,1,0:T(8,128)(2,1)}, bf16[2,128,2048]{2,1,0:T(8,128)(2,1)}, u32[]{:S(2)}, u32[]{:S(2)}) collective-permute-start(bf16[2,128,2048]{2,1,0:T(8,128)(2,1)} %pad_maximum_fusion.1), channel_id=1, source_target_pairs={{0,1},{1,0},{2,3},{3,2},{4,5},{5,4},{6,7},{7,6},{8,9},{9,8},{10,11... | collective-permute-start | bytes 3145736 | tf_op jit(solution)/shard_map/ppermute | solution.py:24
  187.5 11.2 %copy-start.5 = (f32[4]{0:T(128)S(1)}, f32[4]{0:T(128)}, u32[]{:S(2)}) copy-start(f32[4]{0:T(128)} %param.11) | copy-start | bytes 52
  187.6 12.9 %copy-start.2 = (bf16[512,1024]{1,0:T(8,128)(2,1)}, bf16[512,1024]{1,0:T(8,128)(2,1)S(1)}, u32[]{:S(2)}) copy-start(bf16[512,1024]{1,0:T(8,128)(2,1)S(1)} %slice.52.refs_0_) | copy-start | bytes 3145732
  187.6 49.9 %collective-permute-start.2 = (bf16[512,1024]{1,0:T(8,128)(2,1)S(1)}, bf16[512,1024]{1,0:T(8,128)(2,1)S(1)}, u32[]{:S(2)}, u32[]{:S(2)}) collective-permute-start(bf16[512,1024]{1,0:T(8,128)(2,1)S(1)} %slice.52.refs_0_), channel_id=1, source_target_pairs={{0,4},{4,8},{8,12},{12,16},{16,20},{20,24},{24,28},{28,32},{32,36}... | collective-permute-start | bytes 3145736 | tf_op jit(solution)/shard_map/ppermute | solution.py:19
  192.8 84.1 %collective-permute-start.3 = (bf16[512,1024]{1,0:T(8,128)(2,1)S(1)}, bf16[512,1024]{1,0:T(8,128)(2,1)S(1)}, u32[]{:S(2)}, u32[]{:S(2)}) collective-permute-start(bf16[512,1024]{1,0:T(8,128)(2,1)S(1)} %slice.52.refs_0_), channel_id=1, source_target_pairs={{0,8},{4,12},{8,16},{12,20},{16,24},{20,28},{24,32},{28,36},{32,40... | collective-permute-start | bytes 3145736 | tf_op jit(solution)/shard_map/ppermute | solution.py:19
  194.8 104.8 %collective-permute-start.4 = (bf16[512,1024]{1,0:T(8,128)(2,1)S(1)}, bf16[512,1024]{1,0:T(8,128)(2,1)S(1)}, u32[]{:S(2)}, u32[]{:S(2)}) collective-permute-start(bf16[512,1024]{1,0:T(8,128)(2,1)S(1)} %slice.52.refs_0_), channel_id=1, source_target_pairs={{0,12},{4,16},{8,20},{12,24},{16,28},{20,32},{24,36},{28,40},{32,4... | collective-permute-start | bytes 3145736 | tf_op jit(solution)/shard_map/ppermute | solution.py:19
  196.7 137.1 %collective-permute-start.5 = (bf16[512,1024]{1,0:T(8,128)(2,1)S(1)}, bf16[512,1024]{1,0:T(8,128)(2,1)S(1)}, u32[]{:S(2)}, u32[]{:S(2)}) collective-permute-start(bf16[512,1024]{1,0:T(8,128)(2,1)S(1)} %slice.52.refs_0_), channel_id=1, source_target_pairs={{0,16},{4,20},{8,24},{12,28},{16,32},{20,36},{24,40},{28,44},{32,4... | collective-permute-start | bytes 3145736 | tf_op jit(solution)/shard_map/ppermute | solution.py:19
  237.6 96.3 %copy-start.6 = (bf16[512,1024]{1,0:T(8,128)(2,1)}, bf16[512,1024]{1,0:T(8,128)(2,1)S(1)}, u32[]{:S(2)}) copy-start(bf16[512,1024]{1,0:T(8,128)(2,1)S(1)} %collective-permute-done.2.refs_1_) | copy-start | bytes 3145732
  276.9 56.9 %copy-start.7 = (bf16[512,1024]{1,0:T(8,128)(2,1)}, bf16[512,1024]{1,0:T(8,128)(2,1)S(1)}, u32[]{:S(2)}) copy-start(bf16[512,1024]{1,0:T(8,128)(2,1)S(1)} %collective-permute-done.3.refs_2_) | copy-start | bytes 3145732
  299.5 34.3 %copy-start.8 = (bf16[512,1024]{1,0:T(8,128)(2,1)}, bf16[512,1024]{1,0:T(8,128)(2,1)S(1)}, u32[]{:S(2)}) copy-start(bf16[512,1024]{1,0:T(8,128)(2,1)S(1)} %collective-permute-done.4.refs_3_) | copy-start | bytes 3145732
  333.8 1.0 copy-start.9
  377.6 3.3 collective-permute-start.6
  383.0 15.9 %collective-permute-start.7 = (bf16[128,2048]{1,0:T(8,128)(2,1)S(1)}, bf16[128,2048]{1,0:T(8,128)(2,1)S(1)}, u32[]{:S(2)}, u32[]{:S(2)}) collective-permute-start(bf16[128,2048]{1,0:T(8,128)(2,1)S(1)} %fusion.7), channel_id=1, source_target_pairs={{0,2},{1,3},{2,0},{3,1},{4,6},{5,7},{6,4},{7,5},{8,10},{9,11},{10,... | collective-permute-start | bytes 1572872 | tf_op jit(solution)/shard_map/ppermute | solution.py:24

commit v3 on v2

--- a/solution.py
+++ b/solution.py
@@ -126,7 +126,6 @@
 
 
 def on_device(tokens, ln_gain, w_qkv, slopes, w_out, seg_ids):
-    seg_all = lax.all_gather(seg_ids, "seq", axis=0, tiled=True)
     inputs = tokens.astype(jnp.float32)
     normed = layer_norm(inputs, ln_gain)
     rows_dev = normed.shape[0]
@@ -136,8 +135,9 @@
     cross = swapped(normed, "head", 2)
     partner = swapped(jnp.stack([normed, cross]), "head", 1)
     pieces = jnp.stack([normed, partner[0], cross, partner[1]])
-    order = jnp.arange(n_head, dtype=jnp.int32) ^ head
-    block_rows = jnp.take(pieces, order, axis=0).reshape(n_head * rows_dev, normed.shape[1])
+    block_rows = jnp.concatenate(
+        [lax.dynamic_index_in_dim(pieces, j ^ head, 0, keepdims=False) for j in range(n_head)], axis=0
+    )
 
     width_local = w_qkv.shape[2]
     heads_dev = slopes.shape[0]
@@ -148,19 +148,29 @@
     value_cache = qkv_rows[:, 2 * width_local :]
 
     kv_own = qkv_rows[:, width_local:]
-    arrived = [shifted(kv_own, "seq", steps) for steps in range(1, SPAN + 1)]
+    seg_row = jnp.zeros((8, kv_own.shape[1]), jnp.bfloat16).at[0, :block_len].set(
+        seg_ids.astype(jnp.bfloat16)
+    )
+    payload = jnp.concatenate([kv_own, seg_row], axis=0)
+    arrived = [shifted(payload, "seq", steps) for steps in range(1, SPAN + 1)]
 
     seq_index = lax.axis_index("seq")
-    reach = SPAN * block_len
-    seg_padded = jnp.concatenate([jnp.full((reach,), -1, jnp.int32), seg_all])
-    window = lax.dynamic_slice_in_dim(seg_padded, seq_index * block_len, reach + block_len)
-    seg_k = window.reshape(SPAN + 1, block_len)[::-1]
-    context = attention(qkv_rows[:, :width_local], [kv_own] + arrived, seg_ids, seg_k, slopes)
-    partial = jnp.dot(context, w_out, preferred_element_type=jnp.float32).astype(jnp.bfloat16)
+    present = (seq_index - jnp.arange(1, SPAN + 1, dtype=jnp.int32)) >= 0
+    seg_prev = jnp.stack([got[block_len, :block_len] for got in arrived]).astype(jnp.int32)
+    seg_k = jnp.concatenate([seg_ids[None, :], jnp.where(present[:, None], seg_prev, -1)], axis=0)
+    context = attention(qkv_rows[:, :width_local], [payload] + arrived, seg_ids, seg_k, slopes)
 
-    partial4 = partial.reshape(n_head, rows_dev, partial.shape[1])
-    sent = jnp.take(partial4, jnp.stack([head ^ 1, head ^ 3]), axis=0)
-    kept = jnp.take(partial4, jnp.stack([head, head ^ 2]), axis=0)
+    context4 = context.reshape(n_head, rows_dev, context.shape[1])
+
+    def project(owners):
+        rows = jnp.concatenate(
+            [lax.dynamic_index_in_dim(context4, o, 0, keepdims=False) for o in owners], axis=0
+        )
+        out = jnp.dot(rows, w_out, preferred_element_type=jnp.float32).astype(jnp.bfloat16)
+        return out.reshape(len(owners), rows_dev, w_out.shape[1])
+
+    sent = project([head ^ 1, head ^ 3])
+    kept = project([head, head ^ 2])
     chip_sum = kept.astype(jnp.float32) + swapped(sent, "head", 1).astype(jnp.float32)
     other_chip = swapped(chip_sum[1].astype(jnp.bfloat16), "head", 2).astype(jnp.float32)
     hidden = (inputs + chip_sum[0] + other_chip).astype(jnp.bfloat16)

time: 401 us -> 234 us (0.58)
  the two profiles are of different devices: /device:TPU:26 before, /device:TPU:62 now
where the time goes in v3:
time: 234 us; the launch traced here: 233 us
  waiting for transfers between devices  142 us (61%)
  Pallas kernels  33.7 us (14%)
  local copies, waits for them, and re-layouts  22.3 us (10%)
  starting transfers between devices  19.2 us (8%)
  other arithmetic  10.2 us (4%)
  matrix products  4.93 us (2%)
    ppermute x4, waiting for transfers between devices, shifted(): lax.ppermute(value, axis, [(source, source + steps) for source in range(l...  113 us
    pallas_call x1, Pallas kernels, attention(): pl.pallas_call(attention_kernel, out_shape=jax.ShapeDtypeStruct((block_le...  33.7 us
    ppermute x4, waiting for transfers between devices, swapped(): lax.ppermute(value, axis, [(source, source ^ mask) for source in range(co...  29.4 us
    ppermute x4, starting transfers between devices, shifted(): lax.ppermute(value, axis, [(source, source + steps) for source in range(l...  16.1 us
    unnamed x19, local copies, waits for them, and re-layouts  12.1 us
  transfers between devices with their start and end apart: 8, of which 7 were waited for; matrix products, arithmetic and copies ran while one was open for 7% of the time, Pallas kernels for 0%

profile of v3, /device:TPU:62, one launch (start us, length us, event | category | flops | bytes accessed | tf_op | source)
XLA Modules:
  0.0 233.4 jit_solution(12520217794451104985)
XLA Ops:
  0.6 0.0 copy-start
  0.6 0.0 copy-start.1
  0.7 0.0 copy-start.7
  0.7 1.3 convert_reduce_fusion
  2.0 1.3 fusion.11
  3.4 1.4 fusion.13
  4.8 1.5 collective-permute-start
  6.3 0.0 copy-done.1
  6.3 0.0 copy-done.7
  6.3 0.4 fusion.31
  6.7 13.4 %collective-permute-done = bf16[128,2048]{1,0:T(8,128)(2,1)S(1)} collective-permute-done((bf16[128,2048]{1,0:T(8,128)(2,1)S(1)}, bf16[128,2048]{1,0:T(8,128)(2,1)S(1)}, u32[]{:S(2)}, u32[]{:S(2)}) %collective-permute-start) | collective-permute-done | bytes 524320 | tf_op jit(solution)/shard_map/ppermute | solution.py:24
  20.0 0.8 copy-done.4
  20.8 1.1 pad_maximum_fusion.1
  21.9 0.0 collective-permute-start.1
  21.9 8.9 %copy.30 = bf16[2048,3,512]{0,2,1:T(8,128)(2,1)} copy(bf16[2048,3,512]{2,0,1:T(8,128)(2,1)} %param.10) | data formatting | bytes 12582912 | tf_op args[2]
  30.8 0.0 copy-start.5
  30.8 0.1 add_convert_fusion
  30.9 0.0 collective-permute-done.1
  30.9 1.3 fusion.27
  32.3 0.3 pad_maximum_fusion
  32.5 0.2 dynamic-slice_bitcast_fusion.3
  32.8 2.2 copy-done.2
  35.0 3.4 %convolution_convert_fusion = bf16[512,1536]{1,0:T(8,128)(2,1)S(1)} fusion(bf16[2048,1536]{0,1:T(8,128)(2,1)S(1)} %bitcast.40, bf16[128,2048]{1,0:T(8,128)(2,1)S(1)} %get-tuple-element.16, bf16[128,2048]{1,0:T(8,128)(2,1)S(1)} %get-tuple-element.17, bf16[128,2048]{1,0:T(8,128)(2,1)S(1)} %get-tuple-element.18, bf16[128,2048]{1,0:T(8,128)(2,1)S(1)} %get-tuple-element.15), kind=kOutput, calls=%fused_computation | convolution fusion | flops 3230400512 | bytes 9961472 | tf_op jit(solution)/shard_map/dot_general | solution.py:145
  38.5 0.0 copy-start.8
  38.5 0.1 slice.75
  38.6 1.3 fusion.10.refs_0_
  39.9 0.1 copy-done.3
  40.0 3.5 %collective-permute-start.2 = (bf16[520,1024]{1,0:T(8,128)(2,1)}, bf16[520,1024]{1,0:T(8,128)(2,1)}, u32[]{:S(2)}, u32[]{:S(2)}) collective-permute-start(bf16[520,1024]{1,0:T(8,128)(2,1)} %fusion.10.refs_0_), channel_id=1, source_target_pairs={{0,4},{4,8},{8,12},{12,16},{16,20},{20,24},{24,28},{28,32},{32,36}... | collective-permute-start | bytes 3194888 | tf_op jit(solution)/shard_map/ppermute | solution.py:19
  43.5 4.5 %collective-permute-start.3 = (bf16[520,1024]{1,0:T(8,128)(2,1)}, bf16[520,1024]{1,0:T(8,128)(2,1)}, u32[]{:S(2)}, u32[]{:S(2)}) collective-permute-start(bf16[520,1024]{1,0:T(8,128)(2,1)} %fusion.10.refs_0_), channel_id=1, source_target_pairs={{0,8},{4,12},{8,16},{12,20},{16,24},{20,28},{24,32},{28,36},{32,40... | collective-permute-start | bytes 3194888 | tf_op jit(solution)/shard_map/ppermute | solution.py:19
  48.0 3.1 %collective-permute-start.4 = (bf16[520,1024]{1,0:T(8,128)(2,1)}, bf16[520,1024]{1,0:T(8,128)(2,1)}, u32[]{:S(2)}, u32[]{:S(2)}) collective-permute-start(bf16[520,1024]{1,0:T(8,128)(2,1)} %fusion.10.refs_0_), channel_id=1, source_target_pairs={{0,12},{4,16},{8,20},{12,24},{16,28},{20,32},{24,36},{28,40},{32,4... | collective-permute-start | bytes 3194888 | tf_op jit(solution)/shard_map/ppermute | solution.py:19
  51.1 5.0 %collective-permute-start.5 = (bf16[520,1024]{1,0:T(8,128)(2,1)}, bf16[520,1024]{1,0:T(8,128)(2,1)}, u32[]{:S(2)}, u32[]{:S(2)}) collective-permute-start(bf16[520,1024]{1,0:T(8,128)(2,1)} %fusion.10.refs_0_), channel_id=1, source_target_pairs={{0,16},{4,20},{8,24},{12,28},{16,32},{20,36},{24,40},{28,44},{32,4... | collective-permute-start | bytes 3194888 | tf_op jit(solution)/shard_map/ppermute | solution.py:19
  56.2 0.1 pad.11.clone
  56.3 0.9 copy.38.refs_5_
  57.2 0.1 slice_reduce_fusion
  57.3 0.7 broadcast_multiply_fusion.refs_7_
  58.0 2.5 %fusion.26 = (bf16[512,512]{1,0:T(8,128)(2,1)}, bf16[512,512]{1,0:T(8,128)(2,1)}, bf16[512,512]{1,0:T(8,128)(2,1)}) fusion(bf16[512,1536]{1,0:T(8,128)(2,1)} %copy-done.3), kind=kLoop, calls=%fused_computation.58 | loop fusion | bytes 3145728 | tf_op jit(solution)/shard_map/slice | solution.py:148
  60.5 30.4 %collective-permute-done.2.refs_1_ = bf16[520,1024]{1,0:T(8,128)(2,1)} collective-permute-done((bf16[520,1024]{1,0:T(8,128)(2,1)}, bf16[520,1024]{1,0:T(8,128)(2,1)}, u32[]{:S(2)}, u32[]{:S(2)}) %collective-permute-start.2) | collective-permute-done | bytes 1064992 | tf_op jit(solution)/shard_map/ppermute | solution.py:19
  90.9 0.7 slice.76
  91.6 38.0 %collective-permute-done.3.refs_2_ = bf16[520,1024]{1,0:T(8,128)(2,1)} collective-permute-done((bf16[520,1024]{1,0:T(8,128)(2,1)}, bf16[520,1024]{1,0:T(8,128)(2,1)}, u32[]{:S(2)}, u32[]{:S(2)}) %collective-permute-start.3) | collective-permute-done | bytes 1064992 | tf_op jit(solution)/shard_map/ppermute | solution.py:19
  129.6 0.7 slice.77
  130.3 22.3 %collective-permute-done.4.refs_3_ = bf16[520,1024]{1,0:T(8,128)(2,1)} collective-permute-done((bf16[520,1024]{1,0:T(8,128)(2,1)}, bf16[520,1024]{1,0:T(8,128)(2,1)}, u32[]{:S(2)}, u32[]{:S(2)}) %collective-permute-start.4) | collective-permute-done | bytes 1064992 | tf_op jit(solution)/shard_map/ppermute | solution.py:19
  152.6 0.7 slice.78
  153.3 22.3 %collective-permute-done.5.refs_4_ = bf16[520,1024]{1,0:T(8,128)(2,1)} collective-permute-done((bf16[520,1024]{1,0:T(8,128)(2,1)}, bf16[520,1024]{1,0:T(8,128)(2,1)}, u32[]{:S(2)}, u32[]{:S(2)}) %collective-permute-start.5) | collective-permute-done | bytes 1064992 | tf_op jit(solution)/shard_map/ppermute | solution.py:19
  175.6 0.7 slice.79
  176.3 0.1 convert_select_fusion
  176.4 0.1 convert_select_fusion.1
  176.5 0.1 pad_add_fusion
  176.5 0.1 copy.36
  176.6 0.1 copy.37
  176.7 0.1 compare_convert_fusion
  176.8 0.7 reshape.122.flags_ref
  177.5 0.7 add_add_fusion.refs_6_
  178.1 33.7 %shard_map.85 = bf16[512,512]{1,0:T(8,128)(2,1)} custom-call(s32[20]{0:T(128)} %reshape.122.flags_ref, bf16[512,512]{1,0:T(8,128)(2,1)} %get-tuple-element.21.q_ref, bf16[520,1024]{1,0:T(8,128)(2,1)} %fusion.10.refs_0_, bf16[520,1024]{1,0:T(8,128)(2,1)} %collective-permute-done.2.refs_1_, bf16[520,1024]{1,0:T(8,128)(2,1)} %collective-permute-done.3.refs_2_, ...), custom_call_target="tpu_custom_call" | custom-call | flops 2684354560 | bytes 6291456 | tf_op jit(solution)/shard_map/pallas_call | solution.py:112
  211.8 1.1 dynamic-slice_bitcast_fusion.5
  212.9 0.0 copy-done
  212.9 0.7 convolution_convert_fusion.1
  213.7 0.1 collective-permute-start.6
  213.8 0.7 convolution_convert_fusion.2
  214.5 1.9 collective-permute-done.6
  216.4 0.4 convert_add_fusion
  216.8 0.1 fusion.16
  216.9 1.5 collective-permute-start.7
  218.4 14.1 %collective-permute-done.7 = bf16[128,2048]{1,0:T(8,128)(2,1)S(1)} collective-permute-done((bf16[128,2048]{1,0:T(8,128)(2,1)S(1)}, bf16[128,2048]{1,0:T(8,128)(2,1)S(1)}, u32[]{:S(2)}, u32[]{:S(2)}) %collective-permute-start.7) | collective-permute-done | bytes 524320 | tf_op jit(solution)/shard_map/ppermute | solution.py:24
  232.4 1.0 fusion.15
  (18 shorter events, 0.1 us)
Async XLA Ops:
  0.6 212.3 %copy-start = (bf16[512,2048]{1,0:T(8,128)(2,1)S(1)}, bf16[512,2048]{1,0:T(8,128)(2,1)}, u32[]{:S(2)}) copy-start(bf16[512,2048]{1,0:T(8,128)(2,1)} %param.12) | copy-start | bytes 6291460
  0.6 5.6 %copy-start.1 = (bf16[128,2048]{1,0:T(8,128)(2,1)S(1)}, bf16[128,2048]{1,0:T(8,128)(2,1)}, u32[]{:S(2)}) copy-start(bf16[128,2048]{1,0:T(8,128)(2,1)} %param.8) | copy-start | bytes 1572868
  0.7 5.6 %copy-start.7 = (f32[2048]{0:T(1024)S(1)}, f32[2048]{0:T(1024)}, u32[]{:S(2)}) copy-start(f32[2048]{0:T(1024)} %param.9) | copy-start | bytes 24580
  4.8 15.3 %collective-permute-start = (bf16[128,2048]{1,0:T(8,128)(2,1)S(1)}, bf16[128,2048]{1,0:T(8,128)(2,1)S(1)}, u32[]{:S(2)}, u32[]{:S(2)}) collective-permute-start(bf16[128,2048]{1,0:T(8,128)(2,1)S(1)} %fusion.13), channel_id=1, source_target_pairs={{0,2},{1,3},{2,0},{3,1},{4,6},{5,7},{6,4},{7,5},{8,10},{9,11},{10,... | collective-permute-start | bytes 1572872 | tf_op jit(solution)/shard_map/ppermute | solution.py:24
  20.0 0.8 copy-start.4
  21.9 9.0 %collective-permute-start.1 = (bf16[2,128,2048]{2,1,0:T(8,128)(2,1)}, bf16[2,128,2048]{2,1,0:T(8,128)(2,1)}, u32[]{:S(2)}, u32[]{:S(2)}) collective-permute-start(bf16[2,128,2048]{2,1,0:T(8,128)(2,1)} %pad_maximum_fusion.1), channel_id=1, source_target_pairs={{0,1},{1,0},{2,3},{3,2},{4,5},{5,4},{6,7},{7,6},{8,9},{9,8},{10,11... | collective-permute-start | bytes 3145736 | tf_op jit(solution)/shard_map/ppermute | solution.py:24
  21.9 8.9 %copy-start.6 = (s32[512]{0:T(512)S(1)}, s32[512]{0:T(512)}, u32[]{:S(2)}) copy-start(s32[512]{0:T(512)} %param.13) | copy-start | bytes 6148
  30.8 1.4 copy-start.5
  32.3 2.8 %copy-start.2 = (bf16[2048,3,512]{0,2,1:T(8,128)(2,1)S(1)}, bf16[2048,3,512]{0,2,1:T(8,128)(2,1)}, u32[]{:S(2)}) copy-start(bf16[2048,3,512]{0,2,1:T(8,128)(2,1)} %copy.30) | copy-start | bytes 18874372
  38.5 1.5 copy-start.3
  38.5 18.8 %copy-start.8 = (f32[4]{0:T(128)S(1)}, f32[4]{0:T(128)}, u32[]{:S(2)}) copy-start(f32[4]{0:T(128)} %param.11) | copy-start | bytes 52
  40.0 50.9 %collective-permute-start.2 = (bf16[520,1024]{1,0:T(8,128)(2,1)}, bf16[520,1024]{1,0:T(8,128)(2,1)}, u32[]{:S(2)}, u32[]{:S(2)}) collective-permute-start(bf16[520,1024]{1,0:T(8,128)(2,1)} %fusion.10.refs_0_), channel_id=1, source_target_pairs={{0,4},{4,8},{8,12},{12,16},{16,20},{20,24},{24,28},{28,32},{32,36}... | collective-permute-start | bytes 3194888 | tf_op jit(solution)/shard_map/ppermute | solution.py:19
  43.5 86.1 %collective-permute-start.3 = (bf16[520,1024]{1,0:T(8,128)(2,1)}, bf16[520,1024]{1,0:T(8,128)(2,1)}, u32[]{:S(2)}, u32[]{:S(2)}) collective-permute-start(bf16[520,1024]{1,0:T(8,128)(2,1)} %fusion.10.refs_0_), channel_id=1, source_target_pairs={{0,8},{4,12},{8,16},{12,20},{16,24},{20,28},{24,32},{28,36},{32,40... | collective-permute-start | bytes 3194888 | tf_op jit(solution)/shard_map/ppermute | solution.py:19
  48.0 104.6 %collective-permute-start.4 = (bf16[520,1024]{1,0:T(8,128)(2,1)}, bf16[520,1024]{1,0:T(8,128)(2,1)}, u32[]{:S(2)}, u32[]{:S(2)}) collective-permute-start(bf16[520,1024]{1,0:T(8,128)(2,1)} %fusion.10.refs_0_), channel_id=1, source_target_pairs={{0,12},{4,16},{8,20},{12,24},{16,28},{20,32},{24,36},{28,40},{32,4... | collective-permute-start | bytes 3194888 | tf_op jit(solution)/shard_map/ppermute | solution.py:19
  51.1 124.5 %collective-permute-start.5 = (bf16[520,1024]{1,0:T(8,128)(2,1)}, bf16[520,1024]{1,0:T(8,128)(2,1)}, u32[]{:S(2)}, u32[]{:S(2)}) collective-permute-start(bf16[520,1024]{1,0:T(8,128)(2,1)} %fusion.10.refs_0_), channel_id=1, source_target_pairs={{0,16},{4,20},{8,24},{12,28},{16,32},{20,36},{24,40},{28,44},{32,4... | collective-permute-start | bytes 3194888 | tf_op jit(solution)/shard_map/ppermute | solution.py:19
  213.7 2.7 %collective-permute-start.6 = (bf16[2,128,2048]{2,1,0:T(8,128)(2,1)S(1)}, bf16[2,128,2048]{2,1,0:T(8,128)(2,1)S(1)}, u32[]{:S(2)}, u32[]{:S(2)}) collective-permute-start(bf16[2,128,2048]{2,1,0:T(8,128)(2,1)S(1)} %bitcast.44), channel_id=1, source_target_pairs={{0,1},{1,0},{2,3},{3,2},{4,5},{5,4},{6,7},{7,6},{8,9},{9,8},{10,11... | collective-permute-start | bytes 3145736 | tf_op jit(solution)/shard_map/ppermute | solution.py:24
  216.9 15.6 %collective-permute-start.7 = (bf16[128,2048]{1,0:T(8,128)(2,1)S(1)}, bf16[128,2048]{1,0:T(8,128)(2,1)S(1)}, u32[]{:S(2)}, u32[]{:S(2)}) collective-permute-start(bf16[128,2048]{1,0:T(8,128)(2,1)S(1)} %fusion.16), channel_id=1, source_target_pairs={{0,2},{1,3},{2,0},{3,1},{4,6},{5,7},{6,4},{7,5},{8,10},{9,11},{10,... | collective-permute-start | bytes 1572872 | tf_op jit(solution)/shard_map/ppermute | solution.py:24

commit v4 on v3

--- a/solution.py
+++ b/solution.py
@@ -125,6 +125,30 @@
     )(flags, queries, *kv_blocks, seg_q.reshape(block_len, 1), seg_rows, bias)
 
 
+RING = 4
+
+
+def moved(value, pairs):
+    return lax.ppermute(value, "seq", pairs)
+
+
+def relay_earlier_blocks(payload):
+    count = lax.axis_size("seq")
+    y = lax.axis_index("seq") % RING
+    ids = range(count)
+    from_z = moved(payload, [(s, s + RING) for s in ids if s + RING < count])
+    from_below = moved(payload, [(s, s + 1) for s in ids if s % RING < RING - 1])
+    from_wrap = moved(payload, [(s, s + RING - 1) for s in ids if s % RING == 0])
+    passed_up = moved(from_below, [(s, s + 1) for s in ids if 0 < s % RING < RING - 1])
+    passed_down = moved(from_z, [(s, s - 1) for s in ids if s % RING > 0])
+    passed_wrap = moved(from_z, [(s, s - RING + 1) for s in ids if s % RING == RING - 1])
+    passed_twice = moved(passed_down, [(s, s - 1) for s in ids if 0 < s % RING < RING - 1])
+    back1 = jnp.where(y == 0, passed_wrap, from_below)
+    back2 = jnp.where(y <= 1, passed_twice, passed_up)
+    back3 = jnp.where(y <= 2, passed_down, from_wrap)
+    return [back1, back2, back3, from_z]
+
+
 def on_device(tokens, ln_gain, w_qkv, slopes, w_out, seg_ids):
     inputs = tokens.astype(jnp.float32)
     normed = layer_norm(inputs, ln_gain)
@@ -152,7 +176,7 @@
         seg_ids.astype(jnp.bfloat16)
     )
     payload = jnp.concatenate([kv_own, seg_row], axis=0)
-    arrived = [shifted(payload, "seq", steps) for steps in range(1, SPAN + 1)]
+    arrived = relay_earlier_blocks(payload)
 
     seq_index = lax.axis_index("seq")
     present = (seq_index - jnp.arange(1, SPAN + 1, dtype=jnp.int32)) >= 0

time: 234 us -> 194 us (0.83)
  the two profiles are of different devices: /device:TPU:62 before, /device:TPU:6 now
where the time goes in v4:
time: 194 us
  waiting for transfers between devices  86.8 us (45%)
  Pallas kernels  42.6 us (22%)
  starting transfers between devices  23.9 us (12%)
  local copies, waits for them, and re-layouts  21.1 us (11%)
  other arithmetic  13.3 us (7%)
  matrix products  4.93 us (3%)
    ppermute x7, waiting for transfers between devices, moved(): return lax.ppermute(value, 'seq', pairs)  57.1 us
    pallas_call x1, Pallas kernels, attention(): pl.pallas_call(attention_kernel, out_shape=jax.ShapeDtypeStruct((block_le...  42.6 us
    ppermute x4, waiting for transfers between devices, swapped(): lax.ppermute(value, axis, [(source, source ^ mask) for source in range(co...  29.6 us
    ppermute x7, starting transfers between devices, moved(): return lax.ppermute(value, 'seq', pairs)  21.1 us
    unnamed x25, local copies, waits for them, and re-layouts  12.9 us
  transfers between devices with their start and end apart: 11, of which 7 were waited for; matrix products, arithmetic and copies ran while one was open for 9% of the time, Pallas kernels for 0%

profile of v4, /device:TPU:6, one launch (start us, length us, event | category | flops | bytes accessed | tf_op | source)
XLA Modules:
  0.0 193.7 jit_solution(12114643383856399967)
XLA Ops:
  0.6 0.0 copy-start
  0.6 0.0 copy-start.1
  0.7 0.0 copy-start.10
  0.7 1.3 convert_reduce_fusion
  2.0 1.3 fusion.11
  3.4 1.4 fusion.13
  4.8 1.5 collective-permute-start
  6.3 0.4 fusion.31
  6.7 13.4 %collective-permute-done = bf16[128,2048]{1,0:T(8,128)(2,1)S(1)} collective-permute-done((bf16[128,2048]{1,0:T(8,128)(2,1)S(1)}, bf16[128,2048]{1,0:T(8,128)(2,1)S(1)}, u32[]{:S(2)}, u32[]{:S(2)}) %collective-permute-start) | collective-permute-done | bytes 524320 | tf_op jit(solution)/shard_map/ppermute | solution.py:24
  20.0 0.8 copy-done.4
  20.8 1.1 pad_maximum_fusion.1
  21.9 8.8 %copy.30 = bf16[2048,3,512]{0,2,1:T(8,128)(2,1)} copy(bf16[2048,3,512]{2,0,1:T(8,128)(2,1)} %param.10) | data formatting | bytes 12582912 | tf_op args[2]
  30.8 0.0 copy-start.5
  30.8 1.3 fusion.27
  32.1 0.0 copy-done.5
  32.2 0.3 pad_maximum_fusion
  32.4 0.2 dynamic-slice_bitcast_fusion.3
  32.7 2.2 %copy-done.2 = bf16[2048,3,512]{0,2,1:T(8,128)(2,1)S(1)} copy-done((bf16[2048,3,512]{0,2,1:T(8,128)(2,1)S(1)}, bf16[2048,3,512]{0,2,1:T(8,128)(2,1)}, u32[]{:S(2)}) %copy-start.2) | copy-done | bytes 6291480
  34.9 3.4 %convolution_convert_fusion = bf16[512,1536]{1,0:T(8,128)(2,1)S(1)} fusion(bf16[2048,1536]{0,1:T(8,128)(2,1)S(1)} %bitcast.40, bf16[128,2048]{1,0:T(8,128)(2,1)S(1)} %get-tuple-element.16, bf16[128,2048]{1,0:T(8,128)(2,1)S(1)} %get-tuple-element.17, bf16[128,2048]{1,0:T(8,128)(2,1)S(1)} %get-tuple-element.18, bf16[128,2048]{1,0:T(8,128)(2,1)S(1)} %get-tuple-element.15), kind=kOutput, calls=%fused_computation | convolution fusion | flops 3230400512 | bytes 9961472 | tf_op jit(solution)/shard_map/dot_general | solution.py:169
  38.4 0.0 copy-start.11
  38.4 0.1 slice.75
  38.5 1.3 fusion.10.refs_0_
  39.8 0.1 copy-done.3
  39.9 3.8 %collective-permute-start.2 = (bf16[520,1024]{1,0:T(8,128)(2,1)}, bf16[520,1024]{1,0:T(8,128)(2,1)}, u32[]{:S(2)}, u32[]{:S(2)}) collective-permute-start(bf16[520,1024]{1,0:T(8,128)(2,1)} %fusion.10.refs_0_), channel_id=1, source_target_pairs={{0,16},{4,20},{8,24},{12,28},{16,32},{20,36},{24,40},{28,44},{32,4... | collective-permute-start | bytes 3194888 | tf_op jit(solution)/shard_map/ppermute | solution.py:132
  43.7 4.5 %collective-permute-start.4 = (bf16[520,1024]{1,0:T(8,128)(2,1)}, bf16[520,1024]{1,0:T(8,128)(2,1)}, u32[]{:S(2)}, u32[]{:S(2)}) collective-permute-start(bf16[520,1024]{1,0:T(8,128)(2,1)} %fusion.10.refs_0_), channel_id=1, source_target_pairs={{0,4},{4,8},{8,12},{16,20},{20,24},{24,28},{32,36},{36,40},{40,44}... | collective-permute-start | bytes 3194888 | tf_op jit(solution)/shard_map/ppermute | solution.py:132
  48.2 24.2 %collective-permute-done.2.refs_4_ = bf16[520,1024]{1,0:T(8,128)(2,1)} collective-permute-done((bf16[520,1024]{1,0:T(8,128)(2,1)}, bf16[520,1024]{1,0:T(8,128)(2,1)}, u32[]{:S(2)}, u32[]{:S(2)}) %collective-permute-start.2) | collective-permute-done | bytes 1064992 | tf_op jit(solution)/shard_map/ppermute | solution.py:132
  72.4 1.3 collective-permute-start.5
  73.7 0.1 add_convert_fusion
  73.8 8.3 %collective-permute-start.8 = (bf16[520,1024]{1,0:T(8,128)(2,1)}, bf16[520,1024]{1,0:T(8,128)(2,1)}, u32[]{:S(2)}, u32[]{:S(2)}) collective-permute-start(bf16[520,1024]{1,0:T(8,128)(2,1)} %fusion.10.refs_0_), channel_id=1, source_target_pairs={{0,12},{16,28},{32,44},{48,60},{64,76},{80,92},{96,108},{112,124},... | collective-permute-start | bytes 3194888 | tf_op jit(solution)/shard_map/ppermute | solution.py:132
  82.0 1.3 collective-permute-start.3
  83.3 0.7 broadcast_multiply_fusion.refs_7_
  84.0 0.1 pad.11.clone
  84.1 0.9 copy.38.refs_5_
  85.0 0.7 collective-permute-start.7
  85.8 14.2 %collective-permute-done.5 = bf16[520,1024]{1,0:T(8,128)(2,1)} collective-permute-done((bf16[520,1024]{1,0:T(8,128)(2,1)}, bf16[520,1024]{1,0:T(8,128)(2,1)}, u32[]{:S(2)}, u32[]{:S(2)}) %collective-permute-start.5) | collective-permute-done | bytes 1064992 | tf_op jit(solution)/shard_map/ppermute | solution.py:132
  99.9 1.3 collective-permute-start.6
  101.2 0.1 slice_reduce_fusion
  101.3 2.5 %fusion.26 = (bf16[512,512]{1,0:T(8,128)(2,1)}, bf16[512,512]{1,0:T(8,128)(2,1)}, bf16[512,512]{1,0:T(8,128)(2,1)}) fusion(bf16[512,1536]{1,0:T(8,128)(2,1)} %copy-done.3), kind=kLoop, calls=%fused_computation.61 | loop fusion | bytes 3145728 | tf_op jit(solution)/shard_map/slice | solution.py:172
  103.9 0.7 slice.79
  104.6 5.6 %collective-permute-done.3 = bf16[520,1024]{1,0:T(8,128)(2,1)} collective-permute-done((bf16[520,1024]{1,0:T(8,128)(2,1)}, bf16[520,1024]{1,0:T(8,128)(2,1)}, u32[]{:S(2)}, u32[]{:S(2)}) %collective-permute-start.3) | collective-permute-done | bytes 1064992 | tf_op jit(solution)/shard_map/ppermute | solution.py:132
  110.2 1.3 broadcast_select_fusion.2.refs_1_
  111.6 1.7 broadcast_select_fusion.refs_3_
  113.4 13.1 %collective-permute-done.6 = bf16[520,1024]{1,0:T(8,128)(2,1)S(1)} collective-permute-done((bf16[520,1024]{1,0:T(8,128)(2,1)}, bf16[520,1024]{1,0:T(8,128)(2,1)S(1)}, u32[]{:S(2)}, u32[]{:S(2)}) %collective-permute-start.6) | collective-permute-done | bytes 1064992 | tf_op jit(solution)/shard_map/ppermute | solution.py:132
  126.5 0.1 broadcast_select_fusion.1.refs_2_
  126.7 0.1 convert_select_fusion
  126.7 0.9 copy-done.8
  127.6 0.1 convert_select_fusion.1
  127.7 0.1 pad_add_fusion
  127.8 0.1 copy.36
  127.9 0.1 copy.37
  128.0 0.1 compare_convert_fusion
  128.1 0.7 reshape.122.flags_ref
  128.7 0.7 add_add_fusion.refs_6_
  129.4 42.6 %shard_map.85 = bf16[512,512]{1,0:T(8,128)(2,1)} custom-call(s32[20]{0:T(128)} %reshape.122.flags_ref, bf16[512,512]{1,0:T(8,128)(2,1)} %get-tuple-element.21.q_ref, bf16[520,1024]{1,0:T(8,128)(2,1)} %fusion.10.refs_0_, bf16[520,1024]{1,0:T(8,128)(2,1)} %copy-done.6, bf16[520,1024]{1,0:T(8,128)(2,1)} %copy-done.8, bf16[520,1024]{1,0:T(8,128)(2,1)} %copy-done.7, ...), custom_call_target="tpu_custom_call" | custom-call | flops 2684354560 | bytes 6291456 | tf_op jit(solution)/shard_map/pallas_call | solution.py:112
  172.0 1.1 dynamic-slice_bitcast_fusion.5
  173.2 0.7 convolution_convert_fusion.1
  173.9 0.1 collective-permute-start.9
  174.0 0.7 convolution_convert_fusion.2
  174.8 1.9 collective-permute-done.9
  176.7 0.4 convert_add_fusion
  177.0 0.1 fusion.16
  177.1 1.2 collective-permute-start.10
  178.3 14.3 %collective-permute-done.10 = bf16[128,2048]{1,0:T(8,128)(2,1)S(1)} collective-permute-done((bf16[128,2048]{1,0:T(8,128)(2,1)S(1)}, bf16[128,2048]{1,0:T(8,128)(2,1)S(1)}, u32[]{:S(2)}, u32[]{:S(2)}) %collective-permute-start.10) | collective-permute-done | bytes 524320 | tf_op jit(solution)/shard_map/ppermute | solution.py:24
  192.7 1.0 fusion.15
  (33 shorter events, 0.1 us)
Async XLA Ops:
  0.6 172.5 %copy-start = (bf16[512,2048]{1,0:T(8,128)(2,1)S(1)}, bf16[512,2048]{1,0:T(8,128)(2,1)}, u32[]{:S(2)}) copy-start(bf16[512,2048]{1,0:T(8,128)(2,1)} %param.12) | copy-start | bytes 6291460
  0.6 5.6 %copy-start.1 = (bf16[128,2048]{1,0:T(8,128)(2,1)S(1)}, bf16[128,2048]{1,0:T(8,128)(2,1)}, u32[]{:S(2)}) copy-start(bf16[128,2048]{1,0:T(8,128)(2,1)} %param.8) | copy-start | bytes 1572868
  0.7 5.6 %copy-start.10 = (f32[2048]{0:T(1024)S(1)}, f32[2048]{0:T(1024)}, u32[]{:S(2)}) copy-start(f32[2048]{0:T(1024)} %param.9) | copy-start | bytes 24580
  4.8 15.3 %collective-permute-start = (bf16[128,2048]{1,0:T(8,128)(2,1)S(1)}, bf16[128,2048]{1,0:T(8,128)(2,1)S(1)}, u32[]{:S(2)}, u32[]{:S(2)}) collective-permute-start(bf16[128,2048]{1,0:T(8,128)(2,1)S(1)} %fusion.13), channel_id=1, source_target_pairs={{0,2},{1,3},{2,0},{3,1},{4,6},{5,7},{6,4},{7,5},{8,10},{9,11},{10,... | collective-permute-start | bytes 1572872 | tf_op jit(solution)/shard_map/ppermute | solution.py:24
  20.0 0.8 copy-start.4
  21.9 8.9 %collective-permute-start.1 = (bf16[2,128,2048]{2,1,0:T(8,128)(2,1)}, bf16[2,128,2048]{2,1,0:T(8,128)(2,1)}, u32[]{:S(2)}, u32[]{:S(2)}) collective-permute-start(bf16[2,128,2048]{2,1,0:T(8,128)(2,1)} %pad_maximum_fusion.1), channel_id=1, source_target_pairs={{0,1},{1,0},{2,3},{3,2},{4,5},{5,4},{6,7},{7,6},{8,9},{9,8},{10,11... | collective-permute-start | bytes 3145736 | tf_op jit(solution)/shard_map/ppermute | solution.py:24
  21.9 8.9 %copy-start.9 = (s32[512]{0:T(512)S(1)}, s32[512]{0:T(512)}, u32[]{:S(2)}) copy-start(s32[512]{0:T(512)} %param.13) | copy-start | bytes 6148
  30.8 1.4 copy-start.5
  32.1 2.8 %copy-start.2 = (bf16[2048,3,512]{0,2,1:T(8,128)(2,1)S(1)}, bf16[2048,3,512]{0,2,1:T(8,128)(2,1)}, u32[]{:S(2)}) copy-start(bf16[2048,3,512]{0,2,1:T(8,128)(2,1)} %copy.30) | copy-start | bytes 18874372
  38.4 1.5 copy-start.3
  38.4 44.9 %copy-start.11 = (f32[4]{0:T(128)S(1)}, f32[4]{0:T(128)}, u32[]{:S(2)}) copy-start(f32[4]{0:T(128)} %param.11) | copy-start | bytes 52
  39.9 32.5 %collective-permute-start.2 = (bf16[520,1024]{1,0:T(8,128)(2,1)}, bf16[520,1024]{1,0:T(8,128)(2,1)}, u32[]{:S(2)}, u32[]{:S(2)}) collective-permute-start(bf16[520,1024]{1,0:T(8,128)(2,1)} %fusion.10.refs_0_), channel_id=1, source_target_pairs={{0,16},{4,20},{8,24},{12,28},{16,32},{20,36},{24,40},{28,44},{32,4... | collective-permute-start | bytes 3194888 | tf_op jit(solution)/shard_map/ppermute | solution.py:132
  43.7 41.3 %collective-permute-start.4 = (bf16[520,1024]{1,0:T(8,128)(2,1)}, bf16[520,1024]{1,0:T(8,128)(2,1)}, u32[]{:S(2)}, u32[]{:S(2)}) collective-permute-start(bf16[520,1024]{1,0:T(8,128)(2,1)} %fusion.10.refs_0_), channel_id=1, source_target_pairs={{0,4},{4,8},{8,12},{16,20},{20,24},{24,28},{32,36},{36,40},{40,44}... | collective-permute-start | bytes 3194888 | tf_op jit(solution)/shard_map/ppermute | solution.py:132
  72.4 27.5 %collective-permute-start.5 = (bf16[520,1024]{1,0:T(8,128)(2,1)}, bf16[520,1024]{1,0:T(8,128)(2,1)}, u32[]{:S(2)}, u32[]{:S(2)}) collective-permute-start(bf16[520,1024]{1,0:T(8,128)(2,1)} %collective-permute-done.2.refs_4_), channel_id=1, source_target_pairs={{4,0},{8,4},{12,8},{20,16},{24,20},{28,24},{36,32},{40,36},{44,40}... | collective-permute-start | bytes 3194888 | tf_op jit(solution)/shard_map/ppermute | solution.py:132
  73.8 37.8 %collective-permute-start.8 = (bf16[520,1024]{1,0:T(8,128)(2,1)}, bf16[520,1024]{1,0:T(8,128)(2,1)}, u32[]{:S(2)}, u32[]{:S(2)}) collective-permute-start(bf16[520,1024]{1,0:T(8,128)(2,1)} %fusion.10.refs_0_), channel_id=1, source_target_pairs={{0,12},{16,28},{32,44},{48,60},{64,76},{80,92},{96,108},{112,124},... | collective-permute-start | bytes 3194888 | tf_op jit(solution)/shard_map/ppermute | solution.py:132
  82.0 28.2 %collective-permute-start.3 = (bf16[520,1024]{1,0:T(8,128)(2,1)}, bf16[520,1024]{1,0:T(8,128)(2,1)}, u32[]{:S(2)}, u32[]{:S(2)}) collective-permute-start(bf16[520,1024]{1,0:T(8,128)(2,1)} %collective-permute-done.2.refs_4_), channel_id=1, source_target_pairs={{12,0},{28,16},{44,32},{60,48},{76,64},{92,80},{108,96},{124,112},... | collective-permute-start | bytes 3194888 | tf_op jit(solution)/shard_map/ppermute | solution.py:132
  85.0 28.3 %collective-permute-start.7 = (bf16[520,1024]{1,0:T(8,128)(2,1)}, bf16[520,1024]{1,0:T(8,128)(2,1)S(1)}, u32[]{:S(2)}, u32[]{:S(2)}) collective-permute-start(bf16[520,1024]{1,0:T(8,128)(2,1)} %collective-permute-done.4), channel_id=1, source_target_pairs={{4,8},{8,12},{20,24},{24,28},{36,40},{40,44},{52,56},{56,60},{68,7... | collective-permute-start | bytes 3194888 | tf_op jit(solution)/shard_map/ppermute | solution.py:132
  99.9 26.6 %collective-permute-start.6 = (bf16[520,1024]{1,0:T(8,128)(2,1)}, bf16[520,1024]{1,0:T(8,128)(2,1)S(1)}, u32[]{:S(2)}, u32[]{:S(2)}) collective-permute-start(bf16[520,1024]{1,0:T(8,128)(2,1)} %collective-permute-done.5), channel_id=1, source_target_pairs={{4,0},{8,4},{20,16},{24,20},{36,32},{40,36},{52,48},{56,52},{68,64... | collective-permute-start | bytes 3194888 | tf_op jit(solution)/shard_map/ppermute | solution.py:132
  111.6 15.0 %copy-start.6 = (bf16[520,1024]{1,0:T(8,128)(2,1)}, bf16[520,1024]{1,0:T(8,128)(2,1)S(1)}, u32[]{:S(2)}) copy-start(bf16[520,1024]{1,0:T(8,128)(2,1)S(1)} %broadcast_select_fusion.2.refs_1_) | copy-start | bytes 3194884
  113.3 13.3 %copy-start.7 = (bf16[520,1024]{1,0:T(8,128)(2,1)}, bf16[520,1024]{1,0:T(8,128)(2,1)S(1)}, u32[]{:S(2)}) copy-start(bf16[520,1024]{1,0:T(8,128)(2,1)S(1)} %broadcast_select_fusion.refs_3_) | copy-start | bytes 3194884
  126.6 1.0 copy-start.8
  173.9 2.7 %collective-permute-start.9 = (bf16[2,128,2048]{2,1,0:T(8,128)(2,1)S(1)}, bf16[2,128,2048]{2,1,0:T(8,128)(2,1)S(1)}, u32[]{:S(2)}, u32[]{:S(2)}) collective-permute-start(bf16[2,128,2048]{2,1,0:T(8,128)(2,1)S(1)} %bitcast.44), channel_id=1, source_target_pairs={{0,1},{1,0},{2,3},{3,2},{4,5},{5,4},{6,7},{7,6},{8,9},{9,8},{10,11... | collective-permute-start | bytes 3145736 | tf_op jit(solution)/shard_map/ppermute | solution.py:24
  177.1 15.6 %collective-permute-start.10 = (bf16[128,2048]{1,0:T(8,128)(2,1)S(1)}, bf16[128,2048]{1,0:T(8,128)(2,1)S(1)}, u32[]{:S(2)}, u32[]{:S(2)}) collective-permute-start(bf16[128,2048]{1,0:T(8,128)(2,1)S(1)} %fusion.16), channel_id=1, source_target_pairs={{0,2},{1,3},{2,0},{3,1},{4,6},{5,7},{6,4},{7,5},{8,10},{9,11},{10,... | collective-permute-start | bytes 1572872 | tf_op jit(solution)/shard_map/ppermute | solution.py:24

commit v5 on v4

v5 whole, which is shorter than its diff:
```python
import functools

import jax
import jax.numpy as jnp
from jax import lax
from jax.sharding import PartitionSpec as P
from jax.experimental import pallas as pl
from jax.experimental.pallas import tpu as pltpu

HD = 128
SPAN = 4


EPSILON = 1e-05
NEG_FILL = -1e30


def shifted(value, axis, steps):
    count = lax.axis_size(axis)
    leading, last = (max(0, -steps), min(count, count - steps))
    return lax.ppermute(value, axis, [(source, source + steps) for source in range(leading, last)])


def swapped(value, axis, mask):
    count = lax.axis_size(axis)
    return lax.ppermute(value, axis, [(source, source ^ mask) for source in range(count)])


def layer_norm(inputs, ln_gain):
    row_mean = jnp.mean(inputs, axis=-1, keepdims=True)
    centred = inputs - row_mean
    variance = jnp.mean(centred * centred, axis=-1, keepdims=True)
    return (centred * lax.rsqrt(variance + EPSILON) * ln_gain).astype(jnp.bfloat16)


TQ = 256
TK = 256


def part_kernel(n_buf, own, flags_ref, q_ref, *refs):
    bufs = refs[:n_buf]
    (segq_ref, segk_ref, bias_ref, m_in, l_in, acc_in, m_out, l_out, acc_out, m_sc, l_sc) = refs[n_buf:]
    heads = m_sc.shape[0]
    block_len = q_ref.shape[0]
    n_q, n_t = block_len // TQ, block_len // TK
    width = heads * HD
    scale = HD ** (-0.5)
    for h in range(heads):
        m_sc[h] = m_in[:, h : h + 1]
        l_sc[h] = l_in[:, h : h + 1]
    acc_out[...] = acc_in[...]
    for qt in range(n_q):
        rows = pl.ds(qt * TQ, TQ)
        segq = segq_ref[rows, :]
        steps = [(i, t) for i in range(n_buf) for t in range(n_t)]
        if own:
            steps = [(0, qt)] + [(0, t) for t in range(n_t) if t * TK < qt * TQ] + steps[n_t:]
        for i, t in steps:
            diag = own and i == 0 and t == qt

            def body(i=i, t=t, diag=diag):
                valid = segq == segk_ref[pl.ds(i, 1), pl.ds(t * TK, TK)]
                if diag:
                    r = lax.broadcasted_iota(jnp.int32, (TQ, TK), 0)
                    c = lax.broadcasted_iota(jnp.int32, (TQ, TK), 1)
                    valid = valid & (c <= r)

                def one_head(h, carry):
                    lanes = pl.multiple_of(h * HD, HD)
                    q = q_ref[rows, pl.ds(lanes, HD)]
                    k = bufs[i][pl.ds(t * TK, TK), pl.ds(lanes, HD)]
                    v = bufs[i][pl.ds(t * TK, TK), pl.ds(width + lanes, HD)]
                    s = lax.dot_general(
                        q, k, (((1,), (1,)), ((), ())), preferred_element_type=jnp.float32
                    )
                    s = s * scale + bias_ref[pl.ds(i * heads + h, 1), pl.ds(t * TK, TK)]
                    s = jnp.where(valid, s, NEG_FILL)
                    m_prev = m_sc[h, rows, :]
                    m_new = jnp.maximum(m_prev, jnp.max(s, axis=1, keepdims=True))
                    p = jnp.exp(s - m_new)
                    rescale = jnp.exp(m_prev - m_new)
                    l_sc[h, rows, :] = l_sc[h, rows, :] * rescale + jnp.sum(p, axis=1, keepdims=True)
                    acc_out[rows, pl.ds(lanes, HD)] = acc_out[rows, pl.ds(lanes, HD)] * rescale + jnp.dot(
                        p.astype(jnp.bfloat16), v, preferred_element_type=jnp.float32
                    )
                    m_sc[h, rows, :] = m_new
                    return carry

                lax.fori_loop(0, heads, one_head, 0)

            if diag:
                body()
            else:
                pl.when(flags_ref[(qt * n_buf + i) * n_t + t] != 0)(body)
    lane = lax.broadcasted_iota(jnp.int32, m_in.shape, 1)
    m_all, l_all = m_in[...], l_in[...]
    for h in range(heads):
        m_all = jnp.where(lane == h, m_sc[h], m_all)
        l_all = jnp.where(lane == h, l_sc[h], l_all)
    m_out[...] = m_all
    l_out[...] = l_all


def attention_part(state, queries, seg_q, slopes, bufs, steps_back, present, own=False):
    block_len, width = queries.shape
    heads = width // HD
    n_buf = len(bufs)
    n_q, n_t = block_len // TQ, block_len // TK
    seg_k = jnp.stack(
        [
            jnp.where(ok, buf[block_len, :block_len].astype(jnp.int32), -1)
            for buf, ok in zip(bufs, present)
        ]
    )
    if own:
        seg_k = seg_k.at[0].set(seg_q)
    seg_first = seg_q.reshape(n_q, TQ)[:, 0]
    seg_last = seg_k.reshape(n_buf, n_t, TK)[:, :, -1]
    flags = seg_last[None, :, :] >= seg_first[:, None, None]
    if own:
        earlier = jnp.arange(n_t)[None, :] < jnp.arange(n_q)[:, None]
        flags = flags.at[:, 0, :].set(flags[:, 0, :] & earlier)
    flags = flags.astype(jnp.int32).reshape(-1)
    seg_rows = jnp.concatenate(
        [seg_k, jnp.full(((-n_buf) % 8, block_len), -1, jnp.int32)], axis=0
    )
    offsets = jnp.arange(block_len, dtype=jnp.int32)
    rel = offsets[None, :] - jnp.stack(steps_back)[:, None] * block_len
    bias = (rel.astype(jnp.float32)[:, None, :] * slopes[None, :, None]).reshape(n_buf * heads, block_len)
    bias = jnp.concatenate([bias, jnp.zeros(((-n_buf * heads) % 8, block_len), jnp.float32)], axis=0)
    vmem = pl.BlockSpec(memory_space=pltpu.VMEM)
    work = heads * block_len * n_buf * block_len
    m, l, acc = state
    return pl.pallas_call(
        functools.partial(part_kernel, n_buf, own),
        out_shape=(
            jax.ShapeDtypeStruct(m.shape, jnp.float32),
            jax.ShapeDtypeStruct(l.shape, jnp.float32),
            jax.ShapeDtypeStruct(acc.shape, jnp.float32),
        ),
        in_specs=[pl.BlockSpec(memory_space=pltpu.SMEM)] + [vmem] * (n_buf + 7),
        out_specs=(vmem, vmem, vmem),
        scratch_shapes=[
            pltpu.VMEM((heads, block_len, 1), jnp.float32),
            pltpu.VMEM((heads, block_len, 1), jnp.float32),
        ],
        cost_estimate=pl.CostEstimate(
            flops=4 * work * HD,
            transcendentals=work,
            bytes_accessed=(n_buf + 4) * block_len * width * 4,
        ),
    )(flags, queries, *bufs, seg_q.reshape(block_len, 1), seg_rows, bias, m, l, acc)

RING = 4


def moved(value, pairs):
    return lax.ppermute(value, "seq", pairs)


def relay_earlier_blocks(payload):
    count = lax.axis_size("seq")
    y = lax.axis_index("seq") % RING
    ids = range(count)
    from_z = moved(payload, [(s, s + RING) for s in ids if s + RING < count])
    from_below = moved(payload, [(s, s + 1) for s in ids if s % RING < RING - 1])
    from_wrap = moved(payload, [(s, s + RING - 1) for s in ids if s % RING == 0])
    passed_up = moved(from_below, [(s, s + 1) for s in ids if 0 < s % RING < RING - 1])
    passed_down = moved(from_z, [(s, s - 1) for s in ids if s % RING > 0])
    passed_wrap = moved(from_z, [(s, s - RING + 1) for s in ids if s % RING == RING - 1])
    passed_twice = moved(passed_down, [(s, s - 1) for s in ids if 0 < s % RING < RING - 1])
    seq_index = lax.axis_index("seq")
    rounds = [
        [(from_z, 4, seq_index >= 4), (from_below, 1, y >= 1), (from_wrap, 3, y == 3)],
        [
            (passed_up, 2, y >= 2),
            (passed_down, 3, (y <= 2) & (seq_index >= 3)),
            (passed_wrap, 1, (y == 0) & (seq_index >= 1)),
        ],
        [(passed_twice, 2, (y <= 1) & (seq_index >= 2))],
    ]
    return rounds


def on_device(tokens, ln_gain, w_qkv, slopes, w_out, seg_ids):
    inputs = tokens.astype(jnp.float32)
    normed = layer_norm(inputs, ln_gain)
    rows_dev = normed.shape[0]
    head = lax.axis_index("head")
    n_head = lax.axis_size("head")

    cross = swapped(normed, "head", 2)
    partner = swapped(jnp.stack([normed, cross]), "head", 1)
    pieces = jnp.stack([normed, partner[0], cross, partner[1]])
    block_rows = jnp.concatenate(
        [lax.dynamic_index_in_dim(pieces, j ^ head, 0, keepdims=False) for j in range(n_head)], axis=0
    )

    width_local = w_qkv.shape[2]
    heads_dev = slopes.shape[0]
    joined = w_qkv.reshape(w_qkv.shape[0], 3 * width_local)
    qkv_rows = jnp.dot(block_rows, joined, preferred_element_type=jnp.float32).astype(jnp.bfloat16)
    block_len = qkv_rows.shape[0]
    key_cache = qkv_rows[:, width_local : 2 * width_local]
    value_cache = qkv_rows[:, 2 * width_local :]

    kv_own = qkv_rows[:, width_local:]
    seg_row = jnp.zeros((8, kv_own.shape[1]), jnp.bfloat16).at[0, :block_len].set(
        seg_ids.astype(jnp.bfloat16)
    )
    payload = jnp.concatenate([kv_own, seg_row], axis=0)
    rounds = relay_earlier_blocks(payload)

    queries = qkv_rows[:, :width_local]
    state = (
        jnp.full((block_len, HD), NEG_FILL, jnp.float32),
        jnp.zeros((block_len, HD), jnp.float32),
        jnp.zeros((block_len, width_local), jnp.float32),
    )
    state = attention_part(
        state, queries, seg_ids, slopes, [payload], [jnp.int32(0)], [jnp.bool_(True)], own=True
    )
    for arrived in rounds:
        bufs, steps_back, present = zip(*arrived)
        steps_back = [jnp.int32(k) for k in steps_back]
        state = attention_part(state, queries, seg_ids, slopes, list(bufs), steps_back, list(present))
    _, total, acc = state
    denominator = jnp.repeat(total[:, :heads_dev], HD, axis=1)
    context = (acc / denominator).astype(jnp.bfloat16)

    context4 = context.reshape(n_head, rows_dev, context.shape[1])

    def project(owners):
        rows = jnp.concatenate(
            [lax.dynamic_index_in_dim(context4, o, 0, keepdims=False) for o in owners], axis=0
        )
        out = jnp.dot(rows, w_out, preferred_element_type=jnp.float32).astype(jnp.bfloat16)
        return out.reshape(len(owners), rows_dev, w_out.shape[1])

    sent = project([head ^ 1, head ^ 3])
    kept = project([head, head ^ 2])
    chip_sum = kept.astype(jnp.float32) + swapped(sent, "head", 1).astype(jnp.float32)
    other_chip = swapped(chip_sum[1].astype(jnp.bfloat16), "head", 2).astype(jnp.float32)
    hidden = (inputs + chip_sum[0] + other_chip).astype(jnp.bfloat16)
    return (hidden, key_cache, value_cache)


def solution(mesh):
    in_specs = (
        P(("seq", "head"), None),
        P(),
        P(None, None, "head"),
        P("head"),
        P("head", None),
        P("seq"),
    )
    out_specs = (P(("seq", "head"), None), P("seq", "head"), P("seq", "head"))
    return jax.shard_map(
        on_device, mesh=mesh, in_specs=in_specs, out_specs=out_specs, check_vma=False
    )
```

time: 194 us -> 196 us (1.010)
  the two profiles are of different devices: /device:TPU:6 before, /device:TPU:86 now
where the time goes in v5:
time: 196 us; the launch traced here: 195 us
  Pallas kernels  59.3 us (30%)
  waiting for transfers between devices  56 us (29%)
  local copies, waits for them, and re-layouts  29.3 us (15%)
  starting transfers between devices  23.5 us (12%)
  other arithmetic  20.6 us (11%)
  matrix products  4.93 us (3%)
    pallas_call x4, Pallas kernels, attention_part(): pl.pallas_call(functools.partial(part_kernel, n_buf, own), out_shape=(jax...  59.3 us
    ppermute x4, waiting for transfers between devices, swapped(): lax.ppermute(value, axis, [(source, source ^ mask) for source in range(co...  29.4 us
    ppermute x7, waiting for transfers between devices, moved(): return lax.ppermute(value, 'seq', pairs)  26.7 us
    ppermute x7, starting transfers between devices, moved(): return lax.ppermute(value, 'seq', pairs)  20.5 us
    unnamed x24, local copies, waits for them, and re-layouts  12.1 us
    select_n x7, other arithmetic, attention_part(): jnp.where(ok, buf[block_len, :block_len].astype(jnp.int32), -1)  9.33 us
  transfers between devices with their start and end apart: 11, of which 5 were waited for; matrix products, arithmetic and copies ran while one was open for 16% of the time, Pallas kernels for 28%

profile of v5, /device:TPU:86, one launch (start us, length us, event | category | flops | bytes accessed | tf_op | source)
XLA Modules:
  0.0 194.6 jit_solution(13596061416307558270)
XLA Ops:
  0.7 1.3 convert_reduce_fusion
  2.0 1.3 fusion.11
  3.4 1.4 fusion.13
  4.8 1.5 collective-permute-start
  6.3 0.4 fusion.39
  6.7 13.4 %collective-permute-done = bf16[128,2048]{1,0:T(8,128)(2,1)S(1)} collective-permute-done((bf16[128,2048]{1,0:T(8,128)(2,1)S(1)}, bf16[128,2048]{1,0:T(8,128)(2,1)S(1)}, u32[]{:S(2)}, u32[]{:S(2)}) %collective-permute-start) | collective-permute-done | bytes 524320 | tf_op jit(solution)/shard_map/ppermute | solution.py:26
  20.1 0.8 copy-done.4
  20.8 1.1 pad_maximum_fusion.1
  22.0 8.8 %copy.46 = bf16[2048,3,512]{0,2,1:T(8,128)(2,1)} copy(bf16[2048,3,512]{2,0,1:T(8,128)(2,1)} %param.14) | data formatting | bytes 12582912 | tf_op args[2]
  30.8 0.1 slice_reduce_fusion.1
  30.9 0.2 slice_reduce_fusion
  31.1 1.3 fusion.35
  32.4 0.3 pad_maximum_fusion
  32.7 0.2 dynamic-slice_bitcast_fusion.3
  32.9 2.2 %copy-done.2 = bf16[2048,3,512]{0,2,1:T(8,128)(2,1)S(1)} copy-done((bf16[2048,3,512]{0,2,1:T(8,128)(2,1)S(1)}, bf16[2048,3,512]{0,2,1:T(8,128)(2,1)}, u32[]{:S(2)}) %copy-start.2) | copy-done | bytes 6291480
  35.2 3.4 %convolution_convert_fusion = bf16[512,1536]{1,0:T(8,128)(2,1)S(1)} fusion(bf16[2048,1536]{0,1:T(8,128)(2,1)S(1)} %bitcast.46, bf16[128,2048]{1,0:T(8,128)(2,1)S(1)} %get-tuple-element.76, bf16[128,2048]{1,0:T(8,128)(2,1)S(1)} %get-tuple-element.77, bf16[128,2048]{1,0:T(8,128)(2,1)S(1)} %get-tuple-element.78, bf16[128,2048]{1,0:T(8,128)(2,1)S(1)} %get-tuple-element.75), kind=kOutput, calls=%fused_computation | convolution fusion | flops 3230400512 | bytes 9961472 | tf_op jit(solution)/shard_map/dot_general | solution.py:202
  38.7 0.1 slice.146
  38.8 1.3 fusion.10.refs_0_
  40.2 3.8 %collective-permute-start.2 = (bf16[520,1024]{1,0:T(8,128)(2,1)}, bf16[520,1024]{1,0:T(8,128)(2,1)}, u32[]{:S(2)}, u32[]{:S(2)}) collective-permute-start(bf16[520,1024]{1,0:T(8,128)(2,1)} %fusion.10.refs_0_), channel_id=1, source_target_pairs={{0,16},{4,20},{8,24},{12,28},{16,32},{20,36},{24,40},{28,44},{32,4... | collective-permute-start | bytes 3194888 | tf_op jit(solution)/shard_map/ppermute | solution.py:158
  44.0 0.9 copy.55.refs_1_.refs_3_
  44.9 0.7 reshape.337.flags_ref
  45.6 0.6 concatenate.54.refs_2_
  46.3 3.2 %collective-permute-start.5 = (bf16[520,1024]{1,0:T(8,128)(2,1)}, bf16[520,1024]{1,0:T(8,128)(2,1)}, u32[]{:S(2)}, u32[]{:S(2)}) collective-permute-start(bf16[520,1024]{1,0:T(8,128)(2,1)} %fusion.10.refs_0_), channel_id=1, source_target_pairs={{0,4},{4,8},{8,12},{16,20},{20,24},{24,28},{32,36},{36,40},{40,44}... | collective-permute-start | bytes 3194888 | tf_op jit(solution)/shard_map/ppermute | solution.py:158
  49.7 1.7 collective-permute-start.8
  51.5 0.6 concatenate.55.refs_3_
  52.2 0.6 concatenate.53.refs_5_
  52.8 0.6 concatenate.51.refs_5_
  53.4 0.6 concatenate.49.refs_3_
  54.0 14.2 %collective-permute-done.2.refs_0_ = bf16[520,1024]{1,0:T(8,128)(2,1)} collective-permute-done((bf16[520,1024]{1,0:T(8,128)(2,1)}, bf16[520,1024]{1,0:T(8,128)(2,1)}, u32[]{:S(2)}, u32[]{:S(2)}) %collective-permute-start.2) | collective-permute-done | bytes 1064992 | tf_op jit(solution)/shard_map/ppermute | solution.py:158
  68.3 2.3 %collective-permute-start.3 = (bf16[520,1024]{1,0:T(8,128)(2,1)}, bf16[520,1024]{1,0:T(8,128)(2,1)}, u32[]{:S(2)}, u32[]{:S(2)}) collective-permute-start(bf16[520,1024]{1,0:T(8,128)(2,1)} %collective-permute-done.2.refs_0_), channel_id=1, source_target_pairs={{4,0},{8,4},{12,8},{20,16},{24,20},{28,24},{36,32},{40,36},{44,40}... | collective-permute-start | bytes 3194888 | tf_op jit(solution)/shard_map/ppermute | solution.py:158
  70.6 1.6 collective-permute-start.7
  72.3 2.5 %fusion.34 = (bf16[512,512]{1,0:T(8,128)(2,1)}, bf16[512,512]{1,0:T(8,128)(2,1)}, bf16[512,512]{1,0:T(8,128)(2,1)}) fusion(bf16[512,1536]{1,0:T(8,128)(2,1)} %copy-done.3), kind=kLoop, calls=%fused_computation.91 | loop fusion | bytes 3145728 | tf_op jit(solution)/shard_map/slice | solution.py:205
  74.8 1.1 broadcast_in_dim.22.refs_6_
  75.9 0.7 broadcast_in_dim.20.refs_4_
  76.6 0.7 broadcast_in_dim.21.refs_5_
  77.3 11.3 %shard_map.85 = (f32[512,128]{1,0:T(8,128)}, f32[512,128]{1,0:T(8,128)}, f32[512,512]{1,0:T(8,128)}) custom-call(s32[4]{0:T(128)} %reshape.337.flags_ref, bf16[512,512]{1,0:T(8,128)(2,1)} %get-tuple-element.81.q_ref, bf16[520,1024]{1,0:T(8,128)(2,1)} %fusion.10.refs_0_, s32[512,1]{1,0:T(8,128)} %copy.55.refs_1_.refs_3_, s32[8,512]{1,0:T(8,128)} %concatenate.54.refs_2_, ...), custom_call_target="tpu_custom_call" | custom-call | flops 536870912 | bytes 5242880 | tf_op jit(solution)/shard_map/pallas_call | solution.py:134
  88.6 5.1 %collective-permute-start.6 = (bf16[520,1024]{1,0:T(8,128)(2,1)}, bf16[520,1024]{1,0:T(8,128)(2,1)}, u32[]{:S(2)}, u32[]{:S(2)}) collective-permute-start(bf16[520,1024]{1,0:T(8,128)(2,1)} %collective-permute-done.5.refs_1_), channel_id=1, source_target_pairs={{4,8},{8,12},{20,24},{24,28},{36,40},{40,44},{52,56},{56,60},{68,7... | collective-permute-start | bytes 3194888 | tf_op jit(solution)/shard_map/ppermute | solution.py:158
  93.7 0.5 broadcast.269
  94.3 1.3 fusion.28
  95.6 1.3 fusion.29
  97.0 1.3 fusion.27
  98.6 1.3 fusion.31
  99.9 1.3 fusion.32
  101.3 2.7 %collective-permute-start.4 = (bf16[520,1024]{1,0:T(8,128)(2,1)}, bf16[520,1024]{1,0:T(8,128)(2,1)}, u32[]{:S(2)}, u32[]{:S(2)}) collective-permute-start(bf16[520,1024]{1,0:T(8,128)(2,1)} %collective-permute-done.3.refs_1_), channel_id=1, source_target_pairs={{4,0},{8,4},{20,16},{24,20},{36,32},{40,36},{52,48},{56,52},{68,64... | collective-permute-start | bytes 3194888 | tf_op jit(solution)/shard_map/ppermute | solution.py:158
  104.0 12.4 %collective-permute-done.6.refs_0_ = bf16[520,1024]{1,0:T(8,128)(2,1)} collective-permute-done((bf16[520,1024]{1,0:T(8,128)(2,1)}, bf16[520,1024]{1,0:T(8,128)(2,1)}, u32[]{:S(2)}, u32[]{:S(2)}) %collective-permute-start.6) | collective-permute-done | bytes 1064992 | tf_op jit(solution)/shard_map/ppermute | solution.py:158
  116.4 1.3 fusion.30
  118.1 0.7 reshape.336.flags_ref
  118.8 0.7 reshape.335.flags_ref
  119.4 0.7 add_add_fusion.1
  120.1 19.5 %shard_map.86 = (f32[512,128]{1,0:T(8,128)}, f32[512,128]{1,0:T(8,128)}, f32[512,512]{1,0:T(8,128)}) custom-call(s32[12]{0:T(128)} %reshape.336.flags_ref, bf16[512,512]{1,0:T(8,128)(2,1)} %get-tuple-element.81.q_ref, bf16[520,1024]{1,0:T(8,128)(2,1)} %collective-permute-done.2.refs_0_, bf16[520,1024]{1,0:T(8,128)(2,1)} %collective-permute-done.5.refs_1_, ...), custom_call_target="tpu_custom_call" | custom-call | flops 1610612736 | bytes 7340032 | tf_op jit(solution)/shard_map/pallas_call | solution.py:134
  139.6 24.1 %shard_map.87 = (f32[512,128]{1,0:T(8,128)}, f32[512,128]{1,0:T(8,128)}, f32[512,512]{1,0:T(8,128)}) custom-call(s32[12]{0:T(128)} %reshape.335.flags_ref, bf16[512,512]{1,0:T(8,128)(2,1)} %get-tuple-element.81.q_ref, bf16[520,1024]{1,0:T(8,128)(2,1)} %collective-permute-done.6.refs_0_, bf16[520,1024]{1,0:T(8,128)(2,1)} %collective-permute-done.3.refs_1_, ...), custom_call_target="tpu_custom_call" | custom-call | flops 1610612736 | bytes 7340032 | tf_op jit(solution)/shard_map/pallas_call | solution.py:134
  163.8 1.3 fusion.33
  165.1 0.6 concatenate.48.refs_2_
  165.9 0.7 reshape.334.flags_ref
  166.6 4.4 %shard_map.88 = (f32[512,128]{1,0:T(8,128)}, f32[512,128]{1,0:T(8,128)}, f32[512,512]{1,0:T(8,128)}) custom-call(s32[4]{0:T(128)} %reshape.334.flags_ref, bf16[512,512]{1,0:T(8,128)(2,1)} %get-tuple-element.81.q_ref, bf16[520,1024]{1,0:T(8,128)(2,1)} %collective-permute-done.4.refs_0_, s32[512,1]{1,0:T(8,128)} %copy.55.refs_1_.refs_3_, ...), custom_call_target="tpu_custom_call" | custom-call | flops 536870912 | bytes 5242880 | tf_op jit(solution)/shard_map/pallas_call | solution.py:134
  171.0 1.5 broadcast_in_dim.23
  172.6 1.4 fusion.16
  174.1 0.7 convolution_convert_fusion.1
  174.9 0.7 convolution_convert_fusion.2
  175.7 1.9 collective-permute-done.9
  177.6 0.4 convert_add_fusion
  178.0 1.5 collective-permute-start.10
  179.5 14.1 %collective-permute-done.10 = bf16[128,2048]{1,0:T(8,128)(2,1)S(1)} collective-permute-done((bf16[128,2048]{1,0:T(8,128)(2,1)S(1)}, bf16[128,2048]{1,0:T(8,128)(2,1)S(1)}, u32[]{:S(2)}, u32[]{:S(2)}) %collective-permute-start.10) | collective-permute-done | bytes 524320 | tf_op jit(solution)/shard_map/ppermute | solution.py:26
  193.6 1.0 fusion.15
  (67 shorter events, 2.0 us)
Async XLA Ops:
  0.6 173.4 %copy-start = (bf16[512,2048]{1,0:T(8,128)(2,1)S(1)}, bf16[512,2048]{1,0:T(8,128)(2,1)}, u32[]{:S(2)}) copy-start(bf16[512,2048]{1,0:T(8,128)(2,1)} %param.16) | copy-start | bytes 6291460
  0.6 5.6 %copy-start.1 = (bf16[128,2048]{1,0:T(8,128)(2,1)S(1)}, bf16[128,2048]{1,0:T(8,128)(2,1)}, u32[]{:S(2)}) copy-start(bf16[128,2048]{1,0:T(8,128)(2,1)} %param.12) | copy-start | bytes 1572868
  0.7 5.6 %copy-start.7 = (f32[2048]{0:T(1024)S(1)}, f32[2048]{0:T(1024)}, u32[]{:S(2)}) copy-start(f32[2048]{0:T(1024)} %param.13) | copy-start | bytes 24580
  3.4 18.6 %copy-start.6 = (s32[512]{0:T(512)S(1)}, s32[512]{0:T(512)}, u32[]{:S(2)}) copy-start(s32[512]{0:T(512)} %param.17) | copy-start | bytes 6148
  4.8 15.3 %collective-permute-start = (bf16[128,2048]{1,0:T(8,128)(2,1)S(1)}, bf16[128,2048]{1,0:T(8,128)(2,1)S(1)}, u32[]{:S(2)}, u32[]{:S(2)}) collective-permute-start(bf16[128,2048]{1,0:T(8,128)(2,1)S(1)} %fusion.13), channel_id=1, source_target_pairs={{0,2},{1,3},{2,0},{3,1},{4,6},{5,7},{6,4},{7,5},{8,10},{9,11},{10,... | collective-permute-start | bytes 1572872 | tf_op jit(solution)/shard_map/ppermute | solution.py:26
  20.1 0.8 copy-start.4
  21.9 9.2 %collective-permute-start.1 = (bf16[2,128,2048]{2,1,0:T(8,128)(2,1)}, bf16[2,128,2048]{2,1,0:T(8,128)(2,1)}, u32[]{:S(2)}, u32[]{:S(2)}) collective-permute-start(bf16[2,128,2048]{2,1,0:T(8,128)(2,1)} %pad_maximum_fusion.1), channel_id=1, source_target_pairs={{0,1},{1,0},{2,3},{3,2},{4,5},{5,4},{6,7},{7,6},{8,9},{9,8},{10,11... | collective-permute-start | bytes 3145736 | tf_op jit(solution)/shard_map/ppermute | solution.py:26
  30.8 1.6 copy-start.5
  32.4 2.8 %copy-start.2 = (bf16[2048,3,512]{0,2,1:T(8,128)(2,1)S(1)}, bf16[2048,3,512]{0,2,1:T(8,128)(2,1)}, u32[]{:S(2)}) copy-start(bf16[2048,3,512]{0,2,1:T(8,128)(2,1)} %copy.46) | copy-start | bytes 18874372
  38.6 1.5 copy-start.3
  38.6 7.6 %copy-start.10 = (s32[3]{0:T(128)S(1)}, s32[3]{0:T(128)}, u32[]{:S(2)}) copy-start(s32[3]{0:T(128)} %constant.149.clone.1) | copy-start | bytes 40
  38.6 10.9 %copy-start.9 = (s32[3]{0:T(128)S(1)}, s32[3]{0:T(128)}, u32[]{:S(2)}) copy-start(s32[3]{0:T(128)} %constant.150.clone.1) | copy-start | bytes 40
  38.6 11.0 %copy-start.8 = (f32[4]{0:T(128)S(1)}, f32[4]{0:T(128)}, u32[]{:S(2)}) copy-start(f32[4]{0:T(128)} %param.15) | copy-start | bytes 52
  40.2 28.1 %collective-permute-start.2 = (bf16[520,1024]{1,0:T(8,128)(2,1)}, bf16[520,1024]{1,0:T(8,128)(2,1)}, u32[]{:S(2)}, u32[]{:S(2)}) collective-permute-start(bf16[520,1024]{1,0:T(8,128)(2,1)} %fusion.10.refs_0_), channel_id=1, source_target_pairs={{0,16},{4,20},{8,24},{12,28},{16,32},{20,36},{24,40},{28,44},{32,4... | collective-permute-start | bytes 3194888 | tf_op jit(solution)/shard_map/ppermute | solution.py:158
  46.3 42.3 %collective-permute-start.5 = (bf16[520,1024]{1,0:T(8,128)(2,1)}, bf16[520,1024]{1,0:T(8,128)(2,1)}, u32[]{:S(2)}, u32[]{:S(2)}) collective-permute-start(bf16[520,1024]{1,0:T(8,128)(2,1)} %fusion.10.refs_0_), channel_id=1, source_target_pairs={{0,4},{4,8},{8,12},{16,20},{20,24},{24,28},{32,36},{36,40},{40,44}... | collective-permute-start | bytes 3194888 | tf_op jit(solution)/shard_map/ppermute | solution.py:158
  49.7 45.9 %collective-permute-start.8 = (bf16[520,1024]{1,0:T(8,128)(2,1)}, bf16[520,1024]{1,0:T(8,128)(2,1)}, u32[]{:S(2)}, u32[]{:S(2)}) collective-permute-start(bf16[520,1024]{1,0:T(8,128)(2,1)} %fusion.10.refs_0_), channel_id=1, source_target_pairs={{0,12},{16,28},{32,44},{48,60},{64,76},{80,92},{96,108},{112,124},... | collective-permute-start | bytes 3194888 | tf_op jit(solution)/shard_map/ppermute | solution.py:158
  68.3 30.3 %collective-permute-start.3 = (bf16[520,1024]{1,0:T(8,128)(2,1)}, bf16[520,1024]{1,0:T(8,128)(2,1)}, u32[]{:S(2)}, u32[]{:S(2)}) collective-permute-start(bf16[520,1024]{1,0:T(8,128)(2,1)} %collective-permute-done.2.refs_0_), channel_id=1, source_target_pairs={{4,0},{8,4},{12,8},{20,16},{24,20},{28,24},{36,32},{40,36},{44,40}... | collective-permute-start | bytes 3194888 | tf_op jit(solution)/shard_map/ppermute | solution.py:158
  70.6 29.3 %collective-permute-start.7 = (bf16[520,1024]{1,0:T(8,128)(2,1)}, bf16[520,1024]{1,0:T(8,128)(2,1)}, u32[]{:S(2)}, u32[]{:S(2)}) collective-permute-start(bf16[520,1024]{1,0:T(8,128)(2,1)} %collective-permute-done.2.refs_0_), channel_id=1, source_target_pairs={{12,0},{28,16},{44,32},{60,48},{76,64},{92,80},{108,96},{124,112},... | collective-permute-start | bytes 3194888 | tf_op jit(solution)/shard_map/ppermute | solution.py:158
  88.6 27.8 %collective-permute-start.6 = (bf16[520,1024]{1,0:T(8,128)(2,1)}, bf16[520,1024]{1,0:T(8,128)(2,1)}, u32[]{:S(2)}, u32[]{:S(2)}) collective-permute-start(bf16[520,1024]{1,0:T(8,128)(2,1)} %collective-permute-done.5.refs_1_), channel_id=1, source_target_pairs={{4,8},{8,12},{20,24},{24,28},{36,40},{40,44},{52,56},{56,60},{68,7... | collective-permute-start | bytes 3194888 | tf_op jit(solution)/shard_map/ppermute | solution.py:158
  101.3 62.5 %collective-permute-start.4 = (bf16[520,1024]{1,0:T(8,128)(2,1)}, bf16[520,1024]{1,0:T(8,128)(2,1)}, u32[]{:S(2)}, u32[]{:S(2)}) collective-permute-start(bf16[520,1024]{1,0:T(8,128)(2,1)} %collective-permute-done.3.refs_1_), channel_id=1, source_target_pairs={{4,0},{8,4},{20,16},{24,20},{36,32},{40,36},{52,48},{56,52},{68,64... | collective-permute-start | bytes 3194888 | tf_op jit(solution)/shard_map/ppermute | solution.py:158
  174.8 2.7 %collective-permute-start.9 = (bf16[2,128,2048]{2,1,0:T(8,128)(2,1)S(1)}, bf16[2,128,2048]{2,1,0:T(8,128)(2,1)S(1)}, u32[]{:S(2)}, u32[]{:S(2)}) collective-permute-start(bf16[2,128,2048]{2,1,0:T(8,128)(2,1)S(1)} %bitcast.52), channel_id=1, source_target_pairs={{0,1},{1,0},{2,3},{3,2},{4,5},{5,4},{6,7},{7,6},{8,9},{9,8},{10,11... | collective-permute-start | bytes 3145736 | tf_op jit(solution)/shard_map/ppermute | solution.py:26
  178.0 15.6 %collective-permute-start.10 = (bf16[128,2048]{1,0:T(8,128)(2,1)S(1)}, bf16[128,2048]{1,0:T(8,128)(2,1)S(1)}, u32[]{:S(2)}, u32[]{:S(2)}) collective-permute-start(bf16[128,2048]{1,0:T(8,128)(2,1)S(1)} %fusion.17), channel_id=1, source_target_pairs={{0,2},{1,3},{2,0},{3,1},{4,6},{5,7},{6,4},{7,5},{8,10},{9,11},{10,... | collective-permute-start | bytes 1572872 | tf_op jit(solution)/shard_map/ppermute | solution.py:26

commit v6 on v4

--- a/solution.py
+++ b/solution.py
@@ -156,17 +156,22 @@
     head = lax.axis_index("head")
     n_head = lax.axis_size("head")
 
-    cross = swapped(normed, "head", 2)
-    partner = swapped(jnp.stack([normed, cross]), "head", 1)
-    pieces = jnp.stack([normed, partner[0], cross, partner[1]])
-    block_rows = jnp.concatenate(
-        [lax.dynamic_index_in_dim(pieces, j ^ head, 0, keepdims=False) for j in range(n_head)], axis=0
-    )
-
     width_local = w_qkv.shape[2]
     heads_dev = slopes.shape[0]
     joined = w_qkv.reshape(w_qkv.shape[0], 3 * width_local)
-    qkv_rows = jnp.dot(block_rows, joined, preferred_element_type=jnp.float32).astype(jnp.bfloat16)
+
+    def project_rows(rows):
+        return jnp.dot(rows, joined, preferred_element_type=jnp.float32).astype(jnp.bfloat16)
+
+    from_partner = swapped(normed, "head", 1)
+    from_cross = swapped(normed, "head", 2)
+    from_partner_cross = swapped(from_cross, "head", 1)
+    pieces = jnp.stack(
+        [project_rows(r) for r in (normed, from_partner, from_cross, from_partner_cross)]
+    )
+    qkv_rows = jnp.concatenate(
+        [lax.dynamic_index_in_dim(pieces, j ^ head, 0, keepdims=False) for j in range(n_head)], axis=0
+    )
     block_len = qkv_rows.shape[0]
     key_cache = qkv_rows[:, width_local : 2 * width_local]
     value_cache = qkv_rows[:, 2 * width_local :]

time: 194 us -> 183 us (0.943)
  the two profiles are of different devices: /device:TPU:6 before, /device:TPU:104 now
where the time goes in v6:
time: 183 us; the launch traced here: 182 us
  waiting for transfers between devices  66.5 us (36%)
  Pallas kernels  42.6 us (23%)
  starting transfers between devices  26.6 us (15%)
  local copies, waits for them, and re-layouts  17.4 us (10%)
  matrix products  17.2 us (9%)
  other arithmetic  10.8 us (6%)
    ppermute x7, waiting for transfers between devices, moved(): return lax.ppermute(value, 'seq', pairs)  51.8 us
    pallas_call x1, Pallas kernels, attention(): pl.pallas_call(attention_kernel, out_shape=jax.ShapeDtypeStruct((block_le...  42.6 us
    ppermute x7, starting transfers between devices, moved(): return lax.ppermute(value, 'seq', pairs)  20 us
    dot_general x4, matrix products, project_rows(): jnp.dot(rows, joined, preferred_element_type=jnp.float32)  15.7 us
    ppermute x5, waiting for transfers between devices, swapped(): lax.ppermute(value, axis, [(source, source ^ mask) for source in range(co...  14.7 us
    unnamed x21, local copies, waits for them, and re-layouts  10.7 us
    ppermute x5, starting transfers between devices, swapped(): lax.ppermute(value, axis, [(source, source ^ mask) for source in range(co...  6.56 us
  transfers between devices with their start and end apart: 12, of which 5 were waited for; matrix products, arithmetic and copies ran while one was open for 17% of the time, Pallas kernels for 0%

profile of v6, /device:TPU:104, one launch (start us, length us, event | category | flops | bytes accessed | tf_op | source)
XLA Modules:
  0.0 182.0 jit_solution(9944610300032172561)
XLA Ops:
  0.6 0.0 copy-start
  0.6 1.3 convert_reduce_fusion
  2.0 1.3 fusion.8
  3.3 1.4 fusion.10
  4.8 3.1 %collective-permute-start.1 = (bf16[128,2048]{1,0:T(8,128)(2,1)S(1)}, bf16[128,2048]{1,0:T(8,128)(2,1)S(1)}, u32[]{:S(2)}, u32[]{:S(2)}) collective-permute-start(bf16[128,2048]{1,0:T(8,128)(2,1)S(1)} %fusion.10), channel_id=1, source_target_pairs={{0,2},{1,3},{2,0},{3,1},{4,6},{5,7},{6,4},{7,5},{8,10},{9,11},{10,... | collective-permute-start | bytes 1572872 | tf_op jit(solution)/shard_map/ppermute | solution.py:24
  7.9 0.0 collective-permute-start
  7.9 8.8 %copy.30 = bf16[2048,3,512]{0,2,1:T(8,128)(2,1)} copy(bf16[2048,3,512]{2,0,1:T(8,128)(2,1)} %param.10) | data formatting | bytes 12582912 | tf_op args[2]
  16.7 5.0 %fusion = bf16[1,128,1536]{2,1,0:T(8,128)(2,1)S(1)} fusion(bf16[128,2048]{1,0:T(8,128)(2,1)S(1)} %fusion.10, bf16[2048,1536]{0,1:T(8,128)(2,1)} %bitcast.52), kind=kOutput, calls=%fused_computation.6 | convolution fusion | flops 805502976 | bytes 7208960 | tf_op jit(solution)/shard_map/dot_general | solution.py:164
  21.8 0.0 collective-permute-done.1
  21.8 0.6 collective-permute-start.2
  22.4 5.3 %fusion.2 = bf16[1,128,1536]{2,1,0:T(8,128)(2,1)S(1)} fusion(bf16[128,2048]{1,0:T(8,128)(2,1)S(1)} %collective-permute-done.1, bf16[2048,1536]{0,1:T(8,128)(2,1)} %bitcast.53), kind=kOutput, calls=%fused_computation.8 | convolution fusion | flops 805502976 | bytes 7208960 | tf_op jit(solution)/shard_map/dot_general | solution.py:164
  27.7 0.0 collective-permute-done
  27.7 3.3 %fusion.1 = bf16[1,128,1536]{2,1,0:T(8,128)(2,1)S(1)} fusion(bf16[128,2048]{1,0:T(8,128)(2,1)} %collective-permute-done, bf16[2048,1536]{0,1:T(8,128)(2,1)S(1)} %bitcast.54), kind=kOutput, calls=%fused_computation.7 | convolution fusion | flops 805502976 | bytes 7208960 | tf_op jit(solution)/shard_map/dot_general | solution.py:164
  31.0 0.0 collective-permute-done.2
  31.0 2.2 %fusion.3 = bf16[1,128,1536]{2,1,0:T(8,128)(2,1)S(1)} fusion(bf16[128,2048]{1,0:T(8,128)(2,1)S(1)} %collective-permute-done.2, bf16[2048,1536]{0,1:T(8,128)(2,1)S(1)} %bitcast.55), kind=kOutput, calls=%fused_computation.9 | convolution fusion | flops 805502976 | bytes 7208960 | tf_op jit(solution)/shard_map/dot_general | solution.py:164
  33.2 0.2 pad_maximum_fusion
  33.4 0.1 dynamic-slice_bitcast_fusion.3
  33.5 0.1 pad_maximum_fusion.1
  33.6 0.0 copy-start.9
  33.6 0.1 slice.65
  33.8 0.1 fusion.7.refs_0_
  33.9 0.9 copy-done.2
  34.8 5.0 %collective-permute-start.3 = (bf16[520,1024]{1,0:T(8,128)(2,1)S(1)}, bf16[520,1024]{1,0:T(8,128)(2,1)}, u32[]{:S(2)}, u32[]{:S(2)}) collective-permute-start(bf16[520,1024]{1,0:T(8,128)(2,1)S(1)} %fusion.7.refs_0_), channel_id=1, source_target_pairs={{0,16},{4,20},{8,24},{12,28},{16,32},{20,36},{24,40},{28,44},{32,4... | collective-permute-start | bytes 3194888 | tf_op jit(solution)/shard_map/ppermute | solution.py:132
  39.8 3.5 %collective-permute-start.5 = (bf16[520,1024]{1,0:T(8,128)(2,1)S(1)}, bf16[520,1024]{1,0:T(8,128)(2,1)}, u32[]{:S(2)}, u32[]{:S(2)}) collective-permute-start(bf16[520,1024]{1,0:T(8,128)(2,1)S(1)} %fusion.7.refs_0_), channel_id=1, source_target_pairs={{0,4},{4,8},{8,12},{16,20},{20,24},{24,28},{32,36},{36,40},{40,44}... | collective-permute-start | bytes 3194888 | tf_op jit(solution)/shard_map/ppermute | solution.py:132
  43.3 19.3 %collective-permute-done.3.refs_4_ = bf16[520,1024]{1,0:T(8,128)(2,1)} collective-permute-done((bf16[520,1024]{1,0:T(8,128)(2,1)S(1)}, bf16[520,1024]{1,0:T(8,128)(2,1)}, u32[]{:S(2)}, u32[]{:S(2)}) %collective-permute-start.3) | collective-permute-done | bytes 1064992 | tf_op jit(solution)/shard_map/ppermute | solution.py:132
  62.6 2.3 %collective-permute-start.6 = (bf16[520,1024]{1,0:T(8,128)(2,1)}, bf16[520,1024]{1,0:T(8,128)(2,1)}, u32[]{:S(2)}, u32[]{:S(2)}) collective-permute-start(bf16[520,1024]{1,0:T(8,128)(2,1)} %collective-permute-done.3.refs_4_), channel_id=1, source_target_pairs={{4,0},{8,4},{12,8},{20,16},{24,20},{28,24},{36,32},{40,36},{44,40}... | collective-permute-start | bytes 3194888 | tf_op jit(solution)/shard_map/ppermute | solution.py:132
  65.0 0.1 add_convert_fusion
  65.1 1.6 collective-permute-start.9
  66.7 1.6 collective-permute-start.4
  68.3 0.7 broadcast_multiply_fusion.refs_7_
  69.1 0.9 copy.38.refs_5_
  70.0 0.1 pad.11.clone
  70.0 0.0 collective-permute-done.5
  70.1 3.5 %collective-permute-start.8 = (bf16[520,1024]{1,0:T(8,128)(2,1)}, bf16[520,1024]{1,0:T(8,128)(2,1)S(1)}, u32[]{:S(2)}, u32[]{:S(2)}) collective-permute-start(bf16[520,1024]{1,0:T(8,128)(2,1)} %collective-permute-done.5), channel_id=1, source_target_pairs={{4,8},{8,12},{20,24},{24,28},{36,40},{40,44},{52,56},{56,60},{68,7... | collective-permute-start | bytes 3194888 | tf_op jit(solution)/shard_map/ppermute | solution.py:132
  73.6 15.7 %collective-permute-done.6 = bf16[520,1024]{1,0:T(8,128)(2,1)} collective-permute-done((bf16[520,1024]{1,0:T(8,128)(2,1)}, bf16[520,1024]{1,0:T(8,128)(2,1)}, u32[]{:S(2)}, u32[]{:S(2)}) %collective-permute-start.6) | collective-permute-done | bytes 1064992 | tf_op jit(solution)/shard_map/ppermute | solution.py:132
  89.3 2.3 %collective-permute-start.7 = (bf16[520,1024]{1,0:T(8,128)(2,1)}, bf16[520,1024]{1,0:T(8,128)(2,1)S(1)}, u32[]{:S(2)}, u32[]{:S(2)}) collective-permute-start(bf16[520,1024]{1,0:T(8,128)(2,1)} %collective-permute-done.6), channel_id=1, source_target_pairs={{4,0},{8,4},{20,16},{24,20},{36,32},{40,36},{52,48},{56,52},{68,64... | collective-permute-start | bytes 3194888 | tf_op jit(solution)/shard_map/ppermute | solution.py:132
  91.6 0.1 slice_reduce_fusion
  91.8 2.5 %fusion.22 = (bf16[512,512]{1,0:T(8,128)(2,1)}, bf16[512,512]{1,0:T(8,128)(2,1)}, bf16[512,512]{1,0:T(8,128)(2,1)}) fusion(bf16[512,1536]{1,0:T(8,128)(2,1)} %copy-done.2), kind=kLoop, calls=%fused_computation.60 | loop fusion | bytes 3145728 | tf_op jit(solution)/shard_map/slice | solution.py:177
  94.3 0.7 slice.69
  95.0 1.3 broadcast_select_fusion.refs_3_
  96.4 1.7 broadcast_select_fusion.2.refs_1_
  98.1 0.0 collective-permute-done.8
  98.1 16.8 %collective-permute-done.7 = bf16[520,1024]{1,0:T(8,128)(2,1)S(1)} collective-permute-done((bf16[520,1024]{1,0:T(8,128)(2,1)}, bf16[520,1024]{1,0:T(8,128)(2,1)S(1)}, u32[]{:S(2)}, u32[]{:S(2)}) %collective-permute-start.7) | collective-permute-done | bytes 1064992 | tf_op jit(solution)/shard_map/ppermute | solution.py:132
  114.9 0.1 broadcast_select_fusion.1.refs_2_
  115.1 0.1 convert_select_fusion
  115.1 0.9 copy-done.6
  116.0 0.1 convert_select_fusion.1
  116.1 0.1 pad_add_fusion
  116.2 0.1 copy.36
  116.3 0.1 copy.37
  116.4 0.1 compare_convert_fusion
  116.5 0.6 reshape.122.flags_ref
  117.1 0.7 add_add_fusion.refs_6_
  117.7 42.6 %shard_map.85 = bf16[512,512]{1,0:T(8,128)(2,1)} custom-call(s32[20]{0:T(128)} %reshape.122.flags_ref, bf16[512,512]{1,0:T(8,128)(2,1)} %get-tuple-element.17.q_ref, bf16[520,1024]{1,0:T(8,128)(2,1)} %copy-done.7, bf16[520,1024]{1,0:T(8,128)(2,1)} %copy-done.5, bf16[520,1024]{1,0:T(8,128)(2,1)} %copy-done.6, bf16[520,1024]{1,0:T(8,128)(2,1)} %copy-done.4, ...), custom_call_target="tpu_custom_call" | custom-call | flops 2684354560 | bytes 6291456 | tf_op jit(solution)/shard_map/pallas_call | solution.py:112
  160.4 1.1 dynamic-slice_bitcast_fusion.5
  161.5 0.7 convolution_convert_fusion
  162.3 0.1 collective-permute-start.10
  162.4 0.7 convolution_convert_fusion.1
  163.1 1.9 %collective-permute-done.10 = bf16[2,128,2048]{2,1,0:T(8,128)(2,1)S(1)} collective-permute-done((bf16[2,128,2048]{2,1,0:T(8,128)(2,1)S(1)}, bf16[2,128,2048]{2,1,0:T(8,128)(2,1)S(1)}, u32[]{:S(2)}, u32[]{:S(2)}) %collective-permute-start.10) | collective-permute-done | bytes 1048608 | tf_op jit(solution)/shard_map/ppermute | solution.py:24
  165.0 0.4 convert_add_fusion
  165.4 0.1 fusion.13
  165.5 2.8 %collective-permute-start.11 = (bf16[128,2048]{1,0:T(8,128)(2,1)S(1)}, bf16[128,2048]{1,0:T(8,128)(2,1)S(1)}, u32[]{:S(2)}, u32[]{:S(2)}) collective-permute-start(bf16[128,2048]{1,0:T(8,128)(2,1)S(1)} %fusion.13), channel_id=1, source_target_pairs={{0,2},{1,3},{2,0},{3,1},{4,6},{5,7},{6,4},{7,5},{8,10},{9,11},{10,... | collective-permute-start | bytes 1572872 | tf_op jit(solution)/shard_map/ppermute | solution.py:24
  168.2 12.8 %collective-permute-done.11 = bf16[128,2048]{1,0:T(8,128)(2,1)S(1)} collective-permute-done((bf16[128,2048]{1,0:T(8,128)(2,1)S(1)}, bf16[128,2048]{1,0:T(8,128)(2,1)S(1)}, u32[]{:S(2)}, u32[]{:S(2)}) %collective-permute-start.11) | collective-permute-done | bytes 524320 | tf_op jit(solution)/shard_map/ppermute | solution.py:24
  181.0 1.0 fusion.12
  (32 shorter events, 0.1 us)
Async XLA Ops:
  0.6 160.9 %copy-start = (bf16[512,2048]{1,0:T(8,128)(2,1)S(1)}, bf16[512,2048]{1,0:T(8,128)(2,1)}, u32[]{:S(2)}) copy-start(bf16[512,2048]{1,0:T(8,128)(2,1)} %param.12) | copy-start | bytes 6291460
  4.8 17.0 %collective-permute-start.1 = (bf16[128,2048]{1,0:T(8,128)(2,1)S(1)}, bf16[128,2048]{1,0:T(8,128)(2,1)S(1)}, u32[]{:S(2)}, u32[]{:S(2)}) collective-permute-start(bf16[128,2048]{1,0:T(8,128)(2,1)S(1)} %fusion.10), channel_id=1, source_target_pairs={{0,2},{1,3},{2,0},{3,1},{4,6},{5,7},{6,4},{7,5},{8,10},{9,11},{10,... | collective-permute-start | bytes 1572872 | tf_op jit(solution)/shard_map/ppermute | solution.py:24
  7.9 19.8 %collective-permute-start = (bf16[128,2048]{1,0:T(8,128)(2,1)S(1)}, bf16[128,2048]{1,0:T(8,128)(2,1)}, u32[]{:S(2)}, u32[]{:S(2)}) collective-permute-start(bf16[128,2048]{1,0:T(8,128)(2,1)S(1)} %fusion.10), channel_id=1, source_target_pairs={{0,1},{1,0},{2,3},{3,2},{4,5},{5,4},{6,7},{7,6},{8,9},{9,8},{10,11... | collective-permute-start | bytes 1572872 | tf_op jit(solution)/shard_map/ppermute | solution.py:24
  16.7 5.0 %copy-start.8 = (s32[512]{0:T(512)S(1)}, s32[512]{0:T(512)}, u32[]{:S(2)}) copy-start(s32[512]{0:T(512)} %param.13) | copy-start | bytes 6148
  21.8 5.9 %copy-start.1 = (bf16[2048,3,512]{0,2,1:T(8,128)(2,1)S(1)}, bf16[2048,3,512]{0,2,1:T(8,128)(2,1)}, u32[]{:S(2)}) copy-start(bf16[2048,3,512]{0,2,1:T(8,128)(2,1)} %copy.30) | copy-start | bytes 18874372
  21.8 9.2 %collective-permute-start.2 = (bf16[128,2048]{1,0:T(8,128)(2,1)S(1)}, bf16[128,2048]{1,0:T(8,128)(2,1)S(1)}, u32[]{:S(2)}, u32[]{:S(2)}) collective-permute-start(bf16[128,2048]{1,0:T(8,128)(2,1)S(1)} %collective-permute-done.1), channel_id=1, source_target_pairs={{0,1},{1,0},{2,3},{3,2},{4,5},{5,4},{6,7},{7,6},{8,9},{9,8},{10,11... | collective-permute-start | bytes 1572872 | tf_op jit(solution)/shard_map/ppermute | solution.py:24
  33.6 1.2 copy-start.2
  33.6 34.7 %copy-start.9 = (f32[4]{0:T(128)S(1)}, f32[4]{0:T(128)}, u32[]{:S(2)}) copy-start(f32[4]{0:T(128)} %param.11) | copy-start | bytes 52
  34.8 60.2 %copy-start.7 = (bf16[520,1024]{1,0:T(8,128)(2,1)}, bf16[520,1024]{1,0:T(8,128)(2,1)S(1)}, u32[]{:S(2)}) copy-start(bf16[520,1024]{1,0:T(8,128)(2,1)S(1)} %fusion.7.refs_0_) | copy-start | bytes 3194884
  34.8 27.8 %collective-permute-start.3 = (bf16[520,1024]{1,0:T(8,128)(2,1)S(1)}, bf16[520,1024]{1,0:T(8,128)(2,1)}, u32[]{:S(2)}, u32[]{:S(2)}) collective-permute-start(bf16[520,1024]{1,0:T(8,128)(2,1)S(1)} %fusion.7.refs_0_), channel_id=1, source_target_pairs={{0,16},{4,20},{8,24},{12,28},{16,32},{20,36},{24,40},{28,44},{32,4... | collective-permute-start | bytes 3194888 | tf_op jit(solution)/shard_map/ppermute | solution.py:132
  39.8 30.2 %collective-permute-start.5 = (bf16[520,1024]{1,0:T(8,128)(2,1)S(1)}, bf16[520,1024]{1,0:T(8,128)(2,1)}, u32[]{:S(2)}, u32[]{:S(2)}) collective-permute-start(bf16[520,1024]{1,0:T(8,128)(2,1)S(1)} %fusion.7.refs_0_), channel_id=1, source_target_pairs={{0,4},{4,8},{8,12},{16,20},{20,24},{24,28},{32,36},{36,40},{40,44}... | collective-permute-start | bytes 3194888 | tf_op jit(solution)/shard_map/ppermute | solution.py:132
  62.6 26.7 %collective-permute-start.6 = (bf16[520,1024]{1,0:T(8,128)(2,1)}, bf16[520,1024]{1,0:T(8,128)(2,1)}, u32[]{:S(2)}, u32[]{:S(2)}) collective-permute-start(bf16[520,1024]{1,0:T(8,128)(2,1)} %collective-permute-done.3.refs_4_), channel_id=1, source_target_pairs={{4,0},{8,4},{12,8},{20,16},{24,20},{28,24},{36,32},{40,36},{44,40}... | collective-permute-start | bytes 3194888 | tf_op jit(solution)/shard_map/ppermute | solution.py:132
  65.1 29.9 %collective-permute-start.9 = (bf16[520,1024]{1,0:T(8,128)(2,1)S(1)}, bf16[520,1024]{1,0:T(8,128)(2,1)}, u32[]{:S(2)}, u32[]{:S(2)}) collective-permute-start(bf16[520,1024]{1,0:T(8,128)(2,1)S(1)} %fusion.7.refs_0_), channel_id=1, source_target_pairs={{0,12},{16,28},{32,44},{48,60},{64,76},{80,92},{96,108},{112,124},... | collective-permute-start | bytes 3194888 | tf_op jit(solution)/shard_map/ppermute | solution.py:132
  66.7 29.7 %collective-permute-start.4 = (bf16[520,1024]{1,0:T(8,128)(2,1)}, bf16[520,1024]{1,0:T(8,128)(2,1)}, u32[]{:S(2)}, u32[]{:S(2)}) collective-permute-start(bf16[520,1024]{1,0:T(8,128)(2,1)} %collective-permute-done.3.refs_4_), channel_id=1, source_target_pairs={{12,0},{28,16},{44,32},{60,48},{76,64},{92,80},{108,96},{124,112},... | collective-permute-start | bytes 3194888 | tf_op jit(solution)/shard_map/ppermute | solution.py:132
  70.1 28.1 %collective-permute-start.8 = (bf16[520,1024]{1,0:T(8,128)(2,1)}, bf16[520,1024]{1,0:T(8,128)(2,1)S(1)}, u32[]{:S(2)}, u32[]{:S(2)}) collective-permute-start(bf16[520,1024]{1,0:T(8,128)(2,1)} %collective-permute-done.5), channel_id=1, source_target_pairs={{4,8},{8,12},{20,24},{24,28},{36,40},{40,44},{52,56},{56,60},{68,7... | collective-permute-start | bytes 3194888 | tf_op jit(solution)/shard_map/ppermute | solution.py:132
  89.3 25.6 %collective-permute-start.7 = (bf16[520,1024]{1,0:T(8,128)(2,1)}, bf16[520,1024]{1,0:T(8,128)(2,1)S(1)}, u32[]{:S(2)}, u32[]{:S(2)}) collective-permute-start(bf16[520,1024]{1,0:T(8,128)(2,1)} %collective-permute-done.6), channel_id=1, source_target_pairs={{4,0},{8,4},{20,16},{24,20},{36,32},{40,36},{52,48},{56,52},{68,64... | collective-permute-start | bytes 3194888 | tf_op jit(solution)/shard_map/ppermute | solution.py:132
  96.4 18.7 %copy-start.4 = (bf16[520,1024]{1,0:T(8,128)(2,1)}, bf16[520,1024]{1,0:T(8,128)(2,1)S(1)}, u32[]{:S(2)}) copy-start(bf16[520,1024]{1,0:T(8,128)(2,1)S(1)} %broadcast_select_fusion.refs_3_) | copy-start | bytes 3194884
  98.1 16.9 %copy-start.5 = (bf16[520,1024]{1,0:T(8,128)(2,1)}, bf16[520,1024]{1,0:T(8,128)(2,1)S(1)}, u32[]{:S(2)}) copy-start(bf16[520,1024]{1,0:T(8,128)(2,1)S(1)} %broadcast_select_fusion.2.refs_1_) | copy-start | bytes 3194884
  115.0 1.0 copy-start.6
  162.3 2.7 %collective-permute-start.10 = (bf16[2,128,2048]{2,1,0:T(8,128)(2,1)S(1)}, bf16[2,128,2048]{2,1,0:T(8,128)(2,1)S(1)}, u32[]{:S(2)}, u32[]{:S(2)}) collective-permute-start(bf16[2,128,2048]{2,1,0:T(8,128)(2,1)S(1)} %bitcast.57), channel_id=1, source_target_pairs={{0,1},{1,0},{2,3},{3,2},{4,5},{5,4},{6,7},{7,6},{8,9},{9,8},{10,11... | collective-permute-start | bytes 3145736 | tf_op jit(solution)/shard_map/ppermute | solution.py:24
  165.0 16.0 %copy-start.3 = (bf16[128,2048]{1,0:T(8,128)(2,1)S(1)}, bf16[128,2048]{1,0:T(8,128)(2,1)}, u32[]{:S(2)}) copy-start(bf16[128,2048]{1,0:T(8,128)(2,1)} %param.8) | copy-start | bytes 1572868
  165.5 15.6 %collective-permute-start.11 = (bf16[128,2048]{1,0:T(8,128)(2,1)S(1)}, bf16[128,2048]{1,0:T(8,128)(2,1)S(1)}, u32[]{:S(2)}, u32[]{:S(2)}) collective-permute-start(bf16[128,2048]{1,0:T(8,128)(2,1)S(1)} %fusion.13), channel_id=1, source_target_pairs={{0,2},{1,3},{2,0},{3,1},{4,6},{5,7},{6,4},{7,5},{8,10},{9,11},{10,... | collective-permute-start | bytes 1572872 | tf_op jit(solution)/shard_map/ppermute | solution.py:24

commit v7 on v5

--- a/solution.py
+++ b/solution.py
@@ -169,17 +169,10 @@
     passed_down = moved(from_z, [(s, s - 1) for s in ids if s % RING > 0])
     passed_wrap = moved(from_z, [(s, s - RING + 1) for s in ids if s % RING == RING - 1])
     passed_twice = moved(passed_down, [(s, s - 1) for s in ids if 0 < s % RING < RING - 1])
-    seq_index = lax.axis_index("seq")
-    rounds = [
-        [(from_z, 4, seq_index >= 4), (from_below, 1, y >= 1), (from_wrap, 3, y == 3)],
-        [
-            (passed_up, 2, y >= 2),
-            (passed_down, 3, (y <= 2) & (seq_index >= 3)),
-            (passed_wrap, 1, (y == 0) & (seq_index >= 1)),
-        ],
-        [(passed_twice, 2, (y <= 1) & (seq_index >= 2))],
-    ]
-    return rounds
+    back1 = jnp.where(y == 0, passed_wrap, from_below)
+    back2 = jnp.where(y <= 1, passed_twice, passed_up)
+    back3 = jnp.where(y <= 2, passed_down, from_wrap)
+    return [back1, back2, back3, from_z]
 
 
 def on_device(tokens, ln_gain, w_qkv, slopes, w_out, seg_ids):
@@ -189,17 +182,22 @@
     head = lax.axis_index("head")
     n_head = lax.axis_size("head")
 
-    cross = swapped(normed, "head", 2)
-    partner = swapped(jnp.stack([normed, cross]), "head", 1)
-    pieces = jnp.stack([normed, partner[0], cross, partner[1]])
-    block_rows = jnp.concatenate(
-        [lax.dynamic_index_in_dim(pieces, j ^ head, 0, keepdims=False) for j in range(n_head)], axis=0
-    )
-
     width_local = w_qkv.shape[2]
     heads_dev = slopes.shape[0]
     joined = w_qkv.reshape(w_qkv.shape[0], 3 * width_local)
-    qkv_rows = jnp.dot(block_rows, joined, preferred_element_type=jnp.float32).astype(jnp.bfloat16)
+
+    def project_rows(rows):
+        return jnp.dot(rows, joined, preferred_element_type=jnp.float32).astype(jnp.bfloat16)
+
+    from_partner = swapped(normed, "head", 1)
+    from_cross = swapped(normed, "head", 2)
+    from_partner_cross = swapped(from_cross, "head", 1)
+    pieces = jnp.stack(
+        [project_rows(r) for r in (normed, from_partner, from_cross, from_partner_cross)]
+    )
+    qkv_rows = jnp.concatenate(
+        [lax.dynamic_index_in_dim(pieces, j ^ head, 0, keepdims=False) for j in range(n_head)], axis=0
+    )
     block_len = qkv_rows.shape[0]
     key_cache = qkv_rows[:, width_local : 2 * width_local]
     value_cache = qkv_rows[:, 2 * width_local :]
@@ -209,7 +207,7 @@
         seg_ids.astype(jnp.bfloat16)
     )
     payload = jnp.concatenate([kv_own, seg_row], axis=0)
-    rounds = relay_earlier_blocks(payload)
+    arrived = relay_earlier_blocks(payload)
 
     queries = qkv_rows[:, :width_local]
     state = (
@@ -217,13 +215,21 @@
         jnp.zeros((block_len, HD), jnp.float32),
         jnp.zeros((block_len, width_local), jnp.float32),
     )
+    back1, back2, back3, from_z = arrived
+    seq_index_now = lax.axis_index("seq")
     state = attention_part(
-        state, queries, seg_ids, slopes, [payload], [jnp.int32(0)], [jnp.bool_(True)], own=True
-    )
-    for arrived in rounds:
-        bufs, steps_back, present = zip(*arrived)
-        steps_back = [jnp.int32(k) for k in steps_back]
-        state = attention_part(state, queries, seg_ids, slopes, list(bufs), steps_back, list(present))
+        state,
+        queries,
+        seg_ids,
+        slopes,
+        [payload, from_z, back1, back3],
+        [jnp.int32(0), jnp.int32(4), jnp.int32(1), jnp.int32(3)],
+        [jnp.bool_(True), seq_index_now >= 4, seq_index_now >= 1, seq_index_now >= 3],
+        own=True,
+    )
+    state = attention_part(
+        state, queries, seg_ids, slopes, [back2], [jnp.int32(2)], [seq_index_now >= 2]
+    )
     _, total, acc = state
     denominator = jnp.repeat(total[:, :heads_dev], HD, axis=1)
     context = (acc / denominator).astype(jnp.bfloat16)

time: 196 us -> 176 us (0.90)
  the two profiles are of different devices: /device:TPU:86 before, /device:TPU:48 now
where the time goes in v7:
time: 176 us
  Pallas kernels  48.6 us (28%)
  waiting for transfers between devices  45.7 us (26%)
  starting transfers between devices  27 us (15%)
  local copies, waits for them, and re-layouts  23.2 us (13%)
  matrix products  17.2 us (10%)
  other arithmetic  13 us (7%)
    pallas_call x2, Pallas kernels, attention_part(): pl.pallas_call(functools.partial(part_kernel, n_buf, own), out_shape=(jax...  48.6 us
    ppermute x7, waiting for transfers between devices, moved(): return lax.ppermute(value, 'seq', pairs)  30.3 us
    ppermute x7, starting transfers between devices, moved(): return lax.ppermute(value, 'seq', pairs)  21.1 us
    dot_general x4, matrix products, project_rows(): jnp.dot(rows, joined, preferred_element_type=jnp.float32)  15.7 us
    ppermute x5, waiting for transfers between devices, swapped(): lax.ppermute(value, axis, [(source, source ^ mask) for source in range(co...  15.4 us
    unnamed x27, local copies, waits for them, and re-layouts  10.9 us
    ppermute x5, starting transfers between devices, swapped(): lax.ppermute(value, axis, [(source, source ^ mask) for source in range(co...  5.85 us
  transfers between devices with their start and end apart: 12, of which 4 were waited for; matrix products, arithmetic and copies ran while one was open for 21% of the time, Pallas kernels for 20%

profile of v7, /device:TPU:48, one launch (start us, length us, event | category | flops | bytes accessed | tf_op | source)
XLA Modules:
  0.0 175.7 jit_solution(4640190116056010890)
XLA Ops:
  0.6 1.3 convert_reduce_fusion
  2.0 1.3 fusion.8
  3.3 1.4 fusion.10
  4.8 3.1 %collective-permute-start.1 = (bf16[128,2048]{1,0:T(8,128)(2,1)S(1)}, bf16[128,2048]{1,0:T(8,128)(2,1)S(1)}, u32[]{:S(2)}, u32[]{:S(2)}) collective-permute-start(bf16[128,2048]{1,0:T(8,128)(2,1)S(1)} %fusion.10), channel_id=1, source_target_pairs={{0,2},{1,3},{2,0},{3,1},{4,6},{5,7},{6,4},{7,5},{8,10},{9,11},{10,... | collective-permute-start | bytes 1572872 | tf_op jit(solution)/shard_map/ppermute | solution.py:26
  7.9 8.9 %copy.18 = bf16[2048,3,512]{0,2,1:T(8,128)(2,1)} copy(bf16[2048,3,512]{2,0,1:T(8,128)(2,1)} %param.14) | data formatting | bytes 12582912 | tf_op args[2]
  16.7 5.0 %fusion = bf16[1,128,1536]{2,1,0:T(8,128)(2,1)S(1)} fusion(bf16[128,2048]{1,0:T(8,128)(2,1)S(1)} %fusion.10, bf16[2048,1536]{0,1:T(8,128)(2,1)} %bitcast.57), kind=kOutput, calls=%fused_computation.6 | convolution fusion | flops 805502976 | bytes 7208960 | tf_op jit(solution)/shard_map/dot_general | solution.py:190
  21.8 0.6 collective-permute-start.2
  22.4 5.2 %fusion.2 = bf16[1,128,1536]{2,1,0:T(8,128)(2,1)S(1)} fusion(bf16[128,2048]{1,0:T(8,128)(2,1)S(1)} %collective-permute-done.1, bf16[2048,1536]{0,1:T(8,128)(2,1)} %bitcast.58), kind=kOutput, calls=%fused_computation.8 | convolution fusion | flops 805502976 | bytes 7208960 | tf_op jit(solution)/shard_map/dot_general | solution.py:190
  27.7 3.3 %fusion.1 = bf16[1,128,1536]{2,1,0:T(8,128)(2,1)S(1)} fusion(bf16[128,2048]{1,0:T(8,128)(2,1)} %collective-permute-done, bf16[2048,1536]{0,1:T(8,128)(2,1)S(1)} %bitcast.59), kind=kOutput, calls=%fused_computation.7 | convolution fusion | flops 805502976 | bytes 7208960 | tf_op jit(solution)/shard_map/dot_general | solution.py:190
  31.0 2.2 %fusion.3 = bf16[1,128,1536]{2,1,0:T(8,128)(2,1)S(1)} fusion(bf16[128,2048]{1,0:T(8,128)(2,1)S(1)} %collective-permute-done.2, bf16[2048,1536]{0,1:T(8,128)(2,1)S(1)} %bitcast.60), kind=kOutput, calls=%fused_computation.9 | convolution fusion | flops 805502976 | bytes 7208960 | tf_op jit(solution)/shard_map/dot_general | solution.py:190
  33.2 0.2 pad_maximum_fusion
  33.4 0.1 dynamic-slice_bitcast_fusion.3
  33.5 0.1 pad_maximum_fusion.1
  33.6 0.1 slice.120
  33.8 0.1 fusion.7.refs_0_
  33.9 0.9 copy-done.2
  34.8 3.9 %collective-permute-start.3 = (bf16[520,1024]{1,0:T(8,128)(2,1)S(1)}, bf16[520,1024]{1,0:T(8,128)(2,1)}, u32[]{:S(2)}, u32[]{:S(2)}) collective-permute-start(bf16[520,1024]{1,0:T(8,128)(2,1)S(1)} %fusion.7.refs_0_), channel_id=1, source_target_pairs={{0,16},{4,20},{8,24},{12,28},{16,32},{20,36},{24,40},{28,44},{32,4... | collective-permute-start | bytes 3194888 | tf_op jit(solution)/shard_map/ppermute | solution.py:158
  38.6 0.1 slice_reduce_fusion
  38.8 3.2 %collective-permute-start.6 = (bf16[520,1024]{1,0:T(8,128)(2,1)S(1)}, bf16[520,1024]{1,0:T(8,128)(2,1)}, u32[]{:S(2)}, u32[]{:S(2)}) collective-permute-start(bf16[520,1024]{1,0:T(8,128)(2,1)S(1)} %fusion.7.refs_0_), channel_id=1, source_target_pairs={{0,4},{4,8},{8,12},{16,20},{20,24},{24,28},{32,36},{36,40},{40,44}... | collective-permute-start | bytes 3194888 | tf_op jit(solution)/shard_map/ppermute | solution.py:158
  42.0 1.7 collective-permute-start.9
  43.8 18.3 %collective-permute-done.3.refs_1_ = bf16[520,1024]{1,0:T(8,128)(2,1)} collective-permute-done((bf16[520,1024]{1,0:T(8,128)(2,1)S(1)}, bf16[520,1024]{1,0:T(8,128)(2,1)}, u32[]{:S(2)}, u32[]{:S(2)}) %collective-permute-start.3) | collective-permute-done | bytes 1064992 | tf_op jit(solution)/shard_map/ppermute | solution.py:158
  62.1 2.4 %collective-permute-start.4 = (bf16[520,1024]{1,0:T(8,128)(2,1)}, bf16[520,1024]{1,0:T(8,128)(2,1)}, u32[]{:S(2)}, u32[]{:S(2)}) collective-permute-start(bf16[520,1024]{1,0:T(8,128)(2,1)} %collective-permute-done.3.refs_1_), channel_id=1, source_target_pairs={{4,0},{8,4},{12,8},{20,16},{24,20},{28,24},{36,32},{40,36},{44,40}... | collective-permute-start | bytes 3194888 | tf_op jit(solution)/shard_map/ppermute | solution.py:158
  64.5 1.6 collective-permute-start.8
  66.1 0.9 copy.23.refs_4_.refs_1_
  67.0 0.1 mul.66
  67.1 0.6 concatenate.30.refs_3_
  67.7 0.7 broadcast_multiply_fusion.refs_6_
  68.4 2.5 %fusion.24 = (bf16[512,512]{1,0:T(8,128)(2,1)}, bf16[512,512]{1,0:T(8,128)(2,1)}, bf16[512,512]{1,0:T(8,128)(2,1)}) fusion(bf16[512,1536]{1,0:T(8,128)(2,1)} %copy-done.2), kind=kLoop, calls=%fused_computation.71 | loop fusion | bytes 3145728 | tf_op jit(solution)/shard_map/slice | solution.py:203
  70.9 5.0 %collective-permute-start.7 = (bf16[520,1024]{1,0:T(8,128)(2,1)}, bf16[520,1024]{1,0:T(8,128)(2,1)}, u32[]{:S(2)}, u32[]{:S(2)}) collective-permute-start(bf16[520,1024]{1,0:T(8,128)(2,1)} %collective-permute-done.6), channel_id=1, source_target_pairs={{4,8},{8,12},{20,24},{24,28},{36,40},{40,44},{52,56},{56,60},{68,7... | collective-permute-start | bytes 3194888 | tf_op jit(solution)/shard_map/ppermute | solution.py:158
  76.0 0.7 broadcast_select_fusion.5
  76.7 12.0 %collective-permute-done.4 = bf16[520,1024]{1,0:T(8,128)(2,1)} collective-permute-done((bf16[520,1024]{1,0:T(8,128)(2,1)}, bf16[520,1024]{1,0:T(8,128)(2,1)}, u32[]{:S(2)}, u32[]{:S(2)}) %collective-permute-start.4) | collective-permute-done | bytes 1064992 | tf_op jit(solution)/shard_map/ppermute | solution.py:158
  88.7 3.4 %collective-permute-start.5 = (bf16[520,1024]{1,0:T(8,128)(2,1)}, bf16[520,1024]{1,0:T(8,128)(2,1)}, u32[]{:S(2)}, u32[]{:S(2)}) collective-permute-start(bf16[520,1024]{1,0:T(8,128)(2,1)} %collective-permute-done.4), channel_id=1, source_target_pairs={{4,0},{8,4},{20,16},{24,20},{36,32},{40,36},{52,48},{56,52},{68,64... | collective-permute-start | bytes 3194888 | tf_op jit(solution)/shard_map/ppermute | solution.py:158
  92.1 1.3 broadcast_select_fusion.refs_3_
  93.4 1.7 broadcast_select_fusion.1.refs_2_
  95.2 0.9 copy-done.6
  96.2 0.1 slice.128
  96.3 0.1 copy.25
  96.4 0.1 copy.21
  96.5 0.1 broadcast_compare_fusion
  96.7 0.6 reshape.251.flags_ref
  97.3 0.6 concatenate.31.refs_5_
  97.9 0.7 broadcast_in_dim.17.refs_7_
  98.6 0.7 broadcast_in_dim.18.refs_8_
  99.3 1.1 broadcast_in_dim.19.refs_9_
  100.4 34.8 %shard_map.85 = (f32[512,128]{1,0:T(8,128)}, f32[512,128]{1,0:T(8,128)}, f32[512,512]{1,0:T(8,128)}) custom-call(s32[16]{0:T(128)} %reshape.251.flags_ref, bf16[512,512]{1,0:T(8,128)(2,1)} %get-tuple-element.53.q_ref, bf16[520,1024]{1,0:T(8,128)(2,1)} %copy-done.7, bf16[520,1024]{1,0:T(8,128)(2,1)} %collective-permute-done.3.refs_1_, ...), custom_call_target="tpu_custom_call" | custom-call | flops 2147483648 | bytes 8388608 | tf_op jit(solution)/shard_map/pallas_call | solution.py:134
  135.2 1.4 broadcast_select_fusion.2.refs_0_
  136.6 0.6 broadcast.176
  137.2 0.7 fusion.23
  138.0 0.1 slice.122
  138.0 0.1 copy.24
  138.1 0.1 compare_convert_fusion
  138.2 0.6 reshape.249.flags_ref
  138.8 0.6 concatenate.29.refs_2_
  139.4 13.8 %shard_map.86 = (f32[512,128]{1,0:T(8,128)}, f32[512,128]{1,0:T(8,128)}, f32[512,512]{1,0:T(8,128)}) custom-call(s32[4]{0:T(128)} %reshape.249.flags_ref, bf16[512,512]{1,0:T(8,128)(2,1)} %get-tuple-element.53.q_ref, bf16[520,1024]{1,0:T(8,128)(2,1)} %copy-done.4, s32[512,1]{1,0:T(8,128)} %copy.23.refs_4_.refs_1_, s32[8,512]{1,0:T(8,128)} %concatenate.29.refs_2_, ...), custom_call_target="tpu_custom_call" | custom-call | flops 536870912 | bytes 5242880 | tf_op jit(solution)/shard_map/pallas_call | solution.py:134
  153.2 1.6 broadcast_in_dim.20
  154.9 0.3 fusion.13
  155.2 0.7 convolution_convert_fusion
  156.0 0.1 collective-permute-start.10
  156.1 0.7 convolution_convert_fusion.1
  156.8 1.9 %collective-permute-done.10 = bf16[2,128,2048]{2,1,0:T(8,128)(2,1)S(1)} collective-permute-done((bf16[2,128,2048]{2,1,0:T(8,128)(2,1)S(1)}, bf16[2,128,2048]{2,1,0:T(8,128)(2,1)S(1)}, u32[]{:S(2)}, u32[]{:S(2)}) %collective-permute-start.10) | collective-permute-done | bytes 1048608 | tf_op jit(solution)/shard_map/ppermute | solution.py:26
  158.7 0.4 convert_add_fusion
  159.1 2.1 %collective-permute-start.11 = (bf16[128,2048]{1,0:T(8,128)(2,1)S(1)}, bf16[128,2048]{1,0:T(8,128)(2,1)S(1)}, u32[]{:S(2)}, u32[]{:S(2)}) collective-permute-start(bf16[128,2048]{1,0:T(8,128)(2,1)S(1)} %fusion.14), channel_id=1, source_target_pairs={{0,2},{1,3},{2,0},{3,1},{4,6},{5,7},{6,4},{7,5},{8,10},{9,11},{10,... | collective-permute-start | bytes 1572872 | tf_op jit(solution)/shard_map/ppermute | solution.py:26
  161.2 13.5 %collective-permute-done.11 = bf16[128,2048]{1,0:T(8,128)(2,1)S(1)} collective-permute-done((bf16[128,2048]{1,0:T(8,128)(2,1)S(1)}, bf16[128,2048]{1,0:T(8,128)(2,1)S(1)}, u32[]{:S(2)}, u32[]{:S(2)}) %collective-permute-start.11) | collective-permute-done | bytes 524320 | tf_op jit(solution)/shard_map/ppermute | solution.py:26
  174.7 1.0 fusion.12
  (54 shorter events, 0.6 us)
Async XLA Ops:
  0.6 154.6 %copy-start = (bf16[512,2048]{1,0:T(8,128)(2,1)S(1)}, bf16[512,2048]{1,0:T(8,128)(2,1)}, u32[]{:S(2)}) copy-start(bf16[512,2048]{1,0:T(8,128)(2,1)} %param.16) | copy-start | bytes 6291460
  4.8 17.1 %collective-permute-start.1 = (bf16[128,2048]{1,0:T(8,128)(2,1)S(1)}, bf16[128,2048]{1,0:T(8,128)(2,1)S(1)}, u32[]{:S(2)}, u32[]{:S(2)}) collective-permute-start(bf16[128,2048]{1,0:T(8,128)(2,1)S(1)} %fusion.10), channel_id=1, source_target_pairs={{0,2},{1,3},{2,0},{3,1},{4,6},{5,7},{6,4},{7,5},{8,10},{9,11},{10,... | collective-permute-start | bytes 1572872 | tf_op jit(solution)/shard_map/ppermute | solution.py:26
  7.9 19.8 %collective-permute-start = (bf16[128,2048]{1,0:T(8,128)(2,1)S(1)}, bf16[128,2048]{1,0:T(8,128)(2,1)}, u32[]{:S(2)}, u32[]{:S(2)}) collective-permute-start(bf16[128,2048]{1,0:T(8,128)(2,1)S(1)} %fusion.10), channel_id=1, source_target_pairs={{0,1},{1,0},{2,3},{3,2},{4,5},{5,4},{6,7},{7,6},{8,9},{9,8},{10,11... | collective-permute-start | bytes 1572872 | tf_op jit(solution)/shard_map/ppermute | solution.py:26
  16.7 5.0 %copy-start.9 = (s32[512]{0:T(512)S(1)}, s32[512]{0:T(512)}, u32[]{:S(2)}) copy-start(s32[512]{0:T(512)} %param.17) | copy-start | bytes 6148
  21.8 5.9 %copy-start.1 = (bf16[2048,3,512]{0,2,1:T(8,128)(2,1)S(1)}, bf16[2048,3,512]{0,2,1:T(8,128)(2,1)}, u32[]{:S(2)}) copy-start(bf16[2048,3,512]{0,2,1:T(8,128)(2,1)} %copy.18) | copy-start | bytes 18874372
  21.8 9.1 %collective-permute-start.2 = (bf16[128,2048]{1,0:T(8,128)(2,1)S(1)}, bf16[128,2048]{1,0:T(8,128)(2,1)S(1)}, u32[]{:S(2)}, u32[]{:S(2)}) collective-permute-start(bf16[128,2048]{1,0:T(8,128)(2,1)S(1)} %collective-permute-done.1), channel_id=1, source_target_pairs={{0,1},{1,0},{2,3},{3,2},{4,5},{5,4},{6,7},{7,6},{8,9},{9,8},{10,11... | collective-permute-start | bytes 1572872 | tf_op jit(solution)/shard_map/ppermute | solution.py:26
  33.6 1.1 copy-start.2
  33.8 8.2 %copy-start.10 = (f32[4]{0:T(128)S(1)}, f32[4]{0:T(128)}, u32[]{:S(2)}) copy-start(f32[4]{0:T(128)} %param.15) | copy-start | bytes 52
  33.8 30.7 %copy-start.11 = (s32[4]{0:T(128)S(1)}, s32[4]{0:T(128)}, u32[]{:S(2)}) copy-start(s32[4]{0:T(128)} %constant.150.clone.1) | copy-start | bytes 52
  34.8 36.2 %copy-start.7 = (bf16[520,1024]{1,0:T(8,128)(2,1)}, bf16[520,1024]{1,0:T(8,128)(2,1)S(1)}, u32[]{:S(2)}) copy-start(bf16[520,1024]{1,0:T(8,128)(2,1)S(1)} %fusion.7.refs_0_) | copy-start | bytes 3194884
  34.8 27.3 %collective-permute-start.3 = (bf16[520,1024]{1,0:T(8,128)(2,1)S(1)}, bf16[520,1024]{1,0:T(8,128)(2,1)}, u32[]{:S(2)}, u32[]{:S(2)}) collective-permute-start(bf16[520,1024]{1,0:T(8,128)(2,1)S(1)} %fusion.7.refs_0_), channel_id=1, source_target_pairs={{0,16},{4,20},{8,24},{12,28},{16,32},{20,36},{24,40},{28,44},{32,4... | collective-permute-start | bytes 3194888 | tf_op jit(solution)/shard_map/ppermute | solution.py:158
  38.8 32.2 %collective-permute-start.6 = (bf16[520,1024]{1,0:T(8,128)(2,1)S(1)}, bf16[520,1024]{1,0:T(8,128)(2,1)}, u32[]{:S(2)}, u32[]{:S(2)}) collective-permute-start(bf16[520,1024]{1,0:T(8,128)(2,1)S(1)} %fusion.7.refs_0_), channel_id=1, source_target_pairs={{0,4},{4,8},{8,12},{16,20},{20,24},{24,28},{32,36},{36,40},{40,44}... | collective-permute-start | bytes 3194888 | tf_op jit(solution)/shard_map/ppermute | solution.py:158
  42.0 50.0 %collective-permute-start.9 = (bf16[520,1024]{1,0:T(8,128)(2,1)S(1)}, bf16[520,1024]{1,0:T(8,128)(2,1)}, u32[]{:S(2)}, u32[]{:S(2)}) collective-permute-start(bf16[520,1024]{1,0:T(8,128)(2,1)S(1)} %fusion.7.refs_0_), channel_id=1, source_target_pairs={{0,12},{16,28},{32,44},{48,60},{64,76},{80,92},{96,108},{112,124},... | collective-permute-start | bytes 3194888 | tf_op jit(solution)/shard_map/ppermute | solution.py:158
  62.1 26.7 %collective-permute-start.4 = (bf16[520,1024]{1,0:T(8,128)(2,1)}, bf16[520,1024]{1,0:T(8,128)(2,1)}, u32[]{:S(2)}, u32[]{:S(2)}) collective-permute-start(bf16[520,1024]{1,0:T(8,128)(2,1)} %collective-permute-done.3.refs_1_), channel_id=1, source_target_pairs={{4,0},{8,4},{12,8},{20,16},{24,20},{28,24},{36,32},{40,36},{44,40}... | collective-permute-start | bytes 3194888 | tf_op jit(solution)/shard_map/ppermute | solution.py:158
  64.5 28.9 %collective-permute-start.8 = (bf16[520,1024]{1,0:T(8,128)(2,1)}, bf16[520,1024]{1,0:T(8,128)(2,1)}, u32[]{:S(2)}, u32[]{:S(2)}) collective-permute-start(bf16[520,1024]{1,0:T(8,128)(2,1)} %collective-permute-done.3.refs_1_), channel_id=1, source_target_pairs={{12,0},{28,16},{44,32},{60,48},{76,64},{92,80},{108,96},{124,112},... | collective-permute-start | bytes 3194888 | tf_op jit(solution)/shard_map/ppermute | solution.py:158
  70.9 64.3 %collective-permute-start.7 = (bf16[520,1024]{1,0:T(8,128)(2,1)}, bf16[520,1024]{1,0:T(8,128)(2,1)}, u32[]{:S(2)}, u32[]{:S(2)}) collective-permute-start(bf16[520,1024]{1,0:T(8,128)(2,1)} %collective-permute-done.6), channel_id=1, source_target_pairs={{4,8},{8,12},{20,24},{24,28},{36,40},{40,44},{52,56},{56,60},{68,7... | collective-permute-start | bytes 3194888 | tf_op jit(solution)/shard_map/ppermute | solution.py:158
  88.7 46.5 %collective-permute-start.5 = (bf16[520,1024]{1,0:T(8,128)(2,1)}, bf16[520,1024]{1,0:T(8,128)(2,1)}, u32[]{:S(2)}, u32[]{:S(2)}) collective-permute-start(bf16[520,1024]{1,0:T(8,128)(2,1)} %collective-permute-done.4), channel_id=1, source_target_pairs={{4,0},{8,4},{20,16},{24,20},{36,32},{40,36},{52,48},{56,52},{68,64... | collective-permute-start | bytes 3194888 | tf_op jit(solution)/shard_map/ppermute | solution.py:158
  93.4 1.8 copy-start.5
  95.2 1.0 copy-start.6
  136.6 2.8 %copy-start.4 = (bf16[520,1024]{1,0:T(8,128)(2,1)}, bf16[520,1024]{1,0:T(8,128)(2,1)S(1)}, u32[]{:S(2)}) copy-start(bf16[520,1024]{1,0:T(8,128)(2,1)S(1)} %broadcast_select_fusion.2.refs_0_) | copy-start | bytes 3194884
  153.2 1.6 copy-start.8
  156.0 2.7 %collective-permute-start.10 = (bf16[2,128,2048]{2,1,0:T(8,128)(2,1)S(1)}, bf16[2,128,2048]{2,1,0:T(8,128)(2,1)S(1)}, u32[]{:S(2)}, u32[]{:S(2)}) collective-permute-start(bf16[2,128,2048]{2,1,0:T(8,128)(2,1)S(1)} %bitcast.64), channel_id=1, source_target_pairs={{0,1},{1,0},{2,3},{3,2},{4,5},{5,4},{6,7},{7,6},{8,9},{9,8},{10,11... | collective-permute-start | bytes 3145736 | tf_op jit(solution)/shard_map/ppermute | solution.py:26
  158.7 16.0 %copy-start.3 = (bf16[128,2048]{1,0:T(8,128)(2,1)S(1)}, bf16[128,2048]{1,0:T(8,128)(2,1)}, u32[]{:S(2)}) copy-start(bf16[128,2048]{1,0:T(8,128)(2,1)} %param.12) | copy-start | bytes 1572868
  159.1 15.6 %collective-permute-start.11 = (bf16[128,2048]{1,0:T(8,128)(2,1)S(1)}, bf16[128,2048]{1,0:T(8,128)(2,1)S(1)}, u32[]{:S(2)}, u32[]{:S(2)}) collective-permute-start(bf16[128,2048]{1,0:T(8,128)(2,1)S(1)} %fusion.14), channel_id=1, source_target_pairs={{0,2},{1,3},{2,0},{3,1},{4,6},{5,7},{6,4},{7,5},{8,10},{9,11},{10,... | collective-permute-start | bytes 1572872 | tf_op jit(solution)/shard_map/ppermute | solution.py:26

commit v8 on v7

--- a/solution.py
+++ b/solution.py
@@ -192,9 +192,9 @@
     from_partner = swapped(normed, "head", 1)
     from_cross = swapped(normed, "head", 2)
     from_partner_cross = swapped(from_cross, "head", 1)
-    pieces = jnp.stack(
-        [project_rows(r) for r in (normed, from_partner, from_cross, from_partner_cross)]
-    )
+    near = project_rows(jnp.concatenate([normed, from_partner], axis=0))
+    far = project_rows(jnp.concatenate([from_cross, from_partner_cross], axis=0))
+    pieces = jnp.concatenate([near, far], axis=0).reshape(n_head, rows_dev, near.shape[1])
     qkv_rows = jnp.concatenate(
         [lax.dynamic_index_in_dim(pieces, j ^ head, 0, keepdims=False) for j in range(n_head)], axis=0
     )

time: 176 us -> 172 us (0.977)
  the two profiles are of different devices: /device:TPU:48 before, /device:TPU:80 now
where the time goes in v8:
time: 172 us; the launch traced here: 171 us
  waiting for transfers between devices  49.2 us (29%)
  Pallas kernels  48.6 us (28%)
  starting transfers between devices  27.4 us (16%)
  local copies, waits for them, and re-layouts  23 us (13%)
  other arithmetic  13.9 us (8%)
  matrix products  8.23 us (5%)
    pallas_call x2, Pallas kernels, attention_part(): pl.pallas_call(functools.partial(part_kernel, n_buf, own), out_shape=(jax...  48.6 us
    ppermute x7, waiting for transfers between devices, moved(): return lax.ppermute(value, 'seq', pairs)  31.7 us
    ppermute x7, starting transfers between devices, moved(): return lax.ppermute(value, 'seq', pairs)  21.1 us
    ppermute x5, waiting for transfers between devices, swapped(): lax.ppermute(value, axis, [(source, source ^ mask) for source in range(co...  17.6 us
    unnamed x25, local copies, waits for them, and re-layouts  11 us
    dot_general x2, matrix products, project_rows(): jnp.dot(rows, joined, preferred_element_type=jnp.float32)  6.75 us
    ppermute x5, starting transfers between devices, swapped(): lax.ppermute(value, axis, [(source, source ^ mask) for source in range(co...  6.31 us
  transfers between devices with their start and end apart: 12, of which 5 were waited for; matrix products, arithmetic and copies ran while one was open for 16% of the time, Pallas kernels for 20%

profile of v8, /device:TPU:80, one launch (start us, length us, event | category | flops | bytes accessed | tf_op | source)
XLA Modules:
  0.0 171.3 jit_solution(6909449648880625941)
XLA Ops:
  0.7 1.3 convert_reduce_fusion
  2.0 1.3 fusion.4
  3.3 1.4 fusion.6
  4.8 3.1 %collective-permute-start.1 = (bf16[128,2048]{1,0:T(8,128)(2,1)S(1)}, bf16[128,2048]{1,0:T(8,128)(2,1)S(1)}, u32[]{:S(2)}, u32[]{:S(2)}) collective-permute-start(bf16[128,2048]{1,0:T(8,128)(2,1)S(1)} %fusion.6), channel_id=1, source_target_pairs={{0,2},{1,3},{2,0},{3,1},{4,6},{5,7},{6,4},{7,5},{8,10},{9,11},{10,... | collective-permute-start | bytes 1572872 | tf_op jit(solution)/shard_map/ppermute | solution.py:26
  7.9 8.9 %copy.18 = bf16[2048,3,512]{0,2,1:T(8,128)(2,1)} copy(bf16[2048,3,512]{2,0,1:T(8,128)(2,1)} %param.14) | data formatting | bytes 12582912 | tf_op args[2]
  16.8 3.2 %collective-permute-done.1 = bf16[128,2048]{1,0:T(8,128)(2,1)S(1)} collective-permute-done((bf16[128,2048]{1,0:T(8,128)(2,1)S(1)}, bf16[128,2048]{1,0:T(8,128)(2,1)S(1)}, u32[]{:S(2)}, u32[]{:S(2)}) %collective-permute-start.1) | collective-permute-done | bytes 524320 | tf_op jit(solution)/shard_map/ppermute | solution.py:26
  20.0 4.9 %convolution_convert_fusion.3 = bf16[256,1536]{1,0:T(8,128)(2,1)S(1)} fusion(bf16[2048,1536]{0,1:T(8,128)(2,1)} %bitcast.44, bf16[128,2048]{1,0:T(8,128)(2,1)} %collective-permute-done, bf16[128,2048]{1,0:T(8,128)(2,1)S(1)} %fusion.6), kind=kOutput, calls=%fused_computation.3 | convolution fusion | flops 1613103104 | bytes 8126464 | tf_op jit(solution)/shard_map/dot_general | solution.py:190
  25.0 1.8 %convolution_convert_fusion.2 = bf16[256,1536]{1,0:T(8,128)(2,1)S(1)} fusion(bf16[2048,1536]{0,1:T(8,128)(2,1)S(1)} %bitcast.45, bf16[128,2048]{1,0:T(8,128)(2,1)S(1)} %collective-permute-done.2, bf16[128,2048]{1,0:T(8,128)(2,1)S(1)} %collective-permute-done.1), kind=kOutput, calls=%fused_computation.2 | convolution fusion | flops 1613103104 | bytes 8126464 | tf_op jit(solution)/shard_map/dot_general | solution.py:190
  26.8 0.1 pad_maximum_fusion
  26.9 0.1 dynamic-slice_bitcast_fusion.3
  27.1 0.1 pad_maximum_fusion.1
  27.2 0.1 slice.120
  27.3 0.1 fusion.3.refs_0_
  27.4 0.9 copy-done.1
  28.3 3.8 %collective-permute-start.3 = (bf16[520,1024]{1,0:T(8,128)(2,1)S(1)}, bf16[520,1024]{1,0:T(8,128)(2,1)}, u32[]{:S(2)}, u32[]{:S(2)}) collective-permute-start(bf16[520,1024]{1,0:T(8,128)(2,1)S(1)} %fusion.3.refs_0_), channel_id=1, source_target_pairs={{0,16},{4,20},{8,24},{12,28},{16,32},{20,36},{24,40},{28,44},{32,4... | collective-permute-start | bytes 3194888 | tf_op jit(solution)/shard_map/ppermute | solution.py:158
  32.2 0.1 slice_reduce_fusion
  32.3 3.2 %collective-permute-start.6 = (bf16[520,1024]{1,0:T(8,128)(2,1)S(1)}, bf16[520,1024]{1,0:T(8,128)(2,1)}, u32[]{:S(2)}, u32[]{:S(2)}) collective-permute-start(bf16[520,1024]{1,0:T(8,128)(2,1)S(1)} %fusion.3.refs_0_), channel_id=1, source_target_pairs={{0,4},{4,8},{8,12},{16,20},{20,24},{24,28},{32,36},{36,40},{40,44}... | collective-permute-start | bytes 3194888 | tf_op jit(solution)/shard_map/ppermute | solution.py:158
  35.5 0.1 broadcast_multiply_fusion.1
  35.5 1.7 %collective-permute-start.9 = (bf16[520,1024]{1,0:T(8,128)(2,1)S(1)}, bf16[520,1024]{1,0:T(8,128)(2,1)}, u32[]{:S(2)}, u32[]{:S(2)}) collective-permute-start(bf16[520,1024]{1,0:T(8,128)(2,1)S(1)} %fusion.3.refs_0_), channel_id=1, source_target_pairs={{0,12},{16,28},{32,44},{48,60},{64,76},{80,92},{96,108},{112,124},... | collective-permute-start | bytes 3194888 | tf_op jit(solution)/shard_map/ppermute | solution.py:158
  37.3 18.9 %collective-permute-done.3.refs_1_ = bf16[520,1024]{1,0:T(8,128)(2,1)} collective-permute-done((bf16[520,1024]{1,0:T(8,128)(2,1)S(1)}, bf16[520,1024]{1,0:T(8,128)(2,1)}, u32[]{:S(2)}, u32[]{:S(2)}) %collective-permute-start.3) | collective-permute-done | bytes 1064992 | tf_op jit(solution)/shard_map/ppermute | solution.py:158
  56.2 2.3 %collective-permute-start.4 = (bf16[520,1024]{1,0:T(8,128)(2,1)}, bf16[520,1024]{1,0:T(8,128)(2,1)}, u32[]{:S(2)}, u32[]{:S(2)}) collective-permute-start(bf16[520,1024]{1,0:T(8,128)(2,1)} %collective-permute-done.3.refs_1_), channel_id=1, source_target_pairs={{4,0},{8,4},{12,8},{20,16},{24,20},{28,24},{36,32},{40,36},{44,40}... | collective-permute-start | bytes 3194888 | tf_op jit(solution)/shard_map/ppermute | solution.py:158
  58.6 0.1 add_convert_fusion
  58.7 1.6 collective-permute-start.8
  60.3 0.8 copy.23.refs_4_.refs_1_
  61.2 0.1 mul.66
  61.3 0.6 concatenate.42.refs_3_
  61.9 0.7 broadcast_multiply_fusion.refs_6_
  62.5 2.5 %fusion.28 = (bf16[512,512]{1,0:T(8,128)(2,1)}, bf16[512,512]{1,0:T(8,128)(2,1)}, bf16[512,512]{1,0:T(8,128)(2,1)}) fusion(bf16[512,1536]{1,0:T(8,128)(2,1)} %copy-done.1), kind=kLoop, calls=%fused_computation.73 | loop fusion | bytes 3145728 | tf_op jit(solution)/shard_map/slice | solution.py:203
  65.1 5.1 %collective-permute-start.7 = (bf16[520,1024]{1,0:T(8,128)(2,1)}, bf16[520,1024]{1,0:T(8,128)(2,1)}, u32[]{:S(2)}, u32[]{:S(2)}) collective-permute-start(bf16[520,1024]{1,0:T(8,128)(2,1)} %collective-permute-done.6), channel_id=1, source_target_pairs={{4,8},{8,12},{20,24},{24,28},{36,40},{40,44},{52,56},{56,60},{68,7... | collective-permute-start | bytes 3194888 | tf_op jit(solution)/shard_map/ppermute | solution.py:158
  70.1 0.7 broadcast_select_fusion.5
  70.9 12.7 %collective-permute-done.4 = bf16[520,1024]{1,0:T(8,128)(2,1)} collective-permute-done((bf16[520,1024]{1,0:T(8,128)(2,1)}, bf16[520,1024]{1,0:T(8,128)(2,1)}, u32[]{:S(2)}, u32[]{:S(2)}) %collective-permute-start.4) | collective-permute-done | bytes 1064992 | tf_op jit(solution)/shard_map/ppermute | solution.py:158
  83.6 3.3 %collective-permute-start.5 = (bf16[520,1024]{1,0:T(8,128)(2,1)}, bf16[520,1024]{1,0:T(8,128)(2,1)}, u32[]{:S(2)}, u32[]{:S(2)}) collective-permute-start(bf16[520,1024]{1,0:T(8,128)(2,1)} %collective-permute-done.4), channel_id=1, source_target_pairs={{4,0},{8,4},{20,16},{24,20},{36,32},{40,36},{52,48},{56,52},{68,64... | collective-permute-start | bytes 3194888 | tf_op jit(solution)/shard_map/ppermute | solution.py:158
  86.9 1.3 broadcast_select_fusion.refs_3_
  88.3 1.7 %broadcast_select_fusion.1.refs_2_ = bf16[520,1024]{1,0:T(8,128)(2,1)S(1)} fusion(bf16[520,1024]{1,0:T(8,128)(2,1)} %collective-permute-done.8, bf16[520,1024]{1,0:T(8,128)(2,1)} %collective-permute-done.6, pred[]{:T(512)S(6)} %eq.5), kind=kLoop, calls=%fused_computation.16 | loop fusion | flops 532480 | bytes 3194881 | tf_op jit(solution)/shard_map/jit(_where)/select_n | solution.py:172
  90.0 0.9 copy-done.6
  91.1 0.1 slice.128
  91.1 0.1 copy.25
  91.2 0.1 copy.21
  91.3 0.1 broadcast_compare_fusion
  91.5 0.6 reshape.255.flags_ref
  92.1 0.6 concatenate.43.refs_5_
  92.7 0.7 broadcast_in_dim.17.refs_7_
  93.4 0.7 broadcast_in_dim.18.refs_8_
  94.1 1.1 broadcast_in_dim.19.refs_9_
  95.2 34.8 %shard_map.85 = (f32[512,128]{1,0:T(8,128)}, f32[512,128]{1,0:T(8,128)}, f32[512,512]{1,0:T(8,128)}) custom-call(s32[16]{0:T(128)} %reshape.255.flags_ref, bf16[512,512]{1,0:T(8,128)(2,1)} %get-tuple-element.53.q_ref, bf16[520,1024]{1,0:T(8,128)(2,1)} %copy-done.7, bf16[520,1024]{1,0:T(8,128)(2,1)} %collective-permute-done.3.refs_1_, ...), custom_call_target="tpu_custom_call" | custom-call | flops 2147483648 | bytes 8388608 | tf_op jit(solution)/shard_map/pallas_call | solution.py:134
  130.0 1.4 broadcast_select_fusion.2.refs_0_
  131.4 0.5 broadcast.176
  131.9 0.6 fusion.27
  132.5 0.1 slice.122
  132.6 0.1 copy.24
  132.7 0.1 compare_convert_fusion
  132.7 0.6 reshape.253.flags_ref
  133.3 0.6 concatenate.41.refs_2_
  134.0 13.8 %shard_map.86 = (f32[512,128]{1,0:T(8,128)}, f32[512,128]{1,0:T(8,128)}, f32[512,512]{1,0:T(8,128)}) custom-call(s32[4]{0:T(128)} %reshape.253.flags_ref, bf16[512,512]{1,0:T(8,128)(2,1)} %get-tuple-element.53.q_ref, bf16[520,1024]{1,0:T(8,128)(2,1)} %copy-done.4, s32[512,1]{1,0:T(8,128)} %copy.23.refs_4_.refs_1_, s32[8,512]{1,0:T(8,128)} %concatenate.41.refs_2_, ...), custom_call_target="tpu_custom_call" | custom-call | flops 536870912 | bytes 5242880 | tf_op jit(solution)/shard_map/pallas_call | solution.py:134
  147.8 1.5 broadcast_in_dim.20
  149.3 1.4 fusion.9
  150.8 0.7 convolution_convert_fusion
  151.6 0.1 collective-permute-start.10
  151.7 0.7 convolution_convert_fusion.1
  152.4 1.9 %collective-permute-done.10 = bf16[2,128,2048]{2,1,0:T(8,128)(2,1)S(1)} collective-permute-done((bf16[2,128,2048]{2,1,0:T(8,128)(2,1)S(1)}, bf16[2,128,2048]{2,1,0:T(8,128)(2,1)S(1)}, u32[]{:S(2)}, u32[]{:S(2)}) %collective-permute-start.10) | collective-permute-done | bytes 1048608 | tf_op jit(solution)/shard_map/ppermute | solution.py:26
  154.3 0.4 convert_add_fusion
  154.7 3.1 %collective-permute-start.11 = (bf16[128,2048]{1,0:T(8,128)(2,1)S(1)}, bf16[128,2048]{1,0:T(8,128)(2,1)S(1)}, u32[]{:S(2)}, u32[]{:S(2)}) collective-permute-start(bf16[128,2048]{1,0:T(8,128)(2,1)S(1)} %fusion.16), channel_id=1, source_target_pairs={{0,2},{1,3},{2,0},{3,1},{4,6},{5,7},{6,4},{7,5},{8,10},{9,11},{10,... | collective-permute-start | bytes 1572872 | tf_op jit(solution)/shard_map/ppermute | solution.py:26
  157.8 12.4 %collective-permute-done.11 = bf16[128,2048]{1,0:T(8,128)(2,1)S(1)} collective-permute-done((bf16[128,2048]{1,0:T(8,128)(2,1)S(1)}, bf16[128,2048]{1,0:T(8,128)(2,1)S(1)}, u32[]{:S(2)}, u32[]{:S(2)}) %collective-permute-start.11) | collective-permute-done | bytes 524320 | tf_op jit(solution)/shard_map/ppermute | solution.py:26
  170.3 1.0 fusion.8
  (50 shorter events, 0.4 us)
Async XLA Ops:
  0.6 150.2 %copy-start = (bf16[512,2048]{1,0:T(8,128)(2,1)S(1)}, bf16[512,2048]{1,0:T(8,128)(2,1)}, u32[]{:S(2)}) copy-start(bf16[512,2048]{1,0:T(8,128)(2,1)} %param.16) | copy-start | bytes 6291460
  0.6 7.2 %copy-start.8 = (s32[512]{0:T(512)S(1)}, s32[512]{0:T(512)}, u32[]{:S(2)}) copy-start(s32[512]{0:T(512)} %param.17) | copy-start | bytes 6148
  4.8 15.3 %collective-permute-start.1 = (bf16[128,2048]{1,0:T(8,128)(2,1)S(1)}, bf16[128,2048]{1,0:T(8,128)(2,1)S(1)}, u32[]{:S(2)}, u32[]{:S(2)}) collective-permute-start(bf16[128,2048]{1,0:T(8,128)(2,1)S(1)} %fusion.6), channel_id=1, source_target_pairs={{0,2},{1,3},{2,0},{3,1},{4,6},{5,7},{6,4},{7,5},{8,10},{9,11},{10,... | collective-permute-start | bytes 1572872 | tf_op jit(solution)/shard_map/ppermute | solution.py:26
  7.9 12.2 %collective-permute-start = (bf16[128,2048]{1,0:T(8,128)(2,1)S(1)}, bf16[128,2048]{1,0:T(8,128)(2,1)}, u32[]{:S(2)}, u32[]{:S(2)}) collective-permute-start(bf16[128,2048]{1,0:T(8,128)(2,1)S(1)} %fusion.6), channel_id=1, source_target_pairs={{0,1},{1,0},{2,3},{3,2},{4,5},{5,4},{6,7},{7,6},{8,9},{9,8},{10,11... | collective-permute-start | bytes 1572872 | tf_op jit(solution)/shard_map/ppermute | solution.py:26
  20.0 4.9 %collective-permute-start.2 = (bf16[128,2048]{1,0:T(8,128)(2,1)S(1)}, bf16[128,2048]{1,0:T(8,128)(2,1)S(1)}, u32[]{:S(2)}, u32[]{:S(2)}) collective-permute-start(bf16[128,2048]{1,0:T(8,128)(2,1)S(1)} %collective-permute-done.1), channel_id=1, source_target_pairs={{0,1},{1,0},{2,3},{3,2},{4,5},{5,4},{6,7},{7,6},{8,9},{9,8},{10,11... | collective-permute-start | bytes 1572872 | tf_op jit(solution)/shard_map/ppermute | solution.py:26
  20.0 4.9 %copy-start.3 = (bf16[2048,3,512]{0,2,1:T(8,128)(2,1)S(1)}, bf16[2048,3,512]{0,2,1:T(8,128)(2,1)}, u32[]{:S(2)}) copy-start(bf16[2048,3,512]{0,2,1:T(8,128)(2,1)} %copy.18) | copy-start | bytes 18874372
  27.2 1.1 copy-start.1
  27.2 8.3 %copy-start.9 = (f32[4]{0:T(128)S(1)}, f32[4]{0:T(128)}, u32[]{:S(2)}) copy-start(f32[4]{0:T(128)} %param.15) | copy-start | bytes 52
  27.2 31.4 %copy-start.10 = (s32[4]{0:T(128)S(1)}, s32[4]{0:T(128)}, u32[]{:S(2)}) copy-start(s32[4]{0:T(128)} %constant.150.clone.1) | copy-start | bytes 52
  28.3 58.6 %copy-start.7 = (bf16[520,1024]{1,0:T(8,128)(2,1)}, bf16[520,1024]{1,0:T(8,128)(2,1)S(1)}, u32[]{:S(2)}) copy-start(bf16[520,1024]{1,0:T(8,128)(2,1)S(1)} %fusion.3.refs_0_) | copy-start | bytes 3194884
  28.3 27.9 %collective-permute-start.3 = (bf16[520,1024]{1,0:T(8,128)(2,1)S(1)}, bf16[520,1024]{1,0:T(8,128)(2,1)}, u32[]{:S(2)}, u32[]{:S(2)}) collective-permute-start(bf16[520,1024]{1,0:T(8,128)(2,1)S(1)} %fusion.3.refs_0_), channel_id=1, source_target_pairs={{0,16},{4,20},{8,24},{12,28},{16,32},{20,36},{24,40},{28,44},{32,4... | collective-permute-start | bytes 3194888 | tf_op jit(solution)/shard_map/ppermute | solution.py:158
  32.3 32.8 %collective-permute-start.6 = (bf16[520,1024]{1,0:T(8,128)(2,1)S(1)}, bf16[520,1024]{1,0:T(8,128)(2,1)}, u32[]{:S(2)}, u32[]{:S(2)}) collective-permute-start(bf16[520,1024]{1,0:T(8,128)(2,1)S(1)} %fusion.3.refs_0_), channel_id=1, source_target_pairs={{0,4},{4,8},{8,12},{16,20},{20,24},{24,28},{32,36},{36,40},{40,44}... | collective-permute-start | bytes 3194888 | tf_op jit(solution)/shard_map/ppermute | solution.py:158
  35.5 51.3 %collective-permute-start.9 = (bf16[520,1024]{1,0:T(8,128)(2,1)S(1)}, bf16[520,1024]{1,0:T(8,128)(2,1)}, u32[]{:S(2)}, u32[]{:S(2)}) collective-permute-start(bf16[520,1024]{1,0:T(8,128)(2,1)S(1)} %fusion.3.refs_0_), channel_id=1, source_target_pairs={{0,12},{16,28},{32,44},{48,60},{64,76},{80,92},{96,108},{112,124},... | collective-permute-start | bytes 3194888 | tf_op jit(solution)/shard_map/ppermute | solution.py:158
  56.2 27.3 %collective-permute-start.4 = (bf16[520,1024]{1,0:T(8,128)(2,1)}, bf16[520,1024]{1,0:T(8,128)(2,1)}, u32[]{:S(2)}, u32[]{:S(2)}) collective-permute-start(bf16[520,1024]{1,0:T(8,128)(2,1)} %collective-permute-done.3.refs_1_), channel_id=1, source_target_pairs={{4,0},{8,4},{12,8},{20,16},{24,20},{28,24},{36,32},{40,36},{44,40}... | collective-permute-start | bytes 3194888 | tf_op jit(solution)/shard_map/ppermute | solution.py:158
  58.7 29.6 %collective-permute-start.8 = (bf16[520,1024]{1,0:T(8,128)(2,1)}, bf16[520,1024]{1,0:T(8,128)(2,1)}, u32[]{:S(2)}, u32[]{:S(2)}) collective-permute-start(bf16[520,1024]{1,0:T(8,128)(2,1)} %collective-permute-done.3.refs_1_), channel_id=1, source_target_pairs={{12,0},{28,16},{44,32},{60,48},{76,64},{92,80},{108,96},{124,112},... | collective-permute-start | bytes 3194888 | tf_op jit(solution)/shard_map/ppermute | solution.py:158
  65.1 64.9 %collective-permute-start.7 = (bf16[520,1024]{1,0:T(8,128)(2,1)}, bf16[520,1024]{1,0:T(8,128)(2,1)}, u32[]{:S(2)}, u32[]{:S(2)}) collective-permute-start(bf16[520,1024]{1,0:T(8,128)(2,1)} %collective-permute-done.6), channel_id=1, source_target_pairs={{4,8},{8,12},{20,24},{24,28},{36,40},{40,44},{52,56},{56,60},{68,7... | collective-permute-start | bytes 3194888 | tf_op jit(solution)/shard_map/ppermute | solution.py:158
  83.6 46.4 %collective-permute-start.5 = (bf16[520,1024]{1,0:T(8,128)(2,1)}, bf16[520,1024]{1,0:T(8,128)(2,1)}, u32[]{:S(2)}, u32[]{:S(2)}) collective-permute-start(bf16[520,1024]{1,0:T(8,128)(2,1)} %collective-permute-done.4), channel_id=1, source_target_pairs={{4,0},{8,4},{20,16},{24,20},{36,32},{40,36},{52,48},{56,52},{68,64... | collective-permute-start | bytes 3194888 | tf_op jit(solution)/shard_map/ppermute | solution.py:158
  88.2 7.0 %copy-start.5 = (bf16[520,1024]{1,0:T(8,128)(2,1)}, bf16[520,1024]{1,0:T(8,128)(2,1)S(1)}, u32[]{:S(2)}) copy-start(bf16[520,1024]{1,0:T(8,128)(2,1)S(1)} %broadcast_select_fusion.refs_3_) | copy-start | bytes 3194884
  90.0 1.0 copy-start.6
  131.4 2.6 %copy-start.4 = (bf16[520,1024]{1,0:T(8,128)(2,1)}, bf16[520,1024]{1,0:T(8,128)(2,1)S(1)}, u32[]{:S(2)}) copy-start(bf16[520,1024]{1,0:T(8,128)(2,1)S(1)} %broadcast_select_fusion.2.refs_0_) | copy-start | bytes 3194884
  151.6 2.7 %collective-permute-start.10 = (bf16[2,128,2048]{2,1,0:T(8,128)(2,1)S(1)}, bf16[2,128,2048]{2,1,0:T(8,128)(2,1)S(1)}, u32[]{:S(2)}, u32[]{:S(2)}) collective-permute-start(bf16[2,128,2048]{2,1,0:T(8,128)(2,1)S(1)} %bitcast.50), channel_id=1, source_target_pairs={{0,1},{1,0},{2,3},{3,2},{4,5},{5,4},{6,7},{7,6},{8,9},{9,8},{10,11... | collective-permute-start | bytes 3145736 | tf_op jit(solution)/shard_map/ppermute | solution.py:26
  154.3 16.0 %copy-start.2 = (bf16[128,2048]{1,0:T(8,128)(2,1)S(1)}, bf16[128,2048]{1,0:T(8,128)(2,1)}, u32[]{:S(2)}) copy-start(bf16[128,2048]{1,0:T(8,128)(2,1)} %param.12) | copy-start | bytes 1572868
  154.7 15.6 %collective-permute-start.11 = (bf16[128,2048]{1,0:T(8,128)(2,1)S(1)}, bf16[128,2048]{1,0:T(8,128)(2,1)S(1)}, u32[]{:S(2)}, u32[]{:S(2)}) collective-permute-start(bf16[128,2048]{1,0:T(8,128)(2,1)S(1)} %fusion.16), channel_id=1, source_target_pairs={{0,2},{1,3},{2,0},{3,1},{4,6},{5,7},{6,4},{7,5},{8,10},{9,11},{10,... | collective-permute-start | bytes 1572872 | tf_op jit(solution)/shard_map/ppermute | solution.py:26

commit v9 on v8

--- a/solution.py
+++ b/solution.py
@@ -184,15 +184,16 @@
 
     width_local = w_qkv.shape[2]
     heads_dev = slopes.shape[0]
-    joined = w_qkv.reshape(w_qkv.shape[0], 3 * width_local)
 
     def project_rows(rows):
-        return jnp.dot(rows, joined, preferred_element_type=jnp.float32).astype(jnp.bfloat16)
+        out = jnp.einsum("rd,dtc->rtc", rows, w_qkv, preferred_element_type=jnp.float32)
+        return out.astype(jnp.bfloat16).reshape(rows.shape[0], 3 * width_local)
 
     from_partner = swapped(normed, "head", 1)
     from_cross = swapped(normed, "head", 2)
+    near = project_rows(jnp.concatenate([normed, from_partner], axis=0))
+    near, from_cross = lax.optimization_barrier((near, from_cross))
     from_partner_cross = swapped(from_cross, "head", 1)
-    near = project_rows(jnp.concatenate([normed, from_partner], axis=0))
     far = project_rows(jnp.concatenate([from_cross, from_partner_cross], axis=0))
     pieces = jnp.concatenate([near, far], axis=0).reshape(n_head, rows_dev, near.shape[1])
     qkv_rows = jnp.concatenate(

time: 172 us -> 185 us (1.076)
  the two profiles are of different devices: /device:TPU:80 before, /device:TPU:22 now
where the time goes in v9:
time: 185 us
  waiting for transfers between devices  61.6 us (33%)
  Pallas kernels  48.6 us (26%)
  starting transfers between devices  24 us (13%)
  local copies, waits for them, and re-layouts  21.8 us (12%)
  other arithmetic  15 us (8%)
  matrix products  12.8 us (7%)
    pallas_call x2, Pallas kernels, attention_part(): pl.pallas_call(functools.partial(part_kernel, n_buf, own), out_shape=(jax...  48.6 us
    ppermute x7, waiting for transfers between devices, moved(): return lax.ppermute(value, 'seq', pairs)  35.6 us
    ppermute x5, waiting for transfers between devices, swapped(): lax.ppermute(value, axis, [(source, source ^ mask) for source in range(co...  26 us
    ppermute x7, starting transfers between devices, moved(): return lax.ppermute(value, 'seq', pairs)  21.1 us
    dot_general x2, matrix products, project_rows(): jnp.einsum('rd,dtc->rtc', rows, w_qkv, preferred_element_type=jnp.float32)  11.3 us
    convert_element_type x2, local copies, waits for them, and re-layouts, project_rows(): return out.astype(jnp.bfloat16).reshape(rows.shape[0], 3 * width_local)  3.71 us
  transfers between devices with their start and end apart: 12, of which 7 were waited for; matrix products, arithmetic and copies ran while one was open for 11% of the time, Pallas kernels for 19%

profile of v9, /device:TPU:22, one launch (start us, length us, event | category | flops | bytes accessed | tf_op | source)
XLA Modules:
  0.0 184.7 jit_solution(9609252299097672232)
XLA Ops:
  0.6 1.3 convert_reduce_fusion
  2.0 1.3 fusion.4
  3.3 1.4 fusion.6
  4.8 0.1 collective-permute-start
  4.9 1.5 collective-permute-start.1
  6.3 0.4 collective-permute-done
  6.8 5.5 %convolution_convert_fusion.3 = bf16[256,3,512]{2,0,1:T(8,128)(2,1)} fusion(bf16[2048,3,512]{2,0,1:T(8,128)(2,1)} %param.14, bf16[128,2048]{1,0:T(8,128)(2,1)S(1)} %collective-permute-done, bf16[128,2048]{1,0:T(8,128)(2,1)S(1)} %fusion.6), kind=kOutput, calls=%fused_computation.11 | convolution fusion | flops 1613103104 | bytes 8126464 | tf_op jit(solution)/shard_map/rd,dtc->rtc/dot_general | solution.py:189
  12.2 1.4 copy.23
  13.6 7.2 %collective-permute-done.1 = bf16[128,2048]{1,0:T(8,128)(2,1)} collective-permute-done((bf16[128,2048]{1,0:T(8,128)(2,1)S(1)}, bf16[128,2048]{1,0:T(8,128)(2,1)}, u32[]{:S(2)}, u32[]{:S(2)}) %collective-permute-start.1) | collective-permute-done | bytes 524320 | tf_op jit(solution)/shard_map/ppermute | solution.py:26
  20.9 2.2 %collective-permute-done.2 = bf16[128,2048]{1,0:T(8,128)(2,1)} collective-permute-done((bf16[128,2048]{1,0:T(8,128)(2,1)}, bf16[128,2048]{1,0:T(8,128)(2,1)}, u32[]{:S(2)}, u32[]{:S(2)}) %collective-permute-start.2) | collective-permute-done | bytes 524320 | tf_op jit(solution)/shard_map/ppermute | solution.py:26
  23.1 5.8 %convolution_convert_fusion.2 = bf16[256,3,512]{2,0,1:T(8,128)(2,1)} fusion(bf16[2048,3,512]{2,0,1:T(8,128)(2,1)} %param.14, bf16[128,2048]{1,0:T(8,128)(2,1)} %collective-permute-done.2, bf16[128,2048]{1,0:T(8,128)(2,1)} %collective-permute-done.1), kind=kOutput, calls=%fused_computation.10 | convolution fusion | flops 1613103104 | bytes 8126464 | tf_op jit(solution)/shard_map/rd,dtc->rtc/dot_general | solution.py:189
  28.9 2.3 %copy.24 = bf16[256,3,512]{0,2,1:T(8,128)(2,1)} copy(bf16[256,3,512]{2,0,1:T(8,128)(2,1)} %convolution_convert_fusion.2) | data formatting | bytes 1572864 | tf_op jit(solution)/shard_map/convert_element_type | solution.py:190
  31.2 2.4 %pad_maximum_fusion = bf16[512,1536]{0,1:T(8,128)(2,1)} fusion(bf16[256,1536]{0,1:T(8,128)(2,1)} %bitcast.55, bf16[256,1536]{0,1:T(8,128)(2,1)S(1)} %bitcast.54), kind=kLoop, calls=%fused_computation.5 | loop fusion | flops 3145728 | bytes 3145728 | tf_op jit(solution)/shard_map/concatenate | solution.py:198
  33.6 2.6 %copy.34 = bf16[512,1536]{1,0:T(8,128)(2,1)} copy(bf16[512,1536]{0,1:T(8,128)(2,1)} %pad_maximum_fusion) | data formatting | bytes 3145728 | tf_op jit(solution)/shard_map/reshape | solution.py:198
  36.2 1.5 dynamic-slice_bitcast_fusion.3
  37.6 0.1 pad_maximum_fusion.1
  37.7 0.1 slice.120
  37.9 0.1 fusion.3.refs_0_
  38.0 0.9 copy-done.1
  38.9 3.8 %collective-permute-start.3 = (bf16[520,1024]{1,0:T(8,128)(2,1)S(1)}, bf16[520,1024]{1,0:T(8,128)(2,1)}, u32[]{:S(2)}, u32[]{:S(2)}) collective-permute-start(bf16[520,1024]{1,0:T(8,128)(2,1)S(1)} %fusion.3.refs_0_), channel_id=1, source_target_pairs={{0,16},{4,20},{8,24},{12,28},{16,32},{20,36},{24,40},{28,44},{32,4... | collective-permute-start | bytes 3194888 | tf_op jit(solution)/shard_map/ppermute | solution.py:158
  42.7 0.1 slice_reduce_fusion
  42.8 3.2 %collective-permute-start.6 = (bf16[520,1024]{1,0:T(8,128)(2,1)S(1)}, bf16[520,1024]{1,0:T(8,128)(2,1)}, u32[]{:S(2)}, u32[]{:S(2)}) collective-permute-start(bf16[520,1024]{1,0:T(8,128)(2,1)S(1)} %fusion.3.refs_0_), channel_id=1, source_target_pairs={{0,4},{4,8},{8,12},{16,20},{20,24},{24,28},{32,36},{36,40},{40,44}... | collective-permute-start | bytes 3194888 | tf_op jit(solution)/shard_map/ppermute | solution.py:158
  46.1 1.7 collective-permute-start.9
  47.8 23.0 %collective-permute-done.3.refs_1_ = bf16[520,1024]{1,0:T(8,128)(2,1)} collective-permute-done((bf16[520,1024]{1,0:T(8,128)(2,1)S(1)}, bf16[520,1024]{1,0:T(8,128)(2,1)}, u32[]{:S(2)}, u32[]{:S(2)}) %collective-permute-start.3) | collective-permute-done | bytes 1064992 | tf_op jit(solution)/shard_map/ppermute | solution.py:158
  70.8 2.3 %collective-permute-start.4 = (bf16[520,1024]{1,0:T(8,128)(2,1)}, bf16[520,1024]{1,0:T(8,128)(2,1)}, u32[]{:S(2)}, u32[]{:S(2)}) collective-permute-start(bf16[520,1024]{1,0:T(8,128)(2,1)} %collective-permute-done.3.refs_1_), channel_id=1, source_target_pairs={{4,0},{8,4},{12,8},{20,16},{24,20},{28,24},{36,32},{40,36},{44,40}... | collective-permute-start | bytes 3194888 | tf_op jit(solution)/shard_map/ppermute | solution.py:158
  73.2 1.6 collective-permute-start.8
  74.9 0.8 copy.33.refs_4_.refs_1_
  75.8 0.1 mul.66
  75.8 0.6 concatenate.42.refs_3_
  76.5 0.7 broadcast_multiply_fusion.refs_6_
  77.1 2.5 %fusion.26 = (bf16[512,512]{1,0:T(8,128)(2,1)}, bf16[512,512]{1,0:T(8,128)(2,1)}, bf16[512,512]{1,0:T(8,128)(2,1)}) fusion(bf16[512,1536]{1,0:T(8,128)(2,1)} %copy-done.1), kind=kLoop, calls=%fused_computation.73 | loop fusion | bytes 3145728 | tf_op jit(solution)/shard_map/slice | solution.py:204
  79.7 5.1 %collective-permute-start.7 = (bf16[520,1024]{1,0:T(8,128)(2,1)}, bf16[520,1024]{1,0:T(8,128)(2,1)}, u32[]{:S(2)}, u32[]{:S(2)}) collective-permute-start(bf16[520,1024]{1,0:T(8,128)(2,1)} %collective-permute-done.6), channel_id=1, source_target_pairs={{4,8},{8,12},{20,24},{24,28},{36,40},{40,44},{52,56},{56,60},{68,7... | collective-permute-start | bytes 3194888 | tf_op jit(solution)/shard_map/ppermute | solution.py:158
  84.7 0.7 broadcast_select_fusion.5
  85.4 12.6 %collective-permute-done.4 = bf16[520,1024]{1,0:T(8,128)(2,1)} collective-permute-done((bf16[520,1024]{1,0:T(8,128)(2,1)}, bf16[520,1024]{1,0:T(8,128)(2,1)}, u32[]{:S(2)}, u32[]{:S(2)}) %collective-permute-start.4) | collective-permute-done | bytes 1064992 | tf_op jit(solution)/shard_map/ppermute | solution.py:158
  98.0 3.3 %collective-permute-start.5 = (bf16[520,1024]{1,0:T(8,128)(2,1)}, bf16[520,1024]{1,0:T(8,128)(2,1)}, u32[]{:S(2)}, u32[]{:S(2)}) collective-permute-start(bf16[520,1024]{1,0:T(8,128)(2,1)} %collective-permute-done.4), channel_id=1, source_target_pairs={{4,0},{8,4},{20,16},{24,20},{36,32},{40,36},{52,48},{56,52},{68,64... | collective-permute-start | bytes 3194888 | tf_op jit(solution)/shard_map/ppermute | solution.py:158
  101.4 1.3 broadcast_select_fusion.refs_3_
  102.7 1.7 broadcast_select_fusion.1.refs_2_
  104.5 0.9 copy-done.5
  105.6 0.1 copy.36
  105.7 0.1 copy.31
  105.8 0.1 broadcast_compare_fusion
  106.0 0.6 reshape.259.flags_ref
  106.6 0.6 concatenate.43.refs_5_
  107.2 0.7 broadcast_in_dim.17.refs_7_
  107.9 0.7 broadcast_in_dim.18.refs_8_
  108.6 1.1 broadcast_in_dim.19.refs_9_
  109.7 34.8 %shard_map.85 = (f32[512,128]{1,0:T(8,128)}, f32[512,128]{1,0:T(8,128)}, f32[512,512]{1,0:T(8,128)}) custom-call(s32[16]{0:T(128)} %reshape.259.flags_ref, bf16[512,512]{1,0:T(8,128)(2,1)} %get-tuple-element.57.q_ref, bf16[520,1024]{1,0:T(8,128)(2,1)} %copy-done.6, bf16[520,1024]{1,0:T(8,128)(2,1)} %collective-permute-done.3.refs_1_, ...), custom_call_target="tpu_custom_call" | custom-call | flops 2147483648 | bytes 8388608 | tf_op jit(solution)/shard_map/pallas_call | solution.py:134
  144.5 1.4 broadcast_select_fusion.2.refs_0_
  145.9 0.5 broadcast.176
  146.4 0.6 fusion.25
  147.1 0.1 copy.35
  147.2 0.6 reshape.257.flags_ref
  147.8 0.6 concatenate.41.refs_2_
  148.4 13.8 %shard_map.86 = (f32[512,128]{1,0:T(8,128)}, f32[512,128]{1,0:T(8,128)}, f32[512,512]{1,0:T(8,128)}) custom-call(s32[4]{0:T(128)} %reshape.257.flags_ref, bf16[512,512]{1,0:T(8,128)(2,1)} %get-tuple-element.57.q_ref, bf16[520,1024]{1,0:T(8,128)(2,1)} %copy-done.3, s32[512,1]{1,0:T(8,128)} %copy.33.refs_4_.refs_1_, s32[8,512]{1,0:T(8,128)} %concatenate.41.refs_2_, ...), custom_call_target="tpu_custom_call" | custom-call | flops 536870912 | bytes 5242880 | tf_op jit(solution)/shard_map/pallas_call | solution.py:134
  162.2 1.6 broadcast_in_dim.20
  163.9 0.3 fusion.9
  164.2 0.7 convolution_convert_fusion
  165.0 0.1 collective-permute-start.10
  165.1 0.7 convolution_convert_fusion.1
  165.8 1.9 %collective-permute-done.10 = bf16[2,128,2048]{2,1,0:T(8,128)(2,1)S(1)} collective-permute-done((bf16[2,128,2048]{2,1,0:T(8,128)(2,1)S(1)}, bf16[2,128,2048]{2,1,0:T(8,128)(2,1)S(1)}, u32[]{:S(2)}, u32[]{:S(2)}) %collective-permute-start.10) | collective-permute-done | bytes 1048608 | tf_op jit(solution)/shard_map/ppermute | solution.py:26
  167.7 0.4 convert_add_fusion
  168.2 1.2 collective-permute-start.11
  169.4 14.4 %collective-permute-done.11 = bf16[128,2048]{1,0:T(8,128)(2,1)S(1)} collective-permute-done((bf16[128,2048]{1,0:T(8,128)(2,1)S(1)}, bf16[128,2048]{1,0:T(8,128)(2,1)S(1)}, u32[]{:S(2)}, u32[]{:S(2)}) %collective-permute-start.11) | collective-permute-done | bytes 524320 | tf_op jit(solution)/shard_map/ppermute | solution.py:26
  183.7 1.0 fusion.8
  (52 shorter events, 0.8 us)
Async XLA Ops:
  0.6 163.6 %copy-start = (bf16[512,2048]{1,0:T(8,128)(2,1)S(1)}, bf16[512,2048]{1,0:T(8,128)(2,1)}, u32[]{:S(2)}) copy-start(bf16[512,2048]{1,0:T(8,128)(2,1)} %param.16) | copy-start | bytes 6291460
  4.8 2.0 %collective-permute-start = (bf16[128,2048]{1,0:T(8,128)(2,1)S(1)}, bf16[128,2048]{1,0:T(8,128)(2,1)S(1)}, u32[]{:S(2)}, u32[]{:S(2)}) collective-permute-start(bf16[128,2048]{1,0:T(8,128)(2,1)S(1)} %fusion.6), channel_id=1, source_target_pairs={{0,1},{1,0},{2,3},{3,2},{4,5},{5,4},{6,7},{7,6},{8,9},{9,8},{10,11... | collective-permute-start | bytes 1572872 | tf_op jit(solution)/shard_map/ppermute | solution.py:26
  4.9 16.0 %collective-permute-start.1 = (bf16[128,2048]{1,0:T(8,128)(2,1)S(1)}, bf16[128,2048]{1,0:T(8,128)(2,1)}, u32[]{:S(2)}, u32[]{:S(2)}) collective-permute-start(bf16[128,2048]{1,0:T(8,128)(2,1)S(1)} %fusion.6), channel_id=1, source_target_pairs={{0,2},{1,3},{2,0},{3,1},{4,6},{5,7},{6,4},{7,5},{8,10},{9,11},{10,... | collective-permute-start | bytes 1572872 | tf_op jit(solution)/shard_map/ppermute | solution.py:26
  12.2 8.6 %copy-start.8 = (s32[512]{0:T(512)S(1)}, s32[512]{0:T(512)}, u32[]{:S(2)}) copy-start(s32[512]{0:T(512)} %param.17) | copy-start | bytes 6148
  20.8 2.3 %collective-permute-start.2 = (bf16[128,2048]{1,0:T(8,128)(2,1)}, bf16[128,2048]{1,0:T(8,128)(2,1)}, u32[]{:S(2)}, u32[]{:S(2)}) collective-permute-start(bf16[128,2048]{1,0:T(8,128)(2,1)} %collective-permute-done.1), channel_id=1, source_target_pairs={{0,1},{1,0},{2,3},{3,2},{4,5},{5,4},{6,7},{7,6},{8,9},{9,8},{10,11... | collective-permute-start | bytes 1572872 | tf_op jit(solution)/shard_map/ppermute | solution.py:26
  37.7 1.1 copy-start.1
  37.9 8.1 %copy-start.9 = (f32[4]{0:T(128)S(1)}, f32[4]{0:T(128)}, u32[]{:S(2)}) copy-start(f32[4]{0:T(128)} %param.15) | copy-start | bytes 52
  37.9 35.3 %copy-start.10 = (s32[4]{0:T(128)S(1)}, s32[4]{0:T(128)}, u32[]{:S(2)}) copy-start(s32[4]{0:T(128)} %constant.150.clone.1) | copy-start | bytes 52
  38.9 40.8 %copy-start.6 = (bf16[520,1024]{1,0:T(8,128)(2,1)}, bf16[520,1024]{1,0:T(8,128)(2,1)S(1)}, u32[]{:S(2)}) copy-start(bf16[520,1024]{1,0:T(8,128)(2,1)S(1)} %fusion.3.refs_0_) | copy-start | bytes 3194884
  38.9 31.9 %collective-permute-start.3 = (bf16[520,1024]{1,0:T(8,128)(2,1)S(1)}, bf16[520,1024]{1,0:T(8,128)(2,1)}, u32[]{:S(2)}, u32[]{:S(2)}) collective-permute-start(bf16[520,1024]{1,0:T(8,128)(2,1)S(1)} %fusion.3.refs_0_), channel_id=1, source_target_pairs={{0,16},{4,20},{8,24},{12,28},{16,32},{20,36},{24,40},{28,44},{32,4... | collective-permute-start | bytes 3194888 | tf_op jit(solution)/shard_map/ppermute | solution.py:158
  42.8 36.8 %collective-permute-start.6 = (bf16[520,1024]{1,0:T(8,128)(2,1)S(1)}, bf16[520,1024]{1,0:T(8,128)(2,1)}, u32[]{:S(2)}, u32[]{:S(2)}) collective-permute-start(bf16[520,1024]{1,0:T(8,128)(2,1)S(1)} %fusion.3.refs_0_), channel_id=1, source_target_pairs={{0,4},{4,8},{8,12},{16,20},{20,24},{24,28},{32,36},{36,40},{40,44}... | collective-permute-start | bytes 3194888 | tf_op jit(solution)/shard_map/ppermute | solution.py:158
  46.1 55.3 %collective-permute-start.9 = (bf16[520,1024]{1,0:T(8,128)(2,1)S(1)}, bf16[520,1024]{1,0:T(8,128)(2,1)}, u32[]{:S(2)}, u32[]{:S(2)}) collective-permute-start(bf16[520,1024]{1,0:T(8,128)(2,1)S(1)} %fusion.3.refs_0_), channel_id=1, source_target_pairs={{0,12},{16,28},{32,44},{48,60},{64,76},{80,92},{96,108},{112,124},... | collective-permute-start | bytes 3194888 | tf_op jit(solution)/shard_map/ppermute | solution.py:158
  70.8 27.2 %collective-permute-start.4 = (bf16[520,1024]{1,0:T(8,128)(2,1)}, bf16[520,1024]{1,0:T(8,128)(2,1)}, u32[]{:S(2)}, u32[]{:S(2)}) collective-permute-start(bf16[520,1024]{1,0:T(8,128)(2,1)} %collective-permute-done.3.refs_1_), channel_id=1, source_target_pairs={{4,0},{8,4},{12,8},{20,16},{24,20},{28,24},{36,32},{40,36},{44,40}... | collective-permute-start | bytes 3194888 | tf_op jit(solution)/shard_map/ppermute | solution.py:158
  73.2 29.5 %collective-permute-start.8 = (bf16[520,1024]{1,0:T(8,128)(2,1)}, bf16[520,1024]{1,0:T(8,128)(2,1)}, u32[]{:S(2)}, u32[]{:S(2)}) collective-permute-start(bf16[520,1024]{1,0:T(8,128)(2,1)} %collective-permute-done.3.refs_1_), channel_id=1, source_target_pairs={{12,0},{28,16},{44,32},{60,48},{76,64},{92,80},{108,96},{124,112},... | collective-permute-start | bytes 3194888 | tf_op jit(solution)/shard_map/ppermute | solution.py:158
  79.7 64.8 %collective-permute-start.7 = (bf16[520,1024]{1,0:T(8,128)(2,1)}, bf16[520,1024]{1,0:T(8,128)(2,1)}, u32[]{:S(2)}, u32[]{:S(2)}) collective-permute-start(bf16[520,1024]{1,0:T(8,128)(2,1)} %collective-permute-done.6), channel_id=1, source_target_pairs={{4,8},{8,12},{20,24},{24,28},{36,40},{40,44},{52,56},{56,60},{68,7... | collective-permute-start | bytes 3194888 | tf_op jit(solution)/shard_map/ppermute | solution.py:158
  98.0 46.5 %collective-permute-start.5 = (bf16[520,1024]{1,0:T(8,128)(2,1)}, bf16[520,1024]{1,0:T(8,128)(2,1)}, u32[]{:S(2)}, u32[]{:S(2)}) collective-permute-start(bf16[520,1024]{1,0:T(8,128)(2,1)} %collective-permute-done.4), channel_id=1, source_target_pairs={{4,0},{8,4},{20,16},{24,20},{36,32},{40,36},{52,48},{56,52},{68,64... | collective-permute-start | bytes 3194888 | tf_op jit(solution)/shard_map/ppermute | solution.py:158
  102.7 1.8 copy-start.4
  104.5 1.0 copy-start.5
  145.9 2.6 %copy-start.3 = (bf16[520,1024]{1,0:T(8,128)(2,1)}, bf16[520,1024]{1,0:T(8,128)(2,1)S(1)}, u32[]{:S(2)}) copy-start(bf16[520,1024]{1,0:T(8,128)(2,1)S(1)} %broadcast_select_fusion.2.refs_0_) | copy-start | bytes 3194884
  162.2 1.6 copy-start.7
  165.0 2.7 %collective-permute-start.10 = (bf16[2,128,2048]{2,1,0:T(8,128)(2,1)S(1)}, bf16[2,128,2048]{2,1,0:T(8,128)(2,1)S(1)}, u32[]{:S(2)}, u32[]{:S(2)}) collective-permute-start(bf16[2,128,2048]{2,1,0:T(8,128)(2,1)S(1)} %bitcast.57), channel_id=1, source_target_pairs={{0,1},{1,0},{2,3},{3,2},{4,5},{5,4},{6,7},{7,6},{8,9},{9,8},{10,11... | collective-permute-start | bytes 3145736 | tf_op jit(solution)/shard_map/ppermute | solution.py:26
  167.7 16.0 %copy-start.2 = (bf16[128,2048]{1,0:T(8,128)(2,1)S(1)}, bf16[128,2048]{1,0:T(8,128)(2,1)}, u32[]{:S(2)}) copy-start(bf16[128,2048]{1,0:T(8,128)(2,1)} %param.12) | copy-start | bytes 1572868
  168.2 15.6 %collective-permute-start.11 = (bf16[128,2048]{1,0:T(8,128)(2,1)S(1)}, bf16[128,2048]{1,0:T(8,128)(2,1)S(1)}, u32[]{:S(2)}, u32[]{:S(2)}) collective-permute-start(bf16[128,2048]{1,0:T(8,128)(2,1)S(1)} %fusion.14), channel_id=1, source_target_pairs={{0,2},{1,3},{2,0},{3,1},{4,6},{5,7},{6,4},{7,5},{8,10},{9,11},{10,... | collective-permute-start | bytes 1572872 | tf_op jit(solution)/shard_map/ppermute | solution.py:26

commit v10 on v8

--- a/solution.py
+++ b/solution.py
@@ -191,8 +191,9 @@
 
     from_partner = swapped(normed, "head", 1)
     from_cross = swapped(normed, "head", 2)
+    near = project_rows(jnp.concatenate([normed, from_partner], axis=0))
+    near, from_cross = lax.optimization_barrier((near, from_cross))
     from_partner_cross = swapped(from_cross, "head", 1)
-    near = project_rows(jnp.concatenate([normed, from_partner], axis=0))
     far = project_rows(jnp.concatenate([from_cross, from_partner_cross], axis=0))
     pieces = jnp.concatenate([near, far], axis=0).reshape(n_head, rows_dev, near.shape[1])
     qkv_rows = jnp.concatenate(

time: 172 us -> 172 us (level)
  the two profiles are of different devices: /device:TPU:80 before, /device:TPU:202 now
where the time goes in v10:
time: 172 us
  waiting for transfers between devices  50.1 us (29%)
  Pallas kernels  48.6 us (28%)
  local copies, waits for them, and re-layouts  23.8 us (14%)
  starting transfers between devices  23 us (13%)
  other arithmetic  13.9 us (8%)
  matrix products  11.2 us (7%)
    pallas_call x2, Pallas kernels, attention_part(): pl.pallas_call(functools.partial(part_kernel, n_buf, own), out_shape=(jax...  48.6 us
    ppermute x7, waiting for transfers between devices, moved(): return lax.ppermute(value, 'seq', pairs)  32.1 us
    ppermute x7, starting transfers between devices, moved(): return lax.ppermute(value, 'seq', pairs)  18.9 us
    ppermute x5, waiting for transfers between devices, swapped(): lax.ppermute(value, axis, [(source, source ^ mask) for source in range(co...  18 us
    unnamed x25, local copies, waits for them, and re-layouts  11.7 us
    dot_general x2, matrix products, project_rows(): jnp.dot(rows, joined, preferred_element_type=jnp.float32)  9.75 us
    ppermute x5, starting transfers between devices, swapped(): lax.ppermute(value, axis, [(source, source ^ mask) for source in range(co...  4.12 us
  transfers between devices with their start and end apart: 12, of which 5 were waited for; matrix products, arithmetic and copies ran while one was open for 16% of the time, Pallas kernels for 20%

profile of v10, /device:TPU:202, one launch (start us, length us, event | category | flops | bytes accessed | tf_op | source)
XLA Modules:
  0.0 171.6 jit_solution(6956979037664575496)
XLA Ops:
  0.6 1.3 convert_reduce_fusion
  2.0 1.3 fusion.4
  3.3 1.4 fusion.6
  4.8 0.1 collective-permute-start
  4.9 2.2 %collective-permute-start.1 = (bf16[128,2048]{1,0:T(8,128)(2,1)S(1)}, bf16[128,2048]{1,0:T(8,128)(2,1)}, u32[]{:S(2)}, u32[]{:S(2)}) collective-permute-start(bf16[128,2048]{1,0:T(8,128)(2,1)S(1)} %fusion.6), channel_id=1, source_target_pairs={{0,2},{1,3},{2,0},{3,1},{4,6},{5,7},{6,4},{7,5},{8,10},{9,11},{10,... | collective-permute-start | bytes 1572872 | tf_op jit(solution)/shard_map/ppermute | solution.py:26
  7.1 8.9 %copy.18 = bf16[2048,3,512]{0,2,1:T(8,128)(2,1)} copy(bf16[2048,3,512]{2,0,1:T(8,128)(2,1)} %param.14) | data formatting | bytes 12582912 | tf_op args[2]
  16.0 0.8 copy-done.10
  16.8 4.8 %convolution_convert_fusion.3 = bf16[256,1536]{1,0:T(8,128)(2,1)S(1)} fusion(bf16[2048,1536]{0,1:T(8,128)(2,1)} %bitcast.44, bf16[128,2048]{1,0:T(8,128)(2,1)} %copy-done.10, bf16[128,2048]{1,0:T(8,128)(2,1)S(1)} %fusion.6), kind=kOutput, calls=%fused_computation.3 | convolution fusion | flops 1613103104 | bytes 8126464 | tf_op jit(solution)/shard_map/dot_general | solution.py:190
  21.6 0.2 collective-permute-start.2
  21.8 2.1 %collective-permute-done.2 = bf16[128,2048]{1,0:T(8,128)(2,1)} collective-permute-done((bf16[128,2048]{1,0:T(8,128)(2,1)}, bf16[128,2048]{1,0:T(8,128)(2,1)}, u32[]{:S(2)}, u32[]{:S(2)}) %collective-permute-start.2) | collective-permute-done | bytes 524320 | tf_op jit(solution)/shard_map/ppermute | solution.py:26
  23.9 4.9 %convolution_convert_fusion.2 = bf16[256,1536]{1,0:T(8,128)(2,1)S(1)} fusion(bf16[2048,1536]{0,1:T(8,128)(2,1)} %bitcast.45, bf16[128,2048]{1,0:T(8,128)(2,1)} %collective-permute-done.2, bf16[128,2048]{1,0:T(8,128)(2,1)} %collective-permute-done.1), kind=kOutput, calls=%fused_computation.2 | convolution fusion | flops 1613103104 | bytes 8126464 | tf_op jit(solution)/shard_map/dot_general | solution.py:190
  28.9 0.1 pad_maximum_fusion
  29.0 0.1 dynamic-slice_bitcast_fusion.3
  29.1 0.1 pad_maximum_fusion.1
  29.2 0.1 slice.120
  29.4 0.1 fusion.3.refs_0_
  29.5 0.9 copy-done.1
  30.4 2.9 %collective-permute-start.3 = (bf16[520,1024]{1,0:T(8,128)(2,1)S(1)}, bf16[520,1024]{1,0:T(8,128)(2,1)}, u32[]{:S(2)}, u32[]{:S(2)}) collective-permute-start(bf16[520,1024]{1,0:T(8,128)(2,1)S(1)} %fusion.3.refs_0_), channel_id=1, source_target_pairs={{0,16},{4,20},{8,24},{12,28},{16,32},{20,36},{24,40},{28,44},{32,4... | collective-permute-start | bytes 3194888 | tf_op jit(solution)/shard_map/ppermute | solution.py:158
  33.3 0.1 slice_reduce_fusion
  33.4 3.5 %collective-permute-start.6 = (bf16[520,1024]{1,0:T(8,128)(2,1)S(1)}, bf16[520,1024]{1,0:T(8,128)(2,1)}, u32[]{:S(2)}, u32[]{:S(2)}) collective-permute-start(bf16[520,1024]{1,0:T(8,128)(2,1)S(1)} %fusion.3.refs_0_), channel_id=1, source_target_pairs={{0,4},{4,8},{8,12},{16,20},{20,24},{24,28},{32,36},{36,40},{40,44}... | collective-permute-start | bytes 3194888 | tf_op jit(solution)/shard_map/ppermute | solution.py:158
  37.0 1.7 %collective-permute-start.9 = (bf16[520,1024]{1,0:T(8,128)(2,1)S(1)}, bf16[520,1024]{1,0:T(8,128)(2,1)}, u32[]{:S(2)}, u32[]{:S(2)}) collective-permute-start(bf16[520,1024]{1,0:T(8,128)(2,1)S(1)} %fusion.3.refs_0_), channel_id=1, source_target_pairs={{0,12},{16,28},{32,44},{48,60},{64,76},{80,92},{96,108},{112,124},... | collective-permute-start | bytes 3194888 | tf_op jit(solution)/shard_map/ppermute | solution.py:158
  38.7 19.2 %collective-permute-done.3.refs_1_ = bf16[520,1024]{1,0:T(8,128)(2,1)} collective-permute-done((bf16[520,1024]{1,0:T(8,128)(2,1)S(1)}, bf16[520,1024]{1,0:T(8,128)(2,1)}, u32[]{:S(2)}, u32[]{:S(2)}) %collective-permute-start.3) | collective-permute-done | bytes 1064992 | tf_op jit(solution)/shard_map/ppermute | solution.py:158
  57.9 2.3 %collective-permute-start.4 = (bf16[520,1024]{1,0:T(8,128)(2,1)}, bf16[520,1024]{1,0:T(8,128)(2,1)}, u32[]{:S(2)}, u32[]{:S(2)}) collective-permute-start(bf16[520,1024]{1,0:T(8,128)(2,1)} %collective-permute-done.3.refs_1_), channel_id=1, source_target_pairs={{4,0},{8,4},{12,8},{20,16},{24,20},{28,24},{36,32},{40,36},{44,40}... | collective-permute-start | bytes 3194888 | tf_op jit(solution)/shard_map/ppermute | solution.py:158
  60.3 1.6 collective-permute-start.8
  62.0 0.8 copy.23.refs_4_.refs_1_
  62.9 0.1 mul.66
  62.9 0.6 concatenate.42.refs_3_
  63.6 0.7 broadcast_multiply_fusion.refs_6_
  64.2 2.5 %fusion.28 = (bf16[512,512]{1,0:T(8,128)(2,1)}, bf16[512,512]{1,0:T(8,128)(2,1)}, bf16[512,512]{1,0:T(8,128)(2,1)}) fusion(bf16[512,1536]{1,0:T(8,128)(2,1)} %copy-done.1), kind=kLoop, calls=%fused_computation.73 | loop fusion | bytes 3145728 | tf_op jit(solution)/shard_map/slice | solution.py:204
  66.8 4.5 %collective-permute-start.7 = (bf16[520,1024]{1,0:T(8,128)(2,1)}, bf16[520,1024]{1,0:T(8,128)(2,1)}, u32[]{:S(2)}, u32[]{:S(2)}) collective-permute-start(bf16[520,1024]{1,0:T(8,128)(2,1)} %collective-permute-done.6), channel_id=1, source_target_pairs={{4,8},{8,12},{20,24},{24,28},{36,40},{40,44},{52,56},{56,60},{68,7... | collective-permute-start | bytes 3194888 | tf_op jit(solution)/shard_map/ppermute | solution.py:158
  71.3 0.7 broadcast_select_fusion.5
  72.0 12.9 %collective-permute-done.4 = bf16[520,1024]{1,0:T(8,128)(2,1)} collective-permute-done((bf16[520,1024]{1,0:T(8,128)(2,1)}, bf16[520,1024]{1,0:T(8,128)(2,1)}, u32[]{:S(2)}, u32[]{:S(2)}) %collective-permute-start.4) | collective-permute-done | bytes 1064992 | tf_op jit(solution)/shard_map/ppermute | solution.py:158
  84.8 2.3 %collective-permute-start.5 = (bf16[520,1024]{1,0:T(8,128)(2,1)}, bf16[520,1024]{1,0:T(8,128)(2,1)}, u32[]{:S(2)}, u32[]{:S(2)}) collective-permute-start(bf16[520,1024]{1,0:T(8,128)(2,1)} %collective-permute-done.4), channel_id=1, source_target_pairs={{4,0},{8,4},{20,16},{24,20},{36,32},{40,36},{52,48},{56,52},{68,64... | collective-permute-start | bytes 3194888 | tf_op jit(solution)/shard_map/ppermute | solution.py:158
  87.2 1.4 broadcast_select_fusion.refs_3_
  88.6 1.7 %broadcast_select_fusion.1.refs_2_ = bf16[520,1024]{1,0:T(8,128)(2,1)S(1)} fusion(bf16[520,1024]{1,0:T(8,128)(2,1)} %collective-permute-done.8, bf16[520,1024]{1,0:T(8,128)(2,1)} %collective-permute-done.6, pred[]{:T(512)S(6)} %eq.5), kind=kLoop, calls=%fused_computation.16 | loop fusion | flops 532480 | bytes 3194881 | tf_op jit(solution)/shard_map/jit(_where)/select_n | solution.py:172
  90.4 0.9 copy-done.5
  91.4 0.1 slice.128
  91.5 0.1 copy.25
  91.6 0.1 copy.21
  91.7 0.1 broadcast_compare_fusion
  91.8 0.6 reshape.255.flags_ref
  92.4 0.6 concatenate.43.refs_5_
  93.0 0.7 broadcast_in_dim.17.refs_7_
  93.7 0.7 broadcast_in_dim.18.refs_8_
  94.4 1.1 broadcast_in_dim.19.refs_9_
  95.6 34.8 %shard_map.85 = (f32[512,128]{1,0:T(8,128)}, f32[512,128]{1,0:T(8,128)}, f32[512,512]{1,0:T(8,128)}) custom-call(s32[16]{0:T(128)} %reshape.255.flags_ref, bf16[512,512]{1,0:T(8,128)(2,1)} %get-tuple-element.57.q_ref, bf16[520,1024]{1,0:T(8,128)(2,1)} %copy-done.6, bf16[520,1024]{1,0:T(8,128)(2,1)} %collective-permute-done.3.refs_1_, ...), custom_call_target="tpu_custom_call" | custom-call | flops 2147483648 | bytes 8388608 | tf_op jit(solution)/shard_map/pallas_call | solution.py:134
  130.4 1.4 broadcast_select_fusion.2.refs_0_
  131.7 0.5 broadcast.176
  132.3 0.6 fusion.27
  132.8 0.1 slice.122
  132.9 0.1 copy.24
  133.1 0.6 reshape.253.flags_ref
  133.7 0.6 concatenate.41.refs_2_
  134.3 13.8 %shard_map.86 = (f32[512,128]{1,0:T(8,128)}, f32[512,128]{1,0:T(8,128)}, f32[512,512]{1,0:T(8,128)}) custom-call(s32[4]{0:T(128)} %reshape.253.flags_ref, bf16[512,512]{1,0:T(8,128)(2,1)} %get-tuple-element.57.q_ref, bf16[520,1024]{1,0:T(8,128)(2,1)} %copy-done.3, s32[512,1]{1,0:T(8,128)} %copy.23.refs_4_.refs_1_, s32[8,512]{1,0:T(8,128)} %concatenate.41.refs_2_, ...), custom_call_target="tpu_custom_call" | custom-call | flops 536870912 | bytes 5242880 | tf_op jit(solution)/shard_map/pallas_call | solution.py:134
  148.1 1.5 broadcast_in_dim.20
  149.7 1.4 fusion.9
  151.2 0.7 convolution_convert_fusion
  151.9 0.1 collective-permute-start.10
  152.0 0.7 convolution_convert_fusion.1
  152.8 1.9 %collective-permute-done.10 = bf16[2,128,2048]{2,1,0:T(8,128)(2,1)S(1)} collective-permute-done((bf16[2,128,2048]{2,1,0:T(8,128)(2,1)S(1)}, bf16[2,128,2048]{2,1,0:T(8,128)(2,1)S(1)}, u32[]{:S(2)}, u32[]{:S(2)}) %collective-permute-start.10) | collective-permute-done | bytes 1048608 | tf_op jit(solution)/shard_map/ppermute | solution.py:26
  154.7 0.4 convert_add_fusion
  155.1 1.5 collective-permute-start.11
  156.6 14.1 %collective-permute-done.11 = bf16[128,2048]{1,0:T(8,128)(2,1)S(1)} collective-permute-done((bf16[128,2048]{1,0:T(8,128)(2,1)S(1)}, bf16[128,2048]{1,0:T(8,128)(2,1)S(1)}, u32[]{:S(2)}, u32[]{:S(2)}) %collective-permute-start.11) | collective-permute-done | bytes 524320 | tf_op jit(solution)/shard_map/ppermute | solution.py:26
  170.7 1.0 fusion.8
  (50 shorter events, 0.6 us)
Async XLA Ops:
  0.6 150.5 %copy-start = (bf16[512,2048]{1,0:T(8,128)(2,1)S(1)}, bf16[512,2048]{1,0:T(8,128)(2,1)}, u32[]{:S(2)}) copy-start(bf16[512,2048]{1,0:T(8,128)(2,1)} %param.16) | copy-start | bytes 6291460
  4.8 11.2 %collective-permute-start = (bf16[128,2048]{1,0:T(8,128)(2,1)S(1)}, bf16[128,2048]{1,0:T(8,128)(2,1)S(1)}, u32[]{:S(2)}, u32[]{:S(2)}) collective-permute-start(bf16[128,2048]{1,0:T(8,128)(2,1)S(1)} %fusion.6), channel_id=1, source_target_pairs={{0,1},{1,0},{2,3},{3,2},{4,5},{5,4},{6,7},{7,6},{8,9},{9,8},{10,11... | collective-permute-start | bytes 1572872 | tf_op jit(solution)/shard_map/ppermute | solution.py:26
  4.9 16.7 %collective-permute-start.1 = (bf16[128,2048]{1,0:T(8,128)(2,1)S(1)}, bf16[128,2048]{1,0:T(8,128)(2,1)}, u32[]{:S(2)}, u32[]{:S(2)}) collective-permute-start(bf16[128,2048]{1,0:T(8,128)(2,1)S(1)} %fusion.6), channel_id=1, source_target_pairs={{0,2},{1,3},{2,0},{3,1},{4,6},{5,7},{6,4},{7,5},{8,10},{9,11},{10,... | collective-permute-start | bytes 1572872 | tf_op jit(solution)/shard_map/ppermute | solution.py:26
  16.0 0.8 copy-start.10
  16.8 5.1 %copy-start.7 = (s32[512]{0:T(512)S(1)}, s32[512]{0:T(512)}, u32[]{:S(2)}) copy-start(s32[512]{0:T(512)} %param.17) | copy-start | bytes 6148
  21.6 2.3 %collective-permute-start.2 = (bf16[128,2048]{1,0:T(8,128)(2,1)}, bf16[128,2048]{1,0:T(8,128)(2,1)}, u32[]{:S(2)}, u32[]{:S(2)}) collective-permute-start(bf16[128,2048]{1,0:T(8,128)(2,1)} %collective-permute-done.1), channel_id=1, source_target_pairs={{0,1},{1,0},{2,3},{3,2},{4,5},{5,4},{6,7},{7,6},{8,9},{9,8},{10,11... | collective-permute-start | bytes 1572872 | tf_op jit(solution)/shard_map/ppermute | solution.py:26
  29.2 1.1 copy-start.1
  29.2 7.7 %copy-start.8 = (f32[4]{0:T(128)S(1)}, f32[4]{0:T(128)}, u32[]{:S(2)}) copy-start(f32[4]{0:T(128)} %param.15) | copy-start | bytes 52
  29.2 31.0 %copy-start.9 = (s32[4]{0:T(128)S(1)}, s32[4]{0:T(128)}, u32[]{:S(2)}) copy-start(s32[4]{0:T(128)} %constant.150.clone.1) | copy-start | bytes 52
  30.4 56.8 %copy-start.6 = (bf16[520,1024]{1,0:T(8,128)(2,1)}, bf16[520,1024]{1,0:T(8,128)(2,1)S(1)}, u32[]{:S(2)}) copy-start(bf16[520,1024]{1,0:T(8,128)(2,1)S(1)} %fusion.3.refs_0_) | copy-start | bytes 3194884
  30.4 27.6 %collective-permute-start.3 = (bf16[520,1024]{1,0:T(8,128)(2,1)S(1)}, bf16[520,1024]{1,0:T(8,128)(2,1)}, u32[]{:S(2)}, u32[]{:S(2)}) collective-permute-start(bf16[520,1024]{1,0:T(8,128)(2,1)S(1)} %fusion.3.refs_0_), channel_id=1, source_target_pairs={{0,16},{4,20},{8,24},{12,28},{16,32},{20,36},{24,40},{28,44},{32,4... | collective-permute-start | bytes 3194888 | tf_op jit(solution)/shard_map/ppermute | solution.py:158
  33.4 33.4 %collective-permute-start.6 = (bf16[520,1024]{1,0:T(8,128)(2,1)S(1)}, bf16[520,1024]{1,0:T(8,128)(2,1)}, u32[]{:S(2)}, u32[]{:S(2)}) collective-permute-start(bf16[520,1024]{1,0:T(8,128)(2,1)S(1)} %fusion.3.refs_0_), channel_id=1, source_target_pairs={{0,4},{4,8},{8,12},{16,20},{20,24},{24,28},{32,36},{36,40},{40,44}... | collective-permute-start | bytes 3194888 | tf_op jit(solution)/shard_map/ppermute | solution.py:158
  37.0 50.2 %collective-permute-start.9 = (bf16[520,1024]{1,0:T(8,128)(2,1)S(1)}, bf16[520,1024]{1,0:T(8,128)(2,1)}, u32[]{:S(2)}, u32[]{:S(2)}) collective-permute-start(bf16[520,1024]{1,0:T(8,128)(2,1)S(1)} %fusion.3.refs_0_), channel_id=1, source_target_pairs={{0,12},{16,28},{32,44},{48,60},{64,76},{80,92},{96,108},{112,124},... | collective-permute-start | bytes 3194888 | tf_op jit(solution)/shard_map/ppermute | solution.py:158
  57.9 26.9 %collective-permute-start.4 = (bf16[520,1024]{1,0:T(8,128)(2,1)}, bf16[520,1024]{1,0:T(8,128)(2,1)}, u32[]{:S(2)}, u32[]{:S(2)}) collective-permute-start(bf16[520,1024]{1,0:T(8,128)(2,1)} %collective-permute-done.3.refs_1_), channel_id=1, source_target_pairs={{4,0},{8,4},{12,8},{20,16},{24,20},{28,24},{36,32},{40,36},{44,40}... | collective-permute-start | bytes 3194888 | tf_op jit(solution)/shard_map/ppermute | solution.py:158
  60.3 28.3 %collective-permute-start.8 = (bf16[520,1024]{1,0:T(8,128)(2,1)}, bf16[520,1024]{1,0:T(8,128)(2,1)}, u32[]{:S(2)}, u32[]{:S(2)}) collective-permute-start(bf16[520,1024]{1,0:T(8,128)(2,1)} %collective-permute-done.3.refs_1_), channel_id=1, source_target_pairs={{12,0},{28,16},{44,32},{60,48},{76,64},{92,80},{108,96},{124,112},... | collective-permute-start | bytes 3194888 | tf_op jit(solution)/shard_map/ppermute | solution.py:158
  66.8 63.6 %collective-permute-start.7 = (bf16[520,1024]{1,0:T(8,128)(2,1)}, bf16[520,1024]{1,0:T(8,128)(2,1)}, u32[]{:S(2)}, u32[]{:S(2)}) collective-permute-start(bf16[520,1024]{1,0:T(8,128)(2,1)} %collective-permute-done.6), channel_id=1, source_target_pairs={{4,8},{8,12},{20,24},{24,28},{36,40},{40,44},{52,56},{56,60},{68,7... | collective-permute-start | bytes 3194888 | tf_op jit(solution)/shard_map/ppermute | solution.py:158
  84.8 45.5 %collective-permute-start.5 = (bf16[520,1024]{1,0:T(8,128)(2,1)}, bf16[520,1024]{1,0:T(8,128)(2,1)}, u32[]{:S(2)}, u32[]{:S(2)}) collective-permute-start(bf16[520,1024]{1,0:T(8,128)(2,1)} %collective-permute-done.4), channel_id=1, source_target_pairs={{4,0},{8,4},{20,16},{24,20},{36,32},{40,36},{52,48},{56,52},{68,64... | collective-permute-start | bytes 3194888 | tf_op jit(solution)/shard_map/ppermute | solution.py:158
  88.6 7.0 %copy-start.4 = (bf16[520,1024]{1,0:T(8,128)(2,1)}, bf16[520,1024]{1,0:T(8,128)(2,1)S(1)}, u32[]{:S(2)}) copy-start(bf16[520,1024]{1,0:T(8,128)(2,1)S(1)} %broadcast_select_fusion.refs_3_) | copy-start | bytes 3194884
  90.3 1.0 copy-start.5
  131.7 2.6 %copy-start.3 = (bf16[520,1024]{1,0:T(8,128)(2,1)}, bf16[520,1024]{1,0:T(8,128)(2,1)S(1)}, u32[]{:S(2)}) copy-start(bf16[520,1024]{1,0:T(8,128)(2,1)S(1)} %broadcast_select_fusion.2.refs_0_) | copy-start | bytes 3194884
  151.9 2.7 %collective-permute-start.10 = (bf16[2,128,2048]{2,1,0:T(8,128)(2,1)S(1)}, bf16[2,128,2048]{2,1,0:T(8,128)(2,1)S(1)}, u32[]{:S(2)}, u32[]{:S(2)}) collective-permute-start(bf16[2,128,2048]{2,1,0:T(8,128)(2,1)S(1)} %bitcast.50), channel_id=1, source_target_pairs={{0,1},{1,0},{2,3},{3,2},{4,5},{5,4},{6,7},{7,6},{8,9},{9,8},{10,11... | collective-permute-start | bytes 3145736 | tf_op jit(solution)/shard_map/ppermute | solution.py:26
  154.7 16.0 %copy-start.2 = (bf16[128,2048]{1,0:T(8,128)(2,1)S(1)}, bf16[128,2048]{1,0:T(8,128)(2,1)}, u32[]{:S(2)}) copy-start(bf16[128,2048]{1,0:T(8,128)(2,1)} %param.12) | copy-start | bytes 1572868
  155.1 15.6 %collective-permute-start.11 = (bf16[128,2048]{1,0:T(8,128)(2,1)S(1)}, bf16[128,2048]{1,0:T(8,128)(2,1)S(1)}, u32[]{:S(2)}, u32[]{:S(2)}) collective-permute-start(bf16[128,2048]{1,0:T(8,128)(2,1)S(1)} %fusion.16), channel_id=1, source_target_pairs={{0,2},{1,3},{2,0},{3,1},{4,6},{5,7},{6,4},{7,5},{8,10},{9,11},{10,... | collective-permute-start | bytes 1572872 | tf_op jit(solution)/shard_map/ppermute | solution.py:26

commit v11 on v10

--- a/solution.py
+++ b/solution.py
@@ -68,11 +68,9 @@
                 def one_head(h, carry):
                     lanes = pl.multiple_of(h * HD, HD)
                     q = q_ref[rows, pl.ds(lanes, HD)]
-                    k = bufs[i][pl.ds(t * TK, TK), pl.ds(lanes, HD)]
+                    k_t = bufs[i][pl.ds(lanes, HD), pl.ds(t * TK, TK)]
                     v = bufs[i][pl.ds(t * TK, TK), pl.ds(width + lanes, HD)]
-                    s = lax.dot_general(
-                        q, k, (((1,), (1,)), ((), ())), preferred_element_type=jnp.float32
-                    )
+                    s = jnp.dot(q, k_t, preferred_element_type=jnp.float32)
                     s = s * scale + bias_ref[pl.ds(i * heads + h, 1), pl.ds(t * TK, TK)]
                     s = jnp.where(valid, s, NEG_FILL)
                     m_prev = m_sc[h, rows, :]
@@ -203,7 +201,7 @@
     key_cache = qkv_rows[:, width_local : 2 * width_local]
     value_cache = qkv_rows[:, 2 * width_local :]
 
-    kv_own = qkv_rows[:, width_local:]
+    kv_own = jnp.concatenate([key_cache.T, value_cache], axis=1)
     seg_row = jnp.zeros((8, kv_own.shape[1]), jnp.bfloat16).at[0, :block_len].set(
         seg_ids.astype(jnp.bfloat16)
     )

time: 172 us -> 174 us (1.012)
  the two profiles are of different devices: /device:TPU:202 before, /device:TPU:176 now
where the time goes in v11:
time: 174 us
  waiting for transfers between devices  52.7 us (30%)
  Pallas kernels  46.6 us (27%)
  starting transfers between devices  25.1 us (14%)
  local copies, waits for them, and re-layouts  21.9 us (13%)
  other arithmetic  15.1 us (9%)
  matrix products  11.2 us (6%)
    pallas_call x2, Pallas kernels, attention_part(): pl.pallas_call(functools.partial(part_kernel, n_buf, own), out_shape=(jax...  46.6 us
    ppermute x7, waiting for transfers between devices, moved(): return lax.ppermute(value, 'seq', pairs)  34.5 us
    ppermute x7, starting transfers between devices, moved(): return lax.ppermute(value, 'seq', pairs)  20.2 us
    ppermute x5, waiting for transfers between devices, swapped(): lax.ppermute(value, axis, [(source, source ^ mask) for source in range(co...  18.2 us
    unnamed x23, local copies, waits for them, and re-layouts  9.88 us
    dot_general x2, matrix products, project_rows(): jnp.dot(rows, joined, preferred_element_type=jnp.float32)  9.75 us
    ppermute x5, starting transfers between devices, swapped(): lax.ppermute(value, axis, [(source, source ^ mask) for source in range(co...  4.9 us
  transfers between devices with their start and end apart: 12, of which 5 were waited for; matrix products, arithmetic and copies ran while one was open for 14% of the time, Pallas kernels for 19%

profile of v11, /device:TPU:176, one launch (start us, length us, event | category | flops | bytes accessed | tf_op | source)
XLA Modules:
  0.0 173.6 jit_solution(3554882840080344588)
XLA Ops:
  0.6 1.3 convert_reduce_fusion
  2.0 1.3 fusion.4
  3.3 1.4 fusion.6
  4.8 0.1 collective-permute-start
  4.9 3.1 %collective-permute-start.1 = (bf16[128,2048]{1,0:T(8,128)(2,1)S(1)}, bf16[128,2048]{1,0:T(8,128)(2,1)}, u32[]{:S(2)}, u32[]{:S(2)}) collective-permute-start(bf16[128,2048]{1,0:T(8,128)(2,1)S(1)} %fusion.6), channel_id=1, source_target_pairs={{0,2},{1,3},{2,0},{3,1},{4,6},{5,7},{6,4},{7,5},{8,10},{9,11},{10,... | collective-permute-start | bytes 1572872 | tf_op jit(solution)/shard_map/ppermute | solution.py:26
  8.0 8.8 %copy.20 = bf16[2048,3,512]{0,2,1:T(8,128)(2,1)} copy(bf16[2048,3,512]{2,0,1:T(8,128)(2,1)} %param.14) | data formatting | bytes 12582912 | tf_op args[2]
  16.8 0.8 copy-done.9
  17.6 4.8 %convolution_convert_fusion.3 = bf16[256,1536]{1,0:T(8,128)(2,1)S(1)} fusion(bf16[2048,1536]{0,1:T(8,128)(2,1)} %bitcast.45, bf16[128,2048]{1,0:T(8,128)(2,1)} %copy-done.9, bf16[128,2048]{1,0:T(8,128)(2,1)S(1)} %fusion.6), kind=kOutput, calls=%fused_computation.3 | convolution fusion | flops 1613103104 | bytes 8126464 | tf_op jit(solution)/shard_map/dot_general | solution.py:188
  22.4 0.2 collective-permute-start.2
  22.7 2.1 %collective-permute-done.2 = bf16[128,2048]{1,0:T(8,128)(2,1)} collective-permute-done((bf16[128,2048]{1,0:T(8,128)(2,1)}, bf16[128,2048]{1,0:T(8,128)(2,1)}, u32[]{:S(2)}, u32[]{:S(2)}) %collective-permute-start.2) | collective-permute-done | bytes 524320 | tf_op jit(solution)/shard_map/ppermute | solution.py:26
  24.8 4.9 %convolution_convert_fusion.2 = bf16[256,1536]{1,0:T(8,128)(2,1)S(1)} fusion(bf16[2048,1536]{0,1:T(8,128)(2,1)} %bitcast.46, bf16[128,2048]{1,0:T(8,128)(2,1)} %collective-permute-done.2, bf16[128,2048]{1,0:T(8,128)(2,1)} %collective-permute-done.1), kind=kOutput, calls=%fused_computation.2 | convolution fusion | flops 1613103104 | bytes 8126464 | tf_op jit(solution)/shard_map/dot_general | solution.py:188
  29.7 0.1 pad_maximum_fusion
  29.8 0.1 dynamic-slice_bitcast_fusion.3
  30.0 0.1 pad_maximum_fusion.1
  30.1 1.1 fusion.28
  31.2 1.5 copy.21
  32.6 1.1 fusion.3.refs_0_
  33.8 2.9 %collective-permute-start.3 = (bf16[520,1024]{1,0:T(8,128)(2,1)}, bf16[520,1024]{1,0:T(8,128)(2,1)}, u32[]{:S(2)}, u32[]{:S(2)}) collective-permute-start(bf16[520,1024]{1,0:T(8,128)(2,1)} %fusion.3.refs_0_), channel_id=1, source_target_pairs={{0,16},{4,20},{8,24},{12,28},{16,32},{20,36},{24,40},{28,44},{32,4... | collective-permute-start | bytes 3194888 | tf_op jit(solution)/shard_map/ppermute | solution.py:156
  36.7 3.2 %collective-permute-start.6 = (bf16[520,1024]{1,0:T(8,128)(2,1)}, bf16[520,1024]{1,0:T(8,128)(2,1)}, u32[]{:S(2)}, u32[]{:S(2)}) collective-permute-start(bf16[520,1024]{1,0:T(8,128)(2,1)} %fusion.3.refs_0_), channel_id=1, source_target_pairs={{0,4},{4,8},{8,12},{16,20},{20,24},{24,28},{32,36},{36,40},{40,44}... | collective-permute-start | bytes 3194888 | tf_op jit(solution)/shard_map/ppermute | solution.py:156
  39.9 1.6 collective-permute-start.9
  41.6 20.0 %collective-permute-done.3.refs_1_ = bf16[520,1024]{1,0:T(8,128)(2,1)} collective-permute-done((bf16[520,1024]{1,0:T(8,128)(2,1)}, bf16[520,1024]{1,0:T(8,128)(2,1)}, u32[]{:S(2)}, u32[]{:S(2)}) %collective-permute-start.3) | collective-permute-done | bytes 1064992 | tf_op jit(solution)/shard_map/ppermute | solution.py:156
  61.5 2.3 %collective-permute-start.4 = (bf16[520,1024]{1,0:T(8,128)(2,1)}, bf16[520,1024]{1,0:T(8,128)(2,1)}, u32[]{:S(2)}, u32[]{:S(2)}) collective-permute-start(bf16[520,1024]{1,0:T(8,128)(2,1)} %collective-permute-done.3.refs_1_), channel_id=1, source_target_pairs={{4,0},{8,4},{12,8},{20,16},{24,20},{28,24},{36,32},{40,36},{44,40}... | collective-permute-start | bytes 3194888 | tf_op jit(solution)/shard_map/ppermute | solution.py:156
  63.9 0.1 broadcast_multiply_fusion.1
  64.0 1.7 collective-permute-start.8
  65.8 0.9 copy.26.refs_4_.refs_1_
  66.7 0.1 mul.66
  66.8 0.6 concatenate.46.refs_3_
  67.4 0.1 slice_reduce_fusion
  67.5 0.7 broadcast_multiply_fusion.refs_6_
  68.2 5.1 %collective-permute-start.7 = (bf16[520,1024]{1,0:T(8,128)(2,1)}, bf16[520,1024]{1,0:T(8,128)(2,1)}, u32[]{:S(2)}, u32[]{:S(2)}) collective-permute-start(bf16[520,1024]{1,0:T(8,128)(2,1)} %collective-permute-done.6), channel_id=1, source_target_pairs={{4,8},{8,12},{20,24},{24,28},{36,40},{40,44},{52,56},{56,60},{68,7... | collective-permute-start | bytes 3194888 | tf_op jit(solution)/shard_map/ppermute | solution.py:156
  73.3 0.7 broadcast_select_fusion.5
  74.0 14.5 %collective-permute-done.4 = bf16[520,1024]{1,0:T(8,128)(2,1)} collective-permute-done((bf16[520,1024]{1,0:T(8,128)(2,1)}, bf16[520,1024]{1,0:T(8,128)(2,1)}, u32[]{:S(2)}, u32[]{:S(2)}) %collective-permute-start.4) | collective-permute-done | bytes 1064992 | tf_op jit(solution)/shard_map/ppermute | solution.py:156
  88.5 3.3 %collective-permute-start.5 = (bf16[520,1024]{1,0:T(8,128)(2,1)}, bf16[520,1024]{1,0:T(8,128)(2,1)}, u32[]{:S(2)}, u32[]{:S(2)}) collective-permute-start(bf16[520,1024]{1,0:T(8,128)(2,1)} %collective-permute-done.4), channel_id=1, source_target_pairs={{4,0},{8,4},{20,16},{24,20},{36,32},{40,36},{52,48},{56,52},{68,64... | collective-permute-start | bytes 3194888 | tf_op jit(solution)/shard_map/ppermute | solution.py:156
  91.8 1.3 broadcast_select_fusion.refs_3_
  93.2 1.7 broadcast_select_fusion.1.refs_2_
  95.1 0.1 slice.125
  95.1 0.1 copy.28
  95.2 0.1 copy.24
  95.3 0.1 broadcast_compare_fusion
  95.5 0.7 reshape.255.flags_ref
  96.1 0.6 concatenate.47.refs_5_
  96.7 0.7 broadcast_in_dim.17.refs_7_
  97.4 0.7 broadcast_in_dim.18.refs_8_
  98.2 1.1 broadcast_in_dim.19.refs_9_
  99.3 33.4 %shard_map.85 = (f32[512,128]{1,0:T(8,128)}, f32[512,128]{1,0:T(8,128)}, f32[512,512]{1,0:T(8,128)}) custom-call(s32[16]{0:T(128)} %reshape.255.flags_ref, bf16[512,512]{1,0:T(8,128)(2,1)} %get-tuple-element.55.q_ref, bf16[520,1024]{1,0:T(8,128)(2,1)} %fusion.3.refs_0_, bf16[520,1024]{1,0:T(8,128)(2,1)} %collective-permute-done.3.refs_1_, ...), custom_call_target="tpu_custom_call" | custom-call | flops 2147483648 | bytes 8388608 | tf_op jit(solution)/shard_map/pallas_call | solution.py:132
  132.7 1.4 broadcast_select_fusion.2.refs_0_
  134.0 0.6 broadcast.176
  134.7 0.7 fusion.27
  135.4 0.1 slice.119
  135.5 0.1 copy.27
  135.6 0.1 compare_convert_fusion
  135.6 0.6 reshape.253.flags_ref
  136.2 0.6 concatenate.45.refs_2_
  136.9 13.2 %shard_map.86 = (f32[512,128]{1,0:T(8,128)}, f32[512,128]{1,0:T(8,128)}, f32[512,512]{1,0:T(8,128)}) custom-call(s32[4]{0:T(128)} %reshape.253.flags_ref, bf16[512,512]{1,0:T(8,128)(2,1)} %get-tuple-element.55.q_ref, bf16[520,1024]{1,0:T(8,128)(2,1)} %copy-done.2, s32[512,1]{1,0:T(8,128)} %copy.26.refs_4_.refs_1_, s32[8,512]{1,0:T(8,128)} %concatenate.45.refs_2_, ...), custom_call_target="tpu_custom_call" | custom-call | flops 536870912 | bytes 5242880 | tf_op jit(solution)/shard_map/pallas_call | solution.py:132
  150.1 1.5 broadcast_in_dim.20
  151.6 1.4 fusion.9
  153.1 0.7 convolution_convert_fusion
  153.8 0.1 collective-permute-start.10
  153.9 0.7 convolution_convert_fusion.1
  154.7 1.9 %collective-permute-done.10 = bf16[2,128,2048]{2,1,0:T(8,128)(2,1)S(1)} collective-permute-done((bf16[2,128,2048]{2,1,0:T(8,128)(2,1)S(1)}, bf16[2,128,2048]{2,1,0:T(8,128)(2,1)S(1)}, u32[]{:S(2)}, u32[]{:S(2)}) %collective-permute-start.10) | collective-permute-done | bytes 1048608 | tf_op jit(solution)/shard_map/ppermute | solution.py:26
  156.6 0.4 convert_add_fusion
  157.0 1.4 collective-permute-start.11
  158.4 14.2 %collective-permute-done.11 = bf16[128,2048]{1,0:T(8,128)(2,1)S(1)} collective-permute-done((bf16[128,2048]{1,0:T(8,128)(2,1)S(1)}, bf16[128,2048]{1,0:T(8,128)(2,1)S(1)}, u32[]{:S(2)}, u32[]{:S(2)}) %collective-permute-start.11) | collective-permute-done | bytes 524320 | tf_op jit(solution)/shard_map/ppermute | solution.py:26
  172.6 1.0 fusion.8
  (48 shorter events, 0.5 us)
Async XLA Ops:
  0.6 152.5 %copy-start = (bf16[512,2048]{1,0:T(8,128)(2,1)S(1)}, bf16[512,2048]{1,0:T(8,128)(2,1)}, u32[]{:S(2)}) copy-start(bf16[512,2048]{1,0:T(8,128)(2,1)} %param.16) | copy-start | bytes 6291460
  4.8 12.1 %collective-permute-start = (bf16[128,2048]{1,0:T(8,128)(2,1)S(1)}, bf16[128,2048]{1,0:T(8,128)(2,1)S(1)}, u32[]{:S(2)}, u32[]{:S(2)}) collective-permute-start(bf16[128,2048]{1,0:T(8,128)(2,1)S(1)} %fusion.6), channel_id=1, source_target_pairs={{0,1},{1,0},{2,3},{3,2},{4,5},{5,4},{6,7},{7,6},{8,9},{9,8},{10,11... | collective-permute-start | bytes 1572872 | tf_op jit(solution)/shard_map/ppermute | solution.py:26
  4.9 17.6 %collective-permute-start.1 = (bf16[128,2048]{1,0:T(8,128)(2,1)S(1)}, bf16[128,2048]{1,0:T(8,128)(2,1)}, u32[]{:S(2)}, u32[]{:S(2)}) collective-permute-start(bf16[128,2048]{1,0:T(8,128)(2,1)S(1)} %fusion.6), channel_id=1, source_target_pairs={{0,2},{1,3},{2,0},{3,1},{4,6},{5,7},{6,4},{7,5},{8,10},{9,11},{10,... | collective-permute-start | bytes 1572872 | tf_op jit(solution)/shard_map/ppermute | solution.py:26
  16.8 0.8 copy-start.9
  17.6 5.1 %copy-start.6 = (s32[512]{0:T(512)S(1)}, s32[512]{0:T(512)}, u32[]{:S(2)}) copy-start(s32[512]{0:T(512)} %param.17) | copy-start | bytes 6148
  22.4 2.3 %collective-permute-start.2 = (bf16[128,2048]{1,0:T(8,128)(2,1)}, bf16[128,2048]{1,0:T(8,128)(2,1)}, u32[]{:S(2)}, u32[]{:S(2)}) collective-permute-start(bf16[128,2048]{1,0:T(8,128)(2,1)} %collective-permute-done.1), channel_id=1, source_target_pairs={{0,1},{1,0},{2,3},{3,2},{4,5},{5,4},{6,7},{7,6},{8,9},{9,8},{10,11... | collective-permute-start | bytes 1572872 | tf_op jit(solution)/shard_map/ppermute | solution.py:26
  31.2 62.0 %copy-start.3 = (bf16[512,512]{1,0:T(8,128)(2,1)}, bf16[512,512]{1,0:T(8,128)(2,1)S(1)}, u32[]{:S(2)}) copy-start(bf16[512,512]{1,0:T(8,128)(2,1)S(1)} %get-tuple-element.56) | copy-start | bytes 1572868
  31.2 32.7 %copy-start.7 = (f32[4]{0:T(128)S(1)}, f32[4]{0:T(128)}, u32[]{:S(2)}) copy-start(f32[4]{0:T(128)} %param.15) | copy-start | bytes 52
  31.2 34.5 %copy-start.8 = (s32[4]{0:T(128)S(1)}, s32[4]{0:T(128)}, u32[]{:S(2)}) copy-start(s32[4]{0:T(128)} %constant.150.clone.1) | copy-start | bytes 52
  33.8 27.8 %collective-permute-start.3 = (bf16[520,1024]{1,0:T(8,128)(2,1)}, bf16[520,1024]{1,0:T(8,128)(2,1)}, u32[]{:S(2)}, u32[]{:S(2)}) collective-permute-start(bf16[520,1024]{1,0:T(8,128)(2,1)} %fusion.3.refs_0_), channel_id=1, source_target_pairs={{0,16},{4,20},{8,24},{12,28},{16,32},{20,36},{24,40},{28,44},{32,4... | collective-permute-start | bytes 3194888 | tf_op jit(solution)/shard_map/ppermute | solution.py:156
  36.7 31.5 %collective-permute-start.6 = (bf16[520,1024]{1,0:T(8,128)(2,1)}, bf16[520,1024]{1,0:T(8,128)(2,1)}, u32[]{:S(2)}, u32[]{:S(2)}) collective-permute-start(bf16[520,1024]{1,0:T(8,128)(2,1)} %fusion.3.refs_0_), channel_id=1, source_target_pairs={{0,4},{4,8},{8,12},{16,20},{20,24},{24,28},{32,36},{36,40},{40,44}... | collective-permute-start | bytes 3194888 | tf_op jit(solution)/shard_map/ppermute | solution.py:156
  39.9 51.9 %collective-permute-start.9 = (bf16[520,1024]{1,0:T(8,128)(2,1)}, bf16[520,1024]{1,0:T(8,128)(2,1)}, u32[]{:S(2)}, u32[]{:S(2)}) collective-permute-start(bf16[520,1024]{1,0:T(8,128)(2,1)} %fusion.3.refs_0_), channel_id=1, source_target_pairs={{0,12},{16,28},{32,44},{48,60},{64,76},{80,92},{96,108},{112,124},... | collective-permute-start | bytes 3194888 | tf_op jit(solution)/shard_map/ppermute | solution.py:156
  61.5 26.9 %collective-permute-start.4 = (bf16[520,1024]{1,0:T(8,128)(2,1)}, bf16[520,1024]{1,0:T(8,128)(2,1)}, u32[]{:S(2)}, u32[]{:S(2)}) collective-permute-start(bf16[520,1024]{1,0:T(8,128)(2,1)} %collective-permute-done.3.refs_1_), channel_id=1, source_target_pairs={{4,0},{8,4},{12,8},{20,16},{24,20},{28,24},{36,32},{40,36},{44,40}... | collective-permute-start | bytes 3194888 | tf_op jit(solution)/shard_map/ppermute | solution.py:156
  64.0 29.2 %collective-permute-start.8 = (bf16[520,1024]{1,0:T(8,128)(2,1)}, bf16[520,1024]{1,0:T(8,128)(2,1)}, u32[]{:S(2)}, u32[]{:S(2)}) collective-permute-start(bf16[520,1024]{1,0:T(8,128)(2,1)} %collective-permute-done.3.refs_1_), channel_id=1, source_target_pairs={{12,0},{28,16},{44,32},{60,48},{76,64},{92,80},{108,96},{124,112},... | collective-permute-start | bytes 3194888 | tf_op jit(solution)/shard_map/ppermute | solution.py:156
  68.2 64.5 %collective-permute-start.7 = (bf16[520,1024]{1,0:T(8,128)(2,1)}, bf16[520,1024]{1,0:T(8,128)(2,1)}, u32[]{:S(2)}, u32[]{:S(2)}) collective-permute-start(bf16[520,1024]{1,0:T(8,128)(2,1)} %collective-permute-done.6), channel_id=1, source_target_pairs={{4,8},{8,12},{20,24},{24,28},{36,40},{40,44},{52,56},{56,60},{68,7... | collective-permute-start | bytes 3194888 | tf_op jit(solution)/shard_map/ppermute | solution.py:156
  88.5 44.2 %collective-permute-start.5 = (bf16[520,1024]{1,0:T(8,128)(2,1)}, bf16[520,1024]{1,0:T(8,128)(2,1)}, u32[]{:S(2)}, u32[]{:S(2)}) collective-permute-start(bf16[520,1024]{1,0:T(8,128)(2,1)} %collective-permute-done.4), channel_id=1, source_target_pairs={{4,0},{8,4},{20,16},{24,20},{36,32},{40,36},{52,48},{56,52},{68,64... | collective-permute-start | bytes 3194888 | tf_op jit(solution)/shard_map/ppermute | solution.py:156
  93.2 1.8 %copy-start.4 = (bf16[520,1024]{1,0:T(8,128)(2,1)}, bf16[520,1024]{1,0:T(8,128)(2,1)S(1)}, u32[]{:S(2)}) copy-start(bf16[520,1024]{1,0:T(8,128)(2,1)S(1)} %broadcast_select_fusion.refs_3_) | copy-start | bytes 3194884
  94.9 4.4 %copy-start.5 = (bf16[520,1024]{1,0:T(8,128)(2,1)}, bf16[520,1024]{1,0:T(8,128)(2,1)S(1)}, u32[]{:S(2)}) copy-start(bf16[520,1024]{1,0:T(8,128)(2,1)S(1)} %broadcast_select_fusion.1.refs_2_) | copy-start | bytes 3194884
  134.0 2.8 %copy-start.2 = (bf16[520,1024]{1,0:T(8,128)(2,1)}, bf16[520,1024]{1,0:T(8,128)(2,1)S(1)}, u32[]{:S(2)}) copy-start(bf16[520,1024]{1,0:T(8,128)(2,1)S(1)} %broadcast_select_fusion.2.refs_0_) | copy-start | bytes 3194884
  153.8 2.7 %collective-permute-start.10 = (bf16[2,128,2048]{2,1,0:T(8,128)(2,1)S(1)}, bf16[2,128,2048]{2,1,0:T(8,128)(2,1)S(1)}, u32[]{:S(2)}, u32[]{:S(2)}) collective-permute-start(bf16[2,128,2048]{2,1,0:T(8,128)(2,1)S(1)} %bitcast.52), channel_id=1, source_target_pairs={{0,1},{1,0},{2,3},{3,2},{4,5},{5,4},{6,7},{7,6},{8,9},{9,8},{10,11... | collective-permute-start | bytes 3145736 | tf_op jit(solution)/shard_map/ppermute | solution.py:26
  156.6 16.0 %copy-start.1 = (bf16[128,2048]{1,0:T(8,128)(2,1)S(1)}, bf16[128,2048]{1,0:T(8,128)(2,1)}, u32[]{:S(2)}) copy-start(bf16[128,2048]{1,0:T(8,128)(2,1)} %param.12) | copy-start | bytes 1572868
  157.0 15.6 %collective-permute-start.11 = (bf16[128,2048]{1,0:T(8,128)(2,1)S(1)}, bf16[128,2048]{1,0:T(8,128)(2,1)S(1)}, u32[]{:S(2)}, u32[]{:S(2)}) collective-permute-start(bf16[128,2048]{1,0:T(8,128)(2,1)S(1)} %fusion.16), channel_id=1, source_target_pairs={{0,2},{1,3},{2,0},{3,1},{4,6},{5,7},{6,4},{7,5},{8,10},{9,11},{10,... | collective-permute-start | bytes 1572872 | tf_op jit(solution)/shard_map/ppermute | solution.py:26

commit v12 on v11

--- a/solution.py
+++ b/solution.py
@@ -189,9 +189,8 @@
 
     from_partner = swapped(normed, "head", 1)
     from_cross = swapped(normed, "head", 2)
+    from_partner_cross = swapped(from_cross, "head", 1)
     near = project_rows(jnp.concatenate([normed, from_partner], axis=0))
-    near, from_cross = lax.optimization_barrier((near, from_cross))
-    from_partner_cross = swapped(from_cross, "head", 1)
     far = project_rows(jnp.concatenate([from_cross, from_partner_cross], axis=0))
     pieces = jnp.concatenate([near, far], axis=0).reshape(n_head, rows_dev, near.shape[1])
     qkv_rows = jnp.concatenate(

time: 174 us -> 169 us (0.971)
  the two profiles are of different devices: /device:TPU:176 before, /device:TPU:6 now
where the time goes in v12:
time: 169 us; the launch traced here: 166 us
  waiting for transfers between devices  64.1 us (38%)
  Pallas kernels  38 us (22%)
  local copies, waits for them, and re-layouts  21.2 us (13%)
  starting transfers between devices  19.3 us (11%)
  other arithmetic  14.7 us (9%)
  matrix products  8.24 us (5%)
    ppermute x7, waiting for transfers between devices, moved(): return lax.ppermute(value, 'seq', pairs)  42.9 us
    pallas_call x2, Pallas kernels, attention_part(): pl.pallas_call(functools.partial(part_kernel, n_buf, own), out_shape=(jax...  38 us
    ppermute x5, waiting for transfers between devices, swapped(): lax.ppermute(value, axis, [(source, source ^ mask) for source in range(co...  21.1 us
    ppermute x7, starting transfers between devices, moved(): return lax.ppermute(value, 'seq', pairs)  16.5 us
    unnamed x23, local copies, waits for them, and re-layouts  9.1 us
    dot_general x2, matrix products, project_rows(): jnp.dot(rows, joined, preferred_element_type=jnp.float32)  6.75 us
  transfers between devices with their start and end apart: 12, of which 6 were waited for; matrix products, arithmetic and copies ran while one was open for 15% of the time, Pallas kernels for 15%

profile of v12, /device:TPU:6, one launch (start us, length us, event | category | flops | bytes accessed | tf_op | source)
XLA Modules:
  0.0 166.5 jit_solution(12459927733785705890)
XLA Ops:
  0.7 1.3 convert_reduce_fusion
  2.0 1.3 fusion.4
  3.3 1.4 fusion.6
  4.8 1.5 collective-permute-start.1
  6.3 8.9 %copy.20 = bf16[2048,3,512]{0,2,1:T(8,128)(2,1)} copy(bf16[2048,3,512]{2,0,1:T(8,128)(2,1)} %param.14) | data formatting | bytes 12582912 | tf_op args[2]
  15.1 4.9 %collective-permute-done.1 = bf16[128,2048]{1,0:T(8,128)(2,1)S(1)} collective-permute-done((bf16[128,2048]{1,0:T(8,128)(2,1)S(1)}, bf16[128,2048]{1,0:T(8,128)(2,1)S(1)}, u32[]{:S(2)}, u32[]{:S(2)}) %collective-permute-start.1) | collective-permute-done | bytes 524320 | tf_op jit(solution)/shard_map/ppermute | solution.py:26
  20.0 4.9 %convolution_convert_fusion.3 = bf16[256,1536]{1,0:T(8,128)(2,1)S(1)} fusion(bf16[2048,1536]{0,1:T(8,128)(2,1)} %bitcast.45, bf16[128,2048]{1,0:T(8,128)(2,1)} %collective-permute-done, bf16[128,2048]{1,0:T(8,128)(2,1)S(1)} %fusion.6), kind=kOutput, calls=%fused_computation.3 | convolution fusion | flops 1613103104 | bytes 8126464 | tf_op jit(solution)/shard_map/dot_general | solution.py:188
  25.0 1.8 %convolution_convert_fusion.2 = bf16[256,1536]{1,0:T(8,128)(2,1)S(1)} fusion(bf16[2048,1536]{0,1:T(8,128)(2,1)S(1)} %bitcast.46, bf16[128,2048]{1,0:T(8,128)(2,1)S(1)} %collective-permute-done.2, bf16[128,2048]{1,0:T(8,128)(2,1)S(1)} %collective-permute-done.1), kind=kOutput, calls=%fused_computation.2 | convolution fusion | flops 1613103104 | bytes 8126464 | tf_op jit(solution)/shard_map/dot_general | solution.py:188
  26.8 0.1 pad_maximum_fusion
  26.9 0.1 dynamic-slice_bitcast_fusion.3
  27.1 0.1 pad_maximum_fusion.1
  27.2 1.1 fusion.28
  28.3 1.5 copy.21
  29.7 1.1 fusion.3.refs_0_
  30.9 3.8 %collective-permute-start.3 = (bf16[520,1024]{1,0:T(8,128)(2,1)}, bf16[520,1024]{1,0:T(8,128)(2,1)}, u32[]{:S(2)}, u32[]{:S(2)}) collective-permute-start(bf16[520,1024]{1,0:T(8,128)(2,1)} %fusion.3.refs_0_), channel_id=1, source_target_pairs={{0,16},{4,20},{8,24},{12,28},{16,32},{20,36},{24,40},{28,44},{32,4... | collective-permute-start | bytes 3194888 | tf_op jit(solution)/shard_map/ppermute | solution.py:156
  34.7 4.5 %collective-permute-start.6 = (bf16[520,1024]{1,0:T(8,128)(2,1)}, bf16[520,1024]{1,0:T(8,128)(2,1)}, u32[]{:S(2)}, u32[]{:S(2)}) collective-permute-start(bf16[520,1024]{1,0:T(8,128)(2,1)} %fusion.3.refs_0_), channel_id=1, source_target_pairs={{0,4},{4,8},{8,12},{16,20},{20,24},{24,28},{32,36},{36,40},{40,44}... | collective-permute-start | bytes 3194888 | tf_op jit(solution)/shard_map/ppermute | solution.py:156
  39.2 2.7 %collective-permute-start.9 = (bf16[520,1024]{1,0:T(8,128)(2,1)}, bf16[520,1024]{1,0:T(8,128)(2,1)}, u32[]{:S(2)}, u32[]{:S(2)}) collective-permute-start(bf16[520,1024]{1,0:T(8,128)(2,1)} %fusion.3.refs_0_), channel_id=1, source_target_pairs={{0,12},{16,28},{32,44},{48,60},{64,76},{80,92},{96,108},{112,124},... | collective-permute-start | bytes 3194888 | tf_op jit(solution)/shard_map/ppermute | solution.py:156
  41.9 21.5 %collective-permute-done.3.refs_1_ = bf16[520,1024]{1,0:T(8,128)(2,1)} collective-permute-done((bf16[520,1024]{1,0:T(8,128)(2,1)}, bf16[520,1024]{1,0:T(8,128)(2,1)}, u32[]{:S(2)}, u32[]{:S(2)}) %collective-permute-start.3) | collective-permute-done | bytes 1064992 | tf_op jit(solution)/shard_map/ppermute | solution.py:156
  63.4 1.3 collective-permute-start.4
  64.7 0.1 broadcast_multiply_fusion.1
  64.7 1.3 collective-permute-start.8
  66.0 0.1 add_convert_fusion
  66.1 0.9 copy.26.refs_4_.refs_1_
  67.0 0.1 mul.66
  67.1 0.6 concatenate.46.refs_3_
  67.7 0.1 slice_reduce_fusion
  67.8 0.7 broadcast_multiply_fusion.refs_6_
  68.5 1.7 collective-permute-start.7
  70.2 0.7 broadcast_select_fusion.5
  70.9 20.0 %collective-permute-done.4 = bf16[520,1024]{1,0:T(8,128)(2,1)} collective-permute-done((bf16[520,1024]{1,0:T(8,128)(2,1)}, bf16[520,1024]{1,0:T(8,128)(2,1)}, u32[]{:S(2)}, u32[]{:S(2)}) %collective-permute-start.4) | collective-permute-done | bytes 1064992 | tf_op jit(solution)/shard_map/ppermute | solution.py:156
  90.9 1.3 collective-permute-start.5
  92.2 1.4 broadcast_select_fusion.refs_3_
  93.6 1.4 collective-permute-done.8
  95.0 1.3 broadcast_select_fusion.1.refs_2_
  96.5 0.1 slice.125
  96.6 0.1 copy.28
  96.7 0.1 copy.24
  96.8 0.1 broadcast_compare_fusion
  96.9 0.7 reshape.255.flags_ref
  97.6 0.6 concatenate.47.refs_5_
  98.2 0.7 broadcast_in_dim.17.refs_7_
  98.9 0.7 broadcast_in_dim.18.refs_8_
  99.6 1.1 broadcast_in_dim.19.refs_9_
  100.7 24.8 %shard_map.85 = (f32[512,128]{1,0:T(8,128)}, f32[512,128]{1,0:T(8,128)}, f32[512,512]{1,0:T(8,128)}) custom-call(s32[16]{0:T(128)} %reshape.255.flags_ref, bf16[512,512]{1,0:T(8,128)(2,1)} %get-tuple-element.51.q_ref, bf16[520,1024]{1,0:T(8,128)(2,1)} %fusion.3.refs_0_, bf16[520,1024]{1,0:T(8,128)(2,1)} %collective-permute-done.3.refs_1_, ...), custom_call_target="tpu_custom_call" | custom-call | flops 2147483648 | bytes 8388608 | tf_op jit(solution)/shard_map/pallas_call | solution.py:132
  125.6 1.4 broadcast_select_fusion.2.refs_0_
  126.9 0.6 broadcast.176
  127.6 0.7 fusion.27
  128.3 0.1 slice.119
  128.4 0.1 copy.27
  128.5 0.1 compare_convert_fusion
  128.5 0.6 reshape.253.flags_ref
  129.1 0.6 concatenate.45.refs_2_
  129.8 13.2 %shard_map.86 = (f32[512,128]{1,0:T(8,128)}, f32[512,128]{1,0:T(8,128)}, f32[512,512]{1,0:T(8,128)}) custom-call(s32[4]{0:T(128)} %reshape.253.flags_ref, bf16[512,512]{1,0:T(8,128)(2,1)} %get-tuple-element.51.q_ref, bf16[520,1024]{1,0:T(8,128)(2,1)} %copy-done.3, s32[512,1]{1,0:T(8,128)} %copy.26.refs_4_.refs_1_, s32[8,512]{1,0:T(8,128)} %concatenate.45.refs_2_, ...), custom_call_target="tpu_custom_call" | custom-call | flops 536870912 | bytes 5242880 | tf_op jit(solution)/shard_map/pallas_call | solution.py:132
  142.9 1.5 broadcast_in_dim.20
  144.5 1.4 fusion.9
  146.0 0.7 convolution_convert_fusion
  146.7 0.1 collective-permute-start.10
  146.8 0.7 convolution_convert_fusion.1
  147.6 1.9 %collective-permute-done.10 = bf16[2,128,2048]{2,1,0:T(8,128)(2,1)S(1)} collective-permute-done((bf16[2,128,2048]{2,1,0:T(8,128)(2,1)S(1)}, bf16[2,128,2048]{2,1,0:T(8,128)(2,1)S(1)}, u32[]{:S(2)}, u32[]{:S(2)}) %collective-permute-start.10) | collective-permute-done | bytes 1048608 | tf_op jit(solution)/shard_map/ppermute | solution.py:26
  149.5 0.4 convert_add_fusion
  149.9 0.1 fusion.16
  149.9 1.2 collective-permute-start.11
  151.1 14.4 %collective-permute-done.11 = bf16[128,2048]{1,0:T(8,128)(2,1)S(1)} collective-permute-done((bf16[128,2048]{1,0:T(8,128)(2,1)S(1)}, bf16[128,2048]{1,0:T(8,128)(2,1)S(1)}, u32[]{:S(2)}, u32[]{:S(2)}) %collective-permute-start.11) | collective-permute-done | bytes 524320 | tf_op jit(solution)/shard_map/ppermute | solution.py:26
  165.5 1.0 fusion.8
  (48 shorter events, 0.4 us)
Async XLA Ops:
  0.6 145.4 %copy-start = (bf16[512,2048]{1,0:T(8,128)(2,1)S(1)}, bf16[512,2048]{1,0:T(8,128)(2,1)}, u32[]{:S(2)}) copy-start(bf16[512,2048]{1,0:T(8,128)(2,1)} %param.16) | copy-start | bytes 6291460
  0.6 5.6 %copy-start.7 = (s32[512]{0:T(512)S(1)}, s32[512]{0:T(512)}, u32[]{:S(2)}) copy-start(s32[512]{0:T(512)} %param.17) | copy-start | bytes 6148
  4.8 15.3 %collective-permute-start.1 = (bf16[128,2048]{1,0:T(8,128)(2,1)S(1)}, bf16[128,2048]{1,0:T(8,128)(2,1)S(1)}, u32[]{:S(2)}, u32[]{:S(2)}) collective-permute-start(bf16[128,2048]{1,0:T(8,128)(2,1)S(1)} %fusion.6), channel_id=1, source_target_pairs={{0,2},{1,3},{2,0},{3,1},{4,6},{5,7},{6,4},{7,5},{8,10},{9,11},{10,... | collective-permute-start | bytes 1572872 | tf_op jit(solution)/shard_map/ppermute | solution.py:26
  6.3 13.8 %collective-permute-start = (bf16[128,2048]{1,0:T(8,128)(2,1)S(1)}, bf16[128,2048]{1,0:T(8,128)(2,1)}, u32[]{:S(2)}, u32[]{:S(2)}) collective-permute-start(bf16[128,2048]{1,0:T(8,128)(2,1)S(1)} %fusion.6), channel_id=1, source_target_pairs={{0,1},{1,0},{2,3},{3,2},{4,5},{5,4},{6,7},{7,6},{8,9},{9,8},{10,11... | collective-permute-start | bytes 1572872 | tf_op jit(solution)/shard_map/ppermute | solution.py:26
  20.0 4.9 %collective-permute-start.2 = (bf16[128,2048]{1,0:T(8,128)(2,1)S(1)}, bf16[128,2048]{1,0:T(8,128)(2,1)S(1)}, u32[]{:S(2)}, u32[]{:S(2)}) collective-permute-start(bf16[128,2048]{1,0:T(8,128)(2,1)S(1)} %collective-permute-done.1), channel_id=1, source_target_pairs={{0,1},{1,0},{2,3},{3,2},{4,5},{5,4},{6,7},{7,6},{8,9},{9,8},{10,11... | collective-permute-start | bytes 1572872 | tf_op jit(solution)/shard_map/ppermute | solution.py:26
  20.0 4.9 %copy-start.2 = (bf16[2048,3,512]{0,2,1:T(8,128)(2,1)S(1)}, bf16[2048,3,512]{0,2,1:T(8,128)(2,1)}, u32[]{:S(2)}) copy-start(bf16[2048,3,512]{0,2,1:T(8,128)(2,1)} %copy.20) | copy-start | bytes 18874372
  28.3 65.3 %copy-start.4 = (bf16[512,512]{1,0:T(8,128)(2,1)}, bf16[512,512]{1,0:T(8,128)(2,1)S(1)}, u32[]{:S(2)}) copy-start(bf16[512,512]{1,0:T(8,128)(2,1)S(1)} %get-tuple-element.52) | copy-start | bytes 1572868
  28.3 36.4 %copy-start.8 = (f32[4]{0:T(128)S(1)}, f32[4]{0:T(128)}, u32[]{:S(2)}) copy-start(f32[4]{0:T(128)} %param.15) | copy-start | bytes 52
  28.3 37.8 %copy-start.9 = (s32[4]{0:T(128)S(1)}, s32[4]{0:T(128)}, u32[]{:S(2)}) copy-start(s32[4]{0:T(128)} %constant.150.clone.1) | copy-start | bytes 52
  30.9 32.5 %collective-permute-start.3 = (bf16[520,1024]{1,0:T(8,128)(2,1)}, bf16[520,1024]{1,0:T(8,128)(2,1)}, u32[]{:S(2)}, u32[]{:S(2)}) collective-permute-start(bf16[520,1024]{1,0:T(8,128)(2,1)} %fusion.3.refs_0_), channel_id=1, source_target_pairs={{0,16},{4,20},{8,24},{12,28},{16,32},{20,36},{24,40},{28,44},{32,4... | collective-permute-start | bytes 3194888 | tf_op jit(solution)/shard_map/ppermute | solution.py:156
  34.7 33.8 %collective-permute-start.6 = (bf16[520,1024]{1,0:T(8,128)(2,1)}, bf16[520,1024]{1,0:T(8,128)(2,1)}, u32[]{:S(2)}, u32[]{:S(2)}) collective-permute-start(bf16[520,1024]{1,0:T(8,128)(2,1)} %fusion.3.refs_0_), channel_id=1, source_target_pairs={{0,4},{4,8},{8,12},{16,20},{20,24},{24,28},{32,36},{36,40},{40,44}... | collective-permute-start | bytes 3194888 | tf_op jit(solution)/shard_map/ppermute | solution.py:156
  39.2 53.0 %collective-permute-start.9 = (bf16[520,1024]{1,0:T(8,128)(2,1)}, bf16[520,1024]{1,0:T(8,128)(2,1)}, u32[]{:S(2)}, u32[]{:S(2)}) collective-permute-start(bf16[520,1024]{1,0:T(8,128)(2,1)} %fusion.3.refs_0_), channel_id=1, source_target_pairs={{0,12},{16,28},{32,44},{48,60},{64,76},{80,92},{96,108},{112,124},... | collective-permute-start | bytes 3194888 | tf_op jit(solution)/shard_map/ppermute | solution.py:156
  63.4 27.5 %collective-permute-start.4 = (bf16[520,1024]{1,0:T(8,128)(2,1)}, bf16[520,1024]{1,0:T(8,128)(2,1)}, u32[]{:S(2)}, u32[]{:S(2)}) collective-permute-start(bf16[520,1024]{1,0:T(8,128)(2,1)} %collective-permute-done.3.refs_1_), channel_id=1, source_target_pairs={{4,0},{8,4},{12,8},{20,16},{24,20},{28,24},{36,32},{40,36},{44,40}... | collective-permute-start | bytes 3194888 | tf_op jit(solution)/shard_map/ppermute | solution.py:156
  64.7 30.3 %collective-permute-start.8 = (bf16[520,1024]{1,0:T(8,128)(2,1)}, bf16[520,1024]{1,0:T(8,128)(2,1)}, u32[]{:S(2)}, u32[]{:S(2)}) collective-permute-start(bf16[520,1024]{1,0:T(8,128)(2,1)} %collective-permute-done.3.refs_1_), channel_id=1, source_target_pairs={{12,0},{28,16},{44,32},{60,48},{76,64},{92,80},{108,96},{124,112},... | collective-permute-start | bytes 3194888 | tf_op jit(solution)/shard_map/ppermute | solution.py:156
  68.5 57.0 %collective-permute-start.7 = (bf16[520,1024]{1,0:T(8,128)(2,1)}, bf16[520,1024]{1,0:T(8,128)(2,1)}, u32[]{:S(2)}, u32[]{:S(2)}) collective-permute-start(bf16[520,1024]{1,0:T(8,128)(2,1)} %collective-permute-done.6), channel_id=1, source_target_pairs={{4,8},{8,12},{20,24},{24,28},{36,40},{40,44},{52,56},{56,60},{68,7... | collective-permute-start | bytes 3194888 | tf_op jit(solution)/shard_map/ppermute | solution.py:156
  90.9 34.6 %collective-permute-start.5 = (bf16[520,1024]{1,0:T(8,128)(2,1)}, bf16[520,1024]{1,0:T(8,128)(2,1)}, u32[]{:S(2)}, u32[]{:S(2)}) collective-permute-start(bf16[520,1024]{1,0:T(8,128)(2,1)} %collective-permute-done.4), channel_id=1, source_target_pairs={{4,0},{8,4},{20,16},{24,20},{36,32},{40,36},{52,48},{56,52},{68,64... | collective-permute-start | bytes 3194888 | tf_op jit(solution)/shard_map/ppermute | solution.py:156
  93.6 2.8 %copy-start.5 = (bf16[520,1024]{1,0:T(8,128)(2,1)}, bf16[520,1024]{1,0:T(8,128)(2,1)S(1)}, u32[]{:S(2)}) copy-start(bf16[520,1024]{1,0:T(8,128)(2,1)S(1)} %broadcast_select_fusion.refs_3_) | copy-start | bytes 3194884
  96.4 4.4 %copy-start.6 = (bf16[520,1024]{1,0:T(8,128)(2,1)}, bf16[520,1024]{1,0:T(8,128)(2,1)S(1)}, u32[]{:S(2)}) copy-start(bf16[520,1024]{1,0:T(8,128)(2,1)S(1)} %broadcast_select_fusion.1.refs_2_) | copy-start | bytes 3194884
  126.9 2.8 %copy-start.3 = (bf16[520,1024]{1,0:T(8,128)(2,1)}, bf16[520,1024]{1,0:T(8,128)(2,1)S(1)}, u32[]{:S(2)}) copy-start(bf16[520,1024]{1,0:T(8,128)(2,1)S(1)} %broadcast_select_fusion.2.refs_0_) | copy-start | bytes 3194884
  146.7 2.7 %collective-permute-start.10 = (bf16[2,128,2048]{2,1,0:T(8,128)(2,1)S(1)}, bf16[2,128,2048]{2,1,0:T(8,128)(2,1)S(1)}, u32[]{:S(2)}, u32[]{:S(2)}) collective-permute-start(bf16[2,128,2048]{2,1,0:T(8,128)(2,1)S(1)} %bitcast.52), channel_id=1, source_target_pairs={{0,1},{1,0},{2,3},{3,2},{4,5},{5,4},{6,7},{7,6},{8,9},{9,8},{10,11... | collective-permute-start | bytes 3145736 | tf_op jit(solution)/shard_map/ppermute | solution.py:26
  149.5 16.0 %copy-start.1 = (bf16[128,2048]{1,0:T(8,128)(2,1)S(1)}, bf16[128,2048]{1,0:T(8,128)(2,1)}, u32[]{:S(2)}) copy-start(bf16[128,2048]{1,0:T(8,128)(2,1)} %param.12) | copy-start | bytes 1572868
  149.9 15.6 %collective-permute-start.11 = (bf16[128,2048]{1,0:T(8,128)(2,1)S(1)}, bf16[128,2048]{1,0:T(8,128)(2,1)S(1)}, u32[]{:S(2)}, u32[]{:S(2)}) collective-permute-start(bf16[128,2048]{1,0:T(8,128)(2,1)S(1)} %fusion.16), channel_id=1, source_target_pairs={{0,2},{1,3},{2,0},{3,1},{4,6},{5,7},{6,4},{7,5},{8,10},{9,11},{10,... | collective-permute-start | bytes 1572872 | tf_op jit(solution)/shard_map/ppermute | solution.py:26

commit v13 on v12

--- a/solution.py
+++ b/solution.py
@@ -37,18 +37,33 @@
 TK = 256
 
 
-def part_kernel(n_buf, own, flags_ref, q_ref, *refs):
+def part_kernel(n_buf, own, last, flags_ref, q_ref, *refs):
     bufs = refs[:n_buf]
-    (segq_ref, segk_ref, bias_ref, m_in, l_in, acc_in, m_out, l_out, acc_out, m_sc, l_sc) = refs[n_buf:]
+    segq_ref, segk_ref, bias_ref = refs[n_buf : n_buf + 3]
+    rest = list(refs[n_buf + 3 :])
+    if not own:
+        m_in, l_in, acc_in = rest[:3]
+        rest = rest[3:]
+    if last:
+        ctx_ref = rest.pop(0)
+    else:
+        m_out, l_out, acc_out = rest[:3]
+        rest = rest[3:]
+    m_sc, l_sc, acc_sc = rest
     heads = m_sc.shape[0]
     block_len = q_ref.shape[0]
     n_q, n_t = block_len // TQ, block_len // TK
     width = heads * HD
     scale = HD ** (-0.5)
-    for h in range(heads):
-        m_sc[h] = m_in[:, h : h + 1]
-        l_sc[h] = l_in[:, h : h + 1]
-    acc_out[...] = acc_in[...]
+    if own:
+        m_sc[...] = jnp.full(m_sc.shape, NEG_FILL, jnp.float32)
+        l_sc[...] = jnp.zeros(l_sc.shape, jnp.float32)
+        acc_sc[...] = jnp.zeros(acc_sc.shape, jnp.float32)
+    else:
+        for h in range(heads):
+            m_sc[h] = m_in[:, h : h + 1]
+            l_sc[h] = l_in[:, h : h + 1]
+        acc_sc[...] = acc_in[...]
     for qt in range(n_q):
         rows = pl.ds(qt * TQ, TQ)
         segq = segq_ref[rows, :]
@@ -78,7 +93,7 @@
                     p = jnp.exp(s - m_new)
                     rescale = jnp.exp(m_prev - m_new)
                     l_sc[h, rows, :] = l_sc[h, rows, :] * rescale + jnp.sum(p, axis=1, keepdims=True)
-                    acc_out[rows, pl.ds(lanes, HD)] = acc_out[rows, pl.ds(lanes, HD)] * rescale + jnp.dot(
+                    acc_sc[rows, pl.ds(lanes, HD)] = acc_sc[rows, pl.ds(lanes, HD)] * rescale + jnp.dot(
                         p.astype(jnp.bfloat16), v, preferred_element_type=jnp.float32
                     )
                     m_sc[h, rows, :] = m_new
@@ -90,16 +105,23 @@
                 body()
             else:
                 pl.when(flags_ref[(qt * n_buf + i) * n_t + t] != 0)(body)
-    lane = lax.broadcasted_iota(jnp.int32, m_in.shape, 1)
-    m_all, l_all = m_in[...], l_in[...]
+    if last:
+        for h in range(heads):
+            cols = pl.ds(h * HD, HD)
+            ctx_ref[:, cols] = (acc_sc[:, cols] / l_sc[h]).astype(ctx_ref.dtype)
+        return
+    lane = lax.broadcasted_iota(jnp.int32, m_out.shape, 1)
+    m_all = jnp.zeros(m_out.shape, jnp.float32)
+    l_all = jnp.zeros(l_out.shape, jnp.float32)
     for h in range(heads):
         m_all = jnp.where(lane == h, m_sc[h], m_all)
         l_all = jnp.where(lane == h, l_sc[h], l_all)
     m_out[...] = m_all
     l_out[...] = l_all
-
-
-def attention_part(state, queries, seg_q, slopes, bufs, steps_back, present, own=False):
+    acc_out[...] = acc_sc[...]
+
+
+def attention_part(state, queries, seg_q, slopes, bufs, steps_back, present, own=False, last=False):
     block_len, width = queries.shape
     heads = width // HD
     n_buf = len(bufs)
@@ -128,26 +150,33 @@
     bias = jnp.concatenate([bias, jnp.zeros(((-n_buf * heads) % 8, block_len), jnp.float32)], axis=0)
     vmem = pl.BlockSpec(memory_space=pltpu.VMEM)
     work = heads * block_len * n_buf * block_len
-    m, l, acc = state
+    state = () if own else tuple(state)
+    if last:
+        out_shape = jax.ShapeDtypeStruct((block_len, width), jnp.bfloat16)
+        out_specs = vmem
+    else:
+        out_shape = (
+            jax.ShapeDtypeStruct((block_len, HD), jnp.float32),
+            jax.ShapeDtypeStruct((block_len, HD), jnp.float32),
+            jax.ShapeDtypeStruct((block_len, width), jnp.float32),
+        )
+        out_specs = (vmem, vmem, vmem)
     return pl.pallas_call(
-        functools.partial(part_kernel, n_buf, own),
-        out_shape=(
-            jax.ShapeDtypeStruct(m.shape, jnp.float32),
-            jax.ShapeDtypeStruct(l.shape, jnp.float32),
-            jax.ShapeDtypeStruct(acc.shape, jnp.float32),
-        ),
-        in_specs=[pl.BlockSpec(memory_space=pltpu.SMEM)] + [vmem] * (n_buf + 7),
-        out_specs=(vmem, vmem, vmem),
+        functools.partial(part_kernel, n_buf, own, last),
+        out_shape=out_shape,
+        in_specs=[pl.BlockSpec(memory_space=pltpu.SMEM)] + [vmem] * (n_buf + 4 + len(state)),
+        out_specs=out_specs,
         scratch_shapes=[
             pltpu.VMEM((heads, block_len, 1), jnp.float32),
             pltpu.VMEM((heads, block_len, 1), jnp.float32),
+            pltpu.VMEM((block_len, width), jnp.float32),
         ],
         cost_estimate=pl.CostEstimate(
             flops=4 * work * HD,
             transcendentals=work,
             bytes_accessed=(n_buf + 4) * block_len * width * 4,
         ),
-    )(flags, queries, *bufs, seg_q.reshape(block_len, 1), seg_rows, bias, m, l, acc)
+    )(flags, queries, *bufs, seg_q.reshape(block_len, 1), seg_rows, bias, *state)
 
 RING = 4
 
@@ -208,15 +237,10 @@
     arrived = relay_earlier_blocks(payload)
 
     queries = qkv_rows[:, :width_local]
-    state = (
-        jnp.full((block_len, HD), NEG_FILL, jnp.float32),
-        jnp.zeros((block_len, HD), jnp.float32),
-        jnp.zeros((block_len, width_local), jnp.float32),
-    )
     back1, back2, back3, from_z = arrived
     seq_index_now = lax.axis_index("seq")
     state = attention_part(
-        state,
+        None,
         queries,
         seg_ids,
         slopes,
@@ -225,12 +249,9 @@
         [jnp.bool_(True), seq_index_now >= 4, seq_index_now >= 1, seq_index_now >= 3],
         own=True,
     )
-    state = attention_part(
-        state, queries, seg_ids, slopes, [back2], [jnp.int32(2)], [seq_index_now >= 2]
-    )
-    _, total, acc = state
-    denominator = jnp.repeat(total[:, :heads_dev], HD, axis=1)
-    context = (acc / denominator).astype(jnp.bfloat16)
+    context = attention_part(
+        state, queries, seg_ids, slopes, [back2], [jnp.int32(2)], [seq_index_now >= 2], last=True
+    )
 
     context4 = context.reshape(n_head, rows_dev, context.shape[1])
 

time: 169 us -> 169 us (level)
  the two profiles are of different devices: /device:TPU:6 before, /device:TPU:14 now
where the time goes in v13:
time: 169 us
  waiting for transfers between devices  60.4 us (36%)
  Pallas kernels  45.2 us (27%)
  starting transfers between devices  22.6 us (13%)
  local copies, waits for them, and re-layouts  18.1 us (11%)
  other arithmetic  13.7 us (8%)
  matrix products  8.24 us (5%)
    pallas_call x2, Pallas kernels, attention_part(): pl.pallas_call(functools.partial(part_kernel, n_buf, own, last), out_shap...  45.2 us
    ppermute x7, waiting for transfers between devices, moved(): return lax.ppermute(value, 'seq', pairs)  39.2 us
    ppermute x5, waiting for transfers between devices, swapped(): lax.ppermute(value, axis, [(source, source ^ mask) for source in range(co...  21.1 us
    ppermute x7, starting transfers between devices, moved(): return lax.ppermute(value, 'seq', pairs)  19.9 us
    unnamed x23, local copies, waits for them, and re-layouts  9.1 us
    dot_general x2, matrix products, project_rows(): jnp.dot(rows, joined, preferred_element_type=jnp.float32)  6.75 us
  transfers between devices with their start and end apart: 12, of which 5 were waited for; matrix products, arithmetic and copies ran while one was open for 13% of the time, Pallas kernels for 19%

profile of v13, /device:TPU:14, one launch (start us, length us, event | category | flops | bytes accessed | tf_op | source)
XLA Modules:
  0.0 169.2 jit_solution(16469911337388285075)
XLA Ops:
  0.6 0.0 copy-start
  0.7 1.3 convert_reduce_fusion
  2.0 1.3 fusion.4
  3.3 1.4 fusion.6
  4.8 1.5 collective-permute-start.1
  6.3 0.0 collective-permute-start
  6.3 8.9 %copy.20 = bf16[2048,3,512]{0,2,1:T(8,128)(2,1)} copy(bf16[2048,3,512]{2,0,1:T(8,128)(2,1)} %param.14) | data formatting | bytes 12582912 | tf_op args[2]
  15.1 4.9 %collective-permute-done.1 = bf16[128,2048]{1,0:T(8,128)(2,1)S(1)} collective-permute-done((bf16[128,2048]{1,0:T(8,128)(2,1)S(1)}, bf16[128,2048]{1,0:T(8,128)(2,1)S(1)}, u32[]{:S(2)}, u32[]{:S(2)}) %collective-permute-start.1) | collective-permute-done | bytes 524320 | tf_op jit(solution)/shard_map/ppermute | solution.py:26
  20.0 0.0 collective-permute-start.2
  20.0 4.9 %convolution_convert_fusion.3 = bf16[256,1536]{1,0:T(8,128)(2,1)S(1)} fusion(bf16[2048,1536]{0,1:T(8,128)(2,1)} %bitcast.39, bf16[128,2048]{1,0:T(8,128)(2,1)} %collective-permute-done, bf16[128,2048]{1,0:T(8,128)(2,1)S(1)} %fusion.6), kind=kOutput, calls=%fused_computation.3 | convolution fusion | flops 1613103104 | bytes 8126464 | tf_op jit(solution)/shard_map/dot_general | solution.py:217
  25.0 0.0 collective-permute-done.2
  25.0 1.8 %convolution_convert_fusion.2 = bf16[256,1536]{1,0:T(8,128)(2,1)S(1)} fusion(bf16[2048,1536]{0,1:T(8,128)(2,1)S(1)} %bitcast.40, bf16[128,2048]{1,0:T(8,128)(2,1)S(1)} %collective-permute-done.2, bf16[128,2048]{1,0:T(8,128)(2,1)S(1)} %collective-permute-done.1), kind=kOutput, calls=%fused_computation.2 | convolution fusion | flops 1613103104 | bytes 8126464 | tf_op jit(solution)/shard_map/dot_general | solution.py:217
  26.8 0.1 pad_maximum_fusion
  26.9 0.1 dynamic-slice_bitcast_fusion.3
  27.1 0.1 pad_maximum_fusion.1
  27.2 1.1 fusion.27
  28.3 1.5 copy.21
  29.7 1.1 fusion.3.refs_0_
  30.9 3.8 %collective-permute-start.3 = (bf16[520,1024]{1,0:T(8,128)(2,1)}, bf16[520,1024]{1,0:T(8,128)(2,1)}, u32[]{:S(2)}, u32[]{:S(2)}) collective-permute-start(bf16[520,1024]{1,0:T(8,128)(2,1)} %fusion.3.refs_0_), channel_id=1, source_target_pairs={{0,16},{4,20},{8,24},{12,28},{16,32},{20,36},{24,40},{28,44},{32,4... | collective-permute-start | bytes 3194888 | tf_op jit(solution)/shard_map/ppermute | solution.py:185
  34.7 3.5 %collective-permute-start.6 = (bf16[520,1024]{1,0:T(8,128)(2,1)}, bf16[520,1024]{1,0:T(8,128)(2,1)}, u32[]{:S(2)}, u32[]{:S(2)}) collective-permute-start(bf16[520,1024]{1,0:T(8,128)(2,1)} %fusion.3.refs_0_), channel_id=1, source_target_pairs={{0,4},{4,8},{8,12},{16,20},{20,24},{24,28},{32,36},{36,40},{40,44}... | collective-permute-start | bytes 3194888 | tf_op jit(solution)/shard_map/ppermute | solution.py:185
  38.2 1.7 collective-permute-start.9
  39.9 23.5 %collective-permute-done.3.refs_1_ = bf16[520,1024]{1,0:T(8,128)(2,1)} collective-permute-done((bf16[520,1024]{1,0:T(8,128)(2,1)}, bf16[520,1024]{1,0:T(8,128)(2,1)}, u32[]{:S(2)}, u32[]{:S(2)}) %collective-permute-start.3) | collective-permute-done | bytes 1064992 | tf_op jit(solution)/shard_map/ppermute | solution.py:185
  63.4 2.3 %collective-permute-start.4 = (bf16[520,1024]{1,0:T(8,128)(2,1)}, bf16[520,1024]{1,0:T(8,128)(2,1)}, u32[]{:S(2)}, u32[]{:S(2)}) collective-permute-start(bf16[520,1024]{1,0:T(8,128)(2,1)} %collective-permute-done.3.refs_1_), channel_id=1, source_target_pairs={{4,0},{8,4},{12,8},{20,16},{24,20},{28,24},{36,32},{40,36},{44,40}... | collective-permute-start | bytes 3194888 | tf_op jit(solution)/shard_map/ppermute | solution.py:185
  65.7 0.1 broadcast_multiply_fusion.1
  65.8 1.7 %collective-permute-start.8 = (bf16[520,1024]{1,0:T(8,128)(2,1)}, bf16[520,1024]{1,0:T(8,128)(2,1)}, u32[]{:S(2)}, u32[]{:S(2)}) collective-permute-start(bf16[520,1024]{1,0:T(8,128)(2,1)} %collective-permute-done.3.refs_1_), channel_id=1, source_target_pairs={{12,0},{28,16},{44,32},{60,48},{76,64},{92,80},{108,96},{124,112},... | collective-permute-start | bytes 3194888 | tf_op jit(solution)/shard_map/ppermute | solution.py:185
  67.5 0.1 add_convert_fusion
  67.6 0.9 copy.26.refs_4_.refs_1_
  68.5 0.1 mul.66
  68.6 0.6 concatenate.46.refs_3_
  69.2 0.1 slice_reduce_fusion
  69.3 0.7 broadcast_multiply_fusion.refs_6_
  70.0 4.5 %collective-permute-start.7 = (bf16[520,1024]{1,0:T(8,128)(2,1)}, bf16[520,1024]{1,0:T(8,128)(2,1)}, u32[]{:S(2)}, u32[]{:S(2)}) collective-permute-start(bf16[520,1024]{1,0:T(8,128)(2,1)} %collective-permute-done.6), channel_id=1, source_target_pairs={{4,8},{8,12},{20,24},{24,28},{36,40},{40,44},{52,56},{56,60},{68,7... | collective-permute-start | bytes 3194888 | tf_op jit(solution)/shard_map/ppermute | solution.py:185
  74.5 0.7 broadcast_select_fusion.5
  75.2 15.7 %collective-permute-done.4 = bf16[520,1024]{1,0:T(8,128)(2,1)} collective-permute-done((bf16[520,1024]{1,0:T(8,128)(2,1)}, bf16[520,1024]{1,0:T(8,128)(2,1)}, u32[]{:S(2)}, u32[]{:S(2)}) %collective-permute-start.4) | collective-permute-done | bytes 1064992 | tf_op jit(solution)/shard_map/ppermute | solution.py:185
  90.9 2.4 %collective-permute-start.5 = (bf16[520,1024]{1,0:T(8,128)(2,1)}, bf16[520,1024]{1,0:T(8,128)(2,1)}, u32[]{:S(2)}, u32[]{:S(2)}) collective-permute-start(bf16[520,1024]{1,0:T(8,128)(2,1)} %collective-permute-done.4), channel_id=1, source_target_pairs={{4,0},{8,4},{20,16},{24,20},{36,32},{40,36},{52,48},{56,52},{68,64... | collective-permute-start | bytes 3194888 | tf_op jit(solution)/shard_map/ppermute | solution.py:185
  93.3 1.4 broadcast_select_fusion.refs_3_
  94.7 0.0 collective-permute-done.8
  94.7 1.7 %broadcast_select_fusion.1.refs_2_ = bf16[520,1024]{1,0:T(8,128)(2,1)S(1)} fusion(bf16[520,1024]{1,0:T(8,128)(2,1)} %collective-permute-done.8, bf16[520,1024]{1,0:T(8,128)(2,1)} %collective-permute-done.6, pred[]{:T(512)S(6)} %eq.5), kind=kLoop, calls=%fused_computation.16 | loop fusion | flops 532480 | bytes 3194881 | tf_op jit(solution)/shard_map/jit(_where)/select_n | solution.py:199
  96.6 0.1 slice.121
  96.7 0.1 copy.28
  96.8 0.1 copy.24
  96.8 0.1 broadcast_compare_fusion
  97.0 0.6 reshape.251.flags_ref
  97.6 0.6 concatenate.47.refs_5_
  98.2 32.6 %shard_map.85 = (f32[512,128]{1,0:T(8,128)}, f32[512,128]{1,0:T(8,128)}, f32[512,512]{1,0:T(8,128)}) custom-call(s32[16]{0:T(128)} %reshape.251.flags_ref, bf16[512,512]{1,0:T(8,128)(2,1)} %get-tuple-element.47.q_ref, bf16[520,1024]{1,0:T(8,128)(2,1)} %fusion.3.refs_0_, bf16[520,1024]{1,0:T(8,128)(2,1)} %collective-permute-done.3.refs_1_, ...), custom_call_target="tpu_custom_call" | custom-call | flops 2147483648 | bytes 8388608 | tf_op jit(solution)/shard_map/pallas_call | solution.py:164
  130.7 1.4 broadcast_select_fusion.2.refs_0_
  132.1 0.7 broadcast.176
  132.8 0.7 fusion.26
  133.5 0.1 slice.115
  133.6 0.1 copy.27
  133.7 0.1 compare_convert_fusion
  133.7 0.6 reshape.249.flags_ref
  134.3 0.6 concatenate.45.refs_2_
  134.9 12.6 %shard_map.86 = bf16[512,512]{1,0:T(8,128)(2,1)} custom-call(s32[4]{0:T(128)} %reshape.249.flags_ref, bf16[512,512]{1,0:T(8,128)(2,1)} %get-tuple-element.47.q_ref, bf16[520,1024]{1,0:T(8,128)(2,1)} %copy-done.3, s32[512,1]{1,0:T(8,128)} %copy.26.refs_4_.refs_1_, s32[8,512]{1,0:T(8,128)} %concatenate.45.refs_2_, f32[8,512]{1,0:T(8,128)} %concatenate.46.refs_3_, ...), custom_call_target="tpu_custom_call" | custom-call | flops 536870912 | bytes 5242880 | tf_op jit(solution)/shard_map/pallas_call | solution.py:164
  147.6 1.1 dynamic-slice_bitcast_fusion.5
  148.7 0.7 convolution_convert_fusion
  149.5 0.1 collective-permute-start.10
  149.6 0.7 convolution_convert_fusion.1
  150.3 1.9 %collective-permute-done.10 = bf16[2,128,2048]{2,1,0:T(8,128)(2,1)S(1)} collective-permute-done((bf16[2,128,2048]{2,1,0:T(8,128)(2,1)S(1)}, bf16[2,128,2048]{2,1,0:T(8,128)(2,1)S(1)}, u32[]{:S(2)}, u32[]{:S(2)}) %collective-permute-start.10) | collective-permute-done | bytes 1048608 | tf_op jit(solution)/shard_map/ppermute | solution.py:26
  152.2 0.4 convert_add_fusion
  152.6 0.1 fusion.15
  152.7 1.2 collective-permute-start.11
  153.8 14.4 %collective-permute-done.11 = bf16[128,2048]{1,0:T(8,128)(2,1)S(1)} collective-permute-done((bf16[128,2048]{1,0:T(8,128)(2,1)S(1)}, bf16[128,2048]{1,0:T(8,128)(2,1)S(1)}, u32[]{:S(2)}, u32[]{:S(2)}) %collective-permute-start.11) | collective-permute-done | bytes 524320 | tf_op jit(solution)/shard_map/ppermute | solution.py:26
  168.2 1.0 fusion.8
  (43 shorter events, 0.3 us)
Async XLA Ops:
  0.6 148.1 %copy-start = (bf16[512,2048]{1,0:T(8,128)(2,1)S(1)}, bf16[512,2048]{1,0:T(8,128)(2,1)}, u32[]{:S(2)}) copy-start(bf16[512,2048]{1,0:T(8,128)(2,1)} %param.16) | copy-start | bytes 6291460
  0.6 5.6 %copy-start.7 = (s32[512]{0:T(512)S(1)}, s32[512]{0:T(512)}, u32[]{:S(2)}) copy-start(s32[512]{0:T(512)} %param.17) | copy-start | bytes 6148
  4.8 15.3 %collective-permute-start.1 = (bf16[128,2048]{1,0:T(8,128)(2,1)S(1)}, bf16[128,2048]{1,0:T(8,128)(2,1)S(1)}, u32[]{:S(2)}, u32[]{:S(2)}) collective-permute-start(bf16[128,2048]{1,0:T(8,128)(2,1)S(1)} %fusion.6), channel_id=1, source_target_pairs={{0,2},{1,3},{2,0},{3,1},{4,6},{5,7},{6,4},{7,5},{8,10},{9,11},{10,... | collective-permute-start | bytes 1572872 | tf_op jit(solution)/shard_map/ppermute | solution.py:26
  6.3 13.8 %collective-permute-start = (bf16[128,2048]{1,0:T(8,128)(2,1)S(1)}, bf16[128,2048]{1,0:T(8,128)(2,1)}, u32[]{:S(2)}, u32[]{:S(2)}) collective-permute-start(bf16[128,2048]{1,0:T(8,128)(2,1)S(1)} %fusion.6), channel_id=1, source_target_pairs={{0,1},{1,0},{2,3},{3,2},{4,5},{5,4},{6,7},{7,6},{8,9},{9,8},{10,11... | collective-permute-start | bytes 1572872 | tf_op jit(solution)/shard_map/ppermute | solution.py:26
  20.0 4.9 %collective-permute-start.2 = (bf16[128,2048]{1,0:T(8,128)(2,1)S(1)}, bf16[128,2048]{1,0:T(8,128)(2,1)S(1)}, u32[]{:S(2)}, u32[]{:S(2)}) collective-permute-start(bf16[128,2048]{1,0:T(8,128)(2,1)S(1)} %collective-permute-done.1), channel_id=1, source_target_pairs={{0,1},{1,0},{2,3},{3,2},{4,5},{5,4},{6,7},{7,6},{8,9},{9,8},{10,11... | collective-permute-start | bytes 1572872 | tf_op jit(solution)/shard_map/ppermute | solution.py:26
  20.0 4.9 %copy-start.2 = (bf16[2048,3,512]{0,2,1:T(8,128)(2,1)S(1)}, bf16[2048,3,512]{0,2,1:T(8,128)(2,1)}, u32[]{:S(2)}) copy-start(bf16[2048,3,512]{0,2,1:T(8,128)(2,1)} %copy.20) | copy-start | bytes 18874372
  28.3 66.4 %copy-start.4 = (bf16[512,512]{1,0:T(8,128)(2,1)}, bf16[512,512]{1,0:T(8,128)(2,1)S(1)}, u32[]{:S(2)}) copy-start(bf16[512,512]{1,0:T(8,128)(2,1)S(1)} %get-tuple-element.48) | copy-start | bytes 1572868
  28.3 37.5 %copy-start.8 = (f32[4]{0:T(128)S(1)}, f32[4]{0:T(128)}, u32[]{:S(2)}) copy-start(f32[4]{0:T(128)} %param.15) | copy-start | bytes 52
  28.3 39.3 %copy-start.9 = (s32[4]{0:T(128)S(1)}, s32[4]{0:T(128)}, u32[]{:S(2)}) copy-start(s32[4]{0:T(128)} %constant.147.clone.1) | copy-start | bytes 52
  30.9 32.5 %collective-permute-start.3 = (bf16[520,1024]{1,0:T(8,128)(2,1)}, bf16[520,1024]{1,0:T(8,128)(2,1)}, u32[]{:S(2)}, u32[]{:S(2)}) collective-permute-start(bf16[520,1024]{1,0:T(8,128)(2,1)} %fusion.3.refs_0_), channel_id=1, source_target_pairs={{0,16},{4,20},{8,24},{12,28},{16,32},{20,36},{24,40},{28,44},{32,4... | collective-permute-start | bytes 3194888 | tf_op jit(solution)/shard_map/ppermute | solution.py:185
  34.7 35.3 %collective-permute-start.6 = (bf16[520,1024]{1,0:T(8,128)(2,1)}, bf16[520,1024]{1,0:T(8,128)(2,1)}, u32[]{:S(2)}, u32[]{:S(2)}) collective-permute-start(bf16[520,1024]{1,0:T(8,128)(2,1)} %fusion.3.refs_0_), channel_id=1, source_target_pairs={{0,4},{4,8},{8,12},{16,20},{20,24},{24,28},{32,36},{36,40},{40,44}... | collective-permute-start | bytes 3194888 | tf_op jit(solution)/shard_map/ppermute | solution.py:185
  38.2 55.1 %collective-permute-start.9 = (bf16[520,1024]{1,0:T(8,128)(2,1)}, bf16[520,1024]{1,0:T(8,128)(2,1)}, u32[]{:S(2)}, u32[]{:S(2)}) collective-permute-start(bf16[520,1024]{1,0:T(8,128)(2,1)} %fusion.3.refs_0_), channel_id=1, source_target_pairs={{0,12},{16,28},{32,44},{48,60},{64,76},{80,92},{96,108},{112,124},... | collective-permute-start | bytes 3194888 | tf_op jit(solution)/shard_map/ppermute | solution.py:185
  63.4 27.5 %collective-permute-start.4 = (bf16[520,1024]{1,0:T(8,128)(2,1)}, bf16[520,1024]{1,0:T(8,128)(2,1)}, u32[]{:S(2)}, u32[]{:S(2)}) collective-permute-start(bf16[520,1024]{1,0:T(8,128)(2,1)} %collective-permute-done.3.refs_1_), channel_id=1, source_target_pairs={{4,0},{8,4},{12,8},{20,16},{24,20},{28,24},{36,32},{40,36},{44,40}... | collective-permute-start | bytes 3194888 | tf_op jit(solution)/shard_map/ppermute | solution.py:185
  65.8 28.9 %collective-permute-start.8 = (bf16[520,1024]{1,0:T(8,128)(2,1)}, bf16[520,1024]{1,0:T(8,128)(2,1)}, u32[]{:S(2)}, u32[]{:S(2)}) collective-permute-start(bf16[520,1024]{1,0:T(8,128)(2,1)} %collective-permute-done.3.refs_1_), channel_id=1, source_target_pairs={{12,0},{28,16},{44,32},{60,48},{76,64},{92,80},{108,96},{124,112},... | collective-permute-start | bytes 3194888 | tf_op jit(solution)/shard_map/ppermute | solution.py:185
  70.0 60.7 %collective-permute-start.7 = (bf16[520,1024]{1,0:T(8,128)(2,1)}, bf16[520,1024]{1,0:T(8,128)(2,1)}, u32[]{:S(2)}, u32[]{:S(2)}) collective-permute-start(bf16[520,1024]{1,0:T(8,128)(2,1)} %collective-permute-done.6), channel_id=1, source_target_pairs={{4,8},{8,12},{20,24},{24,28},{36,40},{40,44},{52,56},{56,60},{68,7... | collective-permute-start | bytes 3194888 | tf_op jit(solution)/shard_map/ppermute | solution.py:185
  90.9 39.8 %collective-permute-start.5 = (bf16[520,1024]{1,0:T(8,128)(2,1)}, bf16[520,1024]{1,0:T(8,128)(2,1)}, u32[]{:S(2)}, u32[]{:S(2)}) collective-permute-start(bf16[520,1024]{1,0:T(8,128)(2,1)} %collective-permute-done.4), channel_id=1, source_target_pairs={{4,0},{8,4},{20,16},{24,20},{36,32},{40,36},{52,48},{56,52},{68,64... | collective-permute-start | bytes 3194888 | tf_op jit(solution)/shard_map/ppermute | solution.py:185
  94.7 1.8 %copy-start.5 = (bf16[520,1024]{1,0:T(8,128)(2,1)}, bf16[520,1024]{1,0:T(8,128)(2,1)S(1)}, u32[]{:S(2)}) copy-start(bf16[520,1024]{1,0:T(8,128)(2,1)S(1)} %broadcast_select_fusion.refs_3_) | copy-start | bytes 3194884
  96.4 1.7 %copy-start.6 = (bf16[520,1024]{1,0:T(8,128)(2,1)}, bf16[520,1024]{1,0:T(8,128)(2,1)S(1)}, u32[]{:S(2)}) copy-start(bf16[520,1024]{1,0:T(8,128)(2,1)S(1)} %broadcast_select_fusion.1.refs_2_) | copy-start | bytes 3194884
  132.1 2.9 %copy-start.3 = (bf16[520,1024]{1,0:T(8,128)(2,1)}, bf16[520,1024]{1,0:T(8,128)(2,1)S(1)}, u32[]{:S(2)}) copy-start(bf16[520,1024]{1,0:T(8,128)(2,1)S(1)} %broadcast_select_fusion.2.refs_0_) | copy-start | bytes 3194884
  149.5 2.7 %collective-permute-start.10 = (bf16[2,128,2048]{2,1,0:T(8,128)(2,1)S(1)}, bf16[2,128,2048]{2,1,0:T(8,128)(2,1)S(1)}, u32[]{:S(2)}, u32[]{:S(2)}) collective-permute-start(bf16[2,128,2048]{2,1,0:T(8,128)(2,1)S(1)} %bitcast.45), channel_id=1, source_target_pairs={{0,1},{1,0},{2,3},{3,2},{4,5},{5,4},{6,7},{7,6},{8,9},{9,8},{10,11... | collective-permute-start | bytes 3145736 | tf_op jit(solution)/shard_map/ppermute | solution.py:26
  152.2 16.0 %copy-start.1 = (bf16[128,2048]{1,0:T(8,128)(2,1)S(1)}, bf16[128,2048]{1,0:T(8,128)(2,1)}, u32[]{:S(2)}) copy-start(bf16[128,2048]{1,0:T(8,128)(2,1)} %param.12) | copy-start | bytes 1572868
  152.7 15.6 %collective-permute-start.11 = (bf16[128,2048]{1,0:T(8,128)(2,1)S(1)}, bf16[128,2048]{1,0:T(8,128)(2,1)S(1)}, u32[]{:S(2)}, u32[]{:S(2)}) collective-permute-start(bf16[128,2048]{1,0:T(8,128)(2,1)S(1)} %fusion.15), channel_id=1, source_target_pairs={{0,2},{1,3},{2,0},{3,1},{4,6},{5,7},{6,4},{7,5},{8,10},{9,11},{10,... | collective-permute-start | bytes 1572872 | tf_op jit(solution)/shard_map/ppermute | solution.py:26

commit v14 on v13

--- a/solution.py
+++ b/solution.py
@@ -196,10 +196,16 @@
     passed_down = moved(from_z, [(s, s - 1) for s in ids if s % RING > 0])
     passed_wrap = moved(from_z, [(s, s - RING + 1) for s in ids if s % RING == RING - 1])
     passed_twice = moved(passed_down, [(s, s - 1) for s in ids if 0 < s % RING < RING - 1])
-    back1 = jnp.where(y == 0, passed_wrap, from_below)
-    back2 = jnp.where(y <= 1, passed_twice, passed_up)
-    back3 = jnp.where(y <= 2, passed_down, from_wrap)
-    return [back1, back2, back3, from_z]
+    s_now = lax.axis_index("seq")
+    early = [
+        (from_z, 4, s_now >= 4),
+        (from_below, 1, y >= 1),
+        (passed_wrap, 1, (y == 0) & (s_now >= 1)),
+        (passed_down, 3, (y <= 2) & (s_now >= 3)),
+        (from_wrap, 3, y == 3),
+    ]
+    late = [(passed_twice, 2, (y <= 1) & (s_now >= 2)), (passed_up, 2, y >= 2)]
+    return early, late
 
 
 def on_device(tokens, ln_gain, w_qkv, slopes, w_out, seg_ids):
@@ -237,21 +243,19 @@
     arrived = relay_earlier_blocks(payload)
 
     queries = qkv_rows[:, :width_local]
-    back1, back2, back3, from_z = arrived
-    seq_index_now = lax.axis_index("seq")
+    early, late = arrived
+
+    def unzip(entries):
+        bufs, back, present = zip(*entries)
+        return list(bufs), [jnp.int32(k) for k in back], list(present)
+
+    bufs, back, present = unzip(early)
     state = attention_part(
-        None,
-        queries,
-        seg_ids,
-        slopes,
-        [payload, from_z, back1, back3],
-        [jnp.int32(0), jnp.int32(4), jnp.int32(1), jnp.int32(3)],
-        [jnp.bool_(True), seq_index_now >= 4, seq_index_now >= 1, seq_index_now >= 3],
-        own=True,
-    )
-    context = attention_part(
-        state, queries, seg_ids, slopes, [back2], [jnp.int32(2)], [seq_index_now >= 2], last=True
-    )
+        None, queries, seg_ids, slopes, [payload] + bufs, [jnp.int32(0)] + back,
+        [jnp.bool_(True)] + present, own=True,
+    )
+    bufs, back, present = unzip(late)
+    context = attention_part(state, queries, seg_ids, slopes, bufs, back, present, last=True)
 
     context4 = context.reshape(n_head, rows_dev, context.shape[1])
 

time: 169 us -> 167 us (0.988)
  the two profiles are of different devices: /device:TPU:14 before, /device:TPU:102 now
where the time goes in v14:
time: 167 us
  waiting for transfers between devices  58.3 us (35%)
  Pallas kernels  46.1 us (28%)
  starting transfers between devices  20.8 us (12%)
  local copies, waits for them, and re-layouts  16.7 us (10%)
  other arithmetic  15.4 us (9%)
  matrix products  8.23 us (5%)
    pallas_call x2, Pallas kernels, attention_part(): pl.pallas_call(functools.partial(part_kernel, n_buf, own, last), out_shap...  46.1 us
    ppermute x7, waiting for transfers between devices, moved(): return lax.ppermute(value, 'seq', pairs)  37.4 us
    ppermute x5, waiting for transfers between devices, swapped(): lax.ppermute(value, axis, [(source, source ^ mask) for source in range(co...  20.9 us
    ppermute x7, starting transfers between devices, moved(): return lax.ppermute(value, 'seq', pairs)  17.7 us
    unnamed x16, local copies, waits for them, and re-layouts  8.95 us
    dot_general x2, matrix products, project_rows(): jnp.dot(rows, joined, preferred_element_type=jnp.float32)  6.75 us
    select_n x7, other arithmetic, attention_part(): jnp.where(ok, buf[block_len, :block_len].astype(jnp.int32), -1)  6.07 us
  transfers between devices with their start and end apart: 12, of which 6 were waited for; matrix products, arithmetic and copies ran while one was open for 15% of the time, Pallas kernels for 20%

profile of v14, /device:TPU:102, one launch (start us, length us, event | category | flops | bytes accessed | tf_op | source)
XLA Modules:
  0.0 166.5 jit_solution(3986709170518023039)
XLA Ops:
  0.6 0.0 copy-start
  0.6 1.3 convert_reduce_fusion
  2.0 1.3 fusion.4
  3.3 1.4 fusion.6
  4.8 1.5 collective-permute-start.1
  6.3 8.8 %copy.36 = bf16[2048,3,512]{0,2,1:T(8,128)(2,1)} copy(bf16[2048,3,512]{2,0,1:T(8,128)(2,1)} %param.14) | data formatting | bytes 12582912 | tf_op args[2]
  15.1 4.9 %collective-permute-done.1 = bf16[128,2048]{1,0:T(8,128)(2,1)S(1)} collective-permute-done((bf16[128,2048]{1,0:T(8,128)(2,1)S(1)}, bf16[128,2048]{1,0:T(8,128)(2,1)S(1)}, u32[]{:S(2)}, u32[]{:S(2)}) %collective-permute-start.1) | collective-permute-done | bytes 524320 | tf_op jit(solution)/shard_map/ppermute | solution.py:26
  20.0 4.9 %convolution_convert_fusion.3 = bf16[256,1536]{1,0:T(8,128)(2,1)S(1)} fusion(bf16[2048,1536]{0,1:T(8,128)(2,1)} %bitcast.36, bf16[128,2048]{1,0:T(8,128)(2,1)} %collective-permute-done, bf16[128,2048]{1,0:T(8,128)(2,1)S(1)} %fusion.6), kind=kOutput, calls=%fused_computation.3 | convolution fusion | flops 1613103104 | bytes 8126464 | tf_op jit(solution)/shard_map/dot_general | solution.py:223
  25.0 1.8 %convolution_convert_fusion.2 = bf16[256,1536]{1,0:T(8,128)(2,1)S(1)} fusion(bf16[2048,1536]{0,1:T(8,128)(2,1)S(1)} %bitcast.37, bf16[128,2048]{1,0:T(8,128)(2,1)S(1)} %collective-permute-done.2, bf16[128,2048]{1,0:T(8,128)(2,1)S(1)} %collective-permute-done.1), kind=kOutput, calls=%fused_computation.2 | convolution fusion | flops 1613103104 | bytes 8126464 | tf_op jit(solution)/shard_map/dot_general | solution.py:223
  26.8 0.1 pad_maximum_fusion
  26.9 0.1 dynamic-slice_bitcast_fusion.3
  27.0 0.1 pad_maximum_fusion.1
  27.1 1.1 fusion.29
  28.2 1.5 copy.37
  29.7 1.2 fusion.3.refs_0_
  30.9 5.0 %collective-permute-start.3 = (bf16[520,1024]{1,0:T(8,128)(2,1)}, bf16[520,1024]{1,0:T(8,128)(2,1)}, u32[]{:S(2)}, u32[]{:S(2)}) collective-permute-start(bf16[520,1024]{1,0:T(8,128)(2,1)} %fusion.3.refs_0_), channel_id=1, source_target_pairs={{0,16},{4,20},{8,24},{12,28},{16,32},{20,36},{24,40},{28,44},{32,4... | collective-permute-start | bytes 3194888 | tf_op jit(solution)/shard_map/ppermute | solution.py:185
  35.9 4.5 %collective-permute-start.6 = (bf16[520,1024]{1,0:T(8,128)(2,1)}, bf16[520,1024]{1,0:T(8,128)(2,1)}, u32[]{:S(2)}, u32[]{:S(2)}) collective-permute-start(bf16[520,1024]{1,0:T(8,128)(2,1)} %fusion.3.refs_0_), channel_id=1, source_target_pairs={{0,4},{4,8},{8,12},{16,20},{20,24},{24,28},{32,36},{36,40},{40,44}... | collective-permute-start | bytes 3194888 | tf_op jit(solution)/shard_map/ppermute | solution.py:185
  40.4 0.1 add_convert_fusion
  40.5 0.1 mul.70
  40.6 2.8 %collective-permute-start.9 = (bf16[520,1024]{1,0:T(8,128)(2,1)}, bf16[520,1024]{1,0:T(8,128)(2,1)}, u32[]{:S(2)}, u32[]{:S(2)}) collective-permute-start(bf16[520,1024]{1,0:T(8,128)(2,1)} %fusion.3.refs_0_), channel_id=1, source_target_pairs={{0,12},{16,28},{32,44},{48,60},{64,76},{80,92},{96,108},{112,124},... | collective-permute-start | bytes 3194888 | tf_op jit(solution)/shard_map/ppermute | solution.py:185
  43.4 0.7 broadcast_multiply_fusion.refs_8_
  44.1 0.1 mul.64
  44.2 15.5 %collective-permute-done.3.refs_1_ = bf16[520,1024]{1,0:T(8,128)(2,1)} collective-permute-done((bf16[520,1024]{1,0:T(8,128)(2,1)}, bf16[520,1024]{1,0:T(8,128)(2,1)}, u32[]{:S(2)}, u32[]{:S(2)}) %collective-permute-start.3) | collective-permute-done | bytes 1064992 | tf_op jit(solution)/shard_map/ppermute | solution.py:185
  59.7 1.3 collective-permute-start.4
  60.9 0.7 broadcast_multiply_fusion.1.refs_4_
  61.6 1.3 collective-permute-start.8
  63.0 0.9 copy.41.refs_6_.refs_2_
  63.9 0.1 pad.16.clone
  63.9 0.1 slice_reduce_fusion
  64.0 1.6 collective-permute-start.7
  65.7 0.7 broadcast_select_fusion.3
  66.4 0.7 broadcast_select_fusion.4
  67.1 0.7 broadcast_select_fusion
  67.8 19.2 %collective-permute-done.4.refs_4_ = bf16[520,1024]{1,0:T(8,128)(2,1)} collective-permute-done((bf16[520,1024]{1,0:T(8,128)(2,1)}, bf16[520,1024]{1,0:T(8,128)(2,1)}, u32[]{:S(2)}, u32[]{:S(2)}) %collective-permute-start.4) | collective-permute-done | bytes 1064992 | tf_op jit(solution)/shard_map/ppermute | solution.py:185
  87.0 1.3 collective-permute-start.5
  88.3 0.7 broadcast_select_fusion.1
  89.0 2.7 %collective-permute-done.8.refs_3_ = bf16[520,1024]{1,0:T(8,128)(2,1)} collective-permute-done((bf16[520,1024]{1,0:T(8,128)(2,1)}, bf16[520,1024]{1,0:T(8,128)(2,1)}, u32[]{:S(2)}, u32[]{:S(2)}) %collective-permute-start.8) | collective-permute-done | bytes 1064992 | tf_op jit(solution)/shard_map/ppermute | solution.py:185
  91.7 0.7 broadcast_select_fusion.2
  92.4 0.1 scatter.11
  92.5 0.6 concatenate.45.refs_7_
  93.1 0.1 slice.132
  93.2 0.1 copy.42
  93.3 0.1 copy.39
  93.4 0.1 broadcast_compare_fusion
  93.5 0.6 reshape.196.flags_ref
  94.1 0.5 broadcast.153
  94.6 1.3 fusion.28
  95.9 33.2 %shard_map.85 = (f32[512,128]{1,0:T(8,128)}, f32[512,128]{1,0:T(8,128)}, f32[512,512]{1,0:T(8,128)}) custom-call(s32[24]{0:T(128)} %reshape.196.flags_ref, bf16[512,512]{1,0:T(8,128)(2,1)} %get-tuple-element.49.q_ref, bf16[520,1024]{1,0:T(8,128)(2,1)} %fusion.3.refs_0_, bf16[520,1024]{1,0:T(8,128)(2,1)} %collective-permute-done.3.refs_1_, ...), custom_call_target="tpu_custom_call" | custom-call | flops 3221225472 | bytes 10485760 | tf_op jit(solution)/shard_map/pallas_call | solution.py:164
  129.1 1.3 fusion.27
  130.4 0.2 fusion.22
  130.6 0.1 compare_convert_fusion
  130.7 0.6 reshape.194.flags_ref
  131.3 0.7 add_add_fusion.refs_3_
  132.0 12.9 %shard_map.86 = bf16[512,512]{1,0:T(8,128)(2,1)} custom-call(s32[8]{0:T(128)} %reshape.194.flags_ref, bf16[512,512]{1,0:T(8,128)(2,1)} %get-tuple-element.49.q_ref, bf16[520,1024]{1,0:T(8,128)(2,1)} %collective-permute-done.5.refs_0_, bf16[520,1024]{1,0:T(8,128)(2,1)} %collective-permute-done.7.refs_1_, s32[512,1]{1,0:T(8,128)} %copy.41.refs_6_.refs_2_, ...), custom_call_target="tpu_custom_call" | custom-call | flops 1073741824 | bytes 6291456 | tf_op jit(solution)/shard_map/pallas_call | solution.py:164
  144.9 1.1 dynamic-slice_bitcast_fusion.5
  146.1 0.7 convolution_convert_fusion
  146.8 0.1 collective-permute-start.10
  146.9 0.7 convolution_convert_fusion.1
  147.7 1.9 %collective-permute-done.10 = bf16[2,128,2048]{2,1,0:T(8,128)(2,1)S(1)} collective-permute-done((bf16[2,128,2048]{2,1,0:T(8,128)(2,1)S(1)}, bf16[2,128,2048]{2,1,0:T(8,128)(2,1)S(1)}, u32[]{:S(2)}, u32[]{:S(2)}) %collective-permute-start.10) | collective-permute-done | bytes 1048608 | tf_op jit(solution)/shard_map/ppermute | solution.py:26
  149.6 0.4 convert_add_fusion
  149.9 0.1 fusion.15
  150.0 1.5 collective-permute-start.11
  151.5 14.1 %collective-permute-done.11 = bf16[128,2048]{1,0:T(8,128)(2,1)S(1)} collective-permute-done((bf16[128,2048]{1,0:T(8,128)(2,1)S(1)}, bf16[128,2048]{1,0:T(8,128)(2,1)S(1)}, u32[]{:S(2)}, u32[]{:S(2)}) %collective-permute-start.11) | collective-permute-done | bytes 524320 | tf_op jit(solution)/shard_map/ppermute | solution.py:26
  165.6 1.0 fusion.8
  (40 shorter events, 0.3 us)
Async XLA Ops:
  0.6 145.4 %copy-start = (bf16[512,2048]{1,0:T(8,128)(2,1)S(1)}, bf16[512,2048]{1,0:T(8,128)(2,1)}, u32[]{:S(2)}) copy-start(bf16[512,2048]{1,0:T(8,128)(2,1)} %param.16) | copy-start | bytes 6291460
  4.8 15.3 %collective-permute-start.1 = (bf16[128,2048]{1,0:T(8,128)(2,1)S(1)}, bf16[128,2048]{1,0:T(8,128)(2,1)S(1)}, u32[]{:S(2)}, u32[]{:S(2)}) collective-permute-start(bf16[128,2048]{1,0:T(8,128)(2,1)S(1)} %fusion.6), channel_id=1, source_target_pairs={{0,2},{1,3},{2,0},{3,1},{4,6},{5,7},{6,4},{7,5},{8,10},{9,11},{10,... | collective-permute-start | bytes 1572872 | tf_op jit(solution)/shard_map/ppermute | solution.py:26
  6.2 13.8 %collective-permute-start = (bf16[128,2048]{1,0:T(8,128)(2,1)S(1)}, bf16[128,2048]{1,0:T(8,128)(2,1)}, u32[]{:S(2)}, u32[]{:S(2)}) collective-permute-start(bf16[128,2048]{1,0:T(8,128)(2,1)S(1)} %fusion.6), channel_id=1, source_target_pairs={{0,1},{1,0},{2,3},{3,2},{4,5},{5,4},{6,7},{7,6},{8,9},{9,8},{10,11... | collective-permute-start | bytes 1572872 | tf_op jit(solution)/shard_map/ppermute | solution.py:26
  6.3 8.8 %copy-start.4 = (s32[512]{0:T(512)S(1)}, s32[512]{0:T(512)}, u32[]{:S(2)}) copy-start(s32[512]{0:T(512)} %param.17) | copy-start | bytes 6148
  20.0 4.9 %collective-permute-start.2 = (bf16[128,2048]{1,0:T(8,128)(2,1)S(1)}, bf16[128,2048]{1,0:T(8,128)(2,1)S(1)}, u32[]{:S(2)}, u32[]{:S(2)}) collective-permute-start(bf16[128,2048]{1,0:T(8,128)(2,1)S(1)} %collective-permute-done.1), channel_id=1, source_target_pairs={{0,1},{1,0},{2,3},{3,2},{4,5},{5,4},{6,7},{7,6},{8,9},{9,8},{10,11... | collective-permute-start | bytes 1572872 | tf_op jit(solution)/shard_map/ppermute | solution.py:26
  20.0 4.9 %copy-start.2 = (bf16[2048,3,512]{0,2,1:T(8,128)(2,1)S(1)}, bf16[2048,3,512]{0,2,1:T(8,128)(2,1)}, u32[]{:S(2)}) copy-start(bf16[2048,3,512]{0,2,1:T(8,128)(2,1)} %copy.36) | copy-start | bytes 18874372
  28.2 100.9 %copy-start.3 = (bf16[512,512]{1,0:T(8,128)(2,1)}, bf16[512,512]{1,0:T(8,128)(2,1)S(1)}, u32[]{:S(2)}) copy-start(bf16[512,512]{1,0:T(8,128)(2,1)S(1)} %get-tuple-element.50) | copy-start | bytes 1572868
  28.2 12.1 %copy-start.6 = (s32[6]{0:T(128)S(1)}, s32[6]{0:T(128)}, u32[]{:S(2)}) copy-start(s32[6]{0:T(128)} %constant.146.clone.1) | copy-start | bytes 76
  28.2 12.2 %copy-start.5 = (f32[4]{0:T(128)S(1)}, f32[4]{0:T(128)}, u32[]{:S(2)}) copy-start(f32[4]{0:T(128)} %param.15) | copy-start | bytes 52
  30.9 28.8 %collective-permute-start.3 = (bf16[520,1024]{1,0:T(8,128)(2,1)}, bf16[520,1024]{1,0:T(8,128)(2,1)}, u32[]{:S(2)}, u32[]{:S(2)}) collective-permute-start(bf16[520,1024]{1,0:T(8,128)(2,1)} %fusion.3.refs_0_), channel_id=1, source_target_pairs={{0,16},{4,20},{8,24},{12,28},{16,32},{20,36},{24,40},{28,44},{32,4... | collective-permute-start | bytes 3194888 | tf_op jit(solution)/shard_map/ppermute | solution.py:185
  35.9 28.1 %collective-permute-start.6 = (bf16[520,1024]{1,0:T(8,128)(2,1)}, bf16[520,1024]{1,0:T(8,128)(2,1)}, u32[]{:S(2)}, u32[]{:S(2)}) collective-permute-start(bf16[520,1024]{1,0:T(8,128)(2,1)} %fusion.3.refs_0_), channel_id=1, source_target_pairs={{0,4},{4,8},{8,12},{16,20},{20,24},{24,28},{32,36},{36,40},{40,44}... | collective-permute-start | bytes 3194888 | tf_op jit(solution)/shard_map/ppermute | solution.py:185
  40.6 26.5 %collective-permute-start.9 = (bf16[520,1024]{1,0:T(8,128)(2,1)}, bf16[520,1024]{1,0:T(8,128)(2,1)}, u32[]{:S(2)}, u32[]{:S(2)}) collective-permute-start(bf16[520,1024]{1,0:T(8,128)(2,1)} %fusion.3.refs_0_), channel_id=1, source_target_pairs={{0,12},{16,28},{32,44},{48,60},{64,76},{80,92},{96,108},{112,124},... | collective-permute-start | bytes 3194888 | tf_op jit(solution)/shard_map/ppermute | solution.py:185
  59.7 27.3 %collective-permute-start.4 = (bf16[520,1024]{1,0:T(8,128)(2,1)}, bf16[520,1024]{1,0:T(8,128)(2,1)}, u32[]{:S(2)}, u32[]{:S(2)}) collective-permute-start(bf16[520,1024]{1,0:T(8,128)(2,1)} %collective-permute-done.3.refs_1_), channel_id=1, source_target_pairs={{4,0},{8,4},{12,8},{20,16},{24,20},{28,24},{36,32},{40,36},{44,40}... | collective-permute-start | bytes 3194888 | tf_op jit(solution)/shard_map/ppermute | solution.py:185
  61.6 30.1 %collective-permute-start.8 = (bf16[520,1024]{1,0:T(8,128)(2,1)}, bf16[520,1024]{1,0:T(8,128)(2,1)}, u32[]{:S(2)}, u32[]{:S(2)}) collective-permute-start(bf16[520,1024]{1,0:T(8,128)(2,1)} %collective-permute-done.3.refs_1_), channel_id=1, source_target_pairs={{12,0},{28,16},{44,32},{60,48},{76,64},{92,80},{108,96},{124,112},... | collective-permute-start | bytes 3194888 | tf_op jit(solution)/shard_map/ppermute | solution.py:185
  64.0 30.1 %collective-permute-start.7 = (bf16[520,1024]{1,0:T(8,128)(2,1)}, bf16[520,1024]{1,0:T(8,128)(2,1)}, u32[]{:S(2)}, u32[]{:S(2)}) collective-permute-start(bf16[520,1024]{1,0:T(8,128)(2,1)} %collective-permute-done.6.refs_2_), channel_id=1, source_target_pairs={{4,8},{8,12},{20,24},{24,28},{36,40},{40,44},{52,56},{56,60},{68,7... | collective-permute-start | bytes 3194888 | tf_op jit(solution)/shard_map/ppermute | solution.py:185
  87.0 42.1 %collective-permute-start.5 = (bf16[520,1024]{1,0:T(8,128)(2,1)}, bf16[520,1024]{1,0:T(8,128)(2,1)}, u32[]{:S(2)}, u32[]{:S(2)}) collective-permute-start(bf16[520,1024]{1,0:T(8,128)(2,1)} %collective-permute-done.4.refs_4_), channel_id=1, source_target_pairs={{4,0},{8,4},{20,16},{24,20},{36,32},{40,36},{52,48},{56,52},{68,64... | collective-permute-start | bytes 3194888 | tf_op jit(solution)/shard_map/ppermute | solution.py:185
  146.8 2.7 %collective-permute-start.10 = (bf16[2,128,2048]{2,1,0:T(8,128)(2,1)S(1)}, bf16[2,128,2048]{2,1,0:T(8,128)(2,1)S(1)}, u32[]{:S(2)}, u32[]{:S(2)}) collective-permute-start(bf16[2,128,2048]{2,1,0:T(8,128)(2,1)S(1)} %bitcast.42), channel_id=1, source_target_pairs={{0,1},{1,0},{2,3},{3,2},{4,5},{5,4},{6,7},{7,6},{8,9},{9,8},{10,11... | collective-permute-start | bytes 3145736 | tf_op jit(solution)/shard_map/ppermute | solution.py:26
  149.6 16.0 %copy-start.1 = (bf16[128,2048]{1,0:T(8,128)(2,1)S(1)}, bf16[128,2048]{1,0:T(8,128)(2,1)}, u32[]{:S(2)}) copy-start(bf16[128,2048]{1,0:T(8,128)(2,1)} %param.12) | copy-start | bytes 1572868
  150.0 15.6 %collective-permute-start.11 = (bf16[128,2048]{1,0:T(8,128)(2,1)S(1)}, bf16[128,2048]{1,0:T(8,128)(2,1)S(1)}, u32[]{:S(2)}, u32[]{:S(2)}) collective-permute-start(bf16[128,2048]{1,0:T(8,128)(2,1)S(1)} %fusion.15), channel_id=1, source_target_pairs={{0,2},{1,3},{2,0},{3,1},{4,6},{5,7},{6,4},{7,5},{8,10},{9,11},{10,... | collective-permute-start | bytes 1572872 | tf_op jit(solution)/shard_map/ppermute | solution.py:26

commit v15 on v13

--- a/solution.py
+++ b/solution.py
@@ -99,7 +99,7 @@
                     m_sc[h, rows, :] = m_new
                     return carry
 
-                lax.fori_loop(0, heads, one_head, 0)
+                lax.fori_loop(0, heads, one_head, 0, unroll=2)
 
             if diag:
                 body()

time: 169 us -> 167 us (0.988)
  the two profiles are of different devices: /device:TPU:14 before, /device:TPU:142 now
where the time goes in v15:
time: 167 us
  waiting for transfers between devices  57.6 us (34%)
  Pallas kernels  46.1 us (28%)
  starting transfers between devices  22.1 us (13%)
  local copies, waits for them, and re-layouts  18.1 us (11%)
  other arithmetic  13.7 us (8%)
  matrix products  8.23 us (5%)
    pallas_call x2, Pallas kernels, attention_part(): pl.pallas_call(functools.partial(part_kernel, n_buf, own, last), out_shap...  46.1 us
    ppermute x7, waiting for transfers between devices, moved(): return lax.ppermute(value, 'seq', pairs)  36.8 us
    ppermute x5, waiting for transfers between devices, swapped(): lax.ppermute(value, axis, [(source, source ^ mask) for source in range(co...  20.9 us
    ppermute x7, starting transfers between devices, moved(): return lax.ppermute(value, 'seq', pairs)  19 us
    unnamed x23, local copies, waits for them, and re-layouts  9.1 us
    dot_general x2, matrix products, project_rows(): jnp.dot(rows, joined, preferred_element_type=jnp.float32)  6.75 us
  transfers between devices with their start and end apart: 12, of which 5 were waited for; matrix products, arithmetic and copies ran while one was open for 14% of the time, Pallas kernels for 20%

profile of v15, /device:TPU:142, one launch (start us, length us, event | category | flops | bytes accessed | tf_op | source)
XLA Modules:
  0.0 166.8 jit_solution(4449292447061535660)
XLA Ops:
  0.6 0.0 copy-start
  0.7 1.3 convert_reduce_fusion
  2.0 1.3 fusion.4
  3.3 1.4 fusion.6
  4.8 1.5 collective-permute-start.1
  6.3 0.0 collective-permute-start
  6.3 8.9 %copy.20 = bf16[2048,3,512]{0,2,1:T(8,128)(2,1)} copy(bf16[2048,3,512]{2,0,1:T(8,128)(2,1)} %param.14) | data formatting | bytes 12582912 | tf_op args[2]
  15.1 4.9 %collective-permute-done.1 = bf16[128,2048]{1,0:T(8,128)(2,1)S(1)} collective-permute-done((bf16[128,2048]{1,0:T(8,128)(2,1)S(1)}, bf16[128,2048]{1,0:T(8,128)(2,1)S(1)}, u32[]{:S(2)}, u32[]{:S(2)}) %collective-permute-start.1) | collective-permute-done | bytes 524320 | tf_op jit(solution)/shard_map/ppermute | solution.py:26
  20.0 0.0 collective-permute-done
  20.0 4.9 %convolution_convert_fusion.3 = bf16[256,1536]{1,0:T(8,128)(2,1)S(1)} fusion(bf16[2048,1536]{0,1:T(8,128)(2,1)} %bitcast.39, bf16[128,2048]{1,0:T(8,128)(2,1)} %collective-permute-done, bf16[128,2048]{1,0:T(8,128)(2,1)S(1)} %fusion.6), kind=kOutput, calls=%fused_computation.3 | convolution fusion | flops 1613103104 | bytes 8126464 | tf_op jit(solution)/shard_map/dot_general | solution.py:217
  25.0 0.0 collective-permute-done.2
  25.0 1.8 %convolution_convert_fusion.2 = bf16[256,1536]{1,0:T(8,128)(2,1)S(1)} fusion(bf16[2048,1536]{0,1:T(8,128)(2,1)S(1)} %bitcast.40, bf16[128,2048]{1,0:T(8,128)(2,1)S(1)} %collective-permute-done.2, bf16[128,2048]{1,0:T(8,128)(2,1)S(1)} %collective-permute-done.1), kind=kOutput, calls=%fused_computation.2 | convolution fusion | flops 1613103104 | bytes 8126464 | tf_op jit(solution)/shard_map/dot_general | solution.py:217
  26.8 0.1 pad_maximum_fusion
  26.9 0.1 dynamic-slice_bitcast_fusion.3
  27.1 0.1 pad_maximum_fusion.1
  27.2 1.1 fusion.27
  28.3 1.5 copy.21
  29.7 1.1 fusion.3.refs_0_
  30.9 2.9 %collective-permute-start.3 = (bf16[520,1024]{1,0:T(8,128)(2,1)}, bf16[520,1024]{1,0:T(8,128)(2,1)}, u32[]{:S(2)}, u32[]{:S(2)}) collective-permute-start(bf16[520,1024]{1,0:T(8,128)(2,1)} %fusion.3.refs_0_), channel_id=1, source_target_pairs={{0,16},{4,20},{8,24},{12,28},{16,32},{20,36},{24,40},{28,44},{32,4... | collective-permute-start | bytes 3194888 | tf_op jit(solution)/shard_map/ppermute | solution.py:185
  33.8 3.5 %collective-permute-start.6 = (bf16[520,1024]{1,0:T(8,128)(2,1)}, bf16[520,1024]{1,0:T(8,128)(2,1)}, u32[]{:S(2)}, u32[]{:S(2)}) collective-permute-start(bf16[520,1024]{1,0:T(8,128)(2,1)} %fusion.3.refs_0_), channel_id=1, source_target_pairs={{0,4},{4,8},{8,12},{16,20},{20,24},{24,28},{32,36},{36,40},{40,44}... | collective-permute-start | bytes 3194888 | tf_op jit(solution)/shard_map/ppermute | solution.py:185
  37.3 1.7 collective-permute-start.9
  39.0 21.2 %collective-permute-done.3.refs_1_ = bf16[520,1024]{1,0:T(8,128)(2,1)} collective-permute-done((bf16[520,1024]{1,0:T(8,128)(2,1)}, bf16[520,1024]{1,0:T(8,128)(2,1)}, u32[]{:S(2)}, u32[]{:S(2)}) %collective-permute-start.3) | collective-permute-done | bytes 1064992 | tf_op jit(solution)/shard_map/ppermute | solution.py:185
  60.2 2.4 %collective-permute-start.4 = (bf16[520,1024]{1,0:T(8,128)(2,1)}, bf16[520,1024]{1,0:T(8,128)(2,1)}, u32[]{:S(2)}, u32[]{:S(2)}) collective-permute-start(bf16[520,1024]{1,0:T(8,128)(2,1)} %collective-permute-done.3.refs_1_), channel_id=1, source_target_pairs={{4,0},{8,4},{12,8},{20,16},{24,20},{28,24},{36,32},{40,36},{44,40}... | collective-permute-start | bytes 3194888 | tf_op jit(solution)/shard_map/ppermute | solution.py:185
  62.6 0.1 broadcast_multiply_fusion.1
  62.6 1.7 %collective-permute-start.8 = (bf16[520,1024]{1,0:T(8,128)(2,1)}, bf16[520,1024]{1,0:T(8,128)(2,1)}, u32[]{:S(2)}, u32[]{:S(2)}) collective-permute-start(bf16[520,1024]{1,0:T(8,128)(2,1)} %collective-permute-done.3.refs_1_), channel_id=1, source_target_pairs={{12,0},{28,16},{44,32},{60,48},{76,64},{92,80},{108,96},{124,112},... | collective-permute-start | bytes 3194888 | tf_op jit(solution)/shard_map/ppermute | solution.py:185
  64.4 0.1 add_convert_fusion
  64.5 0.9 copy.26.refs_4_.refs_1_
  65.4 0.1 mul.66
  65.4 0.6 concatenate.46.refs_3_
  66.0 0.1 slice_reduce_fusion
  66.2 0.7 broadcast_multiply_fusion.refs_6_
  66.8 4.5 %collective-permute-start.7 = (bf16[520,1024]{1,0:T(8,128)(2,1)}, bf16[520,1024]{1,0:T(8,128)(2,1)}, u32[]{:S(2)}, u32[]{:S(2)}) collective-permute-start(bf16[520,1024]{1,0:T(8,128)(2,1)} %collective-permute-done.6), channel_id=1, source_target_pairs={{4,8},{8,12},{20,24},{24,28},{36,40},{40,44},{52,56},{56,60},{68,7... | collective-permute-start | bytes 3194888 | tf_op jit(solution)/shard_map/ppermute | solution.py:185
  71.3 0.7 broadcast_select_fusion.5
  72.0 15.5 %collective-permute-done.4 = bf16[520,1024]{1,0:T(8,128)(2,1)} collective-permute-done((bf16[520,1024]{1,0:T(8,128)(2,1)}, bf16[520,1024]{1,0:T(8,128)(2,1)}, u32[]{:S(2)}, u32[]{:S(2)}) %collective-permute-start.4) | collective-permute-done | bytes 1064992 | tf_op jit(solution)/shard_map/ppermute | solution.py:185
  87.5 2.4 %collective-permute-start.5 = (bf16[520,1024]{1,0:T(8,128)(2,1)}, bf16[520,1024]{1,0:T(8,128)(2,1)}, u32[]{:S(2)}, u32[]{:S(2)}) collective-permute-start(bf16[520,1024]{1,0:T(8,128)(2,1)} %collective-permute-done.4), channel_id=1, source_target_pairs={{4,0},{8,4},{20,16},{24,20},{36,32},{40,36},{52,48},{56,52},{68,64... | collective-permute-start | bytes 3194888 | tf_op jit(solution)/shard_map/ppermute | solution.py:185
  89.9 1.4 broadcast_select_fusion.refs_3_
  91.3 0.0 collective-permute-done.8
  91.3 1.7 %broadcast_select_fusion.1.refs_2_ = bf16[520,1024]{1,0:T(8,128)(2,1)S(1)} fusion(bf16[520,1024]{1,0:T(8,128)(2,1)} %collective-permute-done.8, bf16[520,1024]{1,0:T(8,128)(2,1)} %collective-permute-done.6, pred[]{:T(512)S(6)} %eq.5), kind=kLoop, calls=%fused_computation.16 | loop fusion | flops 532480 | bytes 3194881 | tf_op jit(solution)/shard_map/jit(_where)/select_n | solution.py:199
  93.2 0.1 slice.121
  93.3 0.1 copy.28
  93.4 0.1 copy.24
  93.5 0.1 broadcast_compare_fusion
  93.6 0.6 reshape.251.flags_ref
  94.2 0.6 concatenate.47.refs_5_
  94.8 33.2 %shard_map.85 = (f32[512,128]{1,0:T(8,128)}, f32[512,128]{1,0:T(8,128)}, f32[512,512]{1,0:T(8,128)}) custom-call(s32[16]{0:T(128)} %reshape.251.flags_ref, bf16[512,512]{1,0:T(8,128)(2,1)} %get-tuple-element.47.q_ref, bf16[520,1024]{1,0:T(8,128)(2,1)} %fusion.3.refs_0_, bf16[520,1024]{1,0:T(8,128)(2,1)} %collective-permute-done.3.refs_1_, ...), custom_call_target="tpu_custom_call" | custom-call | flops 2147483648 | bytes 8388608 | tf_op jit(solution)/shard_map/pallas_call | solution.py:164
  128.0 1.4 broadcast_select_fusion.2.refs_0_
  129.3 0.7 broadcast.176
  130.0 0.7 fusion.26
  130.7 0.1 slice.115
  130.8 0.1 copy.27
  130.9 0.1 compare_convert_fusion
  131.0 0.6 reshape.249.flags_ref
  131.6 0.6 concatenate.45.refs_2_
  132.2 13.0 %shard_map.86 = bf16[512,512]{1,0:T(8,128)(2,1)} custom-call(s32[4]{0:T(128)} %reshape.249.flags_ref, bf16[512,512]{1,0:T(8,128)(2,1)} %get-tuple-element.47.q_ref, bf16[520,1024]{1,0:T(8,128)(2,1)} %copy-done.3, s32[512,1]{1,0:T(8,128)} %copy.26.refs_4_.refs_1_, s32[8,512]{1,0:T(8,128)} %concatenate.45.refs_2_, f32[8,512]{1,0:T(8,128)} %concatenate.46.refs_3_, ...), custom_call_target="tpu_custom_call" | custom-call | flops 536870912 | bytes 5242880 | tf_op jit(solution)/shard_map/pallas_call | solution.py:164
  145.1 1.1 dynamic-slice_bitcast_fusion.5
  146.3 0.7 convolution_convert_fusion
  147.0 0.1 collective-permute-start.10
  147.1 0.7 convolution_convert_fusion.1
  147.9 1.9 %collective-permute-done.10 = bf16[2,128,2048]{2,1,0:T(8,128)(2,1)S(1)} collective-permute-done((bf16[2,128,2048]{2,1,0:T(8,128)(2,1)S(1)}, bf16[2,128,2048]{2,1,0:T(8,128)(2,1)S(1)}, u32[]{:S(2)}, u32[]{:S(2)}) %collective-permute-start.10) | collective-permute-done | bytes 1048608 | tf_op jit(solution)/shard_map/ppermute | solution.py:26
  149.8 0.4 convert_add_fusion
  150.1 0.1 fusion.15
  150.2 1.5 collective-permute-start.11
  151.7 14.1 %collective-permute-done.11 = bf16[128,2048]{1,0:T(8,128)(2,1)S(1)} collective-permute-done((bf16[128,2048]{1,0:T(8,128)(2,1)S(1)}, bf16[128,2048]{1,0:T(8,128)(2,1)S(1)}, u32[]{:S(2)}, u32[]{:S(2)}) %collective-permute-start.11) | collective-permute-done | bytes 524320 | tf_op jit(solution)/shard_map/ppermute | solution.py:26
  165.8 1.0 fusion.8
  (43 shorter events, 0.3 us)
Async XLA Ops:
  0.6 145.6 %copy-start = (bf16[512,2048]{1,0:T(8,128)(2,1)S(1)}, bf16[512,2048]{1,0:T(8,128)(2,1)}, u32[]{:S(2)}) copy-start(bf16[512,2048]{1,0:T(8,128)(2,1)} %param.16) | copy-start | bytes 6291460
  0.6 5.6 %copy-start.7 = (s32[512]{0:T(512)S(1)}, s32[512]{0:T(512)}, u32[]{:S(2)}) copy-start(s32[512]{0:T(512)} %param.17) | copy-start | bytes 6148
  4.8 15.3 %collective-permute-start.1 = (bf16[128,2048]{1,0:T(8,128)(2,1)S(1)}, bf16[128,2048]{1,0:T(8,128)(2,1)S(1)}, u32[]{:S(2)}, u32[]{:S(2)}) collective-permute-start(bf16[128,2048]{1,0:T(8,128)(2,1)S(1)} %fusion.6), channel_id=1, source_target_pairs={{0,2},{1,3},{2,0},{3,1},{4,6},{5,7},{6,4},{7,5},{8,10},{9,11},{10,... | collective-permute-start | bytes 1572872 | tf_op jit(solution)/shard_map/ppermute | solution.py:26
  6.3 13.8 %collective-permute-start = (bf16[128,2048]{1,0:T(8,128)(2,1)S(1)}, bf16[128,2048]{1,0:T(8,128)(2,1)}, u32[]{:S(2)}, u32[]{:S(2)}) collective-permute-start(bf16[128,2048]{1,0:T(8,128)(2,1)S(1)} %fusion.6), channel_id=1, source_target_pairs={{0,1},{1,0},{2,3},{3,2},{4,5},{5,4},{6,7},{7,6},{8,9},{9,8},{10,11... | collective-permute-start | bytes 1572872 | tf_op jit(solution)/shard_map/ppermute | solution.py:26
  20.0 4.9 %collective-permute-start.2 = (bf16[128,2048]{1,0:T(8,128)(2,1)S(1)}, bf16[128,2048]{1,0:T(8,128)(2,1)S(1)}, u32[]{:S(2)}, u32[]{:S(2)}) collective-permute-start(bf16[128,2048]{1,0:T(8,128)(2,1)S(1)} %collective-permute-done.1), channel_id=1, source_target_pairs={{0,1},{1,0},{2,3},{3,2},{4,5},{5,4},{6,7},{7,6},{8,9},{9,8},{10,11... | collective-permute-start | bytes 1572872 | tf_op jit(solution)/shard_map/ppermute | solution.py:26
  20.0 4.9 %copy-start.2 = (bf16[2048,3,512]{0,2,1:T(8,128)(2,1)S(1)}, bf16[2048,3,512]{0,2,1:T(8,128)(2,1)}, u32[]{:S(2)}) copy-start(bf16[2048,3,512]{0,2,1:T(8,128)(2,1)} %copy.20) | copy-start | bytes 18874372
  28.3 63.0 %copy-start.4 = (bf16[512,512]{1,0:T(8,128)(2,1)}, bf16[512,512]{1,0:T(8,128)(2,1)S(1)}, u32[]{:S(2)}) copy-start(bf16[512,512]{1,0:T(8,128)(2,1)S(1)} %get-tuple-element.48) | copy-start | bytes 1572868
  28.3 34.3 %copy-start.8 = (f32[4]{0:T(128)S(1)}, f32[4]{0:T(128)}, u32[]{:S(2)}) copy-start(f32[4]{0:T(128)} %param.15) | copy-start | bytes 52
  28.3 36.1 %copy-start.9 = (s32[4]{0:T(128)S(1)}, s32[4]{0:T(128)}, u32[]{:S(2)}) copy-start(s32[4]{0:T(128)} %constant.147.clone.1) | copy-start | bytes 52
  30.9 29.3 %collective-permute-start.3 = (bf16[520,1024]{1,0:T(8,128)(2,1)}, bf16[520,1024]{1,0:T(8,128)(2,1)}, u32[]{:S(2)}, u32[]{:S(2)}) collective-permute-start(bf16[520,1024]{1,0:T(8,128)(2,1)} %fusion.3.refs_0_), channel_id=1, source_target_pairs={{0,16},{4,20},{8,24},{12,28},{16,32},{20,36},{24,40},{28,44},{32,4... | collective-permute-start | bytes 3194888 | tf_op jit(solution)/shard_map/ppermute | solution.py:185
  33.8 33.0 %collective-permute-start.6 = (bf16[520,1024]{1,0:T(8,128)(2,1)}, bf16[520,1024]{1,0:T(8,128)(2,1)}, u32[]{:S(2)}, u32[]{:S(2)}) collective-permute-start(bf16[520,1024]{1,0:T(8,128)(2,1)} %fusion.3.refs_0_), channel_id=1, source_target_pairs={{0,4},{4,8},{8,12},{16,20},{20,24},{24,28},{32,36},{36,40},{40,44}... | collective-permute-start | bytes 3194888 | tf_op jit(solution)/shard_map/ppermute | solution.py:185
  37.3 52.6 %collective-permute-start.9 = (bf16[520,1024]{1,0:T(8,128)(2,1)}, bf16[520,1024]{1,0:T(8,128)(2,1)}, u32[]{:S(2)}, u32[]{:S(2)}) collective-permute-start(bf16[520,1024]{1,0:T(8,128)(2,1)} %fusion.3.refs_0_), channel_id=1, source_target_pairs={{0,12},{16,28},{32,44},{48,60},{64,76},{80,92},{96,108},{112,124},... | collective-permute-start | bytes 3194888 | tf_op jit(solution)/shard_map/ppermute | solution.py:185
  60.2 27.3 %collective-permute-start.4 = (bf16[520,1024]{1,0:T(8,128)(2,1)}, bf16[520,1024]{1,0:T(8,128)(2,1)}, u32[]{:S(2)}, u32[]{:S(2)}) collective-permute-start(bf16[520,1024]{1,0:T(8,128)(2,1)} %collective-permute-done.3.refs_1_), channel_id=1, source_target_pairs={{4,0},{8,4},{12,8},{20,16},{24,20},{28,24},{36,32},{40,36},{44,40}... | collective-permute-start | bytes 3194888 | tf_op jit(solution)/shard_map/ppermute | solution.py:185
  62.6 28.7 %collective-permute-start.8 = (bf16[520,1024]{1,0:T(8,128)(2,1)}, bf16[520,1024]{1,0:T(8,128)(2,1)}, u32[]{:S(2)}, u32[]{:S(2)}) collective-permute-start(bf16[520,1024]{1,0:T(8,128)(2,1)} %collective-permute-done.3.refs_1_), channel_id=1, source_target_pairs={{12,0},{28,16},{44,32},{60,48},{76,64},{92,80},{108,96},{124,112},... | collective-permute-start | bytes 3194888 | tf_op jit(solution)/shard_map/ppermute | solution.py:185
  66.8 61.1 %collective-permute-start.7 = (bf16[520,1024]{1,0:T(8,128)(2,1)}, bf16[520,1024]{1,0:T(8,128)(2,1)}, u32[]{:S(2)}, u32[]{:S(2)}) collective-permute-start(bf16[520,1024]{1,0:T(8,128)(2,1)} %collective-permute-done.6), channel_id=1, source_target_pairs={{4,8},{8,12},{20,24},{24,28},{36,40},{40,44},{52,56},{56,60},{68,7... | collective-permute-start | bytes 3194888 | tf_op jit(solution)/shard_map/ppermute | solution.py:185
  87.5 40.4 %collective-permute-start.5 = (bf16[520,1024]{1,0:T(8,128)(2,1)}, bf16[520,1024]{1,0:T(8,128)(2,1)}, u32[]{:S(2)}, u32[]{:S(2)}) collective-permute-start(bf16[520,1024]{1,0:T(8,128)(2,1)} %collective-permute-done.4), channel_id=1, source_target_pairs={{4,0},{8,4},{20,16},{24,20},{36,32},{40,36},{52,48},{56,52},{68,64... | collective-permute-start | bytes 3194888 | tf_op jit(solution)/shard_map/ppermute | solution.py:185
  91.3 1.8 %copy-start.5 = (bf16[520,1024]{1,0:T(8,128)(2,1)}, bf16[520,1024]{1,0:T(8,128)(2,1)S(1)}, u32[]{:S(2)}) copy-start(bf16[520,1024]{1,0:T(8,128)(2,1)S(1)} %broadcast_select_fusion.refs_3_) | copy-start | bytes 3194884
  93.1 1.7 %copy-start.6 = (bf16[520,1024]{1,0:T(8,128)(2,1)}, bf16[520,1024]{1,0:T(8,128)(2,1)S(1)}, u32[]{:S(2)}) copy-start(bf16[520,1024]{1,0:T(8,128)(2,1)S(1)} %broadcast_select_fusion.1.refs_2_) | copy-start | bytes 3194884
  129.3 2.9 %copy-start.3 = (bf16[520,1024]{1,0:T(8,128)(2,1)}, bf16[520,1024]{1,0:T(8,128)(2,1)S(1)}, u32[]{:S(2)}) copy-start(bf16[520,1024]{1,0:T(8,128)(2,1)S(1)} %broadcast_select_fusion.2.refs_0_) | copy-start | bytes 3194884
  147.0 2.7 %collective-permute-start.10 = (bf16[2,128,2048]{2,1,0:T(8,128)(2,1)S(1)}, bf16[2,128,2048]{2,1,0:T(8,128)(2,1)S(1)}, u32[]{:S(2)}, u32[]{:S(2)}) collective-permute-start(bf16[2,128,2048]{2,1,0:T(8,128)(2,1)S(1)} %bitcast.45), channel_id=1, source_target_pairs={{0,1},{1,0},{2,3},{3,2},{4,5},{5,4},{6,7},{7,6},{8,9},{9,8},{10,11... | collective-permute-start | bytes 3145736 | tf_op jit(solution)/shard_map/ppermute | solution.py:26
  149.8 16.0 %copy-start.1 = (bf16[128,2048]{1,0:T(8,128)(2,1)S(1)}, bf16[128,2048]{1,0:T(8,128)(2,1)}, u32[]{:S(2)}) copy-start(bf16[128,2048]{1,0:T(8,128)(2,1)} %param.12) | copy-start | bytes 1572868
  150.2 15.6 %collective-permute-start.11 = (bf16[128,2048]{1,0:T(8,128)(2,1)S(1)}, bf16[128,2048]{1,0:T(8,128)(2,1)S(1)}, u32[]{:S(2)}, u32[]{:S(2)}) collective-permute-start(bf16[128,2048]{1,0:T(8,128)(2,1)S(1)} %fusion.15), channel_id=1, source_target_pairs={{0,2},{1,3},{2,0},{3,1},{4,6},{5,7},{6,4},{7,5},{8,10},{9,11},{10,... | collective-permute-start | bytes 1572872 | tf_op jit(solution)/shard_map/ppermute | solution.py:26
